TPU v7x, 32 devices: a whole 2x2x4 slice. The times are simulated.
32 devices in a mesh: groups: 2 (over y), scan: 4 (over z), angle: 2 (over x), tile: 2 (over core).
Axes of the slice: x: 2, y: 2, z: 4, core: 2. Of those that a mesh axis runs over, the one named last changes fastest.
Arguments:
- transmission: float32 [8, 2, 256, 256], P(('groups', 'angle', 'tile'), None, 'scan'), parts along dimension 0, may hold values from -4 to 4
- scaled_dual: float32 [8, 2, 256, 256], P(('groups', 'angle', 'tile'), None, 'scan'), parts along dimension 0, may hold values from -4 to 4
- projected: float32 [8, 2, 256, 256], P(('groups', 'angle', 'tile'), None, 'scan'), parts along dimension 0, may hold values from -4 to 4
- volume: float32 [4, 8, 256, 256], P('groups', ('angle', 'tile'), 'scan'), parts along dimension 0, may hold values from -0.4 to 0.4
- intensities: bfloat16 [8, 16, 128, 128], P(('groups', 'angle', 'tile'), 'scan'), parts along dimension 0, may hold values from 0 to 2
- probe_wave: float32 [4, 128, 128], P('groups'), parts along dimension 0, may hold values from -4 to 4
- slot_first_rows: int32 [8, 16], P(('groups', 'angle', 'tile'), 'scan'), parts along dimension 0, may hold values from 0 to 128
- slot_first_columns: int32 [8, 16], P(('groups', 'angle', 'tile'), 'scan'), parts along dimension 0, may hold values from 0 to 64
- patch_counts: int32 [8, 4], P(('groups', 'angle', 'tile'), 'scan'), parts along dimension 0, may hold values from 1 to 4, as said below
- shift_table: int32 [4, 8], P(None, ('angle', 'tile')), may hold values from -63 to 63, as said below
- tap_weight: float32 [4, 8], P(None, ('angle', 'tile')), may hold values from 0 to 1
Outputs:
- new_transmission: float32 [8, 2, 256, 256], P(('groups', 'angle', 'tile'), None, 'scan'), parts along dimension 0
- new_dual: float32 [8, 2, 256, 256], P(('groups', 'angle', 'tile'), None, 'scan'), parts along dimension 0
- new_volume: float32 [4, 8, 256, 256], P('groups', ('angle', 'tile'), 'scan'), parts along dimension 0
- new_projected: float32 [8, 2, 256, 256], P(('groups', 'angle', 'tile'), None, 'scan'), parts along dimension 0
There are 2 independent parts, one for each index of `groups`. A program takes and returns all parts, laid end to end along the dimension named above; an argument that names none is the same for every part. Nothing has to cross between parts.
Inputs may be any that keep to these rules, and one draw needn't show every extreme that they name: Only the first patch_counts[a, r] slots of region r are live; for each angle some region has all 4 slots live. `shift_table`: for every angle the shift is s = (slope * (2 y - 7)) // 7 for an integer slope of that angle from 1 to 63; some angle has slope 64 - 1.
All inputs are finite; a program needn't handle non-finite values.
Results may differ from a plain program's by a relative error of at most 0.0003.
Values sent between devices are 32-bit elements; how exact they have to be, the bound alone decides.
No kernel may reach another device: no remote copies, remote signals or barrier semaphores. Data moves between devices by JAX's collectives and lax.ppermute only.
A program may use at most 64 MiB of HBM per device.

v0:
```python
from functools import partial
import math

import jax
import jax.numpy as jnp
from jax import lax
from jax.sharding import PartitionSpec as P

penalty = 4.0
amplitude_step = 0.25
tv_weight = 1.0
smoothing = 0.05
step_size = 0.008


def with_halo(block, sides, width):
    for axis, dim in sides:
        count = lax.axis_size(axis)
        forward = [(i, i + 1) for i in range(count - 1)]
        backward = [(target, source) for source, target in forward]
        low = lax.ppermute(
            lax.slice_in_dim(block, block.shape[dim] - width, None, axis=dim), axis, forward
        )
        high = lax.ppermute(lax.slice_in_dim(block, 0, width, axis=dim), axis, backward)
        block = jnp.concatenate([low, block, high], axis=dim)
    return block


def from_behind(block, axis, distance):
    devices = range(lax.axis_size(axis))
    route = [(i - distance, i) for i in devices if i - distance in devices]
    return lax.ppermute(block, axis, route)


def widen(array_in, width):
    return with_halo(array_in, (("scan", 2),), width)


def fold_rims(extended, width):
    rims = jnp.concatenate([extended[:, :, :width], extended[:, :, 2 * width :]], axis=2)
    received = widen(rims, width)
    return extended[:, :, width : 2 * width] + received[:, :, :width] + received[:, :, 3 * width :]


def directed(array_in, upper):

    def going_up(values):
        return from_behind(values, "scan", 1)

    def going_down(values):
        return from_behind(values, "scan", -1)

    return lax.cond(upper, going_up, going_down, array_in)


def dft_tables(length):
    grid_ids = jnp.arange(length, dtype=jnp.int32)
    phases = grid_ids[:, None] * grid_ids[None, :] % length
    radians = phases.astype(jnp.float32) * (2.0 * math.pi / length)
    factor = 1.0 / math.sqrt(length)
    return (jnp.cos(radians) * factor, -jnp.sin(radians) * factor)


def times_left(table, values):
    return jnp.einsum("ij,bjk->bik", table, values, precision=lax.Precision.HIGHEST)


def times_right(values, table):
    return jnp.einsum("bij,jk->bik", values, table, precision=lax.Precision.HIGHEST)


def transform(real_part, imaginary, cosine_table, sine_table):
    half_real = times_left(cosine_table, real_part) - times_left(sine_table, imaginary)
    half_imaginary = times_left(cosine_table, imaginary) + times_left(sine_table, real_part)
    full_real = times_right(half_real, cosine_table) - times_right(half_imaginary, sine_table)
    full_imaginary = times_right(half_real, sine_table) + times_right(half_imaginary, cosine_table)
    return (full_real, full_imaginary)


def patch_sums(
    wide_plane,
    rows_one,
    columns_one,
    intensity_one,
    count_one,
    probe_wave,
    cosine_table,
    sine_table,
):
    patch_side = probe_wave.shape[1]

    def window(row_start, col_start):
        return lax.dynamic_slice(wide_plane, (0, col_start, row_start), (2, patch_side, patch_side))

    windows = jax.vmap(window)(rows_one, columns_one)
    probe_real = probe_wave[0]
    probe_imaginary = probe_wave[1]
    wave_real = probe_real * windows[:, 0] - probe_imaginary * windows[:, 1]
    wave_imaginary = probe_real * windows[:, 1] + probe_imaginary * windows[:, 0]
    far_real, far_imaginary = transform(wave_real, wave_imaginary, cosine_table, sine_table)
    factor = 1.0 - amplitude_step * (
        far_real * far_real + far_imaginary * far_imaginary - intensity_one.astype(jnp.float32)
    )
    near_real, near_imaginary = transform(
        far_real * factor, far_imaginary * factor, cosine_table, -sine_table
    )
    active = (jnp.arange(rows_one.shape[0]) < count_one[0]).astype(jnp.float32)[:, None, None]
    update_real = (probe_real * near_real + probe_imaginary * near_imaginary) * active
    update_imaginary = (probe_real * near_imaginary - probe_imaginary * near_real) * active
    density = (probe_real * probe_real + probe_imaginary * probe_imaginary)[None] * active
    contrib = jnp.stack([update_real, update_imaginary, density], axis=1)
    running_start = jnp.zeros((3, wide_plane.shape[1], wide_plane.shape[2]), jnp.float32)

    def add_patch(slot_number, running):
        corner = (0, columns_one[slot_number], rows_one[slot_number])
        current = lax.dynamic_slice(running, corner, (3, patch_side, patch_side))
        return lax.dynamic_update_slice(running, current + contrib[slot_number], corner)

    return lax.fori_loop(0, rows_one.shape[0], add_patch, running_start)


def tv_core(padded):
    baseline = padded[:, :-1, :-1, :-1]
    along_y = padded[:, 1:, :-1, :-1] - baseline
    along_x = padded[:, :-1, 1:, :-1] - baseline
    along_z = padded[:, :-1, :-1, 1:] - baseline
    inverse = 1.0 / jnp.sqrt(
        along_y * along_y + along_x * along_x + along_z * along_z + smoothing * smoothing
    )
    norm_y = along_y * inverse
    norm_x = along_x * inverse
    norm_z = along_z * inverse
    divergence = (
        norm_y[:, 1:, 1:, 1:]
        - norm_y[:, :-1, 1:, 1:]
        + (norm_x[:, 1:, 1:, 1:] - norm_x[:, 1:, :-1, 1:])
        + (norm_z[:, 1:, 1:, 1:] - norm_z[:, 1:, 1:, :-1])
    )
    return -divergence


def tv_gradient(volume):
    faces = with_halo(volume, (("scan", 2), (("angle", "tile"), 1)), 1)
    padded = jnp.pad(faces, ((0, 0), (0, 0), (0, 0), (1, 1)))
    return tv_core(padded)


def back_fold(shift_table, tap_weight, width, running, pieces, start):

    def add_angle(offset_index, current):
        angle_plane = lax.dynamic_index_in_dim(pieces, offset_index, 0, keepdims=False)
        offsets = lax.dynamic_index_in_dim(shift_table, offset_index, 0, keepdims=False)
        fractions = lax.dynamic_index_in_dim(tap_weight, offset_index, 0, keepdims=False)

        def add_one_row(offset, fraction):
            section = lax.dynamic_slice(
                angle_plane, (0, width - offset - 1, 0), (2, width + 1, angle_plane.shape[2])
            )
            return (1.0 - fraction) * section[:, 1:] + fraction * section[:, :-1]

        return current + jax.vmap(add_one_row, out_axes=1)(offsets, fractions)

    return lax.fori_loop(0, pieces.shape[0], add_angle, running)


def forward_project(volume, shift_table, tap_weight, width):
    padded = jnp.pad(volume, ((0, 0), (0, 0), (2 * width, 2 * width), (0, 0)))
    reach = 3 * width

    def per_angle(element):
        offsets, fractions = element

        def per_one_row(row_plane, offset, fraction):
            section = lax.dynamic_slice(
                row_plane, (0, width + offset, 0), (2, reach + 1, row_plane.shape[2])
            )
            return (1.0 - fraction) * section[:, :-1] + fraction * section[:, 1:]

        return jnp.sum(jax.vmap(per_one_row, in_axes=(1, 0, 0))(padded, offsets, fractions), axis=0)

    return lax.map(per_angle, (shift_table, tap_weight))


def body(
    transmission,
    scaled_dual,
    projected,
    volume,
    intensities,
    probe_wave,
    slot_first_rows,
    slot_first_columns,
    patch_counts,
    shift_table,
    tap_weight,
):
    width = transmission.shape[2]
    upper = lax.axis_index(("angle", "tile")) >= lax.axis_size(("angle", "tile")) // 2
    cosine_table, sine_table = dft_tables(probe_wave.shape[1])
    wide_object = widen(transmission, width)
    patch_totals = jnp.stack(
        [
            patch_sums(
                wide_object[0],
                slot_first_rows[0],
                slot_first_columns[0],
                intensities[0],
                patch_counts[0],
                probe_wave,
                cosine_table,
                sine_table,
            )
        ]
    )
    gathered = fold_rims(patch_totals, width)
    new_transmission = (gathered[:, 0:2] + penalty * (projected - scaled_dual)) / (
        gathered[:, 2:3] + penalty
    )
    residual = projected - new_transmission - scaled_dual
    tv_term = tv_gradient(volume)
    empty_volume = jnp.zeros(volume.shape, jnp.float32)
    folder = partial(back_fold, shift_table, tap_weight, width)
    wide_residual = widen(residual, width)
    back_sum = folder(
        empty_volume,
        lax.all_gather(wide_residual, ("angle", "tile"), axis=0, tiled=True),
        jnp.int32(0),
    )
    new_volume = volume - step_size * (back_sum + tv_weight * tv_term)
    partial_sums = forward_project(new_volume, shift_table, tap_weight, width)
    spill = jnp.where(upper, partial_sums[:, :, :width], partial_sums[:, :, 2 * width :])
    own_columns = partial_sums[:, :, width : 2 * width] + directed(spill, jnp.logical_not(upper))
    new_projected = lax.psum_scatter(
        own_columns, ("angle", "tile"), scatter_dimension=0, tiled=True
    )
    new_dual = scaled_dual + new_transmission - new_projected
    return (new_transmission, new_dual, new_volume, new_projected)


def solution(mesh):
    return jax.shard_map(
        body,
        mesh=mesh,
        in_specs=(
            P(("groups", "angle", "tile"), None, "scan", None),
            P(("groups", "angle", "tile"), None, "scan", None),
            P(("groups", "angle", "tile"), None, "scan", None),
            P("groups", ("angle", "tile"), "scan", None),
            P(("groups", "angle", "tile"), "scan", None, None),
            P("groups", None, None),
            P(("groups", "angle", "tile"), "scan"),
            P(("groups", "angle", "tile"), "scan"),
            P(("groups", "angle", "tile"), "scan"),
            P(None, ("angle", "tile")),
            P(None, ("angle", "tile")),
        ),
        out_specs=(
            P(("groups", "angle", "tile"), None, "scan", None),
            P(("groups", "angle", "tile"), None, "scan", None),
            P("groups", ("angle", "tile"), "scan", None),
            P(("groups", "angle", "tile"), None, "scan", None),
        ),
        check_vma=False,
    )
```

profile of v0, /device:TPU:0, one launch (start us, length us, event | category | flops | bytes accessed | tf_op | source)
XLA Modules:
  0.0 189.4 jit_solution(13806917916022693251)
XLA Ops:
  7.2 5.0 %collective-permute-start.2 = (f32[1,2,64,256]{3,2,1,0:T(8,128)}, f32[1,2,64,256]{3,2,1,0:T(8,128)S(1)}, u32[]{:S(2)}, u32[]{:S(2)}) collective-permute-start(f32[1,2,64,256]{3,2,1,0:T(8,128)} %param.19), channel_id=1, source_target_pairs={{0,4},{4,8},{8,12},{1,5},{5,9},{9,13},{2,6},{6,10},{10,14},{3,7},{... | collective-permute-start | bytes 393224 | tf_op jit(solution)/shard_map/ppermute | solution.py:21
  15.9 3.3 %collective-permute-done.3 = f32[1,2,64,256]{3,2,1,0:T(8,128)S(1)} collective-permute-done((f32[1,2,64,256]{3,2,1,0:T(8,128)}, f32[1,2,64,256]{3,2,1,0:T(8,128)S(1)}, u32[]{:S(2)}, u32[]{:S(2)}) %collective-permute-start.3) | collective-permute-done | bytes 131104 | tf_op jit(solution)/shard_map/ppermute | solution.py:24
  20.2 8.2 %while.46 = (s32[]{:T(128)}, f32[2,192,256]{2,1,0:T(8,128)S(1)}, s32[4,3]{1,0:T(4,128)S(1)}, f32[4,2,128,128]{3,2,0,1:T(8,128)S(1)}, s32[]{:T(128)}) while((s32[]{:T(128)}, f32[2,192,256]{2,1,0:T(8,128)S(1)}, s32[4,3]{1,0:T(4,128)S(1)}, f32[4,2,128,128]{3,2,0,1:T(8,128)S(1)}, s32[]{:T(128)}) %tuple.140), condition=%wide.while_cond, body=%wide.while_body.sunk | while | flops 2 | bytes 262261 | solution.py:93
  20.9 1.4 bitcast_dynamic-update-slice_fusion.2
  22.9 1.4 bitcast_dynamic-update-slice_fusion.2
  25.0 1.4 bitcast_dynamic-update-slice_fusion.2
  40.9 31.9 %while.44 = (s32[]{:T(128)}, f32[3,192,256]{2,1,0:T(8,128)S(1)}, s32[4]{0:T(128)S(1)}, s32[4]{0:T(128)S(1)}, f32[4,3,128,128]{3,2,0,1:T(8,128)S(1)}, /*index=5*/s32[]{:T(128)}, s32[]{:T(128)}, s32[]{:T(128)}, s32[]{:T(128)}) while((s32[]{:T(128)}, f32[3,192,256]{2,1,0:T(8,128)S(1)}, s32[4]{0:T(128)S(1)}, s32[4]{0:T(128)S(1)}, ...), condition=%wide.region_1.2_spmd, body=%wide.region_0.1_spmd.sunk | while | flops 49160 | bytes 983241 | solution.py:119
  46.1 2.7 %dynamic_update_slice.17 = f32[3,192,256]{2,1,0:T(8,128)S(1)} dynamic-update-slice(f32[3,192,256]{2,1,0:T(8,128)S(1)} %get-tuple-element.623, f32[3,128,128]{2,1,0:T(8,128)S(1)} %bitcast_add_fusion.2, s32[]{:T(128)} %constant.205.clone.1..sunk, s32[]{:T(128)S(6)} %select_n.220, s32[]{:T(128)S(6)} %select_n.221) | dynamic-update-slice | bytes 393220 | tf_op jit(solution)/shard_map/while/body/eval_jaxpr/dynamic_update_slice | solution.py:117
  54.0 2.8 %dynamic_update_slice.17 = f32[3,192,256]{2,1,0:T(8,128)S(1)} dynamic-update-slice(f32[3,192,256]{2,1,0:T(8,128)S(1)} %get-tuple-element.623, f32[3,128,128]{2,1,0:T(8,128)S(1)} %bitcast_add_fusion.2, s32[]{:T(128)} %constant.205.clone.1..sunk, s32[]{:T(128)S(6)} %select_n.220, s32[]{:T(128)S(6)} %select_n.221) | dynamic-update-slice | bytes 393220 | tf_op jit(solution)/shard_map/while/body/eval_jaxpr/dynamic_update_slice | solution.py:117
  62.0 2.7 %dynamic_update_slice.17 = f32[3,192,256]{2,1,0:T(8,128)S(1)} dynamic-update-slice(f32[3,192,256]{2,1,0:T(8,128)S(1)} %get-tuple-element.623, f32[3,128,128]{2,1,0:T(8,128)S(1)} %bitcast_add_fusion.2, s32[]{:T(128)} %constant.205.clone.1..sunk, s32[]{:T(128)S(6)} %select_n.220, s32[]{:T(128)S(6)} %select_n.221) | dynamic-update-slice | bytes 393220 | tf_op jit(solution)/shard_map/while/body/eval_jaxpr/dynamic_update_slice | solution.py:117
  70.0 2.8 %dynamic_update_slice.17 = f32[3,192,256]{2,1,0:T(8,128)S(1)} dynamic-update-slice(f32[3,192,256]{2,1,0:T(8,128)S(1)} %get-tuple-element.623, f32[3,128,128]{2,1,0:T(8,128)S(1)} %bitcast_add_fusion.2, s32[]{:T(128)} %constant.205.clone.1..sunk, s32[]{:T(128)S(6)} %select_n.220, s32[]{:T(128)S(6)} %select_n.221) | dynamic-update-slice | bytes 393220 | tf_op jit(solution)/shard_map/while/body/eval_jaxpr/dynamic_update_slice | solution.py:117
  72.9 3.6 %collective-permute-start.4 = (f32[1,3,64,256]{3,2,1,0:T(8,128)S(1)}, f32[1,3,64,256]{3,2,1,0:T(8,128)S(1)}, u32[]{:S(2)}, u32[]{:S(2)}) collective-permute-start(f32[1,3,64,256]{3,2,1,0:T(8,128)S(1)} %get-tuple-element.457), channel_id=1, source_target_pairs={{0,4},{4,8},{8,12},{1,5},{5,9},{9,13},{2,6},{6,10},{10,14},{3,7},{... | collective-permute-start | bytes 589832 | tf_op jit(solution)/shard_map/ppermute | solution.py:21
  77.8 1.9 collective-permute-done.4
  79.7 4.4 %collective-permute-done.5 = f32[1,3,64,256]{3,2,1,0:T(8,128)S(1)} collective-permute-done((f32[1,3,64,256]{3,2,1,0:T(8,128)S(1)}, f32[1,3,64,256]{3,2,1,0:T(8,128)S(1)}, u32[]{:S(2)}, u32[]{:S(2)}) %collective-permute-start.5) | collective-permute-done | bytes 196640 | tf_op jit(solution)/shard_map/ppermute | solution.py:24
  84.9 3.4 %collective-permute-start.6 = (f32[1,2,64,256]{3,2,1,0:T(8,128)S(1)}, f32[1,2,64,256]{3,2,1,0:T(8,128)S(1)}, u32[]{:S(2)}, u32[]{:S(2)}) collective-permute-start(f32[1,2,64,256]{3,2,1,0:T(8,128)S(1)} %get-tuple-element.447), channel_id=1, source_target_pairs={{0,4},{4,8},{8,12},{1,5},{5,9},{9,13},{2,6},{6,10},{10,14},{3,7},{... | collective-permute-start | bytes 393224 | tf_op jit(solution)/shard_map/ppermute | solution.py:21
  90.7 4.4 %collective-permute-done.7 = f32[1,2,64,256]{3,2,1,0:T(8,128)S(1)} collective-permute-done((f32[1,2,64,256]{3,2,1,0:T(8,128)S(1)}, f32[1,2,64,256]{3,2,1,0:T(8,128)S(1)}, u32[]{:S(2)}, u32[]{:S(2)}) %collective-permute-start.7) | collective-permute-done | bytes 131104 | tf_op jit(solution)/shard_map/ppermute | solution.py:24
  96.0 1.9 %collective-permute-start.8 = (f32[2,2,1,256]{3,2,1,0:T(1,128)S(1)}, f32[2,2,1,256]{3,2,1,0:T(1,128)S(1)}, u32[]{:S(2)}, u32[]{:S(2)}) collective-permute-start(f32[2,2,1,256]{3,2,1,0:T(1,128)S(1)} %get-tuple-element.461), channel_id=1, source_target_pairs={{0,4},{4,8},{8,12},{1,5},{5,9},{9,13},{2,6},{6,10},{10,14},{3,7},{... | collective-permute-start | bytes 12296 | tf_op jit(solution)/shard_map/ppermute | solution.py:21
  99.2 4.2 %collective-permute-done.9 = f32[2,2,1,256]{3,2,1,0:T(1,128)S(1)} collective-permute-done((f32[2,2,1,256]{3,2,1,0:T(1,128)S(1)}, f32[2,2,1,256]{3,2,1,0:T(1,128)S(1)}, u32[]{:S(2)}, u32[]{:S(2)}) %collective-permute-start.9) | collective-permute-done | bytes 4128 | tf_op jit(solution)/shard_map/ppermute | solution.py:24
  106.3 3.7 %collective-permute-done.11 = f32[2,1,66,256]{3,2,1,0:T(8,128)S(1)} collective-permute-done((f32[2,1,66,256]{3,2,1,0:T(8,128)S(1)}, f32[2,1,66,256]{3,2,1,0:T(8,128)S(1)}, u32[]{:S(2)}, u32[]{:S(2)}) %collective-permute-start.11) | collective-permute-done | bytes 135200 | tf_op jit(solution)/shard_map/ppermute | solution.py:24
  110.9 3.3 %all-gather.2.cloned.1.call-done = f32[4,2,192,256]{3,2,1,0:T(8,128)} async-done(((f32[1,2,192,256]{3,2,1,0:T(8,128)}), f32[4,2,192,256]{3,2,1,0:T(8,128)}) %all-gather.2.cloned.1.call-update) | async-done | bytes 1572880 | tf_op jit(solution)/shard_map/all_gather | solution.py:226
  114.2 10.6 %while.47 = (s32[]{:T(128)}, f32[2,2,64,256]{3,0,2,1:T(2,128)S(1)}, f32[4,2]{1,0:T(4,128)S(1)}, f32[4,2,192,256]{3,2,1,0:T(8,128)}, s32[4,2]{1,0:T(4,128)S(1)}, /*index=5*/s32[]{:T(128)}, s32[]{:T(128)}) while((s32[]{:T(128)}, f32[2,2,64,256]{3,0,2,1:T(2,128)S(1)}, f32[4,2]{1,0:T(4,128)S(1)}, f32[4,2,192,256]{3,2,1,0:T(8,128)}, ...), condition=%wide.region_3.4_spmd.clone, body=%wide.region_2.3_spmd.clone.sunk | while | flops 327697 | bytes 3154099 | solution.py:163
  125.9 12.3 %while.45 = (s32[]{:T(128)}, f32[4,2,192,256]{3,2,1,0:T(8,128)}, f32[4,2]{1,0:T(4,128)S(1)}, f32[2,2,320,256]{3,0,1,2:T(2,128)S(1)}, s32[4,2]{1,0:T(4,128)S(1)}, /*index=5*/s32[]{:T(128)}) while((s32[]{:T(128)}, f32[4,2,192,256]{3,2,1,0:T(8,128)}, f32[4,2]{1,0:T(4,128)S(1)}, f32[2,2,320,256]{3,0,1,2:T(2,128)S(1)}, s32[4,2]{1,0:T(4,128)S(1)}, ...), condition=%wide.region_6.7_spmd, body=%wide.region_4.6_spmd.sunk | while | flops 688150 | bytes 4334245 | solution.py:181
  126.0 1.5 gather_fusion
  129.0 1.5 gather_fusion
  132.1 1.5 gather_fusion
  135.2 1.5 gather_fusion
  139.6 15.7 %conditional.1 = (f32[4,2,64,256]{3,2,1,0:T(8,128)}) conditional(s32[]{:T(128)} %convert_element_type.57, f32[4,2,64,256]{3,2,1,0:T(8,128)S(1)} %slice_select_fusion, f32[4,2,64,256]{3,2,1,0:T(8,128)S(1)} %slice_select_fusion), branch_computations={%region_7.8_spmd, %region_8.9_spmd} | conditional | bytes 2097200 | solution.py:53
  139.6 5.0 %collective-permute-start.1 = (f32[4,2,64,256]{3,2,1,0:T(8,128)S(1)}, f32[4,2,64,256]{3,2,1,0:T(8,128)}, u32[]{:S(2)}, u32[]{:S(2)}) collective-permute-start(f32[4,2,64,256]{3,2,1,0:T(8,128)S(1)} %param.7), channel_id=1, source_target_pairs={{0,4},{4,8},{8,12},{1,5},{5,9},{9,13},{2,6},{6,10},{10,14},{3,7},{... | collective-permute-start | bytes 1572872 | tf_op jit(solution)/shard_map/cond/branch_1_fun/ppermute | solution.py:32
  144.6 10.8 %collective-permute-done.1 = f32[4,2,64,256]{3,2,1,0:T(8,128)} collective-permute-done((f32[4,2,64,256]{3,2,1,0:T(8,128)S(1)}, f32[4,2,64,256]{3,2,1,0:T(8,128)}, u32[]{:S(2)}, u32[]{:S(2)}) %collective-permute-start.1) | collective-permute-done | bytes 524320 | tf_op jit(solution)/shard_map/cond/branch_1_fun/ppermute | solution.py:32
  155.3 2.1 %slice_add_fusion = f32[4,2,64,256]{3,2,1,0:T(8,128)} fusion(f32[4,2,64,256]{3,2,1,0:T(8,128)} %get-tuple-element.679, f32[4,2,192,256]{3,2,1,0:T(8,128)} %get-tuple-element.340), kind=kLoop, calls=%fused_computation.56 | loop fusion | flops 131072 | bytes 1572864 | tf_op jit(solution)/shard_map/add | solution.py:232
  157.4 23.5 %reduce-scatter.2.cloned.1.call-done = f32[1,2,64,256]{3,2,1,0:T(8,128)} async-done(((f32[4,2,64,256]{3,2,1,0:T(8,128)}), f32[1,2,64,256]{3,2,1,0:T(8,128)}) %reduce-scatter.2.cloned.1.call-update) | async-done | bytes 131088 | tf_op jit(solution)/shard_map/reduce_scatter | solution.py:233
  181.0 1.6 add_subtract_fusion
  (143 shorter events, 55.2 us)
Async XLA Ops:
  7.2 107.1 %all-gather.2.cloned.1.call-start = ((), (), s32[]{:S(2)}) async-start(), calls=%async_computation.1 | async-start | bytes 1966080 | tf_op jit(solution)/shard_map/all_gather | solution.py:226
  7.2 8.7 %collective-permute-start.2 = (f32[1,2,64,256]{3,2,1,0:T(8,128)}, f32[1,2,64,256]{3,2,1,0:T(8,128)S(1)}, u32[]{:S(2)}, u32[]{:S(2)}) collective-permute-start(f32[1,2,64,256]{3,2,1,0:T(8,128)} %param.19), channel_id=1, source_target_pairs={{0,4},{4,8},{8,12},{1,5},{5,9},{9,13},{2,6},{6,10},{10,14},{3,7},{... | collective-permute-start | bytes 393224 | tf_op jit(solution)/shard_map/ppermute | solution.py:21
  12.2 7.1 %collective-permute-start.3 = (f32[1,2,64,256]{3,2,1,0:T(8,128)}, f32[1,2,64,256]{3,2,1,0:T(8,128)S(1)}, u32[]{:S(2)}, u32[]{:S(2)}) collective-permute-start(f32[1,2,64,256]{3,2,1,0:T(8,128)} %param.19), channel_id=1, source_target_pairs={{4,0},{8,4},{12,8},{5,1},{9,5},{13,9},{6,2},{10,6},{14,10},{7,3},{... | collective-permute-start | bytes 393224 | tf_op jit(solution)/shard_map/ppermute | solution.py:24
  31.4 3.0 %copy-start.1 = (bf16[1,4,128,128]{3,2,1,0:T(8,128)(2,1)S(1)}, bf16[1,4,128,128]{3,2,1,0:T(8,128)(2,1)}, u32[]{:S(2)}) copy-start(bf16[1,4,128,128]{3,2,1,0:T(8,128)(2,1)} %param.23) | copy-start | bytes 393220
  39.8 1.1 copy-start.9
  39.8 1.1 copy-start.10
  72.8 11.3 %copy-start.3 = (f32[1,2,64,256]{3,2,1,0:T(8,128)S(1)}, f32[1,2,64,256]{3,2,1,0:T(8,128)}, u32[]{:S(2)}) copy-start(f32[1,2,64,256]{3,2,1,0:T(8,128)} %param.20) | copy-start | bytes 393220
  72.8 11.3 %copy-start.6 = (f32[1,2,64,256]{3,2,1,0:T(8,128)S(1)}, f32[1,2,64,256]{3,2,1,0:T(8,128)}, u32[]{:S(2)}) copy-start(f32[1,2,64,256]{3,2,1,0:T(8,128)} %param.21) | copy-start | bytes 393220
  72.8 23.1 %copy-start = (f32[2,2,64,256]{3,2,1,0:T(8,128)S(1)}, f32[2,2,64,256]{3,2,1,0:T(8,128)}, u32[]{:S(2)}) copy-start(f32[2,2,64,256]{3,2,1,0:T(8,128)} %param.22) | copy-start | bytes 786436
  72.9 6.8 %collective-permute-start.4 = (f32[1,3,64,256]{3,2,1,0:T(8,128)S(1)}, f32[1,3,64,256]{3,2,1,0:T(8,128)S(1)}, u32[]{:S(2)}, u32[]{:S(2)}) collective-permute-start(f32[1,3,64,256]{3,2,1,0:T(8,128)S(1)} %get-tuple-element.457), channel_id=1, source_target_pairs={{0,4},{4,8},{8,12},{1,5},{5,9},{9,13},{2,6},{6,10},{10,14},{3,7},{... | collective-permute-start | bytes 589832 | tf_op jit(solution)/shard_map/ppermute | solution.py:21
  76.5 7.6 %collective-permute-start.5 = (f32[1,3,64,256]{3,2,1,0:T(8,128)S(1)}, f32[1,3,64,256]{3,2,1,0:T(8,128)S(1)}, u32[]{:S(2)}, u32[]{:S(2)}) collective-permute-start(f32[1,3,64,256]{3,2,1,0:T(8,128)S(1)} %get-tuple-element.458), channel_id=1, source_target_pairs={{4,0},{8,4},{12,8},{5,1},{9,5},{13,9},{6,2},{10,6},{14,10},{7,3},{... | collective-permute-start | bytes 589832 | tf_op jit(solution)/shard_map/ppermute | solution.py:24
  84.1 22.0 %copy-start.7 = (s32[4,2]{0,1:T(2,128)S(1)}, s32[4,2]{0,1:T(2,128)}, u32[]{:S(2)}) copy-start(s32[4,2]{0,1:T(2,128)} %param.28) | copy-start | bytes 100
  84.1 22.1 %copy-start.8 = (f32[4,2]{0,1:T(2,128)S(1)}, f32[4,2]{0,1:T(2,128)}, u32[]{:S(2)}) copy-start(f32[4,2]{0,1:T(2,128)} %param.29) | copy-start | bytes 100
  84.9 5.9 %collective-permute-start.6 = (f32[1,2,64,256]{3,2,1,0:T(8,128)S(1)}, f32[1,2,64,256]{3,2,1,0:T(8,128)S(1)}, u32[]{:S(2)}, u32[]{:S(2)}) collective-permute-start(f32[1,2,64,256]{3,2,1,0:T(8,128)S(1)} %get-tuple-element.447), channel_id=1, source_target_pairs={{0,4},{4,8},{8,12},{1,5},{5,9},{9,13},{2,6},{6,10},{10,14},{3,7},{... | collective-permute-start | bytes 393224 | tf_op jit(solution)/shard_map/ppermute | solution.py:21
  88.2 6.9 %collective-permute-start.7 = (f32[1,2,64,256]{3,2,1,0:T(8,128)S(1)}, f32[1,2,64,256]{3,2,1,0:T(8,128)S(1)}, u32[]{:S(2)}, u32[]{:S(2)}) collective-permute-start(f32[1,2,64,256]{3,2,1,0:T(8,128)S(1)} %get-tuple-element.447), channel_id=1, source_target_pairs={{4,0},{8,4},{12,8},{5,1},{9,5},{13,9},{6,2},{10,6},{14,10},{7,3},{... | collective-permute-start | bytes 393224 | tf_op jit(solution)/shard_map/ppermute | solution.py:24
  95.9 85.0 %reduce-scatter.2.cloned.1.call-start = ((), (), s32[]{:S(2)}) async-start(), calls=%async_computation.2 | async-start | bytes 655360 | tf_op jit(solution)/shard_map/reduce_scatter | solution.py:233
  96.0 3.2 %collective-permute-start.8 = (f32[2,2,1,256]{3,2,1,0:T(1,128)S(1)}, f32[2,2,1,256]{3,2,1,0:T(1,128)S(1)}, u32[]{:S(2)}, u32[]{:S(2)}) collective-permute-start(f32[2,2,1,256]{3,2,1,0:T(1,128)S(1)} %get-tuple-element.461), channel_id=1, source_target_pairs={{0,4},{4,8},{8,12},{1,5},{5,9},{9,13},{2,6},{6,10},{10,14},{3,7},{... | collective-permute-start | bytes 12296 | tf_op jit(solution)/shard_map/ppermute | solution.py:21
  97.9 5.5 %collective-permute-start.9 = (f32[2,2,1,256]{3,2,1,0:T(1,128)S(1)}, f32[2,2,1,256]{3,2,1,0:T(1,128)S(1)}, u32[]{:S(2)}, u32[]{:S(2)}) collective-permute-start(f32[2,2,1,256]{3,2,1,0:T(1,128)S(1)} %get-tuple-element.462), channel_id=1, source_target_pairs={{4,0},{8,4},{12,8},{5,1},{9,5},{13,9},{6,2},{10,6},{14,10},{7,3},{... | collective-permute-start | bytes 12296 | tf_op jit(solution)/shard_map/ppermute | solution.py:24
  103.5 2.8 %collective-permute-start.10 = (f32[2,1,66,256]{3,2,1,0:T(8,128)S(1)}, f32[2,1,66,256]{3,2,1,0:T(8,128)S(1)}, u32[]{:S(2)}, u32[]{:S(2)}) collective-permute-start(f32[2,1,66,256]{3,2,1,0:T(8,128)S(1)} %get-tuple-element.459), channel_id=1, source_target_pairs={{0,1},{1,2},{2,3},{4,5},{5,6},{6,7},{8,9},{9,10},{10,11},{12,13},{... | collective-permute-start | bytes 405512 | tf_op jit(solution)/shard_map/ppermute | solution.py:21
  104.8 5.2 %collective-permute-start.11 = (f32[2,1,66,256]{3,2,1,0:T(8,128)S(1)}, f32[2,1,66,256]{3,2,1,0:T(8,128)S(1)}, u32[]{:S(2)}, u32[]{:S(2)}) collective-permute-start(f32[2,1,66,256]{3,2,1,0:T(8,128)S(1)} %get-tuple-element.460), channel_id=1, source_target_pairs={{1,0},{2,1},{3,2},{5,4},{6,5},{7,6},{9,8},{10,9},{11,10},{13,12},{... | collective-permute-start | bytes 405512 | tf_op jit(solution)/shard_map/ppermute | solution.py:24
  125.2 0.7 copy-start.2
  138.2 42.7 %copy-start.4 = (f32[1,2,64,256]{3,2,1,0:T(8,128)S(1)}, f32[1,2,64,256]{3,2,1,0:T(8,128)}, u32[]{:S(2)}) copy-start(f32[1,2,64,256]{3,2,1,0:T(8,128)} %param.20) | copy-start | bytes 393220
  138.2 42.7 %copy-start.5 = (f32[1,2,64,256]{3,2,1,0:T(8,128)S(1)}, f32[1,2,64,256]{3,2,1,0:T(8,128)}, u32[]{:S(2)}) copy-start(f32[1,2,64,256]{3,2,1,0:T(8,128)} %get-tuple-element.448) | copy-start | bytes 393220
  139.6 15.7 %collective-permute-start.1 = (f32[4,2,64,256]{3,2,1,0:T(8,128)S(1)}, f32[4,2,64,256]{3,2,1,0:T(8,128)}, u32[]{:S(2)}, u32[]{:S(2)}) collective-permute-start(f32[4,2,64,256]{3,2,1,0:T(8,128)S(1)} %param.7), channel_id=1, source_target_pairs={{0,4},{4,8},{8,12},{1,5},{5,9},{9,13},{2,6},{6,10},{10,14},{3,7},{... | collective-permute-start | bytes 1572872 | tf_op jit(solution)/shard_map/cond/branch_1_fun/ppermute | solution.py:32
Sparse Core Ops, SparseCore 0:
  96.0 18.1 all-gather.1
  157.5 23.3 reduce-scatter.1
where the time goes:
time: 190 us; the launch traced here: 189 us
  waiting for transfers between devices  60.6 us (32%)
  local copies, waits for them, and re-layouts  42.6 us (22%)
  starting transfers between devices  26.7 us (14%)
  loops' own time  16.1 us (8%)
  other arithmetic  15.9 us (8%)
  between operations  15.2 us (8%)
  matrix products  12.2 us (6%)
    reduce_scatter x1, waiting for transfers between devices, body(): lax.psum_scatter(own_columns, ('angle', 'tile'), scatter_dimension=0, til...  23.5 us
    ppermute x5, waiting for transfers between devices, with_halo(): lax.ppermute(lax.slice_in_dim(block, 0, width, axis=dim), axis, backward)  19.9 us
    another operation x1, loops' own time, patch_sums(): return lax.fori_loop(0, rows_one.shape[0], add_patch, running_start)  15.7 us
    ppermute x5, starting transfers between devices, with_halo(): lax.ppermute(lax.slice_in_dim(block, block.shape[dim] - width, None, axis...  15.2 us
    dynamic_update_slice x4, local copies, waits for them, and re-layouts, add_patch(): lax.dynamic_update_slice(running, current + contrib[slot_number], corner)  11 us
    ppermute x1, waiting for transfers between devices, from_behind(): return lax.ppermute(block, axis, route)  10.8 us
    gather x12, local copies, waits for them, and re-layouts  8.08 us
    ppermute x5, starting transfers between devices, with_halo(): lax.ppermute(lax.slice_in_dim(block, 0, width, axis=dim), axis, backward)  6.46 us
  transfers between devices with their start and end apart: 13, of which 10 were waited for; matrix products, arithmetic and copies ran while one was open for 2% of the time, Pallas kernels for 0%

commit v1 on v0

v1 whole, which is shorter than its diff:
```python
import math

import jax
import jax.numpy as jnp
import numpy as np
from jax import lax
from jax.experimental import pallas as pl
from jax.experimental.pallas import tpu as pltpu
from jax.sharding import PartitionSpec as P

penalty = 4.0
amplitude_step = 0.25
tv_weight = 1.0
smoothing = 0.05
step_size = 0.008

VMEM = pl.BlockSpec(memory_space=pltpu.VMEM)
SMEM = pl.BlockSpec(memory_space=pltpu.SMEM)
LANES = 128


def split(values):
    high = values.astype(jnp.bfloat16)
    return (high, (values - high.astype(jnp.float32)).astype(jnp.bfloat16))


def product(left, right):
    total = jnp.dot(left[0], right[0], preferred_element_type=jnp.float32)
    total += jnp.dot(left[0], right[1], preferred_element_type=jnp.float32)
    return total + jnp.dot(left[1], right[0], preferred_element_type=jnp.float32)


def dft_tables(length):
    grid_ids = np.arange(length)
    radians = (grid_ids[:, None] * grid_ids[None, :] % length) * (2.0 * math.pi / length)
    cosine = np.cos(radians) / math.sqrt(length)
    sine = np.sin(radians) / math.sqrt(length)
    forward = np.block([[cosine, sine], [-sine, cosine]])
    tables = []
    for table in (forward, forward.T):
        high = table.astype(jnp.bfloat16)
        tables += [high, (table - high.astype(np.float64)).astype(jnp.bfloat16)]
    return tables


def tile_is_first():
    return lax.axis_index("tile") == 0


def scan_is_even():
    return lax.rem(lax.axis_index("scan"), 2) == 0


def outer_rows(ya_ref, yb_ref, channel):
    last = ya_ref.shape[1] - 1
    first = tile_is_first()
    below = jnp.where(first, yb_ref[channel, last], ya_ref[channel, last])
    above = jnp.where(first, ya_ref[channel, 0], yb_ref[channel, 0])
    return (below, above)


def patch_kernel(
    rows_ref,
    columns_ref,
    count_ref,
    plane_ref,
    plane_a_ref,
    plane_b_ref,
    intensity_ref,
    probe_ref,
    forward_high_ref,
    forward_low_ref,
    inverse_high_ref,
    inverse_low_ref,
    volume_ref,
    ya_ref,
    yb_ref,
    own_ref,
    rim_a_ref,
    rim_b_ref,
    wide,
    totals,
):
    width = plane_ref.shape[2]
    side = probe_ref.shape[1]
    slots = intensity_ref.shape[1]
    even = scan_is_even()
    at_a = pl.multiple_of(jnp.where(even, 2 * width, 0), width)
    at_b = pl.multiple_of(jnp.where(even, 0, 2 * width), width)
    wide[:, width : 2 * width] = plane_ref[0]
    wide[:, pl.ds(at_a, width)] = plane_a_ref[0]
    wide[:, pl.ds(at_b, width)] = plane_b_ref[0]
    lanes = lax.broadcasted_iota(jnp.int32, (side, side), 1)
    sublanes = lax.broadcasted_iota(jnp.int32, (side, side), 0)
    forward = (forward_high_ref[...], forward_low_ref[...])
    inverse = (inverse_high_ref[...], inverse_low_ref[...])
    probes, waves, masks = [], [], []
    for slot in range(slots):
        column = columns_ref[0, slot]
        row = rows_ref[0, slot]
        turn = lax.rem(row, side)
        probe = [pltpu.roll(pltpu.roll(probe_ref[part], column, 0), turn, 1) for part in range(2)]
        near_lanes = lanes >= row
        near_columns = sublanes >= column
        window = []
        for part in range(2):
            near = jnp.where(near_lanes, wide[part, :side, :side], wide[part, :side, side:])
            wrapped = jnp.where(
                near_lanes[:width], wide[part, side:, :side], wide[part, side:, side:]
            )
            wrapped = jnp.concatenate([wrapped, near[width:]], axis=0)
            window.append(jnp.where(near_columns, near, wrapped))
        wave_real = probe[0] * window[0] - probe[1] * window[1]
        wave_imaginary = probe[0] * window[1] + probe[1] * window[0]
        probes.append(probe)
        waves.append(jnp.concatenate([wave_real, wave_imaginary], axis=1))
        live = jnp.full((side, side), slot < count_ref[0, 0])
        masks.append((near_lanes, near_columns, live))
    half = product(split(jnp.concatenate(waves, axis=0)), inverse)
    half = jnp.concatenate(
        [
            jnp.concatenate(
                [half[slot * side : (slot + 1) * side, part * side : (part + 1) * side] for slot in range(slots)],
                axis=1,
            )
            for part in range(2)
        ],
        axis=0,
    )
    far = product(forward, split(half))
    far_real, far_imaginary = far[:side], far[side:]
    intensity = jnp.concatenate(
        [intensity_ref[0, slot].astype(jnp.float32) for slot in range(slots)], axis=1
    )
    factor = 1.0 - amplitude_step * (
        far_real * far_real + far_imaginary * far_imaginary - intensity
    )
    corrected = jnp.concatenate([far_real * factor, far_imaginary * factor], axis=0)
    half = product(inverse, split(corrected))
    half = jnp.concatenate(
        [
            jnp.concatenate(
                [half[part * side : (part + 1) * side, slot * side : (slot + 1) * side] for part in range(2)],
                axis=1,
            )
            for slot in range(slots)
        ],
        axis=0,
    )
    near = product(split(half), forward)
    totals[...] = jnp.zeros_like(totals)
    for slot in range(slots):
        probe = probes[slot]
        near_real = near[slot * side : (slot + 1) * side, :side]
        near_imaginary = near[slot * side : (slot + 1) * side, side:]
        terms = (
            probe[0] * near_real + probe[1] * near_imaginary,
            probe[0] * near_imaginary - probe[1] * near_real,
            probe[0] * probe[0] + probe[1] * probe[1],
        )
        near_lanes, near_columns, live = masks[slot]
        inner = live & near_columns
        outer = (live & jnp.logical_not(near_columns))[:width]
        for part, term in enumerate(terms):
            for start, lane_mask in ((0, near_lanes), (side, jnp.logical_not(near_lanes))):
                at = slice(start, start + side)
                totals[part, :side, at] += jnp.where(inner & lane_mask, term, 0.0)
                totals[part, side:, at] += jnp.where(outer & lane_mask[:width], term[:width], 0.0)
    own_ref[...] = totals[:, width : 2 * width]
    below_above = [outer_rows(ya_ref, yb_ref, channel) for channel in range(2)]
    parts = totals.shape[0]
    count = volume_ref.shape[1]
    for rim_ref, at, low in ((rim_a_ref, at_a, jnp.logical_not(even)), (rim_b_ref, at_b, even)):
        for part in range(parts):
            rim_ref[part * width : (part + 1) * width] = totals[part, pl.ds(at, width)]
        edge_rows = []
        for channel in range(2):
            planes = [below_above[channel][0]]
            planes += [volume_ref[channel, row] for row in range(count)]
            planes.append(below_above[channel][1])
            for plane in planes:
                edge_rows.append(jnp.where(low, plane[:1], plane[width - 1 :]))
        rim_ref[parts * width :] = jnp.concatenate(edge_rows, axis=0)


def fold_kernel(own_ref, rim_a_ref, rim_b_ref, projected_ref, dual_ref, object_ref, residual_ref):
    width = own_ref.shape[1]
    sums = [
        own_ref[part]
        + rim_a_ref[part * width : (part + 1) * width]
        + rim_b_ref[part * width : (part + 1) * width]
        for part in range(3)
    ]
    for part in range(2):
        target = projected_ref[0, part]
        dual = dual_ref[0, part]
        updated = (sums[part] + penalty * (target - dual)) / (sums[2] + penalty)
        object_ref[0, part] = updated
        residual_ref[part] = target - updated - dual


def variation_kernel(volume_ref, ya_ref, yb_ref, rim_a_ref, rim_b_ref, base_ref, padded, norms):
    width = volume_ref.shape[2]
    length = volume_ref.shape[3]
    count = volume_ref.shape[1]
    margin = 8
    edges_at = rim_a_ref.shape[0] - 2 * (count + 2)
    even = scan_is_even()
    lanes = lax.broadcasted_iota(jnp.int32, (width, length), 1)
    first_lane = lanes == 0
    last_lane = lanes == length - 1
    for channel in range(2):
        below, above = outer_rows(ya_ref, yb_ref, channel)
        planes = [below] + [volume_ref[channel, row] for row in range(count)] + [above]
        for row, plane in enumerate(planes):
            at = edges_at + channel * (count + 2) + row
            edge_a = rim_a_ref[at : at + 1]
            edge_b = rim_b_ref[at : at + 1]
            padded[row, margin : margin + width] = plane
            padded[row, margin - 1 : margin] = jnp.where(even, edge_b, edge_a)
            padded[row, margin + width : margin + width + 1] = jnp.where(even, edge_a, edge_b)
        previous_y = None
        for row in range(count + 1):
            here = padded[row, margin : margin + width]
            along_y = padded[row + 1, margin : margin + width] - here
            along_x = padded[row, margin + 1 : margin + width + 1] - here
            along_z = jnp.where(last_lane, 0.0, pltpu.roll(here, length - 1, 1)) - here
            inverse = lax.rsqrt(
                along_y * along_y + along_x * along_x + along_z * along_z + smoothing * smoothing
            )
            norm_y = along_y * inverse
            if row > 0:
                norm_x = along_x * inverse
                norm_z = along_z * inverse
                corner = padded[row, margin - 1 : margin]
                corner_y = padded[row + 1, margin - 1 : margin] - corner
                corner_x = here[:1] - corner
                corner_z = (
                    jnp.where(last_lane[:1], 0.0, pltpu.roll(corner, length - 1, 1)) - corner
                )
                corner_norm = corner_x * lax.rsqrt(
                    corner_y * corner_y
                    + corner_x * corner_x
                    + corner_z * corner_z
                    + smoothing * smoothing
                )
                norms[margin : margin + width] = norm_x
                norms[margin - 1 : margin] = corner_norm
                behind_x = norms[margin - 1 : margin + width - 1]
                ahead = here * lax.rsqrt(here * here + smoothing * smoothing)
                behind_z = jnp.where(first_lane, ahead, pltpu.roll(norm_z, 1, 1))
                divergence = (
                    norm_y - previous_y + (norm_x - behind_x) + (norm_z - behind_z)
                )
                base_ref[channel, row - 1] = here + (step_size * tv_weight) * divergence
            previous_y = norm_y


def project_kernel(
    shift_ref,
    weight_ref,
    here_ref,
    side_ref,
    other_ref,
    base_ref,
    beside_ref,
    volume_ref,
    keep_ref,
    send_ref,
    wide,
    updated,
):
    width = base_ref.shape[2]
    count = base_ref.shape[1]
    angles = here_ref.shape[0]
    tiles = lax.axis_size("tile")
    columns = angles // tiles
    me, tile, scan = lax.axis_index("angle"), lax.axis_index("tile"), lax.axis_index("scan")
    upper = me >= columns // 2
    right = lax.rem(scan + tile, 2) == 0
    side_at = pl.multiple_of(jnp.where(right, 2 * width, 0), width)
    other_at = pl.multiple_of(jnp.where(right, 0, 2 * width), width)

    def angle_of(turn, flip):
        return lax.rem(me + turn, columns) * tiles + (tile if flip == 0 else 1 - tile)

    chunks = [slice(at, at + LANES) for at in range(0, base_ref.shape[3], LANES)]
    for turn in range(columns):
        for flip in range(tiles):
            block = turn * tiles + flip
            for chunk, at in enumerate(chunks):
                near, far = angle_of(turn, flip), angle_of(turn, 1 - flip)
                wide[near, :, chunk, width : 2 * width] = here_ref[block, :, :, at]
                wide[near, :, chunk, pl.ds(side_at, width)] = side_ref[block, :, :, at]
                wide[far, :, chunk, pl.ds(other_at, width)] = other_ref[block, :, :, at]
    exists = jnp.where(upper, scan < lax.axis_size("scan") - 1, scan > 0).astype(jnp.float32)
    own_at = pl.multiple_of(jnp.where(upper, 0, width), width)
    beside_at = pl.multiple_of(jnp.where(upper, width, 0), width)
    for row in range(count):
        for channel in range(2):
            for chunk, at in enumerate(chunks):
                total = jnp.zeros((2 * width, LANES), jnp.float32)
                for angle in range(angles):
                    start = jnp.where(upper, width, 0) - shift_ref[angle, row]
                    fraction = weight_ref[angle, row]
                    total += (1.0 - fraction) * wide[angle, channel, chunk, pl.ds(start, 2 * width)]
                    total += fraction * wide[angle, channel, chunk, pl.ds(start - 1, 2 * width)]
                updated[row, channel, chunk] = total
                part = updated.at[row, channel, chunk]
                own = base_ref[channel, row, :, at] - step_size * part[pl.ds(own_at, width)]
                beside = beside_ref[channel, row, :, at] - step_size * part[pl.ds(beside_at, width)]
                volume_ref[channel, row, :, at] = own
                part[pl.ds(own_at, width)] = own
                part[pl.ds(beside_at, width)] = beside * exists
    for turn in range(columns):
        for flip, out_ref in ((0, keep_ref), (1, send_ref)):
            angle = angle_of(turn, flip)
            for channel in range(2):
                for chunk, at in enumerate(chunks):
                    total = jnp.zeros((width, LANES), jnp.float32)
                    for row in range(count):
                        start = jnp.where(upper, 0, width) + shift_ref[angle, row]
                        fraction = weight_ref[angle, row]
                        total += (1.0 - fraction) * updated[row, channel, chunk, pl.ds(start, width)]
                        total += fraction * updated[row, channel, chunk, pl.ds(start + 1, width)]
                    out_ref[turn, channel, :, at] = total


def call(kernel, shapes, in_specs, scratch, flops, name):
    moved = 4 * sum(math.prod(shape) for shape in shapes)
    return pl.pallas_call(
        kernel,
        name=name,
        out_shape=[jax.ShapeDtypeStruct(shape, jnp.float32) for shape in shapes],
        in_specs=in_specs,
        out_specs=[VMEM] * len(shapes),
        scratch_shapes=[pltpu.VMEM(shape, jnp.float32) for shape in scratch],
        cost_estimate=pl.CostEstimate(flops=flops, bytes_accessed=2 * moved, transcendentals=0),
    )


def body(
    transmission,
    scaled_dual,
    projected,
    volume,
    intensities,
    probe_wave,
    slot_first_rows,
    slot_first_columns,
    patch_counts,
    shift_table,
    tap_weight,
):
    width, length = transmission.shape[2:]
    count = volume.shape[1]
    scans, columns, tiles = (lax.axis_size(axis) for axis in ("scan", "angle", "tile"))
    rounds = [[(i, i + 1) for i in range(first, scans - 1, 2)] for first in (0, 1)]
    both = [pairs + [(target, source) for source, target in pairs] for pairs in rounds]
    swap = [(0, 1), (1, 0)]

    def exchange(block, number):
        return lax.ppermute(block, "scan", both[number])

    def across(block):
        return lax.ppermute(block, "tile", swap)

    plane_a = exchange(transmission, 0)
    plane_b = exchange(transmission, 1)
    rows_a = across(volume)
    bridge = [(i * tiles + 1, (i + 1) * tiles) for i in range(columns - 1)]
    bridge += [(target, source) for source, target in bridge]
    rows_b = lax.ppermute(volume, ("angle", "tile"), bridge)
    tables = [jnp.asarray(table) for table in dft_tables(probe_wave.shape[1])]
    rim_rows = 3 * width + 2 * (count + 2)
    own, rim_a, rim_b = call(
        patch_kernel,
        [(3, width, length), (rim_rows, length), (rim_rows, length)],
        [SMEM] * 3 + [VMEM] * 12,
        [(2, 3 * width, length), (3, 3 * width, length)],
        10**9,
        "patches",
    )(
        slot_first_rows,
        slot_first_columns,
        patch_counts,
        transmission,
        plane_a,
        plane_b,
        intensities,
        probe_wave,
        *tables,
        volume,
        rows_a,
        rows_b,
    )
    rim_a = exchange(rim_a, 0)
    rim_b = exchange(rim_b, 1)
    new_transmission, residual = call(
        fold_kernel,
        [transmission.shape, transmission.shape[1:]],
        [VMEM] * 5,
        [],
        10**6,
        "fold",
    )(own, rim_a, rim_b, projected, scaled_dual)
    by_column = [residual]
    for turn in range(1, columns):
        route = [(i, (i - turn) % columns) for i in range(columns)]
        by_column.append(lax.ppermute(residual, "angle", route))
    (base,) = call(
        variation_kernel,
        [volume.shape],
        [VMEM] * 5,
        [(count + 2, width + 16, length), (width + 16, length)],
        10**7,
        "variation",
    )(volume, rows_a, rows_b, rim_a, rim_b)
    lower = range(columns // 2)
    route = []
    for scan in range(scans):
        for column in range(columns):
            target = scan + 1 if column in lower else scan - 1
            if 0 <= target < scans:
                route.append((scan * columns + column, target * columns + column))
    beside = lax.ppermute(base, ("scan", "angle"), route)
    here = jnp.stack([block for pair in ((b, across(b)) for b in by_column) for block in pair])
    route = [(s * tiles + t, d * tiles + t) for t in range(tiles) for s, d in both[t]]
    side = lax.ppermute(here, ("scan", "tile"), route)
    other = across(side)
    new_volume, keep, send = call(
        project_kernel,
        [volume.shape, (columns, 2, width, length), (columns, 2, width, length)],
        [SMEM] * 2 + [VMEM] * 5,
        [
            (columns * tiles, 2, length // LANES, 3 * width, LANES),
            (count, 2, length // LANES, 2 * width, LANES),
        ],
        10**8,
        "project",
    )(shift_table, tap_weight, here, side, other, base, beside)
    sums = keep + across(send)
    new_projected = sums[0]
    for turn in range(1, columns):
        route = [(i, (i + turn) % columns) for i in range(columns)]
        new_projected = new_projected + lax.ppermute(sums[turn], "angle", route)
    new_projected = new_projected[None]
    new_dual = scaled_dual + new_transmission - new_projected
    return (new_transmission, new_dual, new_volume, new_projected)


def solution(mesh):
    plane = P(("groups", "angle", "tile"), None, "scan", None)
    cells = P("groups", ("angle", "tile"), "scan", None)
    slots = P(("groups", "angle", "tile"), "scan")
    return jax.shard_map(
        body,
        mesh=mesh,
        in_specs=(
            plane,
            plane,
            plane,
            cells,
            P(("groups", "angle", "tile"), "scan", None, None),
            P("groups", None, None),
            slots,
            slots,
            slots,
            P(None, ("angle", "tile")),
            P(None, ("angle", "tile")),
        ),
        out_specs=(plane, plane, cells, plane),
        check_vma=False,
    )
```

time: 190 us -> 76.4 us (0.40)
  local copies, waits for them, and re-layouts: 42.6 us -> 5.1 us
  waiting for transfers between devices: 60.6 us -> 30.8 us
  loops' own time: 16.1 us -> 0 us
  between operations: 15.2 us -> 1.42 us
  other arithmetic: 15.9 us -> 2.66 us
  matrix products: 12.2 us -> 0 us
  Pallas kernels: 0 us -> 12 us
  starting transfers between devices: 26.7 us -> 24.1 us
    reduce_scatter x1 -> x0, waiting for transfers between devices: 23.5 us -> none  [body(): lax.psum_scatter(own_columns, ('angle', 'tile'), scatter_dimension=0, til...]
    gather x20 -> x0, local copies, waits for them, and re-layouts: 17.3 us -> none
    another operation x5 -> x0, loops' own time: 16.1 us -> none  [the longest x1 15.7 us: patch_sums(): return lax.fori_loop(0, rows_one.shape[0], add_patch, running_start)]
    dynamic_update_slice x8 -> x0, local copies, waits for them, and re-layouts: 14.1 us -> none  [the longest x4 11 us: add_patch(): lax.dynamic_update_slice(running, current + contrib[slot_number], corner)]
    dot_general x16 -> x0, matrix products: 12.2 us -> none  [the longest x8 6.22 us: times_left(): jnp.einsum('ij,bjk->bik', table, values, precision=lax.Precision.HIGHEST)]
    pallas_call x0 -> x4, Pallas kernels: none -> 12 us  [the longest x1 4.37 us: body(): call(patch_kernel, [(3, width, length), (rim_rows, length), (rim_rows, le...]
    dynamic_slice x16 -> x0, local copies, waits for them, and re-layouts: 10 us -> none  [the longest x8 5.32 us: add_angle(): lax.dynamic_index_in_dim(pieces, offset_index, 0, keepdims=False)]
    unnamed x25 -> x30, local copies, waits for them, and re-layouts: 0.58 us -> 5.09 us
  transfers between devices with their start and end apart: 13 -> 14, of which waited for: 10 -> 8; matrix products, arithmetic and copies ran while one was open for 2% -> 2% of each run, Pallas kernels for 0% -> 4%
where the time goes in v1:
time: 76.4 us; the launch traced here: 76 us
  waiting for transfers between devices  30.8 us (40%)
  starting transfers between devices  24.1 us (32%)
  Pallas kernels  12 us (16%)
  local copies, waits for them, and re-layouts  5.1 us (7%)
  other arithmetic  2.66 us (3%)
  between operations  1.42 us (2%)
    ppermute x4, starting transfers between devices, exchange(): return lax.ppermute(block, 'scan', both[number])  7.45 us
    ppermute x1, waiting for transfers between devices, body(): side = lax.ppermute(here, ('scan', 'tile'), route)  7.14 us
    ppermute x4, waiting for transfers between devices, exchange(): return lax.ppermute(block, 'scan', both[number])  6.81 us
    ppermute x1, starting transfers between devices, body(): side = lax.ppermute(here, ('scan', 'tile'), route)  5.58 us
    unnamed x30, local copies, waits for them, and re-layouts  5.09 us
    ppermute x1, waiting for transfers between devices, body(): beside = lax.ppermute(base, ('scan', 'angle'), route)  4.99 us
    ppermute x1, waiting for transfers between devices, body(): by_column.append(lax.ppermute(residual, 'angle', route))  4.5 us
    ppermute x5, starting transfers between devices, across(): return lax.ppermute(block, 'tile', swap)  4.39 us
  transfers between devices with their start and end apart: 14, of which 8 were waited for; matrix products, arithmetic and copies ran while one was open for 2% of the time, Pallas kernels for 4%

profile of v1, /device:TPU:0, one launch (start us, length us, event | category | flops | bytes accessed | tf_op | source)
XLA Modules:
  0.0 76.0 jit_solution(9549495244380753096)
XLA Ops:
  0.6 0.7 collective-permute-start.3
  1.3 4.4 %collective-permute-start.2 = (f32[2,2,64,256]{3,2,1,0:T(8,128)}, f32[2,2,64,256]{3,2,1,0:T(8,128)S(1)}, u32[]{:S(2)}, u32[]{:S(2)}) collective-permute-start(f32[2,2,64,256]{3,2,1,0:T(8,128)} %volume_ref.3), channel_id=1, source_target_pairs={{0,1},{1,0},{2,3},{3,2},{4,5},{5,4},{6,7},{7,6},{8,9},{9,8},{10,11... | collective-permute-start | bytes 786440 | tf_op jit(solution)/shard_map/ppermute | solution.py:366
  5.7 1.6 %collective-permute-start = (f32[1,2,64,256]{3,2,1,0:T(8,128)}, f32[1,2,64,256]{3,2,1,0:T(8,128)S(1)}, u32[]{:S(2)}, u32[]{:S(2)}) collective-permute-start(f32[1,2,64,256]{3,2,1,0:T(8,128)} %plane_ref.1), channel_id=1, source_target_pairs={{0,4},{8,12},{4,0},{12,8},{1,5},{9,13},{5,1},{13,9},{2,6},{10,14},... | collective-permute-start | bytes 393224 | tf_op jit(solution)/shard_map/ppermute | solution.py:363
  7.3 0.7 collective-permute-start.1
  8.6 2.8 %collective-permute-done.plane_a_ref = f32[1,2,64,256]{3,2,1,0:T(8,128)S(1)} collective-permute-done((f32[1,2,64,256]{3,2,1,0:T(8,128)}, f32[1,2,64,256]{3,2,1,0:T(8,128)S(1)}, u32[]{:S(2)}, u32[]{:S(2)}) %collective-permute-start) | collective-permute-done | bytes 131104 | tf_op jit(solution)/shard_map/ppermute | solution.py:363
  11.4 0.6 copy-done.12
  12.2 0.7 copy-done.7
  12.9 4.4 %patches.1 = (f32[3,64,256]{2,1,0:T(8,128)}, f32[200,256]{1,0:T(8,128)}, f32[200,256]{1,0:T(8,128)}) custom-call(s32[1,4]{1,0:T(1,128)} %rows_ref.1, s32[1,4]{1,0:T(1,128)} %columns_ref.1, s32[1,1]{1,0:T(1,128)S(6)} %copy.21.count_ref, f32[1,2,64,256]{3,2,1,0:T(8,128)} %plane_ref.1, f32[1,2,64,256]{3,2,1,0:T(8,128)} %copy-done.12, ...), custom_call_target="tpu_custom_call" | custom-call | flops 1000000000 | bytes 1212416 | tf_op jit(solution)/shard_map/patches/pallas_call | solution.py:376
  17.3 4.6 %collective-permute-start.4 = (f32[200,256]{1,0:T(8,128)}, f32[200,256]{1,0:T(8,128)S(1)}, u32[]{:S(2)}, u32[]{:S(2)}) collective-permute-start(f32[200,256]{1,0:T(8,128)} %get-tuple-element.13), channel_id=1, source_target_pairs={{0,4},{8,12},{4,0},{12,8},{1,5},{9,13},{5,1},{13,9},{2,6},{10,14},... | collective-permute-start | bytes 614408 | tf_op jit(solution)/shard_map/ppermute | solution.py:363
  21.8 0.7 collective-permute-start.5
  22.5 4.0 %collective-permute-done.4.rim_a_ref = f32[200,256]{1,0:T(8,128)S(1)} collective-permute-done((f32[200,256]{1,0:T(8,128)}, f32[200,256]{1,0:T(8,128)S(1)}, u32[]{:S(2)}, u32[]{:S(2)}) %collective-permute-start.4) | collective-permute-done | bytes 204832 | tf_op jit(solution)/shard_map/ppermute | solution.py:363
  26.5 0.7 copy-done.1
  27.3 2.0 %fold.1 = (f32[1,2,64,256]{3,2,1,0:T(8,128)}, f32[2,64,256]{2,1,0:T(8,128)}) custom-call(f32[3,64,256]{2,1,0:T(8,128)} %get-tuple-element.12.own_ref, f32[200,256]{1,0:T(8,128)} %copy-done.1, f32[200,256]{1,0:T(8,128)} %copy-done.2, f32[1,2,64,256]{3,2,1,0:T(8,128)} %projected_ref.1, f32[1,2,64,256]{3,2,1,0:T(8,128)} %dual_ref.1), custom_call_target="tpu_custom_call" | custom-call | flops 1000000 | bytes 524288 | tf_op jit(solution)/shard_map/fold/pallas_call | solution.py:399
  29.2 0.7 collective-permute-start.7
  29.9 4.5 %collective-permute-done.7 = f32[2,64,256]{2,1,0:T(8,128)S(1)} collective-permute-done((f32[2,64,256]{2,1,0:T(8,128)}, f32[2,64,256]{2,1,0:T(8,128)S(1)}, u32[]{:S(2)}, u32[]{:S(2)}) %collective-permute-start.7) | collective-permute-done | bytes 131104 | tf_op jit(solution)/shard_map/ppermute | solution.py:410
  34.4 1.3 %collective-permute-done.8 = f32[2,64,256]{2,1,0:T(8,128)S(1)} collective-permute-done((f32[2,64,256]{2,1,0:T(8,128)S(1)}, f32[2,64,256]{2,1,0:T(8,128)S(1)}, u32[]{:S(2)}, u32[]{:S(2)}) %collective-permute-start.8) | collective-permute-done | bytes 131104 | tf_op jit(solution)/shard_map/ppermute | solution.py:366
  35.8 0.9 %pad_maximum_fusion.here_ref = f32[4,2,64,256]{3,2,1,0:T(8,128)S(1)} fusion(f32[1,2,64,256]{3,2,1,0:T(8,128)S(1)} %bitcast.19, f32[1,2,64,256]{3,2,1,0:T(8,128)S(1)} %bitcast.17, f32[1,2,64,256]{3,2,1,0:T(8,128)S(1)} %bitcast.18, f32[1,2,64,256]{3,2,1,0:T(8,128)} %bitcast.16), kind=kLoop, calls=%fused_computation | loop fusion | flops 393216 | bytes 1048576 | tf_op jit(solution)/shard_map/stack | solution.py:427
  36.7 5.6 %collective-permute-start.9 = (f32[4,2,64,256]{3,2,1,0:T(8,128)S(1)}, f32[4,2,64,256]{3,2,1,0:T(8,128)S(1)}, u32[]{:S(2)}, u32[]{:S(2)}) collective-permute-start(f32[4,2,64,256]{3,2,1,0:T(8,128)S(1)} %pad_maximum_fusion.here_ref), channel_id=1, source_target_pairs={{0,4},{8,12},{4,0},{12,8},{5,9},{9,5},{2,6},{10,14},{6,2},{14,10},... | collective-permute-start | bytes 1572872 | tf_op jit(solution)/shard_map/ppermute | solution.py:429
  42.3 7.1 %collective-permute-done.9.side_ref = f32[4,2,64,256]{3,2,1,0:T(8,128)S(1)} collective-permute-done((f32[4,2,64,256]{3,2,1,0:T(8,128)S(1)}, f32[4,2,64,256]{3,2,1,0:T(8,128)S(1)}, u32[]{:S(2)}, u32[]{:S(2)}) %collective-permute-start.9) | collective-permute-done | bytes 524320 | tf_op jit(solution)/shard_map/ppermute | solution.py:429
  49.5 2.7 %variation.1.base_ref = f32[2,2,64,256]{3,2,1,0:T(8,128)} custom-call(f32[2,2,64,256]{3,2,1,0:T(8,128)} %volume_ref.3, f32[2,2,64,256]{3,2,1,0:T(8,128)} %copy-done.7, f32[2,2,64,256]{3,2,1,0:T(8,128)} %copy-done.6, f32[200,256]{1,0:T(8,128)} %copy-done.1, f32[200,256]{1,0:T(8,128)} %copy-done.2), custom_call_target="tpu_custom_call" | custom-call | flops 10000000 | bytes 524288 | tf_op jit(solution)/shard_map/variation/pallas_call | solution.py:411
  52.1 3.9 %collective-permute-start.11 = (f32[2,2,64,256]{3,2,1,0:T(8,128)}, f32[2,2,64,256]{3,2,1,0:T(8,128)S(1)}, u32[]{:S(2)}, u32[]{:S(2)}) collective-permute-start(f32[2,2,64,256]{3,2,1,0:T(8,128)} %variation.1.base_ref), channel_id=1, source_target_pairs={{0,4},{4,8},{6,2},{8,12},{10,6},{14,10},{1,5},{5,9},{7,3},{9,13},{... | collective-permute-start | bytes 786440 | tf_op jit(solution)/shard_map/ppermute | solution.py:426
  56.1 0.7 copy.19.shift_ref
  56.8 0.7 copy.20.weight_ref
  57.4 5.0 %collective-permute-done.11.beside_ref = f32[2,2,64,256]{3,2,1,0:T(8,128)S(1)} collective-permute-done((f32[2,2,64,256]{3,2,1,0:T(8,128)}, f32[2,2,64,256]{3,2,1,0:T(8,128)S(1)}, u32[]{:S(2)}, u32[]{:S(2)}) %collective-permute-start.11) | collective-permute-done | bytes 262176 | tf_op jit(solution)/shard_map/ppermute | solution.py:426
  62.4 0.7 copy-done.8
  63.1 0.8 %copy-done.4 = f32[4,2,64,256]{3,2,1,0:T(8,128)} copy-done((f32[4,2,64,256]{3,2,1,0:T(8,128)}, f32[4,2,64,256]{3,2,1,0:T(8,128)S(1)}, u32[]{:S(2)}) %copy-start.4) | copy-done | bytes 524312
  63.9 3.0 %project.1 = (f32[2,2,64,256]{3,2,1,0:T(8,128)}, f32[2,2,64,256]{3,2,1,0:T(8,128)}, f32[2,2,64,256]{3,2,1,0:T(8,128)}) custom-call(s32[4,2]{1,0:T(4,128)} %copy.19.shift_ref, f32[4,2]{1,0:T(4,128)} %copy.20.weight_ref, f32[4,2,64,256]{3,2,1,0:T(8,128)} %copy-done, f32[4,2,64,256]{3,2,1,0:T(8,128)} %copy-done.3, f32[4,2,64,256]{3,2,1,0:T(8,128)} %copy-done.4, ...), custom_call_target="tpu_custom_call" | custom-call | flops 100000000 | bytes 1572864 | tf_op jit(solution)/shard_map/project/pallas_call | solution.py:431
  66.9 1.7 %collective-permute-done.12 = f32[2,2,64,256]{3,2,1,0:T(8,128)S(1)} collective-permute-done((f32[2,2,64,256]{3,2,1,0:T(8,128)}, f32[2,2,64,256]{3,2,1,0:T(8,128)S(1)}, u32[]{:S(2)}, u32[]{:S(2)}) %collective-permute-start.12) | collective-permute-done | bytes 262176 | tf_op jit(solution)/shard_map/ppermute | solution.py:366
  68.6 1.0 %add.10 = f32[2,2,64,256]{3,2,1,0:T(8,128)S(1)} add(f32[2,2,64,256]{3,2,1,0:T(8,128)} %get-tuple-element.17, f32[2,2,64,256]{3,2,1,0:T(8,128)S(1)} %collective-permute-done.12) | non-fusion elementwise | flops 65536 | bytes 786432 | tf_op jit(solution)/shard_map/add | solution.py:442
  69.7 1.4 %collective-permute-start.13 = (f32[2,64,256]{2,1,0:T(8,128)S(1)}, f32[2,64,256]{2,1,0:T(8,128)S(1)}, u32[]{:S(2)}, u32[]{:S(2)}) collective-permute-start(f32[2,64,256]{2,1,0:T(8,128)S(1)} %slice_bitcast_fusion), channel_id=1, source_target_pairs={{0,2},{2,0},{1,3},{3,1},{4,6},{6,4},{5,7},{7,5},{8,10},{10,8},{9,1... | collective-permute-start | bytes 393224 | tf_op jit(solution)/shard_map/ppermute | solution.py:446
  71.0 4.2 %collective-permute-done.13 = f32[2,64,256]{2,1,0:T(8,128)S(1)} collective-permute-done((f32[2,64,256]{2,1,0:T(8,128)S(1)}, f32[2,64,256]{2,1,0:T(8,128)S(1)}, u32[]{:S(2)}, u32[]{:S(2)}) %collective-permute-start.13) | collective-permute-done | bytes 131104 | tf_op jit(solution)/shard_map/ppermute | solution.py:446
  75.3 0.7 add_subtract_fusion
  (34 shorter events, 0.3 us)
Async XLA Ops:
  0.6 10.8 %collective-permute-start.3 = (f32[2,2,64,256]{3,2,1,0:T(8,128)}, f32[2,2,64,256]{3,2,1,0:T(8,128)S(1)}, u32[]{:S(2)}, u32[]{:S(2)}) collective-permute-start(f32[2,2,64,256]{3,2,1,0:T(8,128)} %volume_ref.3), channel_id=1, source_target_pairs={{1,2},{2,1},{5,6},{6,5},{9,10},{10,9},{13,14},{14,13},{17,18},{18,... | collective-permute-start | bytes 786440 | tf_op jit(solution)/shard_map/ppermute | solution.py:373
  1.3 10.1 %collective-permute-start.2 = (f32[2,2,64,256]{3,2,1,0:T(8,128)}, f32[2,2,64,256]{3,2,1,0:T(8,128)S(1)}, u32[]{:S(2)}, u32[]{:S(2)}) collective-permute-start(f32[2,2,64,256]{3,2,1,0:T(8,128)} %volume_ref.3), channel_id=1, source_target_pairs={{0,1},{1,0},{2,3},{3,2},{4,5},{5,4},{6,7},{7,6},{8,9},{9,8},{10,11... | collective-permute-start | bytes 786440 | tf_op jit(solution)/shard_map/ppermute | solution.py:366
  5.7 5.7 %collective-permute-start = (f32[1,2,64,256]{3,2,1,0:T(8,128)}, f32[1,2,64,256]{3,2,1,0:T(8,128)S(1)}, u32[]{:S(2)}, u32[]{:S(2)}) collective-permute-start(f32[1,2,64,256]{3,2,1,0:T(8,128)} %plane_ref.1), channel_id=1, source_target_pairs={{0,4},{8,12},{4,0},{12,8},{1,5},{9,13},{5,1},{13,9},{2,6},{10,14},... | collective-permute-start | bytes 393224 | tf_op jit(solution)/shard_map/ppermute | solution.py:363
  7.3 4.1 %collective-permute-start.1 = (f32[1,2,64,256]{3,2,1,0:T(8,128)}, f32[1,2,64,256]{3,2,1,0:T(8,128)S(1)}, u32[]{:S(2)}, u32[]{:S(2)}) collective-permute-start(f32[1,2,64,256]{3,2,1,0:T(8,128)} %plane_ref.1), channel_id=1, source_target_pairs={{4,8},{8,4},{5,9},{9,5},{6,10},{10,6},{7,11},{11,7},{20,24},{24,20... | collective-permute-start | bytes 393224 | tf_op jit(solution)/shard_map/ppermute | solution.py:363
  11.4 0.7 copy-start.12
  11.4 0.7 copy-start.13
  11.4 0.8 %copy-start.6 = (f32[2,2,64,256]{3,2,1,0:T(8,128)}, f32[2,2,64,256]{3,2,1,0:T(8,128)S(1)}, u32[]{:S(2)}) copy-start(f32[2,2,64,256]{3,2,1,0:T(8,128)S(1)} %collective-permute-done.3.yb_ref) | copy-start | bytes 786436
  12.2 0.7 copy-start.7
  17.3 9.2 %collective-permute-start.4 = (f32[200,256]{1,0:T(8,128)}, f32[200,256]{1,0:T(8,128)S(1)}, u32[]{:S(2)}, u32[]{:S(2)}) collective-permute-start(f32[200,256]{1,0:T(8,128)} %get-tuple-element.13), channel_id=1, source_target_pairs={{0,4},{8,12},{4,0},{12,8},{1,5},{9,13},{5,1},{13,9},{2,6},{10,14},... | collective-permute-start | bytes 614408 | tf_op jit(solution)/shard_map/ppermute | solution.py:363
  21.8 4.7 %collective-permute-start.5 = (f32[200,256]{1,0:T(8,128)}, f32[200,256]{1,0:T(8,128)S(1)}, u32[]{:S(2)}, u32[]{:S(2)}) collective-permute-start(f32[200,256]{1,0:T(8,128)} %get-tuple-element.14), channel_id=1, source_target_pairs={{4,8},{8,4},{5,9},{9,5},{6,10},{10,6},{7,11},{11,7},{20,24},{24,20... | collective-permute-start | bytes 614408 | tf_op jit(solution)/shard_map/ppermute | solution.py:363
  26.5 0.7 copy-start.1
  26.5 0.8 %copy-start.2 = (f32[200,256]{1,0:T(8,128)}, f32[200,256]{1,0:T(8,128)S(1)}, u32[]{:S(2)}) copy-start(f32[200,256]{1,0:T(8,128)S(1)} %collective-permute-done.5.rim_b_ref) | copy-start | bytes 614404
  29.2 5.2 %collective-permute-start.7 = (f32[2,64,256]{2,1,0:T(8,128)}, f32[2,64,256]{2,1,0:T(8,128)S(1)}, u32[]{:S(2)}, u32[]{:S(2)}) collective-permute-start(f32[2,64,256]{2,1,0:T(8,128)} %get-tuple-element.16), channel_id=1, source_target_pairs={{0,2},{2,0},{1,3},{3,1},{4,6},{6,4},{5,7},{7,5},{8,10},{10,8},{9,1... | collective-permute-start | bytes 393224 | tf_op jit(solution)/shard_map/ppermute | solution.py:410
  29.9 4.5 %collective-permute-start.6 = (f32[2,64,256]{2,1,0:T(8,128)}, f32[2,64,256]{2,1,0:T(8,128)S(1)}, u32[]{:S(2)}, u32[]{:S(2)}) collective-permute-start(f32[2,64,256]{2,1,0:T(8,128)} %get-tuple-element.16), channel_id=1, source_target_pairs={{0,1},{1,0},{2,3},{3,2},{4,5},{5,4},{6,7},{7,6},{8,9},{9,8},{10,11... | collective-permute-start | bytes 393224 | tf_op jit(solution)/shard_map/ppermute | solution.py:366
  34.4 1.3 %collective-permute-start.8 = (f32[2,64,256]{2,1,0:T(8,128)S(1)}, f32[2,64,256]{2,1,0:T(8,128)S(1)}, u32[]{:S(2)}, u32[]{:S(2)}) collective-permute-start(f32[2,64,256]{2,1,0:T(8,128)S(1)} %collective-permute-done.7), channel_id=1, source_target_pairs={{0,1},{1,0},{2,3},{3,2},{4,5},{5,4},{6,7},{7,6},{8,9},{9,8},{10,11... | collective-permute-start | bytes 393224 | tf_op jit(solution)/shard_map/ppermute | solution.py:366
  36.7 15.4 %copy-start = (f32[4,2,64,256]{3,2,1,0:T(8,128)}, f32[4,2,64,256]{3,2,1,0:T(8,128)S(1)}, u32[]{:S(2)}) copy-start(f32[4,2,64,256]{3,2,1,0:T(8,128)S(1)} %pad_maximum_fusion.here_ref) | copy-start | bytes 1572868
  36.7 19.4 %copy-start.10 = (s32[4,2]{0,1:T(2,128)S(1)}, s32[4,2]{0,1:T(2,128)}, u32[]{:S(2)}) copy-start(s32[4,2]{0,1:T(2,128)} %param.24) | copy-start | bytes 100
  36.7 12.7 %collective-permute-start.9 = (f32[4,2,64,256]{3,2,1,0:T(8,128)S(1)}, f32[4,2,64,256]{3,2,1,0:T(8,128)S(1)}, u32[]{:S(2)}, u32[]{:S(2)}) collective-permute-start(f32[4,2,64,256]{3,2,1,0:T(8,128)S(1)} %pad_maximum_fusion.here_ref), channel_id=1, source_target_pairs={{0,4},{8,12},{4,0},{12,8},{5,9},{9,5},{2,6},{10,14},{6,2},{14,10},... | collective-permute-start | bytes 1572872 | tf_op jit(solution)/shard_map/ppermute | solution.py:429
  49.5 2.7 %copy-start.3 = (f32[4,2,64,256]{3,2,1,0:T(8,128)}, f32[4,2,64,256]{3,2,1,0:T(8,128)S(1)}, u32[]{:S(2)}) copy-start(f32[4,2,64,256]{3,2,1,0:T(8,128)S(1)} %collective-permute-done.9.side_ref) | copy-start | bytes 1572868
  49.5 13.0 %collective-permute-start.10 = (f32[4,2,64,256]{3,2,1,0:T(8,128)S(1)}, f32[4,2,64,256]{3,2,1,0:T(8,128)S(1)}, u32[]{:S(2)}, u32[]{:S(2)}) collective-permute-start(f32[4,2,64,256]{3,2,1,0:T(8,128)S(1)} %collective-permute-done.9.side_ref), channel_id=1, source_target_pairs={{0,1},{1,0},{2,3},{3,2},{4,5},{5,4},{6,7},{7,6},{8,9},{9,8},{10,11... | collective-permute-start | bytes 1572872 | tf_op jit(solution)/shard_map/ppermute | solution.py:366
  52.1 4.6 %copy-start.11 = (f32[4,2]{0,1:T(2,128)S(1)}, f32[4,2]{0,1:T(2,128)}, u32[]{:S(2)}) copy-start(f32[4,2]{0,1:T(2,128)} %param.25) | copy-start | bytes 100
  52.1 10.3 %collective-permute-start.11 = (f32[2,2,64,256]{3,2,1,0:T(8,128)}, f32[2,2,64,256]{3,2,1,0:T(8,128)S(1)}, u32[]{:S(2)}, u32[]{:S(2)}) collective-permute-start(f32[2,2,64,256]{3,2,1,0:T(8,128)} %variation.1.base_ref), channel_id=1, source_target_pairs={{0,4},{4,8},{6,2},{8,12},{10,6},{14,10},{1,5},{5,9},{7,3},{9,13},{... | collective-permute-start | bytes 786440 | tf_op jit(solution)/shard_map/ppermute | solution.py:426
  62.4 0.7 copy-start.8
  63.1 0.8 %copy-start.4 = (f32[4,2,64,256]{3,2,1,0:T(8,128)}, f32[4,2,64,256]{3,2,1,0:T(8,128)S(1)}, u32[]{:S(2)}) copy-start(f32[4,2,64,256]{3,2,1,0:T(8,128)S(1)} %collective-permute-done.10.other_ref) | copy-start | bytes 1572868
  66.9 1.7 %collective-permute-start.12 = (f32[2,2,64,256]{3,2,1,0:T(8,128)}, f32[2,2,64,256]{3,2,1,0:T(8,128)S(1)}, u32[]{:S(2)}, u32[]{:S(2)}) collective-permute-start(f32[2,2,64,256]{3,2,1,0:T(8,128)} %get-tuple-element.18), channel_id=1, source_target_pairs={{0,1},{1,0},{2,3},{3,2},{4,5},{5,4},{6,7},{7,6},{8,9},{9,8},{10,11... | collective-permute-start | bytes 786440 | tf_op jit(solution)/shard_map/ppermute | solution.py:366
  69.6 5.6 %copy-start.5 = (f32[1,2,64,256]{3,2,1,0:T(8,128)S(1)}, f32[1,2,64,256]{3,2,1,0:T(8,128)}, u32[]{:S(2)}) copy-start(f32[1,2,64,256]{3,2,1,0:T(8,128)} %dual_ref.1) | copy-start | bytes 393220
  69.6 5.6 %copy-start.9 = (f32[1,2,64,256]{3,2,1,0:T(8,128)S(1)}, f32[1,2,64,256]{3,2,1,0:T(8,128)}, u32[]{:S(2)}) copy-start(f32[1,2,64,256]{3,2,1,0:T(8,128)} %get-tuple-element.8) | copy-start | bytes 393220
  69.7 5.6 %collective-permute-start.13 = (f32[2,64,256]{2,1,0:T(8,128)S(1)}, f32[2,64,256]{2,1,0:T(8,128)S(1)}, u32[]{:S(2)}, u32[]{:S(2)}) collective-permute-start(f32[2,64,256]{2,1,0:T(8,128)S(1)} %slice_bitcast_fusion), channel_id=1, source_target_pairs={{0,2},{2,0},{1,3},{3,1},{4,6},{6,4},{5,7},{7,5},{8,10},{10,8},{9,1... | collective-permute-start | bytes 393224 | tf_op jit(solution)/shard_map/ppermute | solution.py:446

commit v2 on v1

--- a/solution.py
+++ b/solution.py
@@ -8,6 +8,7 @@
 from jax.experimental.pallas import tpu as pltpu
 from jax.sharding import PartitionSpec as P
 
+
 penalty = 4.0
 amplitude_step = 0.25
 tv_weight = 1.0
@@ -16,7 +17,9 @@
 
 VMEM = pl.BlockSpec(memory_space=pltpu.VMEM)
 SMEM = pl.BlockSpec(memory_space=pltpu.SMEM)
+HBM = pl.BlockSpec(memory_space=pltpu.MemorySpace.HBM)
 LANES = 128
+SPARE_BYTES = 8 << 20
 
 
 def split(values):
@@ -59,20 +62,67 @@
     return (below, above)
 
 
+def slot_masks(rows_ref, columns_ref, count_ref, slot, side):
+    lanes = lax.broadcasted_iota(jnp.int32, (side, side), 1)
+    sublanes = lax.broadcasted_iota(jnp.int32, (side, side), 0)
+    near_lanes = lanes >= rows_ref[0, slot]
+    near_columns = sublanes >= columns_ref[0, slot]
+    return (near_lanes, near_columns, jnp.full((side, side), slot < count_ref[0, 0]))
+
+
+def place(totals, part, term, masks, width):
+    side = term.shape[0]
+    near_lanes, near_columns, live = masks
+    inner = live & near_columns
+    outer = (live & jnp.logical_not(near_columns))[:width]
+    for start, lane_mask in ((0, near_lanes), (side, jnp.logical_not(near_lanes))):
+        at = slice(start, start + side)
+        totals[part, :side, at] += jnp.where(inner & lane_mask, term, 0.0)
+        totals[part, side:, at] += jnp.where(outer & lane_mask[:width], term[:width], 0.0)
+
+
+def prepare_kernel(rows_ref, columns_ref, count_ref, probe_ref, *refs):
+    half = (len(refs) - 3) // 2
+    sources, (probes_ref, density_ref), targets, done = refs[:half], refs[half : half + 2], refs[half + 2 : -1], refs[-1]
+    copies = [
+        pltpu.make_async_copy(source, target, done.at[number])
+        for number, (source, target) in enumerate(zip(sources, targets))
+    ]
+    for copy in copies:
+        copy.start()
+    side = probe_ref.shape[1]
+    slots = probes_ref.shape[0]
+    width = density_ref.shape[1] - side
+    density_ref[...] = jnp.zeros_like(density_ref)
+    for slot in range(slots):
+        turn = lax.rem(rows_ref[0, slot], side)
+        probe = [
+            pltpu.roll(pltpu.roll(probe_ref[part], columns_ref[0, slot], 0), turn, 1)
+            for part in range(2)
+        ]
+        for part in range(2):
+            probes_ref[slot, part] = probe[part]
+        masks = slot_masks(rows_ref, columns_ref, count_ref, slot, side)
+        place(density_ref, 0, probe[0] * probe[0] + probe[1] * probe[1], masks, width)
+    for copy in copies:
+        copy.wait()
+
+
 def patch_kernel(
     rows_ref,
     columns_ref,
     count_ref,
+    probes_ref,
+    density_ref,
     plane_ref,
-    plane_a_ref,
-    plane_b_ref,
     intensity_ref,
-    probe_ref,
+    volume_ref,
     forward_high_ref,
     forward_low_ref,
     inverse_high_ref,
     inverse_low_ref,
-    volume_ref,
+    plane_a_ref,
+    plane_b_ref,
     ya_ref,
     yb_ref,
     own_ref,
@@ -82,26 +132,20 @@
     totals,
 ):
     width = plane_ref.shape[2]
-    side = probe_ref.shape[1]
-    slots = intensity_ref.shape[1]
+    slots, _, side, _ = probes_ref.shape
     even = scan_is_even()
     at_a = pl.multiple_of(jnp.where(even, 2 * width, 0), width)
     at_b = pl.multiple_of(jnp.where(even, 0, 2 * width), width)
     wide[:, width : 2 * width] = plane_ref[0]
     wide[:, pl.ds(at_a, width)] = plane_a_ref[0]
     wide[:, pl.ds(at_b, width)] = plane_b_ref[0]
-    lanes = lax.broadcasted_iota(jnp.int32, (side, side), 1)
-    sublanes = lax.broadcasted_iota(jnp.int32, (side, side), 0)
     forward = (forward_high_ref[...], forward_low_ref[...])
     inverse = (inverse_high_ref[...], inverse_low_ref[...])
-    probes, waves, masks = [], [], []
+    waves, masks = [], []
     for slot in range(slots):
-        column = columns_ref[0, slot]
-        row = rows_ref[0, slot]
-        turn = lax.rem(row, side)
-        probe = [pltpu.roll(pltpu.roll(probe_ref[part], column, 0), turn, 1) for part in range(2)]
-        near_lanes = lanes >= row
-        near_columns = sublanes >= column
+        probe = probes_ref[slot]
+        masks.append(slot_masks(rows_ref, columns_ref, count_ref, slot, side))
+        near_lanes, near_columns, _ = masks[slot]
         window = []
         for part in range(2):
             near = jnp.where(near_lanes, wide[part, :side, :side], wide[part, :side, side:])
@@ -112,10 +156,7 @@
             window.append(jnp.where(near_columns, near, wrapped))
         wave_real = probe[0] * window[0] - probe[1] * window[1]
         wave_imaginary = probe[0] * window[1] + probe[1] * window[0]
-        probes.append(probe)
         waves.append(jnp.concatenate([wave_real, wave_imaginary], axis=1))
-        live = jnp.full((side, side), slot < count_ref[0, 0])
-        masks.append((near_lanes, near_columns, live))
     half = product(split(jnp.concatenate(waves, axis=0)), inverse)
     half = jnp.concatenate(
         [
@@ -148,24 +189,14 @@
         axis=0,
     )
     near = product(split(half), forward)
-    totals[...] = jnp.zeros_like(totals)
+    totals[:2] = jnp.zeros_like(totals[:2])
+    totals[2:] = density_ref[...]
     for slot in range(slots):
-        probe = probes[slot]
+        probe = probes_ref[slot]
         near_real = near[slot * side : (slot + 1) * side, :side]
         near_imaginary = near[slot * side : (slot + 1) * side, side:]
-        terms = (
-            probe[0] * near_real + probe[1] * near_imaginary,
-            probe[0] * near_imaginary - probe[1] * near_real,
-            probe[0] * probe[0] + probe[1] * probe[1],
-        )
-        near_lanes, near_columns, live = masks[slot]
-        inner = live & near_columns
-        outer = (live & jnp.logical_not(near_columns))[:width]
-        for part, term in enumerate(terms):
-            for start, lane_mask in ((0, near_lanes), (side, jnp.logical_not(near_lanes))):
-                at = slice(start, start + side)
-                totals[part, :side, at] += jnp.where(inner & lane_mask, term, 0.0)
-                totals[part, side:, at] += jnp.where(outer & lane_mask[:width], term[:width], 0.0)
+        place(totals, 0, probe[0] * near_real + probe[1] * near_imaginary, masks[slot], width)
+        place(totals, 1, probe[0] * near_imaginary - probe[1] * near_real, masks[slot], width)
     own_ref[...] = totals[:, width : 2 * width]
     below_above = [outer_rows(ya_ref, yb_ref, channel) for channel in range(2)]
     parts = totals.shape[0]
@@ -260,8 +291,11 @@
     shift_ref,
     weight_ref,
     here_ref,
-    side_ref,
-    other_ref,
+    side_a_ref,
+    side_b_ref,
+    here_too_ref,
+    side_a_too_ref,
+    side_b_too_ref,
     base_ref,
     beside_ref,
     volume_ref,
@@ -272,27 +306,26 @@
 ):
     width = base_ref.shape[2]
     count = base_ref.shape[1]
-    angles = here_ref.shape[0]
+    columns = here_ref.shape[0]
     tiles = lax.axis_size("tile")
-    columns = angles // tiles
+    angles = columns * tiles
     me, tile, scan = lax.axis_index("angle"), lax.axis_index("tile"), lax.axis_index("scan")
     upper = me >= columns // 2
-    right = lax.rem(scan + tile, 2) == 0
-    side_at = pl.multiple_of(jnp.where(right, 2 * width, 0), width)
-    other_at = pl.multiple_of(jnp.where(right, 0, 2 * width), width)
+    even = scan_is_even()
+    at_a = pl.multiple_of(jnp.where(even, 2 * width, 0), width)
+    at_b = pl.multiple_of(jnp.where(even, 0, 2 * width), width)
 
     def angle_of(turn, flip):
         return lax.rem(me + turn, columns) * tiles + (tile if flip == 0 else 1 - tile)
 
     chunks = [slice(at, at + LANES) for at in range(0, base_ref.shape[3], LANES)]
+    blocks = ((here_ref, side_a_ref, side_b_ref), (here_too_ref, side_a_too_ref, side_b_too_ref))
     for turn in range(columns):
         for flip in range(tiles):
-            block = turn * tiles + flip
+            angle = angle_of(turn, flip)
             for chunk, at in enumerate(chunks):
-                near, far = angle_of(turn, flip), angle_of(turn, 1 - flip)
-                wide[near, :, chunk, width : 2 * width] = here_ref[block, :, :, at]
-                wide[near, :, chunk, pl.ds(side_at, width)] = side_ref[block, :, :, at]
-                wide[far, :, chunk, pl.ds(other_at, width)] = other_ref[block, :, :, at]
+                for ref, start in zip(blocks[flip], (width, at_a, at_b)):
+                    wide[angle, :, chunk, pl.ds(start, width)] = ref[turn, :, :, at]
     exists = jnp.where(upper, scan < lax.axis_size("scan") - 1, scan > 0).astype(jnp.float32)
     own_at = pl.multiple_of(jnp.where(upper, 0, width), width)
     beside_at = pl.multiple_of(jnp.where(upper, width, 0), width)
@@ -301,8 +334,8 @@
             for chunk, at in enumerate(chunks):
                 total = jnp.zeros((2 * width, LANES), jnp.float32)
                 for angle in range(angles):
-                    start = jnp.where(upper, width, 0) - shift_ref[angle, row]
-                    fraction = weight_ref[angle, row]
+                    start = jnp.where(upper, width, 0) - shift_ref[row, angle]
+                    fraction = weight_ref[row, angle]
                     total += (1.0 - fraction) * wide[angle, channel, chunk, pl.ds(start, 2 * width)]
                     total += fraction * wide[angle, channel, chunk, pl.ds(start - 1, 2 * width)]
                 updated[row, channel, chunk] = total
@@ -319,24 +352,32 @@
                 for chunk, at in enumerate(chunks):
                     total = jnp.zeros((width, LANES), jnp.float32)
                     for row in range(count):
-                        start = jnp.where(upper, 0, width) + shift_ref[angle, row]
-                        fraction = weight_ref[angle, row]
+                        start = jnp.where(upper, 0, width) + shift_ref[row, angle]
+                        fraction = weight_ref[row, angle]
                         total += (1.0 - fraction) * updated[row, channel, chunk, pl.ds(start, width)]
                         total += fraction * updated[row, channel, chunk, pl.ds(start + 1, width)]
                     out_ref[turn, channel, :, at] = total
 
 
-def call(kernel, shapes, in_specs, scratch, flops, name):
-    moved = 4 * sum(math.prod(shape) for shape in shapes)
+def call(kernel, shapes, operands, scratch, flops, scalars=0, staged=()):
+    held = sum(operand.nbytes for operand in operands[scalars:] + staged)
+    held += 4 * sum(math.prod(shape) for shape in shapes)
+    own = 4 * sum(math.prod(shape) for shape in scratch)
+    outputs = [jax.ShapeDtypeStruct(shape, jnp.float32) for shape in shapes]
+    outputs += [jax.ShapeDtypeStruct(array.shape, array.dtype) for array in staged]
+    scratch_shapes = [pltpu.VMEM(shape, jnp.float32) for shape in scratch]
+    if staged:
+        scratch_shapes.append(pltpu.SemaphoreType.DMA((len(staged),)))
+    in_specs = [SMEM] * scalars + [VMEM] * (len(operands) - scalars) + [HBM] * len(staged)
     return pl.pallas_call(
         kernel,
-        name=name,
-        out_shape=[jax.ShapeDtypeStruct(shape, jnp.float32) for shape in shapes],
+        out_shape=outputs,
         in_specs=in_specs,
-        out_specs=[VMEM] * len(shapes),
-        scratch_shapes=[pltpu.VMEM(shape, jnp.float32) for shape in scratch],
-        cost_estimate=pl.CostEstimate(flops=flops, bytes_accessed=2 * moved, transcendentals=0),
-    )
+        out_specs=[VMEM] * len(outputs),
+        scratch_shapes=scratch_shapes,
+        compiler_params=pltpu.CompilerParams(vmem_limit_bytes=held + own + SPARE_BYTES),
+        cost_estimate=pl.CostEstimate(flops=flops, bytes_accessed=held, transcendentals=0),
+    )(*operands, *(pltpu.with_memory_space_constraint(array, pltpu.HBM) for array in staged))
 
 
 def body(
@@ -367,43 +408,42 @@
 
     plane_a = exchange(transmission, 0)
     plane_b = exchange(transmission, 1)
-    rows_a = across(volume)
     bridge = [(i * tiles + 1, (i + 1) * tiles) for i in range(columns - 1)]
     bridge += [(target, source) for source, target in bridge]
     rows_b = lax.ppermute(volume, ("angle", "tile"), bridge)
+    rows_a = across(volume)
     tables = [jnp.asarray(table) for table in dft_tables(probe_wave.shape[1])]
     rim_rows = 3 * width + 2 * (count + 2)
+    scalars = (slot_first_rows, slot_first_columns, patch_counts)
+    slots = slot_first_rows.shape[1]
+    side = probe_wave.shape[1]
+    prepared = call(
+        prepare_kernel,
+        [(slots, 2, side, side), (1, 3 * width, length)],
+        (*scalars, probe_wave),
+        [],
+        10**7,
+        3,
+        (transmission, intensities, volume, *tables),
+    )
+    volume_here = prepared[4]
     own, rim_a, rim_b = call(
         patch_kernel,
         [(3, width, length), (rim_rows, length), (rim_rows, length)],
-        [SMEM] * 3 + [VMEM] * 12,
+        (*scalars, *prepared, plane_a, plane_b, rows_a, rows_b),
         [(2, 3 * width, length), (3, 3 * width, length)],
         10**9,
-        "patches",
-    )(
-        slot_first_rows,
-        slot_first_columns,
-        patch_counts,
-        transmission,
-        plane_a,
-        plane_b,
-        intensities,
-        probe_wave,
-        *tables,
-        volume,
-        rows_a,
-        rows_b,
+        3,
     )
     rim_a = exchange(rim_a, 0)
     rim_b = exchange(rim_b, 1)
     new_transmission, residual = call(
         fold_kernel,
         [transmission.shape, transmission.shape[1:]],
-        [VMEM] * 5,
+        (own, rim_a, rim_b, projected, scaled_dual),
         [],
         10**6,
-        "fold",
-    )(own, rim_a, rim_b, projected, scaled_dual)
+    )
     by_column = [residual]
     for turn in range(1, columns):
         route = [(i, (i - turn) % columns) for i in range(columns)]
@@ -411,11 +451,10 @@
     (base,) = call(
         variation_kernel,
         [volume.shape],
-        [VMEM] * 5,
+        (volume_here, rows_a, rows_b, rim_a, rim_b),
         [(count + 2, width + 16, length), (width + 16, length)],
         10**7,
-        "variation",
-    )(volume, rows_a, rows_b, rim_a, rim_b)
+    )
     lower = range(columns // 2)
     route = []
     for scan in range(scans):
@@ -424,26 +463,27 @@
             if 0 <= target < scans:
                 route.append((scan * columns + column, target * columns + column))
     beside = lax.ppermute(base, ("scan", "angle"), route)
-    here = jnp.stack([block for pair in ((b, across(b)) for b in by_column) for block in pair])
-    route = [(s * tiles + t, d * tiles + t) for t in range(tiles) for s, d in both[t]]
-    side = lax.ppermute(here, ("scan", "tile"), route)
-    other = across(side)
+    here = jnp.stack(by_column)
+    side_a = exchange(here, 0)
+    side_b = exchange(here, 1)
+    shared = [across(block) for block in (here, side_a, side_b)]
     new_volume, keep, send = call(
         project_kernel,
         [volume.shape, (columns, 2, width, length), (columns, 2, width, length)],
-        [SMEM] * 2 + [VMEM] * 5,
+        (shift_table.T, tap_weight.T, here, side_a, side_b, *shared, base, beside),
         [
             (columns * tiles, 2, length // LANES, 3 * width, LANES),
             (count, 2, length // LANES, 2 * width, LANES),
         ],
         10**8,
-        "project",
-    )(shift_table, tap_weight, here, side, other, base, beside)
-    sums = keep + across(send)
-    new_projected = sums[0]
+        2,
+    )
+    received = across(send)
+    new_projected = keep[0] + received[0]
     for turn in range(1, columns):
         route = [(i, (i + turn) % columns) for i in range(columns)]
-        new_projected = new_projected + lax.ppermute(sums[turn], "angle", route)
+        part = lax.ppermute(keep[turn] + received[turn], "angle", route)
+        new_projected = new_projected + part
     new_projected = new_projected[None]
     new_dual = scaled_dual + new_transmission - new_projected
     return (new_transmission, new_dual, new_volume, new_projected)

time: 76.4 us -> 54.8 us (0.72)
  waiting for transfers between devices: 30.8 us -> 19 us
  Pallas kernels: 12 us -> 7.47 us
  local copies, waits for them, and re-layouts: 5.1 us -> 1.59 us
  other arithmetic: 2.66 us -> 0.78 us
    ppermute x2 -> x1, waiting for transfers between devices: 11.4 us -> 3.8 us  [body(): part = lax.ppermute(keep[turn] + received[turn], 'angle', route)]
    ppermute x4 -> x6, starting transfers between devices: 7.45 us -> 13.6 us  [exchange(): return lax.ppermute(block, 'scan', both[number])]
    ppermute x2 -> x1, starting transfers between devices: 6.95 us -> 2.41 us  [body(): part = lax.ppermute(keep[turn] + received[turn], 'angle', route)]
    pallas_call x4 -> x5, Pallas kernels: 12 us -> 7.47 us  [call(): pl.pallas_call(kernel, out_shape=outputs, in_specs=in_specs, out_specs=[V...]
    unnamed x30 -> x16, local copies, waits for them, and re-layouts: 5.09 us -> 1.59 us
    ppermute x1, waiting for transfers between devices: 4.99 us -> 2.81 us  [body(): beside = lax.ppermute(base, ('scan', 'angle'), route)]
    ppermute x1, starting transfers between devices: 3.93 us -> 1.95 us  [body(): beside = lax.ppermute(base, ('scan', 'angle'), route)]
    ppermute x5, waiting for transfers between devices: 3.09 us -> 1.54 us  [across(): return lax.ppermute(block, 'tile', swap)]
  transfers between devices with their start and end apart: 14 -> 15, of which waited for: 8 -> 7; matrix products, arithmetic and copies ran while one was open for 2% -> 0% of each run, Pallas kernels for 4% -> 4%
where the time goes in v2:
time: 54.8 us; the launch traced here: 54.6 us
  starting transfers between devices  24.3 us (44%)
  waiting for transfers between devices  19 us (35%)
  Pallas kernels  7.47 us (14%)
  local copies, waits for them, and re-layouts  1.59 us (3%)
  between operations  1.46 us (3%)
  other arithmetic  0.78 us (1%)
    ppermute x6, starting transfers between devices, exchange(): return lax.ppermute(block, 'scan', both[number])  13.6 us
    pallas_call x5, Pallas kernels, call(): pl.pallas_call(kernel, out_shape=outputs, in_specs=in_specs, out_specs=[V...  7.47 us
    ppermute x6, waiting for transfers between devices, exchange(): return lax.ppermute(block, 'scan', both[number])  6.43 us
    ppermute x5, starting transfers between devices, across(): return lax.ppermute(block, 'tile', swap)  4.94 us
    ppermute x1, waiting for transfers between devices, body(): by_column.append(lax.ppermute(residual, 'angle', route))  4.38 us
    ppermute x1, waiting for transfers between devices, body(): part = lax.ppermute(keep[turn] + received[turn], 'angle', route)  3.8 us
    ppermute x1, waiting for transfers between devices, body(): beside = lax.ppermute(base, ('scan', 'angle'), route)  2.81 us
    ppermute x1, starting transfers between devices, body(): part = lax.ppermute(keep[turn] + received[turn], 'angle', route)  2.41 us
  transfers between devices with their start and end apart: 15, of which 7 were waited for; matrix products, arithmetic and copies ran while one was open for 0% of the time, Pallas kernels for 4%

profile of v2, /device:TPU:0, one launch (start us, length us, event | category | flops | bytes accessed | tf_op | source)
XLA Modules:
  0.0 54.6 jit_solution(11399561437530914005)
XLA Ops:
  0.7 0.8 %collective-permute-start.3 = (f32[2,2,64,256]{3,2,1,0:T(8,128)}, f32[2,2,64,256]{3,2,1,0:T(8,128)S(1)}, u32[]{:S(2)}, u32[]{:S(2)}) collective-permute-start(f32[2,2,64,256]{3,2,1,0:T(8,128)} %refs_2_.1), channel_id=1, source_target_pairs={{1,2},{2,1},{5,6},{6,5},{9,10},{10,9},{13,14},{14,13},{17,18},{18,... | collective-permute-start | bytes 786440 | tf_op jit(solution)/shard_map/ppermute | solution.py:413
  1.5 4.4 %collective-permute-start.2 = (f32[2,2,64,256]{3,2,1,0:T(8,128)}, f32[2,2,64,256]{3,2,1,0:T(8,128)S(1)}, u32[]{:S(2)}, u32[]{:S(2)}) collective-permute-start(f32[2,2,64,256]{3,2,1,0:T(8,128)} %refs_2_.1), channel_id=1, source_target_pairs={{0,1},{1,0},{2,3},{3,2},{4,5},{5,4},{6,7},{7,6},{8,9},{9,8},{10,11... | collective-permute-start | bytes 786440 | tf_op jit(solution)/shard_map/ppermute | solution.py:407
  5.8 0.7 %collective-permute-start.1 = (f32[1,2,64,256]{3,2,1,0:T(8,128)}, f32[1,2,64,256]{3,2,1,0:T(8,128)S(1)}, u32[]{:S(2)}, u32[]{:S(2)}) collective-permute-start(f32[1,2,64,256]{3,2,1,0:T(8,128)} %refs_0_.1), channel_id=1, source_target_pairs={{4,8},{8,4},{5,9},{9,5},{6,10},{10,6},{7,11},{11,7},{20,24},{24,20... | collective-permute-start | bytes 393224 | tf_op jit(solution)/shard_map/ppermute | solution.py:404
  6.5 4.5 %collective-permute-start = (f32[1,2,64,256]{3,2,1,0:T(8,128)}, f32[1,2,64,256]{3,2,1,0:T(8,128)S(1)}, u32[]{:S(2)}, u32[]{:S(2)}) collective-permute-start(f32[1,2,64,256]{3,2,1,0:T(8,128)} %refs_0_.1), channel_id=1, source_target_pairs={{0,4},{8,12},{4,0},{12,8},{1,5},{9,13},{5,1},{13,9},{2,6},{10,14},... | collective-permute-start | bytes 393224 | tf_op jit(solution)/shard_map/ppermute | solution.py:404
  11.7 0.9 %copy-done.1 = f32[2,128,128]{2,1,0:T(8,128)S(1)} copy-done((f32[2,128,128]{2,1,0:T(8,128)S(1)}, f32[2,128,128]{2,1,0:T(8,128)}, u32[]{:S(2)}) %copy-start.1) | copy-done | bytes 131096
  12.5 1.9 %shard_map.174 = (f32[4,2,128,128]{3,2,1,0:T(8,128)S(1)}, f32[1,192,256]{2,1,0:T(8,128)S(1)}, f32[1,2,64,256]{3,2,1,0:T(8,128)S(1)}, bf16[1,4,128,128]{3,2,1,0:T...) custom-call(s32[1,4]{1,0:T(1,128)S(1)} %copy-done.5, ...), custom_call_target="tpu_custom_call" | custom-call | flops 10000000 | bytes 1900544 | tf_op jit(solution)/shard_map/pallas_call | solution.py:372
  14.5 0.1 collective-permute-done.plane_a_ref
  14.6 0.0 collective-permute-done.3.yb_ref
  14.6 0.0 collective-permute-done.2.ya_ref
  14.6 0.0 copy-start.2
  14.6 2.4 %shard_map.175 = (f32[3,64,256]{2,1,0:T(8,128)S(1)}, f32[200,256]{1,0:T(8,128)S(1)}, f32[200,256]{1,0:T(8,128)S(1)}) custom-call(s32[1,4]{1,0:T(1,128)S(1)} %copy-done.5, s32[1,4]{1,0:T(1,128)S(1)} %copy-done.6, s32[1,1]{1,0:T(1,128)S(6)} %copy.19.count_ref, f32[4,2,128,128]{3,2,1,0:T(8,128)S(1)} %get-tuple-element.21.probes_ref, ...), custom_call_target="tpu_custom_call" | custom-call | flops 1000000000 | bytes 3162112 | tf_op jit(solution)/shard_map/pallas_call | solution.py:372
  17.1 1.8 %collective-permute-start.4 = (f32[200,256]{1,0:T(8,128)S(1)}, f32[200,256]{1,0:T(8,128)S(1)}, u32[]{:S(2)}, u32[]{:S(2)}) collective-permute-start(f32[200,256]{1,0:T(8,128)S(1)} %get-tuple-element.31), channel_id=1, source_target_pairs={{0,4},{8,12},{4,0},{12,8},{1,5},{9,13},{5,1},{13,9},{2,6},{10,14},... | collective-permute-start | bytes 614408 | tf_op jit(solution)/shard_map/ppermute | solution.py:404
  18.9 0.7 %collective-permute-start.5 = (f32[200,256]{1,0:T(8,128)S(1)}, f32[200,256]{1,0:T(8,128)S(1)}, u32[]{:S(2)}, u32[]{:S(2)}) collective-permute-start(f32[200,256]{1,0:T(8,128)S(1)} %get-tuple-element.32), channel_id=1, source_target_pairs={{4,8},{8,4},{5,9},{9,5},{6,10},{10,6},{7,11},{11,7},{20,24},{24,20... | collective-permute-start | bytes 614408 | tf_op jit(solution)/shard_map/ppermute | solution.py:404
  19.5 4.0 %collective-permute-done.4.rim_a_ref = f32[200,256]{1,0:T(8,128)S(1)} collective-permute-done((f32[200,256]{1,0:T(8,128)S(1)}, f32[200,256]{1,0:T(8,128)S(1)}, u32[]{:S(2)}, u32[]{:S(2)}) %collective-permute-start.4) | collective-permute-done | bytes 204832 | tf_op jit(solution)/shard_map/ppermute | solution.py:404
  23.5 0.7 %shard_map.176 = (f32[1,2,64,256]{3,2,1,0:T(8,128)}, f32[2,64,256]{2,1,0:T(8,128)S(1)}) custom-call(f32[3,64,256]{2,1,0:T(8,128)S(1)} %get-tuple-element.30.own_ref, f32[200,256]{1,0:T(8,128)S(1)} %collective-permute-done.4.rim_a_ref, f32[200,256]{1,0:T(8,128)S(1)} %collective-permute-done.5.rim_b_ref, f32[1,2,64,256]{3,2,1,0:T(8,128)S(1)} %copy-done.2, ...), custom_call_target="tpu_custom_call" | custom-call | flops 1000000 | bytes 1130496 | tf_op jit(solution)/shard_map/pallas_call | solution.py:372
  24.3 0.6 %collective-permute-start.6 = (f32[2,64,256]{2,1,0:T(8,128)S(1)}, f32[2,64,256]{2,1,0:T(8,128)S(1)}, u32[]{:S(2)}, u32[]{:S(2)}) collective-permute-start(f32[2,64,256]{2,1,0:T(8,128)S(1)} %get-tuple-element.34), channel_id=1, source_target_pairs={{0,2},{2,0},{1,3},{3,1},{4,6},{6,4},{5,7},{7,5},{8,10},{10,8},{9,1... | collective-permute-start | bytes 393224 | tf_op jit(solution)/shard_map/ppermute | solution.py:450
  24.8 4.4 %collective-permute-done.6 = f32[2,64,256]{2,1,0:T(8,128)S(1)} collective-permute-done((f32[2,64,256]{2,1,0:T(8,128)S(1)}, f32[2,64,256]{2,1,0:T(8,128)S(1)}, u32[]{:S(2)}, u32[]{:S(2)}) %collective-permute-start.6) | collective-permute-done | bytes 131104 | tf_op jit(solution)/shard_map/ppermute | solution.py:450
  29.2 0.7 %collective-permute-start.8 = (f32[2,2,64,256]{3,2,1,0:T(8,128)S(1)}, f32[2,2,64,256]{3,2,1,0:T(8,128)S(1)}, u32[]{:S(2)}, u32[]{:S(2)}) collective-permute-start(f32[2,2,64,256]{3,2,1,0:T(8,128)S(1)} %pad_maximum_fusion.here_ref), channel_id=1, source_target_pairs={{4,8},{8,4},{5,9},{9,5},{6,10},{10,6},{7,11},{11,7},{20,24},{24,20... | collective-permute-start | bytes 786440 | tf_op jit(solution)/shard_map/ppermute | solution.py:404
  29.9 5.4 %collective-permute-start.7 = (f32[2,2,64,256]{3,2,1,0:T(8,128)S(1)}, f32[2,2,64,256]{3,2,1,0:T(8,128)S(1)}, u32[]{:S(2)}, u32[]{:S(2)}) collective-permute-start(f32[2,2,64,256]{3,2,1,0:T(8,128)S(1)} %pad_maximum_fusion.here_ref), channel_id=1, source_target_pairs={{0,4},{8,12},{4,0},{12,8},{1,5},{9,13},{5,1},{13,9},{2,6},{10,14},... | collective-permute-start | bytes 786440 | tf_op jit(solution)/shard_map/ppermute | solution.py:404
  35.3 0.5 shard_map.177.base_ref
  35.8 1.9 %collective-permute-start.12 = (f32[2,2,64,256]{3,2,1,0:T(8,128)S(1)}, f32[2,2,64,256]{3,2,1,0:T(8,128)S(1)}, u32[]{:S(2)}, u32[]{:S(2)}) collective-permute-start(f32[2,2,64,256]{3,2,1,0:T(8,128)S(1)} %shard_map.177.base_ref), channel_id=1, source_target_pairs={{0,4},{4,8},{6,2},{8,12},{10,6},{14,10},{1,5},{5,9},{7,3},{9,13},{... | collective-permute-start | bytes 786440 | tf_op jit(solution)/shard_map/ppermute | solution.py:465
  37.8 0.1 collective-permute-start.9
  37.9 0.5 collective-permute-start.11
  38.3 2.4 %collective-permute-done.7.side_a_ref = f32[2,2,64,256]{3,2,1,0:T(8,128)S(1)} collective-permute-done((f32[2,2,64,256]{3,2,1,0:T(8,128)S(1)}, f32[2,2,64,256]{3,2,1,0:T(8,128)S(1)}, u32[]{:S(2)}, u32[]{:S(2)}) %collective-permute-start.7) | collective-permute-done | bytes 262176 | tf_op jit(solution)/shard_map/ppermute | solution.py:404
  40.7 2.8 %collective-permute-done.12.beside_ref = f32[2,2,64,256]{3,2,1,0:T(8,128)S(1)} collective-permute-done((f32[2,2,64,256]{3,2,1,0:T(8,128)S(1)}, f32[2,2,64,256]{3,2,1,0:T(8,128)S(1)}, u32[]{:S(2)}, u32[]{:S(2)}) %collective-permute-start.12) | collective-permute-done | bytes 262176 | tf_op jit(solution)/shard_map/ppermute | solution.py:465
  43.5 0.0 copy-start.3
  43.5 0.7 %copy-done.3 = s32[4,2]{0,1:T(2,128)S(1)} copy-done((s32[4,2]{0,1:T(2,128)S(1)}, s32[4,2]{0,1:T(2,128)}, u32[]{:S(2)}) %copy-start.3) | copy-done | bytes 56
  44.2 1.9 %shard_map.178 = (f32[2,2,64,256]{3,2,1,0:T(8,128)}, f32[2,2,64,256]{3,2,1,0:T(8,128)S(1)}, f32[2,2,64,256]{3,2,1,0:T(8,128)S(1)}) custom-call(s32[2,4]{1,0:T(2,128)S(1)} %bitcast.17, f32[2,4]{1,0:T(2,128)S(1)} %bitcast.18, f32[2,2,64,256]{3,2,1,0:T(8,128)S(1)} %pad_maximum_fusion.here_ref, f32[2,2,64,256]{3,2,1,0:T(8,128)S(1)} %collective-permute-done.7.side_a_ref, ...), custom_call_target="tpu_custom_call" | custom-call | flops 100000000 | bytes 2883584 | tf_op jit(solution)/shard_map/pallas_call | solution.py:372
  46.1 1.5 %collective-permute-done.13 = f32[2,2,64,256]{3,2,1,0:T(8,128)S(1)} collective-permute-done((f32[2,2,64,256]{3,2,1,0:T(8,128)S(1)}, f32[2,2,64,256]{3,2,1,0:T(8,128)S(1)}, u32[]{:S(2)}, u32[]{:S(2)}) %collective-permute-start.13) | collective-permute-done | bytes 262176 | tf_op jit(solution)/shard_map/ppermute | solution.py:407
  47.6 2.4 %collective-permute-start.14 = (f32[2,64,256]{2,1,0:T(8,128)S(1)}, f32[2,64,256]{2,1,0:T(8,128)S(1)}, u32[]{:S(2)}, u32[]{:S(2)}) collective-permute-start(f32[2,64,256]{2,1,0:T(8,128)S(1)} %fusion), channel_id=1, source_target_pairs={{0,2},{2,0},{1,3},{3,1},{4,6},{6,4},{5,7},{7,5},{8,10},{10,8},{9,1... | collective-permute-start | bytes 393224 | tf_op jit(solution)/shard_map/ppermute | solution.py:485
  50.0 3.8 %collective-permute-done.14 = f32[2,64,256]{2,1,0:T(8,128)S(1)} collective-permute-done((f32[2,64,256]{2,1,0:T(8,128)S(1)}, f32[2,64,256]{2,1,0:T(8,128)S(1)}, u32[]{:S(2)}, u32[]{:S(2)}) %collective-permute-start.14) | collective-permute-done | bytes 131104 | tf_op jit(solution)/shard_map/ppermute | solution.py:485
  53.8 0.7 %add_subtract_fusion = (f32[1,2,64,256]{3,2,1,0:T(8,128)}, f32[1,2,64,256]{3,2,1,0:T(8,128)}) fusion(f32[1,2,64,256]{3,2,1,0:T(8,128)S(1)} %copy-done, f32[1,2,64,256]{3,2,1,0:T(8,128)S(1)} %copy-done.7, f32[2,64,256]{2,1,0:T(8,128)S(1)} %collective-permute-done.14, f32[2,2,64,256]{3,2,1,0:T(8,128)S(1)} %collective-permute-done.13, ...), kind=kLoop, calls=%fused_computation.7 | loop fusion | flops 131072 | bytes 917504 | tf_op jit(solution)/shard_map/sub | solution.py:488
  (22 shorter events, 0.1 us)
Async XLA Ops:
  0.6 11.0 %copy-start.6 = (s32[1,4]{1,0:T(1,128)S(1)}, s32[1,4]{1,0:T(1,128)}, u32[]{:S(2)}) copy-start(s32[1,4]{1,0:T(1,128)} %columns_ref.3) | copy-start | bytes 52
  0.6 11.0 %copy-start.5 = (s32[1,4]{1,0:T(1,128)S(1)}, s32[1,4]{1,0:T(1,128)}, u32[]{:S(2)}) copy-start(s32[1,4]{1,0:T(1,128)} %rows_ref.3) | copy-start | bytes 52
  0.7 13.9 %collective-permute-start.3 = (f32[2,2,64,256]{3,2,1,0:T(8,128)}, f32[2,2,64,256]{3,2,1,0:T(8,128)S(1)}, u32[]{:S(2)}, u32[]{:S(2)}) collective-permute-start(f32[2,2,64,256]{3,2,1,0:T(8,128)} %refs_2_.1), channel_id=1, source_target_pairs={{1,2},{2,1},{5,6},{6,5},{9,10},{10,9},{13,14},{14,13},{17,18},{18,... | collective-permute-start | bytes 786440 | tf_op jit(solution)/shard_map/ppermute | solution.py:413
  1.5 13.1 %collective-permute-start.2 = (f32[2,2,64,256]{3,2,1,0:T(8,128)}, f32[2,2,64,256]{3,2,1,0:T(8,128)S(1)}, u32[]{:S(2)}, u32[]{:S(2)}) collective-permute-start(f32[2,2,64,256]{3,2,1,0:T(8,128)} %refs_2_.1), channel_id=1, source_target_pairs={{0,1},{1,0},{2,3},{3,2},{4,5},{5,4},{6,7},{7,6},{8,9},{9,8},{10,11... | collective-permute-start | bytes 786440 | tf_op jit(solution)/shard_map/ppermute | solution.py:407
  5.8 8.7 %collective-permute-start.1 = (f32[1,2,64,256]{3,2,1,0:T(8,128)}, f32[1,2,64,256]{3,2,1,0:T(8,128)S(1)}, u32[]{:S(2)}, u32[]{:S(2)}) collective-permute-start(f32[1,2,64,256]{3,2,1,0:T(8,128)} %refs_0_.1), channel_id=1, source_target_pairs={{4,8},{8,4},{5,9},{9,5},{6,10},{10,6},{7,11},{11,7},{20,24},{24,20... | collective-permute-start | bytes 393224 | tf_op jit(solution)/shard_map/ppermute | solution.py:404
  6.5 8.1 %collective-permute-start = (f32[1,2,64,256]{3,2,1,0:T(8,128)}, f32[1,2,64,256]{3,2,1,0:T(8,128)S(1)}, u32[]{:S(2)}, u32[]{:S(2)}) collective-permute-start(f32[1,2,64,256]{3,2,1,0:T(8,128)} %refs_0_.1), channel_id=1, source_target_pairs={{0,4},{8,12},{4,0},{12,8},{1,5},{9,13},{5,1},{13,9},{2,6},{10,14},... | collective-permute-start | bytes 393224 | tf_op jit(solution)/shard_map/ppermute | solution.py:404
  11.6 0.9 %copy-start.1 = (f32[2,128,128]{2,1,0:T(8,128)S(1)}, f32[2,128,128]{2,1,0:T(8,128)}, u32[]{:S(2)}) copy-start(f32[2,128,128]{2,1,0:T(8,128)} %probe_ref.1) | copy-start | bytes 393220
  14.6 8.9 %copy-start = (f32[1,2,64,256]{3,2,1,0:T(8,128)S(1)}, f32[1,2,64,256]{3,2,1,0:T(8,128)}, u32[]{:S(2)}) copy-start(f32[1,2,64,256]{3,2,1,0:T(8,128)} %dual_ref.1) | copy-start | bytes 393220
  14.6 8.9 %copy-start.2 = (f32[1,2,64,256]{3,2,1,0:T(8,128)S(1)}, f32[1,2,64,256]{3,2,1,0:T(8,128)}, u32[]{:S(2)}) copy-start(f32[1,2,64,256]{3,2,1,0:T(8,128)} %projected_ref.1) | copy-start | bytes 393220
  17.1 6.5 %collective-permute-start.4 = (f32[200,256]{1,0:T(8,128)S(1)}, f32[200,256]{1,0:T(8,128)S(1)}, u32[]{:S(2)}, u32[]{:S(2)}) collective-permute-start(f32[200,256]{1,0:T(8,128)S(1)} %get-tuple-element.31), channel_id=1, source_target_pairs={{0,4},{8,12},{4,0},{12,8},{1,5},{9,13},{5,1},{13,9},{2,6},{10,14},... | collective-permute-start | bytes 614408 | tf_op jit(solution)/shard_map/ppermute | solution.py:404
  18.9 4.7 %collective-permute-start.5 = (f32[200,256]{1,0:T(8,128)S(1)}, f32[200,256]{1,0:T(8,128)S(1)}, u32[]{:S(2)}, u32[]{:S(2)}) collective-permute-start(f32[200,256]{1,0:T(8,128)S(1)} %get-tuple-element.32), channel_id=1, source_target_pairs={{4,8},{8,4},{5,9},{9,5},{6,10},{10,6},{7,11},{11,7},{20,24},{24,20... | collective-permute-start | bytes 614408 | tf_op jit(solution)/shard_map/ppermute | solution.py:404
  24.3 5.0 %collective-permute-start.6 = (f32[2,64,256]{2,1,0:T(8,128)S(1)}, f32[2,64,256]{2,1,0:T(8,128)S(1)}, u32[]{:S(2)}, u32[]{:S(2)}) collective-permute-start(f32[2,64,256]{2,1,0:T(8,128)S(1)} %get-tuple-element.34), channel_id=1, source_target_pairs={{0,2},{2,0},{1,3},{3,1},{4,6},{6,4},{5,7},{7,5},{8,10},{10,8},{9,1... | collective-permute-start | bytes 393224 | tf_op jit(solution)/shard_map/ppermute | solution.py:450
  29.2 8.6 %collective-permute-start.8 = (f32[2,2,64,256]{3,2,1,0:T(8,128)S(1)}, f32[2,2,64,256]{3,2,1,0:T(8,128)S(1)}, u32[]{:S(2)}, u32[]{:S(2)}) collective-permute-start(f32[2,2,64,256]{3,2,1,0:T(8,128)S(1)} %pad_maximum_fusion.here_ref), channel_id=1, source_target_pairs={{4,8},{8,4},{5,9},{9,5},{6,10},{10,6},{7,11},{11,7},{20,24},{24,20... | collective-permute-start | bytes 786440 | tf_op jit(solution)/shard_map/ppermute | solution.py:404
  29.9 10.8 %collective-permute-start.7 = (f32[2,2,64,256]{3,2,1,0:T(8,128)S(1)}, f32[2,2,64,256]{3,2,1,0:T(8,128)S(1)}, u32[]{:S(2)}, u32[]{:S(2)}) collective-permute-start(f32[2,2,64,256]{3,2,1,0:T(8,128)S(1)} %pad_maximum_fusion.here_ref), channel_id=1, source_target_pairs={{0,4},{8,12},{4,0},{12,8},{1,5},{9,13},{5,1},{13,9},{2,6},{10,14},... | collective-permute-start | bytes 786440 | tf_op jit(solution)/shard_map/ppermute | solution.py:404
  35.3 8.2 %copy-start.4 = (f32[4,2]{0,1:T(2,128)S(1)}, f32[4,2]{0,1:T(2,128)}, u32[]{:S(2)}) copy-start(f32[4,2]{0,1:T(2,128)} %param.25) | copy-start | bytes 100
  35.8 7.7 %collective-permute-start.12 = (f32[2,2,64,256]{3,2,1,0:T(8,128)S(1)}, f32[2,2,64,256]{3,2,1,0:T(8,128)S(1)}, u32[]{:S(2)}, u32[]{:S(2)}) collective-permute-start(f32[2,2,64,256]{3,2,1,0:T(8,128)S(1)} %shard_map.177.base_ref), channel_id=1, source_target_pairs={{0,4},{4,8},{6,2},{8,12},{10,6},{14,10},{1,5},{5,9},{7,3},{9,13},{... | collective-permute-start | bytes 786440 | tf_op jit(solution)/shard_map/ppermute | solution.py:465
  37.8 5.7 %collective-permute-start.9 = (f32[2,2,64,256]{3,2,1,0:T(8,128)S(1)}, f32[2,2,64,256]{3,2,1,0:T(8,128)S(1)}, u32[]{:S(2)}, u32[]{:S(2)}) collective-permute-start(f32[2,2,64,256]{3,2,1,0:T(8,128)S(1)} %pad_maximum_fusion.here_ref), channel_id=1, source_target_pairs={{0,1},{1,0},{2,3},{3,2},{4,5},{5,4},{6,7},{7,6},{8,9},{9,8},{10,11... | collective-permute-start | bytes 786440 | tf_op jit(solution)/shard_map/ppermute | solution.py:407
  37.9 5.7 %collective-permute-start.11 = (f32[2,2,64,256]{3,2,1,0:T(8,128)S(1)}, f32[2,2,64,256]{3,2,1,0:T(8,128)S(1)}, u32[]{:S(2)}, u32[]{:S(2)}) collective-permute-start(f32[2,2,64,256]{3,2,1,0:T(8,128)S(1)} %collective-permute-done.8.side_b_ref), channel_id=1, source_target_pairs={{0,1},{1,0},{2,3},{3,2},{4,5},{5,4},{6,7},{7,6},{8,9},{9,8},{10,11... | collective-permute-start | bytes 786440 | tf_op jit(solution)/shard_map/ppermute | solution.py:407
  40.7 2.8 %collective-permute-start.10 = (f32[2,2,64,256]{3,2,1,0:T(8,128)S(1)}, f32[2,2,64,256]{3,2,1,0:T(8,128)S(1)}, u32[]{:S(2)}, u32[]{:S(2)}) collective-permute-start(f32[2,2,64,256]{3,2,1,0:T(8,128)S(1)} %collective-permute-done.7.side_a_ref), channel_id=1, source_target_pairs={{0,1},{1,0},{2,3},{3,2},{4,5},{5,4},{6,7},{7,6},{8,9},{9,8},{10,11... | collective-permute-start | bytes 786440 | tf_op jit(solution)/shard_map/ppermute | solution.py:407
  43.5 0.7 %copy-start.3 = (s32[4,2]{0,1:T(2,128)S(1)}, s32[4,2]{0,1:T(2,128)}, u32[]{:S(2)}) copy-start(s32[4,2]{0,1:T(2,128)} %param.24) | copy-start | bytes 100
  46.1 1.5 %collective-permute-start.13 = (f32[2,2,64,256]{3,2,1,0:T(8,128)S(1)}, f32[2,2,64,256]{3,2,1,0:T(8,128)S(1)}, u32[]{:S(2)}, u32[]{:S(2)}) collective-permute-start(f32[2,2,64,256]{3,2,1,0:T(8,128)S(1)} %get-tuple-element.36), channel_id=1, source_target_pairs={{0,1},{1,0},{2,3},{3,2},{4,5},{5,4},{6,7},{7,6},{8,9},{9,8},{10,11... | collective-permute-start | bytes 786440 | tf_op jit(solution)/shard_map/ppermute | solution.py:407
  47.6 6.2 %copy-start.7 = (f32[1,2,64,256]{3,2,1,0:T(8,128)S(1)}, f32[1,2,64,256]{3,2,1,0:T(8,128)}, u32[]{:S(2)}) copy-start(f32[1,2,64,256]{3,2,1,0:T(8,128)} %get-tuple-element.17) | copy-start | bytes 393220
  47.6 6.2 %collective-permute-start.14 = (f32[2,64,256]{2,1,0:T(8,128)S(1)}, f32[2,64,256]{2,1,0:T(8,128)S(1)}, u32[]{:S(2)}, u32[]{:S(2)}) collective-permute-start(f32[2,64,256]{2,1,0:T(8,128)S(1)} %fusion), channel_id=1, source_target_pairs={{0,2},{2,0},{1,3},{3,1},{4,6},{6,4},{5,7},{7,5},{8,10},{10,8},{9,1... | collective-permute-start | bytes 393224 | tf_op jit(solution)/shard_map/ppermute | solution.py:485

commit v3 on v2

--- a/solution.py
+++ b/solution.py
@@ -19,6 +19,7 @@
 SMEM = pl.BlockSpec(memory_space=pltpu.SMEM)
 HBM = pl.BlockSpec(memory_space=pltpu.MemorySpace.HBM)
 LANES = 128
+SUBLANES = 8
 SPARE_BYTES = 8 << 20
 
 
@@ -81,9 +82,12 @@
         totals[part, side:, at] += jnp.where(outer & lane_mask[:width], term[:width], 0.0)
 
 
-def prepare_kernel(rows_ref, columns_ref, count_ref, probe_ref, *refs):
-    half = (len(refs) - 3) // 2
-    sources, (probes_ref, density_ref), targets, done = refs[:half], refs[half : half + 2], refs[half + 2 : -1], refs[-1]
+def prepare_kernel(
+    rows_ref, columns_ref, count_ref, shift_ref, weight_ref, probe_ref, *refs
+):
+    half = (len(refs) - 4) // 2
+    sources, targets, done = refs[:half], refs[half + 3 : -1], refs[-1]
+    probes_ref, density_ref, tables_ref = refs[half : half + 3]
     copies = [
         pltpu.make_async_copy(source, target, done.at[number])
         for number, (source, target) in enumerate(zip(sources, targets))
@@ -104,6 +108,13 @@
             probes_ref[slot, part] = probe[part]
         masks = slot_masks(rows_ref, columns_ref, count_ref, slot, side)
         place(density_ref, 0, probe[0] * probe[0] + probe[1] * probe[1], masks, width)
+    places = lax.broadcasted_iota(jnp.int32, tables_ref.shape[1:], 0)
+    for angle in range(tables_ref.shape[0]):
+        table = jnp.zeros(tables_ref.shape[1:], jnp.float32)
+        for row in range(shift_ref.shape[0]):
+            table = jnp.where(places == 2 * row, shift_ref[row, angle].astype(jnp.float32), table)
+            table = jnp.where(places == 2 * row + 1, weight_ref[row, angle], table)
+        tables_ref[angle] = table
     for copy in copies:
         copy.wait()
 
@@ -227,7 +238,7 @@
         dual = dual_ref[0, part]
         updated = (sums[part] + penalty * (target - dual)) / (sums[2] + penalty)
         object_ref[0, part] = updated
-        residual_ref[part] = target - updated - dual
+        residual_ref[part * width : (part + 1) * width] = target - updated - dual
 
 
 def variation_kernel(volume_ref, ya_ref, yb_ref, rim_a_ref, rim_b_ref, base_ref, padded, norms):
@@ -287,83 +298,138 @@
             previous_y = norm_y
 
 
-def project_kernel(
-    shift_ref,
-    weight_ref,
-    here_ref,
-    side_a_ref,
-    side_b_ref,
-    here_too_ref,
-    side_a_too_ref,
-    side_b_too_ref,
-    base_ref,
-    beside_ref,
-    volume_ref,
-    keep_ref,
-    send_ref,
-    wide,
-    updated,
-):
+def spread_kernel(shift_ref, weight_ref, base_ref, beside_ref, keep_ref, send_ref, padded):
     width = base_ref.shape[2]
     count = base_ref.shape[1]
-    columns = here_ref.shape[0]
-    tiles = lax.axis_size("tile")
-    angles = columns * tiles
+    columns, tiles = keep_ref.shape[0], lax.axis_size("tile")
     me, tile, scan = lax.axis_index("angle"), lax.axis_index("tile"), lax.axis_index("scan")
     upper = me >= columns // 2
-    even = scan_is_even()
-    at_a = pl.multiple_of(jnp.where(even, 2 * width, 0), width)
-    at_b = pl.multiple_of(jnp.where(even, 0, 2 * width), width)
-
-    def angle_of(turn, flip):
-        return lax.rem(me + turn, columns) * tiles + (tile if flip == 0 else 1 - tile)
-
     chunks = [slice(at, at + LANES) for at in range(0, base_ref.shape[3], LANES)]
-    blocks = ((here_ref, side_a_ref, side_b_ref), (here_too_ref, side_a_too_ref, side_b_too_ref))
-    for turn in range(columns):
-        for flip in range(tiles):
-            angle = angle_of(turn, flip)
-            for chunk, at in enumerate(chunks):
-                for ref, start in zip(blocks[flip], (width, at_a, at_b)):
-                    wide[angle, :, chunk, pl.ds(start, width)] = ref[turn, :, :, at]
     exists = jnp.where(upper, scan < lax.axis_size("scan") - 1, scan > 0).astype(jnp.float32)
     own_at = pl.multiple_of(jnp.where(upper, 0, width), width)
     beside_at = pl.multiple_of(jnp.where(upper, width, 0), width)
     for row in range(count):
         for channel in range(2):
             for chunk, at in enumerate(chunks):
-                total = jnp.zeros((2 * width, LANES), jnp.float32)
-                for angle in range(angles):
-                    start = jnp.where(upper, width, 0) - shift_ref[row, angle]
-                    fraction = weight_ref[row, angle]
-                    total += (1.0 - fraction) * wide[angle, channel, chunk, pl.ds(start, 2 * width)]
-                    total += fraction * wide[angle, channel, chunk, pl.ds(start - 1, 2 * width)]
-                updated[row, channel, chunk] = total
-                part = updated.at[row, channel, chunk]
-                own = base_ref[channel, row, :, at] - step_size * part[pl.ds(own_at, width)]
-                beside = beside_ref[channel, row, :, at] - step_size * part[pl.ds(beside_at, width)]
-                volume_ref[channel, row, :, at] = own
-                part[pl.ds(own_at, width)] = own
-                part[pl.ds(beside_at, width)] = beside * exists
+                padded[row, channel, chunk, pl.ds(own_at, width)] = base_ref[channel, row, :, at]
+                padded[row, channel, chunk, pl.ds(beside_at, width)] = (
+                    beside_ref[channel, row, :, at] * exists
+                )
     for turn in range(columns):
         for flip, out_ref in ((0, keep_ref), (1, send_ref)):
-            angle = angle_of(turn, flip)
+            angle = lax.rem(me + turn, columns) * tiles + (tile if flip == 0 else 1 - tile)
             for channel in range(2):
                 for chunk, at in enumerate(chunks):
                     total = jnp.zeros((width, LANES), jnp.float32)
                     for row in range(count):
                         start = jnp.where(upper, 0, width) + shift_ref[row, angle]
                         fraction = weight_ref[row, angle]
-                        total += (1.0 - fraction) * updated[row, channel, chunk, pl.ds(start, width)]
-                        total += fraction * updated[row, channel, chunk, pl.ds(start + 1, width)]
+                        total += (1.0 - fraction) * padded[row, channel, chunk, pl.ds(start, width)]
+                        total += fraction * padded[row, channel, chunk, pl.ds(start + 1, width)]
                     out_ref[turn, channel, :, at] = total
 
 
-def call(kernel, shapes, operands, scratch, flops, scalars=0, staged=()):
+def operator_kernel(*refs):
+    rays, (high_ref, low_ref) = refs[:-2], refs[-2:]
+    tiles = lax.axis_size("tile")
+    columns = len(rays) // tiles
+    rows_out, reach = high_ref.shape[1:]
+    width = reach // 3
+    count = rows_out // (2 * width) - 1
+    me, tile, scan = lax.axis_index("angle"), lax.axis_index("tile"), lax.axis_index("scan")
+
+    def taps(shape, first, table, row, step):
+        lanes = lax.broadcasted_iota(jnp.int32, shape, 1)
+        sublanes = lax.broadcasted_iota(jnp.int32, shape, 0)
+        offset = (lanes - sublanes).astype(jnp.float32) - first
+        shift = step * table[2 * row : 2 * row + 1, : shape[1]]
+        fraction = table[2 * row + 1 : 2 * row + 2, : shape[1]]
+        return jnp.where(offset == shift, 1.0 - fraction, 0.0) + jnp.where(
+            offset == shift + step, fraction, 0.0
+        )
+
+    def angle_of(turn, flip):
+        return lax.rem(me + turn, columns) * tiles + (tile if flip == 0 else 1 - tile)
+
+    cells = lax.broadcasted_iota(jnp.int32, (width, 2 * width), 1)
+    forward = []
+    backward = [[] for _ in range(columns)]
+    for turn in range(columns):
+        upper = lax.rem(me + turn, columns) >= columns // 2
+        base_at = jnp.where(upper, 0, width)
+        first_cell = jnp.where(upper, 0, jnp.where(scan > 0, 0, width))
+        end_cell = jnp.where(upper & (scan == lax.axis_size("scan") - 1), width, 2 * width)
+        inside = (cells >= first_cell) & (cells < end_cell)
+        for flip in range(tiles):
+            for row in range(count):
+                parts = []
+                for own in range(tiles):
+                    table = rays[turn * tiles + flip][angle_of(0, own)]
+                    part = taps((width, 2 * width), base_at.astype(jnp.float32), table, row, 1.0)
+                    parts.append(jnp.where(inside, part, 0.0))
+                forward.append(jnp.concatenate(parts, axis=0))
+                for source in range(columns):
+                    table = rays[turn * tiles + flip][angle_of(source, 0)]
+                    first = (width - base_at).astype(jnp.float32)
+                    backward[source].append(taps((2 * width, reach), first, table, row, -1.0))
+    left = split(jnp.concatenate(forward, axis=1))
+    for source in range(columns):
+        both = product(left, split(jnp.concatenate(backward[source], axis=0)))
+        blocks = [both]
+        for flip in range(tiles):
+            for row in range(count):
+                table = rays[flip][angle_of(source, 0)]
+                blocks.append(taps((width, reach), float(width), table, row, -1.0))
+        high_ref[source], low_ref[source] = split(jnp.concatenate(blocks, axis=0))
+
+
+def apply_kernel(here_ref, side_a_ref, side_b_ref, high_ref, low_ref, keep_ref, own_ref, send_ref, wide):
+    width = keep_ref.shape[1]
+    columns = here_ref.shape[0]
+    count = own_ref.shape[1]
+    even = scan_is_even()
+    at_a = pl.multiple_of(jnp.where(even, 2 * width, 0), width)
+    at_b = pl.multiple_of(jnp.where(even, 0, 2 * width), width)
+    for source in range(columns):
+        for channel in range(2):
+            at = slice(channel * width, (channel + 1) * width)
+            wide[source, channel, width : 2 * width] = here_ref[source, at]
+            wide[source, channel, pl.ds(at_a, width)] = side_a_ref[source, at]
+            wide[source, channel, pl.ds(at_b, width)] = side_b_ref[source, at]
+    for channel in range(2):
+        total = 0.0
+        for source in range(columns):
+            total += product((high_ref[source], low_ref[source]), split(wide[source, channel]))
+        keep_ref[channel] = total[:width]
+        send_ref[channel * width : (channel + 1) * width] = total[width : 2 * width]
+        for row in range(count):
+            at = (2 + row) * width
+            own_ref[channel, row] = total[at : at + width]
+            target = (2 + channel * count + row) * width
+            send_ref[target : target + width] = total[at + count * width : at + (count + 1) * width]
+
+
+def finish_kernel(
+    keep_ref, own_ref, received_ref, base_ref, spread_ref, object_ref, dual_ref, dual_out_ref, volume_ref, projected_ref
+):
+    width = keep_ref.shape[1]
+    count = own_ref.shape[1]
+    for channel in range(2):
+        received = received_ref[channel * width : (channel + 1) * width]
+        projection = spread_ref[channel] - step_size * (keep_ref[channel] + received)
+        projected_ref[0, channel] = projection
+        dual_out_ref[0, channel] = dual_ref[0, channel] + object_ref[0, channel] - projection
+        for row in range(count):
+            at = (2 + channel * count + row) * width
+            descent = own_ref[channel, row] + received_ref[at : at + width]
+            volume_ref[channel, row] = base_ref[channel, row] - step_size * descent
+
+
+def call(kernel, shapes, operands, scratch, flops, scalars=0, staged=(), kind=jnp.float32):
     held = sum(operand.nbytes for operand in operands[scalars:] + staged)
     held += 4 * sum(math.prod(shape) for shape in shapes)
     own = 4 * sum(math.prod(shape) for shape in scratch)
-    outputs = [jax.ShapeDtypeStruct(shape, jnp.float32) for shape in shapes]
+    outputs = [jax.ShapeDtypeStruct(shape, kind) for shape in shapes]
     outputs += [jax.ShapeDtypeStruct(array.shape, array.dtype) for array in staged]
     scratch_shapes = [pltpu.VMEM(shape, jnp.float32) for shape in scratch]
     if staged:
@@ -417,37 +483,49 @@
     scalars = (slot_first_rows, slot_first_columns, patch_counts)
     slots = slot_first_rows.shape[1]
     side = probe_wave.shape[1]
-    prepared = call(
+    probes, density, rays, *held = call(
         prepare_kernel,
-        [(slots, 2, side, side), (1, 3 * width, length)],
-        (*scalars, probe_wave),
+        [(slots, 2, side, side), (1, 3 * width, length), (columns * tiles, SUBLANES, length)],
+        (*scalars, shift_table.T, tap_weight.T, probe_wave),
         [],
         10**7,
-        3,
+        5,
         (transmission, intensities, volume, *tables),
     )
-    volume_here = prepared[4]
+    volume_here = held[2]
+    turns = [[(i, (i - turn) % columns) for i in range(columns)] for turn in range(columns)]
+    by_row = [rays]
+    for turn in range(1, columns):
+        by_row.append(lax.ppermute(rays, "angle", turns[turn]))
+    by_row = [block for table in by_row for block in (table, across(table))]
     own, rim_a, rim_b = call(
         patch_kernel,
         [(3, width, length), (rim_rows, length), (rim_rows, length)],
-        (*scalars, *prepared, plane_a, plane_b, rows_a, rows_b),
+        (*scalars, probes, density, *held, plane_a, plane_b, rows_a, rows_b),
         [(2, 3 * width, length), (3, 3 * width, length)],
         10**9,
         3,
     )
     rim_a = exchange(rim_a, 0)
     rim_b = exchange(rim_b, 1)
+    high, low = call(
+        operator_kernel,
+        [(columns, (2 + 2 * count) * width, 3 * width)] * 2,
+        tuple(by_row),
+        [],
+        10**8,
+        kind=jnp.bfloat16,
+    )
     new_transmission, residual = call(
         fold_kernel,
-        [transmission.shape, transmission.shape[1:]],
+        [transmission.shape, (2 * width, length)],
         (own, rim_a, rim_b, projected, scaled_dual),
         [],
         10**6,
     )
     by_column = [residual]
     for turn in range(1, columns):
-        route = [(i, (i - turn) % columns) for i in range(columns)]
-        by_column.append(lax.ppermute(residual, "angle", route))
+        by_column.append(lax.ppermute(residual, "angle", turns[turn]))
     (base,) = call(
         variation_kernel,
         [volume.shape],
@@ -466,26 +544,35 @@
     here = jnp.stack(by_column)
     side_a = exchange(here, 0)
     side_b = exchange(here, 1)
-    shared = [across(block) for block in (here, side_a, side_b)]
-    new_volume, keep, send = call(
-        project_kernel,
-        [volume.shape, (columns, 2, width, length), (columns, 2, width, length)],
-        (shift_table.T, tap_weight.T, here, side_a, side_b, *shared, base, beside),
-        [
-            (columns * tiles, 2, length // LANES, 3 * width, LANES),
-            (count, 2, length // LANES, 2 * width, LANES),
-        ],
-        10**8,
+    block = (columns, 2, width, length)
+    keep, send = call(
+        spread_kernel,
+        [block, block],
+        (shift_table.T, tap_weight.T, base, beside),
+        [(count, 2, length // LANES, 2 * width, LANES)],
+        10**7,
         2,
     )
     received = across(send)
-    new_projected = keep[0] + received[0]
+    spread = keep[0] + received[0]
     for turn in range(1, columns):
         route = [(i, (i + turn) % columns) for i in range(columns)]
-        part = lax.ppermute(keep[turn] + received[turn], "angle", route)
-        new_projected = new_projected + part
-    new_projected = new_projected[None]
-    new_dual = scaled_dual + new_transmission - new_projected
+        spread = spread + lax.ppermute(keep[turn] + received[turn], "angle", route)
+    keep, own, send = call(
+        apply_kernel,
+        [(2, width, length), volume.shape, ((2 + 2 * count) * width, length)],
+        (here, side_a, side_b, high, low),
+        [(columns, 2, 3 * width, length)],
+        10**9,
+    )
+    received = across(send)
+    new_dual, new_volume, new_projected = call(
+        finish_kernel,
+        [transmission.shape, volume.shape, transmission.shape],
+        (keep, own, received, base, spread, new_transmission, scaled_dual),
+        [],
+        10**6,
+    )
     return (new_transmission, new_dual, new_volume, new_projected)
 
 

time: 54.8 us -> 53.4 us (0.974)
  waiting for transfers between devices: 19 us -> 14.4 us
  Pallas kernels: 7.47 us -> 9.42 us
  starting transfers between devices: 24.3 us -> 26.1 us
  other arithmetic: 0.78 us -> 0.07 us
    ppermute x1, starting transfers between devices: 1.95 us -> 5.54 us  [body(): beside = lax.ppermute(base, ('scan', 'angle'), route)]
    ppermute x6, starting transfers between devices: 13.6 us -> 11.4 us  [exchange(): return lax.ppermute(block, 'scan', both[number])]
    pallas_call x5 -> x8, Pallas kernels: 7.47 us -> 9.42 us  [call(): pl.pallas_call(kernel, out_shape=outputs, in_specs=in_specs, out_specs=[V...]
    ppermute x2 -> x3, waiting for transfers between devices: 8.18 us -> 6.35 us  [the longest x1 4.17 us: body(): spread = spread + lax.ppermute(keep[turn] + received[turn], 'angle', route)]
    ppermute x6, waiting for transfers between devices: 6.43 us -> 4.79 us  [exchange(): return lax.ppermute(block, 'scan', both[number])]
    ppermute x1, waiting for transfers between devices: 2.81 us -> 2.06 us  [body(): beside = lax.ppermute(base, ('scan', 'angle'), route)]
    sub x1 -> x0, other arithmetic: 0.74 us -> none  [body(): new_dual = scaled_dual + new_transmission - new_projected]
    ppermute x2 -> x3, starting transfers between devices: 2.99 us -> 3.68 us  [the longest x1 1.65 us: body(): by_row.append(lax.ppermute(rays, 'angle', turns[turn]))]
  transfers between devices with their start and end apart: 15 -> 16, of which waited for: 7 -> 5; matrix products, arithmetic and copies ran while one was open for 0% -> 0% of each run, Pallas kernels for 4% -> 10%
where the time goes in v3:
time: 53.4 us; the launch traced here: 53.2 us
  starting transfers between devices  26.1 us (49%)
  waiting for transfers between devices  14.4 us (27%)
  Pallas kernels  9.42 us (18%)
  local copies, waits for them, and re-layouts  1.6 us (3%)
  between operations  1.52 us (3%)
    ppermute x6, starting transfers between devices, exchange(): return lax.ppermute(block, 'scan', both[number])  11.4 us
    pallas_call x8, Pallas kernels, call(): pl.pallas_call(kernel, out_shape=outputs, in_specs=in_specs, out_specs=[V...  9.42 us
    ppermute x1, starting transfers between devices, body(): beside = lax.ppermute(base, ('scan', 'angle'), route)  5.54 us
    ppermute x5, starting transfers between devices, across(): return lax.ppermute(block, 'tile', swap)  4.83 us
    ppermute x6, waiting for transfers between devices, exchange(): return lax.ppermute(block, 'scan', both[number])  4.79 us
    ppermute x1, waiting for transfers between devices, body(): spread = spread + lax.ppermute(keep[turn] + received[turn], 'angle', route)  4.17 us
    ppermute x1, waiting for transfers between devices, body(): by_row.append(lax.ppermute(rays, 'angle', turns[turn]))  2.18 us
    ppermute x1, waiting for transfers between devices, body(): beside = lax.ppermute(base, ('scan', 'angle'), route)  2.06 us
  transfers between devices with their start and end apart: 16, of which 5 were waited for; matrix products, arithmetic and copies ran while one was open for 0% of the time, Pallas kernels for 10%

profile of v3, /device:TPU:0, one launch (start us, length us, event | category | flops | bytes accessed | tf_op | source)
XLA Modules:
  0.0 53.2 jit_solution(11125666469059208085)
XLA Ops:
  0.6 0.7 %collective-permute-start.3 = (f32[2,2,64,256]{3,2,1,0:T(8,128)}, f32[2,2,64,256]{3,2,1,0:T(8,128)S(1)}, u32[]{:S(2)}, u32[]{:S(2)}) collective-permute-start(f32[2,2,64,256]{3,2,1,0:T(8,128)} %refs_2_.1), channel_id=1, source_target_pairs={{1,2},{2,1},{5,6},{6,5},{9,10},{10,9},{13,14},{14,13},{17,18},{18,... | collective-permute-start | bytes 786440 | tf_op jit(solution)/shard_map/ppermute | solution.py:479
  1.3 4.4 %collective-permute-start.2 = (f32[2,2,64,256]{3,2,1,0:T(8,128)}, f32[2,2,64,256]{3,2,1,0:T(8,128)S(1)}, u32[]{:S(2)}, u32[]{:S(2)}) collective-permute-start(f32[2,2,64,256]{3,2,1,0:T(8,128)} %refs_2_.1), channel_id=1, source_target_pairs={{0,1},{1,0},{2,3},{3,2},{4,5},{5,4},{6,7},{7,6},{8,9},{9,8},{10,11... | collective-permute-start | bytes 786440 | tf_op jit(solution)/shard_map/ppermute | solution.py:473
  5.7 0.7 %collective-permute-start.1 = (f32[1,2,64,256]{3,2,1,0:T(8,128)}, f32[1,2,64,256]{3,2,1,0:T(8,128)S(1)}, u32[]{:S(2)}, u32[]{:S(2)}) collective-permute-start(f32[1,2,64,256]{3,2,1,0:T(8,128)} %refs_0_.1), channel_id=1, source_target_pairs={{4,8},{8,4},{5,9},{9,5},{6,10},{10,6},{7,11},{11,7},{20,24},{24,20... | collective-permute-start | bytes 393224 | tf_op jit(solution)/shard_map/ppermute | solution.py:470
  6.4 4.5 %collective-permute-start = (f32[1,2,64,256]{3,2,1,0:T(8,128)}, f32[1,2,64,256]{3,2,1,0:T(8,128)S(1)}, u32[]{:S(2)}, u32[]{:S(2)}) collective-permute-start(f32[1,2,64,256]{3,2,1,0:T(8,128)} %refs_0_.1), channel_id=1, source_target_pairs={{0,4},{8,12},{4,0},{12,8},{1,5},{9,13},{5,1},{13,9},{2,6},{10,14},... | collective-permute-start | bytes 393224 | tf_op jit(solution)/shard_map/ppermute | solution.py:470
  11.5 0.6 %copy-done.5 = f32[4,2]{0,1:T(2,128)S(1)} copy-done((f32[4,2]{0,1:T(2,128)S(1)}, f32[4,2]{0,1:T(2,128)}, u32[]{:S(2)}) %copy-start.5) | copy-done | bytes 56
  12.2 0.0 copy-done.4
  12.2 0.9 %copy-done.1 = f32[2,128,128]{2,1,0:T(8,128)S(1)} copy-done((f32[2,128,128]{2,1,0:T(8,128)S(1)}, f32[2,128,128]{2,1,0:T(8,128)}, u32[]{:S(2)}) %copy-start.1) | copy-done | bytes 131096
  13.1 2.0 %shard_map.174 = (f32[4,2,128,128]{3,2,1,0:T(8,128)S(1)}, f32[1,192,256]{2,1,0:T(8,128)S(1)}, f32[4,8,256]{2,1,0:T(8,128)S(1)}, f32[1,2,64,256]{3,2,1,0:T(8,128)...) custom-call(s32[1,4]{1,0:T(1,128)S(1)} %copy-done.6, ...), custom_call_target="tpu_custom_call" | custom-call | flops 10000000 | bytes 1933312 | tf_op jit(solution)/shard_map/pallas_call | solution.py:438
  15.2 2.4 %shard_map.175 = (f32[3,64,256]{2,1,0:T(8,128)S(1)}, f32[200,256]{1,0:T(8,128)S(1)}, f32[200,256]{1,0:T(8,128)S(1)}) custom-call(s32[1,4]{1,0:T(1,128)S(1)} %copy-done.6, s32[1,4]{1,0:T(1,128)S(1)} %copy-done.7, s32[1,1]{1,0:T(1,128)S(6)} %copy.19.count_ref, f32[4,2,128,128]{3,2,1,0:T(8,128)S(1)} %get-tuple-element.29.probes_ref, ...), custom_call_target="tpu_custom_call" | custom-call | flops 1000000000 | bytes 3162112 | tf_op jit(solution)/shard_map/pallas_call | solution.py:438
  17.6 1.1 %collective-permute-start.4 = (f32[200,256]{1,0:T(8,128)S(1)}, f32[200,256]{1,0:T(8,128)S(1)}, u32[]{:S(2)}, u32[]{:S(2)}) collective-permute-start(f32[200,256]{1,0:T(8,128)S(1)} %get-tuple-element.39), channel_id=1, source_target_pairs={{0,4},{8,12},{4,0},{12,8},{1,5},{9,13},{5,1},{13,9},{2,6},{10,14},... | collective-permute-start | bytes 614408 | tf_op jit(solution)/shard_map/ppermute | solution.py:470
  18.7 0.7 %collective-permute-start.5 = (f32[200,256]{1,0:T(8,128)S(1)}, f32[200,256]{1,0:T(8,128)S(1)}, u32[]{:S(2)}, u32[]{:S(2)}) collective-permute-start(f32[200,256]{1,0:T(8,128)S(1)} %get-tuple-element.40), channel_id=1, source_target_pairs={{4,8},{8,4},{5,9},{9,5},{6,10},{10,6},{7,11},{11,7},{20,24},{24,20... | collective-permute-start | bytes 614408 | tf_op jit(solution)/shard_map/ppermute | solution.py:470
  19.4 4.8 %collective-permute-done.4.rim_a_ref = f32[200,256]{1,0:T(8,128)S(1)} collective-permute-done((f32[200,256]{1,0:T(8,128)S(1)}, f32[200,256]{1,0:T(8,128)S(1)}, u32[]{:S(2)}, u32[]{:S(2)}) %collective-permute-start.4) | collective-permute-done | bytes 204832 | tf_op jit(solution)/shard_map/ppermute | solution.py:470
  24.2 0.7 %shard_map.176 = (f32[1,2,64,256]{3,2,1,0:T(8,128)}, f32[128,256]{1,0:T(8,128)S(1)}) custom-call(f32[3,64,256]{2,1,0:T(8,128)S(1)} %get-tuple-element.38.own_ref, f32[200,256]{1,0:T(8,128)S(1)} %collective-permute-done.4.rim_a_ref, f32[200,256]{1,0:T(8,128)S(1)} %collective-permute-done.5.rim_b_ref, f32[1,2,64,256]{3,2,1,0:T(8,128)S(1)} %copy-done.2, ...), custom_call_target="tpu_custom_call" | custom-call | flops 1000000 | bytes 1130496 | tf_op jit(solution)/shard_map/pallas_call | solution.py:438
  24.9 0.4 collective-permute-start.6
  25.3 0.5 shard_map.179.base_ref
  25.8 5.5 %collective-permute-start.13 = (f32[2,2,64,256]{3,2,1,0:T(8,128)S(1)}, f32[2,2,64,256]{3,2,1,0:T(8,128)S(1)}, u32[]{:S(2)}, u32[]{:S(2)}) collective-permute-start(f32[2,2,64,256]{3,2,1,0:T(8,128)S(1)} %shard_map.179.base_ref), channel_id=1, source_target_pairs={{0,4},{4,8},{6,2},{8,12},{10,6},{14,10},{1,5},{5,9},{7,3},{9,13},{... | collective-permute-start | bytes 786440 | tf_op jit(solution)/shard_map/ppermute | solution.py:543
  31.4 0.7 %collective-permute-start.8 = (f32[2,128,256]{2,1,0:T(8,128)S(1)}, f32[2,128,256]{2,1,0:T(8,128)S(1)}, u32[]{:S(2)}, u32[]{:S(2)}) collective-permute-start(f32[2,128,256]{2,1,0:T(8,128)S(1)} %pad_maximum_fusion.here_ref), channel_id=1, source_target_pairs={{4,8},{8,4},{5,9},{9,5},{6,10},{10,6},{7,11},{11,7},{20,24},{24,20... | collective-permute-start | bytes 786440 | tf_op jit(solution)/shard_map/ppermute | solution.py:470
  32.1 3.9 %collective-permute-start.7 = (f32[2,128,256]{2,1,0:T(8,128)S(1)}, f32[2,128,256]{2,1,0:T(8,128)S(1)}, u32[]{:S(2)}, u32[]{:S(2)}) collective-permute-start(f32[2,128,256]{2,1,0:T(8,128)S(1)} %pad_maximum_fusion.here_ref), channel_id=1, source_target_pairs={{0,4},{8,12},{4,0},{12,8},{1,5},{9,13},{5,1},{13,9},{2,6},{10,14},... | collective-permute-start | bytes 786440 | tf_op jit(solution)/shard_map/ppermute | solution.py:470
  35.9 2.1 %collective-permute-done.13.beside_ref = f32[2,2,64,256]{3,2,1,0:T(8,128)S(1)} collective-permute-done((f32[2,2,64,256]{3,2,1,0:T(8,128)S(1)}, f32[2,2,64,256]{3,2,1,0:T(8,128)S(1)}, u32[]{:S(2)}, u32[]{:S(2)}) %collective-permute-start.13) | collective-permute-done | bytes 262176 | tf_op jit(solution)/shard_map/ppermute | solution.py:543
  38.0 0.7 %shard_map.180 = (f32[2,2,64,256]{3,2,1,0:T(8,128)S(1)}, f32[2,2,64,256]{3,2,1,0:T(8,128)S(1)}) custom-call(s32[2,4]{1,0:T(2,128)S(1)} %bitcast.12, f32[2,4]{1,0:T(2,128)S(1)} %bitcast.14, f32[2,2,64,256]{3,2,1,0:T(8,128)S(1)} %shard_map.179.base_ref, f32[2,2,64,256]{3,2,1,0:T(8,128)S(1)} %collective-permute-done.13.beside_ref), custom_call_target="tpu_custom_call" | custom-call | flops 10000000 | bytes 1048576 | tf_op jit(solution)/shard_map/pallas_call | solution.py:438
  38.7 0.1 collective-permute-start.14
  38.8 1.6 %collective-permute-start.10 = (f32[4,8,256]{2,1,0:T(8,128)S(1)}, f32[4,8,256]{2,1,0:T(8,128)S(1)}, u32[]{:S(2)}, u32[]{:S(2)}) collective-permute-start(f32[4,8,256]{2,1,0:T(8,128)S(1)} %get-tuple-element.43.refs_0_), channel_id=1, source_target_pairs={{0,2},{2,0},{1,3},{3,1},{4,6},{6,4},{5,7},{7,5},{8,10},{10,8},{9,1... | collective-permute-start | bytes 98312 | tf_op jit(solution)/shard_map/ppermute | solution.py:499
  40.5 0.2 collective-permute-start.9
  40.6 2.2 %collective-permute-done.10.refs_2_ = f32[4,8,256]{2,1,0:T(8,128)S(1)} collective-permute-done((f32[4,8,256]{2,1,0:T(8,128)S(1)}, f32[4,8,256]{2,1,0:T(8,128)S(1)}, u32[]{:S(2)}, u32[]{:S(2)}) %collective-permute-start.10) | collective-permute-done | bytes 32800 | tf_op jit(solution)/shard_map/ppermute | solution.py:499
  42.8 1.2 %collective-permute-done.11.refs_3_ = f32[4,8,256]{2,1,0:T(8,128)S(1)} collective-permute-done((f32[4,8,256]{2,1,0:T(8,128)S(1)}, f32[4,8,256]{2,1,0:T(8,128)S(1)}, u32[]{:S(2)}, u32[]{:S(2)}) %collective-permute-start.11) | collective-permute-done | bytes 32800 | tf_op jit(solution)/shard_map/ppermute | solution.py:473
  44.0 1.3 %shard_map.177 = (bf16[2,384,192]{2,1,0:T(8,128)(2,1)S(1)}, bf16[2,384,192]{2,1,0:T(8,128)(2,1)S(1)}) custom-call(f32[4,8,256]{2,1,0:T(8,128)S(1)} %get-tuple-element.43.refs_0_, f32[4,8,256]{2,1,0:T(8,128)S(1)} %collective-permute-done.9.refs_1_, f32[4,8,256]{2,1,0:T(8,128)S(1)} %collective-permute-done.10.refs_2_, ...), custom_call_target="tpu_custom_call" | custom-call | flops 100000000 | bytes 1310720 | tf_op jit(solution)/shard_map/pallas_call | solution.py:438
  45.3 0.8 %shard_map.178 = (f32[2,64,256]{2,1,0:T(8,128)S(1)}, f32[2,2,64,256]{3,2,1,0:T(8,128)S(1)}, f32[384,256]{1,0:T(8,128)S(1)}) custom-call(f32[2,128,256]{2,1,0:T(8,128)S(1)} %pad_maximum_fusion.here_ref, f32[2,128,256]{2,1,0:T(8,128)S(1)} %collective-permute-done.7.side_a_ref, f32[2,128,256]{2,1,0:T(8,128)S(1)} %collective-permute-done.8.side_b_ref, ...), custom_call_target="tpu_custom_call" | custom-call | flops 1000000000 | bytes 2162688 | tf_op jit(solution)/shard_map/pallas_call | solution.py:438
  46.2 0.2 collective-permute-start.12
  46.4 0.0 copy-start.3
  46.4 1.6 %collective-permute-start.15 = (f32[2,64,256]{2,1,0:T(8,128)S(1)}, f32[2,64,256]{2,1,0:T(8,128)S(1)}, u32[]{:S(2)}, u32[]{:S(2)}) collective-permute-start(f32[2,64,256]{2,1,0:T(8,128)S(1)} %fusion), channel_id=1, source_target_pairs={{0,2},{2,0},{1,3},{3,1},{4,6},{6,4},{5,7},{7,5},{8,10},{10,8},{9,1... | collective-permute-start | bytes 393224 | tf_op jit(solution)/shard_map/ppermute | solution.py:560
  48.1 4.2 %collective-permute-done.15 = f32[2,64,256]{2,1,0:T(8,128)S(1)} collective-permute-done((f32[2,64,256]{2,1,0:T(8,128)S(1)}, f32[2,64,256]{2,1,0:T(8,128)S(1)}, u32[]{:S(2)}, u32[]{:S(2)}) %collective-permute-start.15) | collective-permute-done | bytes 131104 | tf_op jit(solution)/shard_map/ppermute | solution.py:560
  52.3 0.9 %shard_map.181 = (f32[1,2,64,256]{3,2,1,0:T(8,128)}, f32[2,2,64,256]{3,2,1,0:T(8,128)}, f32[1,2,64,256]{3,2,1,0:T(8,128)}) custom-call(f32[2,64,256]{2,1,0:T(8,128)S(1)} %get-tuple-element.46.keep_ref, f32[2,2,64,256]{3,2,1,0:T(8,128)S(1)} %get-tuple-element.47.own_ref, f32[384,256]{1,0:T(8,128)S(1)} %collective-permute-done.12.received_ref, ...), custom_call_target="tpu_custom_call" | custom-call | flops 1000000 | bytes 1966080 | tf_op jit(solution)/shard_map/pallas_call | solution.py:438
  (27 shorter events, 0.1 us)
Async XLA Ops:
  0.6 14.5 %collective-permute-start.3 = (f32[2,2,64,256]{3,2,1,0:T(8,128)}, f32[2,2,64,256]{3,2,1,0:T(8,128)S(1)}, u32[]{:S(2)}, u32[]{:S(2)}) collective-permute-start(f32[2,2,64,256]{3,2,1,0:T(8,128)} %refs_2_.1), channel_id=1, source_target_pairs={{1,2},{2,1},{5,6},{6,5},{9,10},{10,9},{13,14},{14,13},{17,18},{18,... | collective-permute-start | bytes 786440 | tf_op jit(solution)/shard_map/ppermute | solution.py:479
  1.3 13.8 %collective-permute-start.2 = (f32[2,2,64,256]{3,2,1,0:T(8,128)}, f32[2,2,64,256]{3,2,1,0:T(8,128)S(1)}, u32[]{:S(2)}, u32[]{:S(2)}) collective-permute-start(f32[2,2,64,256]{3,2,1,0:T(8,128)} %refs_2_.1), channel_id=1, source_target_pairs={{0,1},{1,0},{2,3},{3,2},{4,5},{5,4},{6,7},{7,6},{8,9},{9,8},{10,11... | collective-permute-start | bytes 786440 | tf_op jit(solution)/shard_map/ppermute | solution.py:473
  5.7 9.4 %collective-permute-start.1 = (f32[1,2,64,256]{3,2,1,0:T(8,128)}, f32[1,2,64,256]{3,2,1,0:T(8,128)S(1)}, u32[]{:S(2)}, u32[]{:S(2)}) collective-permute-start(f32[1,2,64,256]{3,2,1,0:T(8,128)} %refs_0_.1), channel_id=1, source_target_pairs={{4,8},{8,4},{5,9},{9,5},{6,10},{10,6},{7,11},{11,7},{20,24},{24,20... | collective-permute-start | bytes 393224 | tf_op jit(solution)/shard_map/ppermute | solution.py:470
  6.4 8.8 %collective-permute-start = (f32[1,2,64,256]{3,2,1,0:T(8,128)}, f32[1,2,64,256]{3,2,1,0:T(8,128)S(1)}, u32[]{:S(2)}, u32[]{:S(2)}) collective-permute-start(f32[1,2,64,256]{3,2,1,0:T(8,128)} %refs_0_.1), channel_id=1, source_target_pairs={{0,4},{8,12},{4,0},{12,8},{1,5},{9,13},{5,1},{13,9},{2,6},{10,14},... | collective-permute-start | bytes 393224 | tf_op jit(solution)/shard_map/ppermute | solution.py:470
  11.5 0.7 %copy-start.5 = (f32[4,2]{0,1:T(2,128)S(1)}, f32[4,2]{0,1:T(2,128)}, u32[]{:S(2)}) copy-start(f32[4,2]{0,1:T(2,128)} %param.25) | copy-start | bytes 100
  11.5 0.7 %copy-start.7 = (s32[1,4]{1,0:T(1,128)S(1)}, s32[1,4]{1,0:T(1,128)}, u32[]{:S(2)}) copy-start(s32[1,4]{1,0:T(1,128)} %columns_ref.3) | copy-start | bytes 52
  11.5 0.7 %copy-start.4 = (s32[4,2]{0,1:T(2,128)S(1)}, s32[4,2]{0,1:T(2,128)}, u32[]{:S(2)}) copy-start(s32[4,2]{0,1:T(2,128)} %param.24) | copy-start | bytes 100
  11.5 0.7 %copy-start.6 = (s32[1,4]{1,0:T(1,128)S(1)}, s32[1,4]{1,0:T(1,128)}, u32[]{:S(2)}) copy-start(s32[1,4]{1,0:T(1,128)} %rows_ref.3) | copy-start | bytes 52
  12.2 0.9 %copy-start.1 = (f32[2,128,128]{2,1,0:T(8,128)S(1)}, f32[2,128,128]{2,1,0:T(8,128)}, u32[]{:S(2)}) copy-start(f32[2,128,128]{2,1,0:T(8,128)} %probe_ref.1) | copy-start | bytes 393220
  15.2 9.0 %copy-start = (f32[1,2,64,256]{3,2,1,0:T(8,128)S(1)}, f32[1,2,64,256]{3,2,1,0:T(8,128)}, u32[]{:S(2)}) copy-start(f32[1,2,64,256]{3,2,1,0:T(8,128)} %dual_ref.3) | copy-start | bytes 393220
  15.2 9.0 %copy-start.2 = (f32[1,2,64,256]{3,2,1,0:T(8,128)S(1)}, f32[1,2,64,256]{3,2,1,0:T(8,128)}, u32[]{:S(2)}) copy-start(f32[1,2,64,256]{3,2,1,0:T(8,128)} %projected_ref.1) | copy-start | bytes 393220
  17.6 6.5 %collective-permute-start.4 = (f32[200,256]{1,0:T(8,128)S(1)}, f32[200,256]{1,0:T(8,128)S(1)}, u32[]{:S(2)}, u32[]{:S(2)}) collective-permute-start(f32[200,256]{1,0:T(8,128)S(1)} %get-tuple-element.39), channel_id=1, source_target_pairs={{0,4},{8,12},{4,0},{12,8},{1,5},{9,13},{5,1},{13,9},{2,6},{10,14},... | collective-permute-start | bytes 614408 | tf_op jit(solution)/shard_map/ppermute | solution.py:470
  18.7 5.4 %collective-permute-start.5 = (f32[200,256]{1,0:T(8,128)S(1)}, f32[200,256]{1,0:T(8,128)S(1)}, u32[]{:S(2)}, u32[]{:S(2)}) collective-permute-start(f32[200,256]{1,0:T(8,128)S(1)} %get-tuple-element.40), channel_id=1, source_target_pairs={{4,8},{8,4},{5,9},{9,5},{6,10},{10,6},{7,11},{11,7},{20,24},{24,20... | collective-permute-start | bytes 614408 | tf_op jit(solution)/shard_map/ppermute | solution.py:470
  24.9 6.4 %collective-permute-start.6 = (f32[128,256]{1,0:T(8,128)S(1)}, f32[128,256]{1,0:T(8,128)S(1)}, u32[]{:S(2)}, u32[]{:S(2)}) collective-permute-start(f32[128,256]{1,0:T(8,128)S(1)} %get-tuple-element.42), channel_id=1, source_target_pairs={{0,2},{2,0},{1,3},{3,1},{4,6},{6,4},{5,7},{7,5},{8,10},{10,8},{9,1... | collective-permute-start | bytes 393224 | tf_op jit(solution)/shard_map/ppermute | solution.py:528
  25.8 12.2 %collective-permute-start.13 = (f32[2,2,64,256]{3,2,1,0:T(8,128)S(1)}, f32[2,2,64,256]{3,2,1,0:T(8,128)S(1)}, u32[]{:S(2)}, u32[]{:S(2)}) collective-permute-start(f32[2,2,64,256]{3,2,1,0:T(8,128)S(1)} %shard_map.179.base_ref), channel_id=1, source_target_pairs={{0,4},{4,8},{6,2},{8,12},{10,6},{14,10},{1,5},{5,9},{7,3},{9,13},{... | collective-permute-start | bytes 786440 | tf_op jit(solution)/shard_map/ppermute | solution.py:543
  31.4 14.0 %collective-permute-start.8 = (f32[2,128,256]{2,1,0:T(8,128)S(1)}, f32[2,128,256]{2,1,0:T(8,128)S(1)}, u32[]{:S(2)}, u32[]{:S(2)}) collective-permute-start(f32[2,128,256]{2,1,0:T(8,128)S(1)} %pad_maximum_fusion.here_ref), channel_id=1, source_target_pairs={{4,8},{8,4},{5,9},{9,5},{6,10},{10,6},{7,11},{11,7},{20,24},{24,20... | collective-permute-start | bytes 786440 | tf_op jit(solution)/shard_map/ppermute | solution.py:470
  32.1 13.3 %collective-permute-start.7 = (f32[2,128,256]{2,1,0:T(8,128)S(1)}, f32[2,128,256]{2,1,0:T(8,128)S(1)}, u32[]{:S(2)}, u32[]{:S(2)}) collective-permute-start(f32[2,128,256]{2,1,0:T(8,128)S(1)} %pad_maximum_fusion.here_ref), channel_id=1, source_target_pairs={{0,4},{8,12},{4,0},{12,8},{1,5},{9,13},{5,1},{13,9},{2,6},{10,14},... | collective-permute-start | bytes 786440 | tf_op jit(solution)/shard_map/ppermute | solution.py:470
  38.7 7.7 %collective-permute-start.14 = (f32[2,2,64,256]{3,2,1,0:T(8,128)S(1)}, f32[2,2,64,256]{3,2,1,0:T(8,128)S(1)}, u32[]{:S(2)}, u32[]{:S(2)}) collective-permute-start(f32[2,2,64,256]{3,2,1,0:T(8,128)S(1)} %get-tuple-element.50), channel_id=1, source_target_pairs={{0,1},{1,0},{2,3},{3,2},{4,5},{5,4},{6,7},{7,6},{8,9},{9,8},{10,11... | collective-permute-start | bytes 786440 | tf_op jit(solution)/shard_map/ppermute | solution.py:473
  38.8 4.0 %collective-permute-start.10 = (f32[4,8,256]{2,1,0:T(8,128)S(1)}, f32[4,8,256]{2,1,0:T(8,128)S(1)}, u32[]{:S(2)}, u32[]{:S(2)}) collective-permute-start(f32[4,8,256]{2,1,0:T(8,128)S(1)} %get-tuple-element.43.refs_0_), channel_id=1, source_target_pairs={{0,2},{2,0},{1,3},{3,1},{4,6},{6,4},{5,7},{7,5},{8,10},{10,8},{9,1... | collective-permute-start | bytes 98312 | tf_op jit(solution)/shard_map/ppermute | solution.py:499
  40.5 2.3 %collective-permute-start.9 = (f32[4,8,256]{2,1,0:T(8,128)S(1)}, f32[4,8,256]{2,1,0:T(8,128)S(1)}, u32[]{:S(2)}, u32[]{:S(2)}) collective-permute-start(f32[4,8,256]{2,1,0:T(8,128)S(1)} %get-tuple-element.43.refs_0_), channel_id=1, source_target_pairs={{0,1},{1,0},{2,3},{3,2},{4,5},{5,4},{6,7},{7,6},{8,9},{9,8},{10,11... | collective-permute-start | bytes 98312 | tf_op jit(solution)/shard_map/ppermute | solution.py:473
  42.8 1.2 %collective-permute-start.11 = (f32[4,8,256]{2,1,0:T(8,128)S(1)}, f32[4,8,256]{2,1,0:T(8,128)S(1)}, u32[]{:S(2)}, u32[]{:S(2)}) collective-permute-start(f32[4,8,256]{2,1,0:T(8,128)S(1)} %collective-permute-done.10.refs_2_), channel_id=1, source_target_pairs={{0,1},{1,0},{2,3},{3,2},{4,5},{5,4},{6,7},{7,6},{8,9},{9,8},{10,11... | collective-permute-start | bytes 98312 | tf_op jit(solution)/shard_map/ppermute | solution.py:473
  46.2 6.1 %collective-permute-start.12 = (f32[384,256]{1,0:T(8,128)S(1)}, f32[384,256]{1,0:T(8,128)S(1)}, u32[]{:S(2)}, u32[]{:S(2)}) collective-permute-start(f32[384,256]{1,0:T(8,128)S(1)} %get-tuple-element.48), channel_id=1, source_target_pairs={{0,1},{1,0},{2,3},{3,2},{4,5},{5,4},{6,7},{7,6},{8,9},{9,8},{10,11... | collective-permute-start | bytes 1179656 | tf_op jit(solution)/shard_map/ppermute | solution.py:473
  46.4 5.9 %copy-start.3 = (f32[1,2,64,256]{3,2,1,0:T(8,128)S(1)}, f32[1,2,64,256]{3,2,1,0:T(8,128)}, u32[]{:S(2)}) copy-start(f32[1,2,64,256]{3,2,1,0:T(8,128)} %get-tuple-element.25.object_ref) | copy-start | bytes 393220
  46.4 5.8 %collective-permute-start.15 = (f32[2,64,256]{2,1,0:T(8,128)S(1)}, f32[2,64,256]{2,1,0:T(8,128)S(1)}, u32[]{:S(2)}, u32[]{:S(2)}) collective-permute-start(f32[2,64,256]{2,1,0:T(8,128)S(1)} %fusion), channel_id=1, source_target_pairs={{0,2},{2,0},{1,3},{3,1},{4,6},{6,4},{5,7},{7,5},{8,10},{10,8},{9,1... | collective-permute-start | bytes 393224 | tf_op jit(solution)/shard_map/ppermute | solution.py:560

commit v4 on v3

--- a/solution.py
+++ b/solution.py
@@ -55,12 +55,39 @@
     return lax.rem(lax.axis_index("scan"), 2) == 0
 
 
-def outer_rows(ya_ref, yb_ref, channel):
-    last = ya_ref.shape[1] - 1
-    first = tile_is_first()
-    below = jnp.where(first, yb_ref[channel, last], ya_ref[channel, last])
-    above = jnp.where(first, ya_ref[channel, 0], yb_ref[channel, 0])
-    return (below, above)
+def pack_kernel(plane_ref, volume_ref, packed_ref, slabs, done):
+    width = plane_ref.shape[2]
+    count = volume_ref.shape[1]
+    copies = [
+        (plane_ref.at[0, channel], packed_ref.at[channel * width : (channel + 1) * width])
+        for channel in range(2)
+    ]
+    for channel in range(2):
+        for row in range(count):
+            for side, at in enumerate((0, width - SUBLANES)):
+                source = volume_ref.at[channel, row, at : at + SUBLANES]
+                copies.append((source, slabs.at[(channel * count + row) * 2 + side]))
+    copies = [
+        pltpu.make_async_copy(source, target, done.at[number])
+        for number, (source, target) in enumerate(copies)
+    ]
+    for copy in copies:
+        copy.start()
+    for copy in copies[2:]:
+        copy.wait()
+    for edge in range(slabs.shape[0]):
+        take = 0 if edge % 2 == 0 else SUBLANES - 1
+        packed_ref[2 * width + edge : 2 * width + edge + 1] = slabs[edge, take : take + 1]
+    for copy in copies[:2]:
+        copy.wait()
+
+
+def edges_of(plane_a_ref, plane_b_ref, number, width):
+    even = scan_is_even()
+    at = 2 * width + 2 * number
+    first_a, last_a = plane_a_ref[at : at + 1], plane_a_ref[at + 1 : at + 2]
+    first_b, last_b = plane_b_ref[at : at + 1], plane_b_ref[at + 1 : at + 2]
+    return (jnp.where(even, last_b, last_a), jnp.where(even, first_a, first_b))
 
 
 def slot_masks(rows_ref, columns_ref, count_ref, slot, side):
@@ -83,7 +110,7 @@
 
 
 def prepare_kernel(
-    rows_ref, columns_ref, count_ref, shift_ref, weight_ref, probe_ref, *refs
+    rows_ref, columns_ref, count_ref, shift_ref, weight_ref, *refs
 ):
     half = (len(refs) - 4) // 2
     sources, targets, done = refs[:half], refs[half + 3 : -1], refs[-1]
@@ -94,10 +121,12 @@
     ]
     for copy in copies:
         copy.start()
+    probe_ref = targets[0]
     side = probe_ref.shape[1]
     slots = probes_ref.shape[0]
     width = density_ref.shape[1] - side
     density_ref[...] = jnp.zeros_like(density_ref)
+    copies[0].wait()
     for slot in range(slots):
         turn = lax.rem(rows_ref[0, slot], side)
         probe = [
@@ -115,7 +144,7 @@
             table = jnp.where(places == 2 * row, shift_ref[row, angle].astype(jnp.float32), table)
             table = jnp.where(places == 2 * row + 1, weight_ref[row, angle], table)
         tables_ref[angle] = table
-    for copy in copies:
+    for copy in copies[1:]:
         copy.wait()
 
 
@@ -134,22 +163,24 @@
     inverse_low_ref,
     plane_a_ref,
     plane_b_ref,
-    ya_ref,
-    yb_ref,
     own_ref,
     rim_a_ref,
     rim_b_ref,
+    row_a_ref,
+    row_b_ref,
     wide,
     totals,
 ):
-    width = plane_ref.shape[2]
+    width = volume_ref.shape[2]
     slots, _, side, _ = probes_ref.shape
     even = scan_is_even()
     at_a = pl.multiple_of(jnp.where(even, 2 * width, 0), width)
     at_b = pl.multiple_of(jnp.where(even, 0, 2 * width), width)
-    wide[:, width : 2 * width] = plane_ref[0]
-    wide[:, pl.ds(at_a, width)] = plane_a_ref[0]
-    wide[:, pl.ds(at_b, width)] = plane_b_ref[0]
+    for part in range(2):
+        at = slice(part * width, (part + 1) * width)
+        wide[part, width : 2 * width] = plane_ref[at]
+        wide[part, pl.ds(at_a, width)] = plane_a_ref[at]
+        wide[part, pl.ds(at_b, width)] = plane_b_ref[at]
     forward = (forward_high_ref[...], forward_low_ref[...])
     inverse = (inverse_high_ref[...], inverse_low_ref[...])
     waves, masks = [], []
@@ -209,20 +240,19 @@
         place(totals, 0, probe[0] * near_real + probe[1] * near_imaginary, masks[slot], width)
         place(totals, 1, probe[0] * near_imaginary - probe[1] * near_real, masks[slot], width)
     own_ref[...] = totals[:, width : 2 * width]
-    below_above = [outer_rows(ya_ref, yb_ref, channel) for channel in range(2)]
-    parts = totals.shape[0]
+    for rim_ref, at in ((rim_a_ref, at_a), (rim_b_ref, at_b)):
+        for part in range(totals.shape[0]):
+            rim_ref[part * width : (part + 1) * width] = totals[part, pl.ds(at, width)]
+    first_tile = tile_is_first()
     count = volume_ref.shape[1]
-    for rim_ref, at, low in ((rim_a_ref, at_a, jnp.logical_not(even)), (rim_b_ref, at_b, even)):
-        for part in range(parts):
-            rim_ref[part * width : (part + 1) * width] = totals[part, pl.ds(at, width)]
-        edge_rows = []
-        for channel in range(2):
-            planes = [below_above[channel][0]]
-            planes += [volume_ref[channel, row] for row in range(count)]
-            planes.append(below_above[channel][1])
-            for plane in planes:
-                edge_rows.append(jnp.where(low, plane[:1], plane[width - 1 :]))
-        rim_ref[parts * width :] = jnp.concatenate(edge_rows, axis=0)
+    for channel in range(2):
+        rows = []
+        for row in (0, count - 1):
+            before, after = edges_of(plane_a_ref, plane_b_ref, channel * count + row, width)
+            rows.append((volume_ref[channel, row], jnp.concatenate([before, after], axis=0)))
+        for low, row_ref in ((jnp.logical_not(first_tile), row_a_ref), (first_tile, row_b_ref)):
+            row_ref[channel, :width] = jnp.where(low, rows[0][0], rows[1][0])
+            row_ref[channel, width : width + 2] = jnp.where(low, rows[0][1], rows[1][1])
 
 
 def fold_kernel(own_ref, rim_a_ref, rim_b_ref, projected_ref, dual_ref, object_ref, residual_ref):
@@ -241,26 +271,31 @@
         residual_ref[part * width : (part + 1) * width] = target - updated - dual
 
 
-def variation_kernel(volume_ref, ya_ref, yb_ref, rim_a_ref, rim_b_ref, base_ref, padded, norms):
+def variation_kernel(
+    volume_ref, plane_a_ref, plane_b_ref, row_a_ref, row_b_ref, base_ref, padded, norms
+):
     width = volume_ref.shape[2]
     length = volume_ref.shape[3]
     count = volume_ref.shape[1]
     margin = 8
-    edges_at = rim_a_ref.shape[0] - 2 * (count + 2)
-    even = scan_is_even()
+    first_tile = tile_is_first()
     lanes = lax.broadcasted_iota(jnp.int32, (width, length), 1)
     first_lane = lanes == 0
     last_lane = lanes == length - 1
     for channel in range(2):
-        below, above = outer_rows(ya_ref, yb_ref, channel)
-        planes = [below] + [volume_ref[channel, row] for row in range(count)] + [above]
-        for row, plane in enumerate(planes):
-            at = edges_at + channel * (count + 2) + row
-            edge_a = rim_a_ref[at : at + 1]
-            edge_b = rim_b_ref[at : at + 1]
-            padded[row, margin : margin + width] = plane
-            padded[row, margin - 1 : margin] = jnp.where(even, edge_b, edge_a)
-            padded[row, margin + width : margin + width + 1] = jnp.where(even, edge_a, edge_b)
+        for row in range(count):
+            before, after = edges_of(plane_a_ref, plane_b_ref, channel * count + row, width)
+            padded[row + 1, margin : margin + width] = volume_ref[channel, row]
+            padded[row + 1, margin - 1 : margin] = before
+            padded[row + 1, margin + width : margin + width + 1] = after
+        row_a, row_b = row_a_ref[channel], row_b_ref[channel]
+        for row, beside in (
+            (0, jnp.where(first_tile, row_b, row_a)),
+            (count + 1, jnp.where(first_tile, row_a, row_b)),
+        ):
+            padded[row, margin : margin + width] = beside[:width]
+            padded[row, margin - 1 : margin] = beside[width : width + 1]
+            padded[row, margin + width : margin + width + 1] = beside[width + 1 : width + 2]
         previous_y = None
         for row in range(count + 1):
             here = padded[row, margin : margin + width]
@@ -425,15 +460,17 @@
             volume_ref[channel, row] = base_ref[channel, row] - step_size * descent
 
 
-def call(kernel, shapes, operands, scratch, flops, scalars=0, staged=(), kind=jnp.float32):
+def call(kernel, shapes, operands, scratch, flops, scalars=0, staged=(), copies=0, kind=jnp.float32):
     held = sum(operand.nbytes for operand in operands[scalars:] + staged)
     held += 4 * sum(math.prod(shape) for shape in shapes)
     own = 4 * sum(math.prod(shape) for shape in scratch)
     outputs = [jax.ShapeDtypeStruct(shape, kind) for shape in shapes]
-    outputs += [jax.ShapeDtypeStruct(array.shape, array.dtype) for array in staged]
     scratch_shapes = [pltpu.VMEM(shape, jnp.float32) for shape in scratch]
-    if staged:
-        scratch_shapes.append(pltpu.SemaphoreType.DMA((len(staged),)))
+    if staged and not copies:
+        outputs += [jax.ShapeDtypeStruct(array.shape, array.dtype) for array in staged]
+        copies = len(staged)
+    if copies:
+        scratch_shapes.append(pltpu.SemaphoreType.DMA((copies,)))
     in_specs = [SMEM] * scalars + [VMEM] * (len(operands) - scalars) + [HBM] * len(staged)
     return pl.pallas_call(
         kernel,
@@ -472,42 +509,53 @@
     def across(block):
         return lax.ppermute(block, "tile", swap)
 
-    plane_a = exchange(transmission, 0)
-    plane_b = exchange(transmission, 1)
-    bridge = [(i * tiles + 1, (i + 1) * tiles) for i in range(columns - 1)]
-    bridge += [(target, source) for source, target in bridge]
-    rows_b = lax.ppermute(volume, ("angle", "tile"), bridge)
-    rows_a = across(volume)
+    edges = 2 * 2 * count
+    (plane,) = call(
+        pack_kernel,
+        [(2 * width + -(-edges // SUBLANES) * SUBLANES, length)],
+        (),
+        [(edges, SUBLANES, length)],
+        10**5,
+        staged=(transmission, volume),
+        copies=2 + edges,
+    )
+    plane_a = exchange(plane, 0)
+    plane_b = exchange(plane, 1)
     tables = [jnp.asarray(table) for table in dft_tables(probe_wave.shape[1])]
-    rim_rows = 3 * width + 2 * (count + 2)
     scalars = (slot_first_rows, slot_first_columns, patch_counts)
     slots = slot_first_rows.shape[1]
     side = probe_wave.shape[1]
-    probes, density, rays, *held = call(
+    probes, density, rays, _, *held = call(
         prepare_kernel,
         [(slots, 2, side, side), (1, 3 * width, length), (columns * tiles, SUBLANES, length)],
-        (*scalars, shift_table.T, tap_weight.T, probe_wave),
+        (*scalars, shift_table.T, tap_weight.T),
         [],
         10**7,
         5,
-        (transmission, intensities, volume, *tables),
-    )
-    volume_here = held[2]
+        (probe_wave, intensities, volume, *tables),
+    )
+    volume_here = held[1]
     turns = [[(i, (i - turn) % columns) for i in range(columns)] for turn in range(columns)]
     by_row = [rays]
     for turn in range(1, columns):
         by_row.append(lax.ppermute(rays, "angle", turns[turn]))
     by_row = [block for table in by_row for block in (table, across(table))]
-    own, rim_a, rim_b = call(
+    own, rim_a, rim_b, row_a, row_b = call(
         patch_kernel,
-        [(3, width, length), (rim_rows, length), (rim_rows, length)],
-        (*scalars, probes, density, *held, plane_a, plane_b, rows_a, rows_b),
+        [(3, width, length)]
+        + [(3 * width, length)] * 2
+        + [(2, width + SUBLANES, length)] * 2,
+        (*scalars, probes, density, plane, *held, plane_a, plane_b),
         [(2, 3 * width, length), (3, 3 * width, length)],
         10**9,
         3,
     )
     rim_a = exchange(rim_a, 0)
     rim_b = exchange(rim_b, 1)
+    bridge = [(i * tiles + 1, (i + 1) * tiles) for i in range(columns - 1)]
+    bridge += [(target, source) for source, target in bridge]
+    row_b = lax.ppermute(row_b, ("angle", "tile"), bridge)
+    row_a = across(row_a)
     high, low = call(
         operator_kernel,
         [(columns, (2 + 2 * count) * width, 3 * width)] * 2,
@@ -529,7 +577,7 @@
     (base,) = call(
         variation_kernel,
         [volume.shape],
-        (volume_here, rows_a, rows_b, rim_a, rim_b),
+        (volume_here, plane_a, plane_b, row_a, row_b),
         [(count + 2, width + 16, length), (width + 16, length)],
         10**7,
     )

time: 53.4 us -> 51.2 us (0.959)
  starting transfers between devices: 26.1 us -> 20.8 us
  waiting for transfers between devices: 14.4 us -> 16.9 us
  Pallas kernels: 9.42 us -> 10.9 us
  local copies, waits for them, and re-layouts: 1.6 us -> 0.68 us
    ppermute x5, starting transfers between devices: 4.83 us -> 0.8 us  [across(): return lax.ppermute(block, 'tile', swap)]
    ppermute x1, starting transfers between devices: 1.65 us -> 0.07 us  [body(): by_row.append(lax.ppermute(rays, 'angle', turns[turn]))]
    ppermute x1, waiting for transfers between devices: 4.17 us -> 5.66 us  [body(): spread = spread + lax.ppermute(keep[turn] + received[turn], 'angle', route)]
    ppermute x1, starting transfers between devices: 1.65 us -> 0.16 us  [body(): spread = spread + lax.ppermute(keep[turn] + received[turn], 'angle', route)]
    pallas_call x8 -> x9, Pallas kernels: 9.42 us -> 10.9 us  [call(): pl.pallas_call(kernel, out_shape=outputs, in_specs=in_specs, out_specs=[V...]
    ppermute x6, waiting for transfers between devices: 4.79 us -> 3.47 us  [exchange(): return lax.ppermute(block, 'scan', both[number])]
    ppermute x1, waiting for transfers between devices: 2.18 us -> 3.48 us  [body(): by_row.append(lax.ppermute(rays, 'angle', turns[turn]))]
    ppermute x1, starting transfers between devices: 0.38 us -> 1.49 us  [body(): by_column.append(lax.ppermute(residual, 'angle', turns[turn]))]
  transfers between devices with their start and end apart: 16 -> 16, of which waited for: 5 -> 5; matrix products, arithmetic and copies ran while one was open for 0% -> 0% of each run, Pallas kernels for 10% -> 13%
where the time goes in v4:
time: 51.2 us; the launch traced here: 50.9 us
  starting transfers between devices  20.8 us (41%)
  waiting for transfers between devices  16.9 us (33%)
  Pallas kernels  10.9 us (21%)
  between operations  1.54 us (3%)
  local copies, waits for them, and re-layouts  0.68 us (1%)
    ppermute x6, starting transfers between devices, exchange(): return lax.ppermute(block, 'scan', both[number])  12.1 us
    pallas_call x9, Pallas kernels, call(): pl.pallas_call(kernel, out_shape=outputs, in_specs=in_specs, out_specs=[V...  10.9 us
    ppermute x1, waiting for transfers between devices, body(): spread = spread + lax.ppermute(keep[turn] + received[turn], 'angle', route)  5.66 us
    ppermute x1, starting transfers between devices, body(): beside = lax.ppermute(base, ('scan', 'angle'), route)  5.54 us
    ppermute x1, waiting for transfers between devices, body(): by_row.append(lax.ppermute(rays, 'angle', turns[turn]))  3.48 us
    ppermute x6, waiting for transfers between devices, exchange(): return lax.ppermute(block, 'scan', both[number])  3.47 us
    ppermute x1, waiting for transfers between devices, body(): beside = lax.ppermute(base, ('scan', 'angle'), route)  3.05 us
    ppermute x1, starting transfers between devices, body(): by_column.append(lax.ppermute(residual, 'angle', turns[turn]))  1.49 us
  transfers between devices with their start and end apart: 16, of which 5 were waited for; matrix products, arithmetic and copies ran while one was open for 0% of the time, Pallas kernels for 13%

profile of v4, /device:TPU:0, one launch (start us, length us, event | category | flops | bytes accessed | tf_op | source)
XLA Modules:
  0.0 50.9 jit_solution(18218928539822871679)
XLA Ops:
  0.7 1.0 %shard_map.175.plane_ref = f32[136,256]{1,0:T(8,128)S(1)} custom-call(f32[1,2,64,256]{3,2,1,0:T(8,128)} %plane_ref.1, f32[2,2,64,256]{3,2,1,0:T(8,128)} %volume_ref.1), custom_call_target="tpu_custom_call" | custom-call | flops 100000 | bytes 532480 | tf_op jit(solution)/shard_map/pallas_call | solution.py:475
  1.6 0.7 %collective-permute-start.1 = (f32[136,256]{1,0:T(8,128)S(1)}, f32[136,256]{1,0:T(8,128)S(1)}, u32[]{:S(2)}, u32[]{:S(2)}) collective-permute-start(f32[136,256]{1,0:T(8,128)S(1)} %shard_map.175.plane_ref), channel_id=1, source_target_pairs={{4,8},{8,4},{5,9},{9,5},{6,10},{10,6},{7,11},{11,7},{20,24},{24,20... | collective-permute-start | bytes 417800 | tf_op jit(solution)/shard_map/ppermute | solution.py:507
  2.3 5.9 %collective-permute-start = (f32[136,256]{1,0:T(8,128)S(1)}, f32[136,256]{1,0:T(8,128)S(1)}, u32[]{:S(2)}, u32[]{:S(2)}) collective-permute-start(f32[136,256]{1,0:T(8,128)S(1)} %shard_map.175.plane_ref), channel_id=1, source_target_pairs={{0,4},{8,12},{4,0},{12,8},{1,5},{9,13},{5,1},{13,9},{2,6},{10,14},... | collective-permute-start | bytes 417800 | tf_op jit(solution)/shard_map/ppermute | solution.py:507
  8.9 0.0 copy-start.3
  8.9 0.6 %copy-done.3 = s32[4,2]{0,1:T(2,128)S(1)} copy-done((s32[4,2]{0,1:T(2,128)S(1)}, s32[4,2]{0,1:T(2,128)}, u32[]{:S(2)}) %copy-start.3) | copy-done | bytes 56
  9.6 2.5 %shard_map.174 = (f32[4,2,128,128]{3,2,1,0:T(8,128)S(1)}, f32[1,192,256]{2,1,0:T(8,128)S(1)}, f32[4,8,256]{2,1,0:T(8,128)S(1)}, f32[2,128,128]{2,1,0:T(8,128)}, ...) custom-call(s32[1,4]{1,0:T(1,128)S(1)} %copy-done.5, ...), custom_call_target="tpu_custom_call" | custom-call | flops 10000000 | bytes 1802240 | tf_op jit(solution)/shard_map/pallas_call | solution.py:475
  12.2 2.5 %shard_map.176 = (f32[3,64,256]{2,1,0:T(8,128)S(1)}, f32[192,256]{1,0:T(8,128)S(1)}, f32[192,256]{1,0:T(8,128)S(1)}, f32[2,72,256]{2,1,0:T(8,128)S(1)}, f32[2,72,256]{2,1,0:T(8,128)S(1)}) custom-call(s32[1,4]{1,0:T(1,128)S(1)} %copy-done.5, s32[1,4]{1,0:T(1,128)S(1)} %copy-done.6, s32[1,1]{1,0:T(1,128)S(6)} %copy.19.count_ref, ...), custom_call_target="tpu_custom_call" | custom-call | flops 1000000000 | bytes 2940928 | tf_op jit(solution)/shard_map/pallas_call | solution.py:475
  14.6 1.3 %collective-permute-start.2 = (f32[192,256]{1,0:T(8,128)S(1)}, f32[192,256]{1,0:T(8,128)S(1)}, u32[]{:S(2)}, u32[]{:S(2)}) collective-permute-start(f32[192,256]{1,0:T(8,128)S(1)} %get-tuple-element.39), channel_id=1, source_target_pairs={{0,4},{8,12},{4,0},{12,8},{1,5},{9,13},{5,1},{13,9},{2,6},{10,14},... | collective-permute-start | bytes 589832 | tf_op jit(solution)/shard_map/ppermute | solution.py:507
  15.9 0.7 %collective-permute-start.3 = (f32[192,256]{1,0:T(8,128)S(1)}, f32[192,256]{1,0:T(8,128)S(1)}, u32[]{:S(2)}, u32[]{:S(2)}) collective-permute-start(f32[192,256]{1,0:T(8,128)S(1)} %get-tuple-element.40), channel_id=1, source_target_pairs={{4,8},{8,4},{5,9},{9,5},{6,10},{10,6},{7,11},{11,7},{20,24},{24,20... | collective-permute-start | bytes 589832 | tf_op jit(solution)/shard_map/ppermute | solution.py:507
  16.6 0.1 collective-permute-start.11
  16.6 0.7 %collective-permute-start.12 = (f32[2,72,256]{2,1,0:T(8,128)S(1)}, f32[2,72,256]{2,1,0:T(8,128)S(1)}, u32[]{:S(2)}, u32[]{:S(2)}) collective-permute-start(f32[2,72,256]{2,1,0:T(8,128)S(1)} %get-tuple-element.50), channel_id=1, source_target_pairs={{1,2},{2,1},{5,6},{6,5},{9,10},{10,9},{13,14},{14,13},{17,18},{18,... | collective-permute-start | bytes 442376 | tf_op jit(solution)/shard_map/ppermute | solution.py:557
  17.3 3.5 %collective-permute-done.2.rim_a_ref = f32[192,256]{1,0:T(8,128)S(1)} collective-permute-done((f32[192,256]{1,0:T(8,128)S(1)}, f32[192,256]{1,0:T(8,128)S(1)}, u32[]{:S(2)}, u32[]{:S(2)}) %collective-permute-start.2) | collective-permute-done | bytes 196640 | tf_op jit(solution)/shard_map/ppermute | solution.py:507
  20.8 0.7 %shard_map.177 = (f32[1,2,64,256]{3,2,1,0:T(8,128)}, f32[128,256]{1,0:T(8,128)S(1)}) custom-call(f32[3,64,256]{2,1,0:T(8,128)S(1)} %get-tuple-element.38.own_ref, f32[192,256]{1,0:T(8,128)S(1)} %collective-permute-done.2.rim_a_ref, f32[192,256]{1,0:T(8,128)S(1)} %collective-permute-done.3.rim_b_ref, f32[1,2,64,256]{3,2,1,0:T(8,128)S(1)} %copy-done.1, ...), custom_call_target="tpu_custom_call" | custom-call | flops 1000000 | bytes 1114112 | tf_op jit(solution)/shard_map/pallas_call | solution.py:475
  21.5 1.5 %collective-permute-start.4 = (f32[128,256]{1,0:T(8,128)S(1)}, f32[128,256]{1,0:T(8,128)S(1)}, u32[]{:S(2)}, u32[]{:S(2)}) collective-permute-start(f32[128,256]{1,0:T(8,128)S(1)} %get-tuple-element.42), channel_id=1, source_target_pairs={{0,2},{2,0},{1,3},{3,1},{4,6},{6,4},{5,7},{7,5},{8,10},{10,8},{9,1... | collective-permute-start | bytes 393224 | tf_op jit(solution)/shard_map/ppermute | solution.py:576
  23.0 0.5 shard_map.180.base_ref
  23.5 5.5 %collective-permute-start.13 = (f32[2,2,64,256]{3,2,1,0:T(8,128)S(1)}, f32[2,2,64,256]{3,2,1,0:T(8,128)S(1)}, u32[]{:S(2)}, u32[]{:S(2)}) collective-permute-start(f32[2,2,64,256]{3,2,1,0:T(8,128)S(1)} %shard_map.180.base_ref), channel_id=1, source_target_pairs={{0,4},{4,8},{6,2},{8,12},{10,6},{14,10},{1,5},{5,9},{7,3},{9,13},{... | collective-permute-start | bytes 786440 | tf_op jit(solution)/shard_map/ppermute | solution.py:591
  29.1 0.7 %collective-permute-start.6 = (f32[2,128,256]{2,1,0:T(8,128)S(1)}, f32[2,128,256]{2,1,0:T(8,128)S(1)}, u32[]{:S(2)}, u32[]{:S(2)}) collective-permute-start(f32[2,128,256]{2,1,0:T(8,128)S(1)} %pad_maximum_fusion.here_ref), channel_id=1, source_target_pairs={{4,8},{8,4},{5,9},{9,5},{6,10},{10,6},{7,11},{11,7},{20,24},{24,20... | collective-permute-start | bytes 786440 | tf_op jit(solution)/shard_map/ppermute | solution.py:507
  29.8 2.9 %collective-permute-start.5 = (f32[2,128,256]{2,1,0:T(8,128)S(1)}, f32[2,128,256]{2,1,0:T(8,128)S(1)}, u32[]{:S(2)}, u32[]{:S(2)}) collective-permute-start(f32[2,128,256]{2,1,0:T(8,128)S(1)} %pad_maximum_fusion.here_ref), channel_id=1, source_target_pairs={{0,4},{8,12},{4,0},{12,8},{1,5},{9,13},{5,1},{13,9},{2,6},{10,14},... | collective-permute-start | bytes 786440 | tf_op jit(solution)/shard_map/ppermute | solution.py:507
  32.7 3.1 %collective-permute-done.13.beside_ref = f32[2,2,64,256]{3,2,1,0:T(8,128)S(1)} collective-permute-done((f32[2,2,64,256]{3,2,1,0:T(8,128)S(1)}, f32[2,2,64,256]{3,2,1,0:T(8,128)S(1)}, u32[]{:S(2)}, u32[]{:S(2)}) %collective-permute-start.13) | collective-permute-done | bytes 262176 | tf_op jit(solution)/shard_map/ppermute | solution.py:591
  35.7 0.7 %shard_map.181 = (f32[2,2,64,256]{3,2,1,0:T(8,128)S(1)}, f32[2,2,64,256]{3,2,1,0:T(8,128)S(1)}) custom-call(s32[2,4]{1,0:T(2,128)S(1)} %bitcast.12, f32[2,4]{1,0:T(2,128)S(1)} %bitcast.14, f32[2,2,64,256]{3,2,1,0:T(8,128)S(1)} %shard_map.180.base_ref, f32[2,2,64,256]{3,2,1,0:T(8,128)S(1)} %collective-permute-done.13.beside_ref), custom_call_target="tpu_custom_call" | custom-call | flops 10000000 | bytes 1048576 | tf_op jit(solution)/shard_map/pallas_call | solution.py:475
  36.5 0.1 collective-permute-start.14
  36.5 0.1 collective-permute-start.8
  36.6 0.4 collective-permute-start.7
  37.0 3.5 %collective-permute-done.8.refs_2_ = f32[4,8,256]{2,1,0:T(8,128)S(1)} collective-permute-done((f32[4,8,256]{2,1,0:T(8,128)S(1)}, f32[4,8,256]{2,1,0:T(8,128)S(1)}, u32[]{:S(2)}, u32[]{:S(2)}) %collective-permute-start.8) | collective-permute-done | bytes 32800 | tf_op jit(solution)/shard_map/ppermute | solution.py:541
  40.5 1.2 %collective-permute-done.9.refs_3_ = f32[4,8,256]{2,1,0:T(8,128)S(1)} collective-permute-done((f32[4,8,256]{2,1,0:T(8,128)S(1)}, f32[4,8,256]{2,1,0:T(8,128)S(1)}, u32[]{:S(2)}, u32[]{:S(2)}) %collective-permute-start.9) | collective-permute-done | bytes 32800 | tf_op jit(solution)/shard_map/ppermute | solution.py:510
  41.7 1.3 %shard_map.178 = (bf16[2,384,192]{2,1,0:T(8,128)(2,1)S(1)}, bf16[2,384,192]{2,1,0:T(8,128)(2,1)S(1)}) custom-call(f32[4,8,256]{2,1,0:T(8,128)S(1)} %get-tuple-element.43.refs_0_, f32[4,8,256]{2,1,0:T(8,128)S(1)} %collective-permute-done.7.refs_1_, f32[4,8,256]{2,1,0:T(8,128)S(1)} %collective-permute-done.8.refs_2_, ...), custom_call_target="tpu_custom_call" | custom-call | flops 100000000 | bytes 1310720 | tf_op jit(solution)/shard_map/pallas_call | solution.py:475
  43.1 0.8 %shard_map.179 = (f32[2,64,256]{2,1,0:T(8,128)S(1)}, f32[2,2,64,256]{3,2,1,0:T(8,128)S(1)}, f32[384,256]{1,0:T(8,128)S(1)}) custom-call(f32[2,128,256]{2,1,0:T(8,128)S(1)} %pad_maximum_fusion.here_ref, f32[2,128,256]{2,1,0:T(8,128)S(1)} %collective-permute-done.5.side_a_ref, f32[2,128,256]{2,1,0:T(8,128)S(1)} %collective-permute-done.6.side_b_ref, ...), custom_call_target="tpu_custom_call" | custom-call | flops 1000000000 | bytes 2162688 | tf_op jit(solution)/shard_map/pallas_call | solution.py:475
  43.9 0.2 collective-permute-start.10
  44.1 0.0 copy-start.2
  44.2 0.2 collective-permute-start.15
  44.3 5.7 %collective-permute-done.15 = f32[2,64,256]{2,1,0:T(8,128)S(1)} collective-permute-done((f32[2,64,256]{2,1,0:T(8,128)S(1)}, f32[2,64,256]{2,1,0:T(8,128)S(1)}, u32[]{:S(2)}, u32[]{:S(2)}) %collective-permute-start.15) | collective-permute-done | bytes 131104 | tf_op jit(solution)/shard_map/ppermute | solution.py:608
  50.0 0.9 %shard_map.182 = (f32[1,2,64,256]{3,2,1,0:T(8,128)}, f32[2,2,64,256]{3,2,1,0:T(8,128)}, f32[1,2,64,256]{3,2,1,0:T(8,128)}) custom-call(f32[2,64,256]{2,1,0:T(8,128)S(1)} %get-tuple-element.46.keep_ref, f32[2,2,64,256]{3,2,1,0:T(8,128)S(1)} %get-tuple-element.47.own_ref, f32[384,256]{1,0:T(8,128)S(1)} %collective-permute-done.10.received_ref, ...), custom_call_target="tpu_custom_call" | custom-call | flops 1000000 | bytes 1966080 | tf_op jit(solution)/shard_map/pallas_call | solution.py:475
  (26 shorter events, 0.1 us)
Async XLA Ops:
  0.6 8.3 %copy-start.4 = (f32[4,2]{0,1:T(2,128)S(1)}, f32[4,2]{0,1:T(2,128)}, u32[]{:S(2)}) copy-start(f32[4,2]{0,1:T(2,128)} %param.25) | copy-start | bytes 100
  0.6 8.3 %copy-start.6 = (s32[1,4]{1,0:T(1,128)S(1)}, s32[1,4]{1,0:T(1,128)}, u32[]{:S(2)}) copy-start(s32[1,4]{1,0:T(1,128)} %columns_ref.3) | copy-start | bytes 52
  1.6 10.5 %collective-permute-start.1 = (f32[136,256]{1,0:T(8,128)S(1)}, f32[136,256]{1,0:T(8,128)S(1)}, u32[]{:S(2)}, u32[]{:S(2)}) collective-permute-start(f32[136,256]{1,0:T(8,128)S(1)} %shard_map.175.plane_ref), channel_id=1, source_target_pairs={{4,8},{8,4},{5,9},{9,5},{6,10},{10,6},{7,11},{11,7},{20,24},{24,20... | collective-permute-start | bytes 417800 | tf_op jit(solution)/shard_map/ppermute | solution.py:507
  2.3 9.8 %collective-permute-start = (f32[136,256]{1,0:T(8,128)S(1)}, f32[136,256]{1,0:T(8,128)S(1)}, u32[]{:S(2)}, u32[]{:S(2)}) collective-permute-start(f32[136,256]{1,0:T(8,128)S(1)} %shard_map.175.plane_ref), channel_id=1, source_target_pairs={{0,4},{8,12},{4,0},{12,8},{1,5},{9,13},{5,1},{13,9},{2,6},{10,14},... | collective-permute-start | bytes 417800 | tf_op jit(solution)/shard_map/ppermute | solution.py:507
  8.9 0.7 %copy-start.3 = (s32[4,2]{0,1:T(2,128)S(1)}, s32[4,2]{0,1:T(2,128)}, u32[]{:S(2)}) copy-start(s32[4,2]{0,1:T(2,128)} %param.24) | copy-start | bytes 100
  8.9 0.7 %copy-start.5 = (s32[1,4]{1,0:T(1,128)S(1)}, s32[1,4]{1,0:T(1,128)}, u32[]{:S(2)}) copy-start(s32[1,4]{1,0:T(1,128)} %rows_ref.3) | copy-start | bytes 52
  12.1 8.6 %copy-start = (f32[1,2,64,256]{3,2,1,0:T(8,128)S(1)}, f32[1,2,64,256]{3,2,1,0:T(8,128)}, u32[]{:S(2)}) copy-start(f32[1,2,64,256]{3,2,1,0:T(8,128)} %dual_ref.3) | copy-start | bytes 393220
  12.1 8.6 %copy-start.1 = (f32[1,2,64,256]{3,2,1,0:T(8,128)S(1)}, f32[1,2,64,256]{3,2,1,0:T(8,128)}, u32[]{:S(2)}) copy-start(f32[1,2,64,256]{3,2,1,0:T(8,128)} %projected_ref.1) | copy-start | bytes 393220
  14.6 6.2 %collective-permute-start.2 = (f32[192,256]{1,0:T(8,128)S(1)}, f32[192,256]{1,0:T(8,128)S(1)}, u32[]{:S(2)}, u32[]{:S(2)}) collective-permute-start(f32[192,256]{1,0:T(8,128)S(1)} %get-tuple-element.39), channel_id=1, source_target_pairs={{0,4},{8,12},{4,0},{12,8},{1,5},{9,13},{5,1},{13,9},{2,6},{10,14},... | collective-permute-start | bytes 589832 | tf_op jit(solution)/shard_map/ppermute | solution.py:507
  15.9 4.9 %collective-permute-start.3 = (f32[192,256]{1,0:T(8,128)S(1)}, f32[192,256]{1,0:T(8,128)S(1)}, u32[]{:S(2)}, u32[]{:S(2)}) collective-permute-start(f32[192,256]{1,0:T(8,128)S(1)} %get-tuple-element.40), channel_id=1, source_target_pairs={{4,8},{8,4},{5,9},{9,5},{6,10},{10,6},{7,11},{11,7},{20,24},{24,20... | collective-permute-start | bytes 589832 | tf_op jit(solution)/shard_map/ppermute | solution.py:507
  16.6 6.4 %collective-permute-start.11 = (f32[2,72,256]{2,1,0:T(8,128)S(1)}, f32[2,72,256]{2,1,0:T(8,128)S(1)}, u32[]{:S(2)}, u32[]{:S(2)}) collective-permute-start(f32[2,72,256]{2,1,0:T(8,128)S(1)} %get-tuple-element.49), channel_id=1, source_target_pairs={{0,1},{1,0},{2,3},{3,2},{4,5},{5,4},{6,7},{7,6},{8,9},{9,8},{10,11... | collective-permute-start | bytes 442376 | tf_op jit(solution)/shard_map/ppermute | solution.py:510
  16.6 6.4 %collective-permute-start.12 = (f32[2,72,256]{2,1,0:T(8,128)S(1)}, f32[2,72,256]{2,1,0:T(8,128)S(1)}, u32[]{:S(2)}, u32[]{:S(2)}) collective-permute-start(f32[2,72,256]{2,1,0:T(8,128)S(1)} %get-tuple-element.50), channel_id=1, source_target_pairs={{1,2},{2,1},{5,6},{6,5},{9,10},{10,9},{13,14},{14,13},{17,18},{18,... | collective-permute-start | bytes 442376 | tf_op jit(solution)/shard_map/ppermute | solution.py:557
  21.5 7.6 %collective-permute-start.4 = (f32[128,256]{1,0:T(8,128)S(1)}, f32[128,256]{1,0:T(8,128)S(1)}, u32[]{:S(2)}, u32[]{:S(2)}) collective-permute-start(f32[128,256]{1,0:T(8,128)S(1)} %get-tuple-element.42), channel_id=1, source_target_pairs={{0,2},{2,0},{1,3},{3,1},{4,6},{6,4},{5,7},{7,5},{8,10},{10,8},{9,1... | collective-permute-start | bytes 393224 | tf_op jit(solution)/shard_map/ppermute | solution.py:576
  23.5 12.2 %collective-permute-start.13 = (f32[2,2,64,256]{3,2,1,0:T(8,128)S(1)}, f32[2,2,64,256]{3,2,1,0:T(8,128)S(1)}, u32[]{:S(2)}, u32[]{:S(2)}) collective-permute-start(f32[2,2,64,256]{3,2,1,0:T(8,128)S(1)} %shard_map.180.base_ref), channel_id=1, source_target_pairs={{0,4},{4,8},{6,2},{8,12},{10,6},{14,10},{1,5},{5,9},{7,3},{9,13},{... | collective-permute-start | bytes 786440 | tf_op jit(solution)/shard_map/ppermute | solution.py:591
  29.1 14.0 %collective-permute-start.6 = (f32[2,128,256]{2,1,0:T(8,128)S(1)}, f32[2,128,256]{2,1,0:T(8,128)S(1)}, u32[]{:S(2)}, u32[]{:S(2)}) collective-permute-start(f32[2,128,256]{2,1,0:T(8,128)S(1)} %pad_maximum_fusion.here_ref), channel_id=1, source_target_pairs={{4,8},{8,4},{5,9},{9,5},{6,10},{10,6},{7,11},{11,7},{20,24},{24,20... | collective-permute-start | bytes 786440 | tf_op jit(solution)/shard_map/ppermute | solution.py:507
  29.8 13.3 %collective-permute-start.5 = (f32[2,128,256]{2,1,0:T(8,128)S(1)}, f32[2,128,256]{2,1,0:T(8,128)S(1)}, u32[]{:S(2)}, u32[]{:S(2)}) collective-permute-start(f32[2,128,256]{2,1,0:T(8,128)S(1)} %pad_maximum_fusion.here_ref), channel_id=1, source_target_pairs={{0,4},{8,12},{4,0},{12,8},{1,5},{9,13},{5,1},{13,9},{2,6},{10,14},... | collective-permute-start | bytes 786440 | tf_op jit(solution)/shard_map/ppermute | solution.py:507
  36.5 7.7 %collective-permute-start.14 = (f32[2,2,64,256]{3,2,1,0:T(8,128)S(1)}, f32[2,2,64,256]{3,2,1,0:T(8,128)S(1)}, u32[]{:S(2)}, u32[]{:S(2)}) collective-permute-start(f32[2,2,64,256]{3,2,1,0:T(8,128)S(1)} %get-tuple-element.52), channel_id=1, source_target_pairs={{0,1},{1,0},{2,3},{3,2},{4,5},{5,4},{6,7},{7,6},{8,9},{9,8},{10,11... | collective-permute-start | bytes 786440 | tf_op jit(solution)/shard_map/ppermute | solution.py:510
  36.5 4.0 %collective-permute-start.8 = (f32[4,8,256]{2,1,0:T(8,128)S(1)}, f32[4,8,256]{2,1,0:T(8,128)S(1)}, u32[]{:S(2)}, u32[]{:S(2)}) collective-permute-start(f32[4,8,256]{2,1,0:T(8,128)S(1)} %get-tuple-element.43.refs_0_), channel_id=1, source_target_pairs={{0,2},{2,0},{1,3},{3,1},{4,6},{6,4},{5,7},{7,5},{8,10},{10,8},{9,1... | collective-permute-start | bytes 98312 | tf_op jit(solution)/shard_map/ppermute | solution.py:541
  36.6 3.9 %collective-permute-start.7 = (f32[4,8,256]{2,1,0:T(8,128)S(1)}, f32[4,8,256]{2,1,0:T(8,128)S(1)}, u32[]{:S(2)}, u32[]{:S(2)}) collective-permute-start(f32[4,8,256]{2,1,0:T(8,128)S(1)} %get-tuple-element.43.refs_0_), channel_id=1, source_target_pairs={{0,1},{1,0},{2,3},{3,2},{4,5},{5,4},{6,7},{7,6},{8,9},{9,8},{10,11... | collective-permute-start | bytes 98312 | tf_op jit(solution)/shard_map/ppermute | solution.py:510
  40.5 1.2 %collective-permute-start.9 = (f32[4,8,256]{2,1,0:T(8,128)S(1)}, f32[4,8,256]{2,1,0:T(8,128)S(1)}, u32[]{:S(2)}, u32[]{:S(2)}) collective-permute-start(f32[4,8,256]{2,1,0:T(8,128)S(1)} %collective-permute-done.8.refs_2_), channel_id=1, source_target_pairs={{0,1},{1,0},{2,3},{3,2},{4,5},{5,4},{6,7},{7,6},{8,9},{9,8},{10,11... | collective-permute-start | bytes 98312 | tf_op jit(solution)/shard_map/ppermute | solution.py:510
  43.9 6.1 %collective-permute-start.10 = (f32[384,256]{1,0:T(8,128)S(1)}, f32[384,256]{1,0:T(8,128)S(1)}, u32[]{:S(2)}, u32[]{:S(2)}) collective-permute-start(f32[384,256]{1,0:T(8,128)S(1)} %get-tuple-element.48), channel_id=1, source_target_pairs={{0,1},{1,0},{2,3},{3,2},{4,5},{5,4},{6,7},{7,6},{8,9},{9,8},{10,11... | collective-permute-start | bytes 1179656 | tf_op jit(solution)/shard_map/ppermute | solution.py:510
  44.1 5.9 %copy-start.2 = (f32[1,2,64,256]{3,2,1,0:T(8,128)S(1)}, f32[1,2,64,256]{3,2,1,0:T(8,128)}, u32[]{:S(2)}) copy-start(f32[1,2,64,256]{3,2,1,0:T(8,128)} %get-tuple-element.26.object_ref) | copy-start | bytes 393220
  44.2 5.8 %collective-permute-start.15 = (f32[2,64,256]{2,1,0:T(8,128)S(1)}, f32[2,64,256]{2,1,0:T(8,128)S(1)}, u32[]{:S(2)}, u32[]{:S(2)}) collective-permute-start(f32[2,64,256]{2,1,0:T(8,128)S(1)} %fusion), channel_id=1, source_target_pairs={{0,2},{2,0},{1,3},{3,1},{4,6},{6,4},{5,7},{7,5},{8,10},{10,8},{9,1... | collective-permute-start | bytes 393224 | tf_op jit(solution)/shard_map/ppermute | solution.py:608

commit v5 on v4

--- a/solution.py
+++ b/solution.py
@@ -109,12 +109,12 @@
         totals[part, side:, at] += jnp.where(outer & lane_mask[:width], term[:width], 0.0)
 
 
-def prepare_kernel(
-    rows_ref, columns_ref, count_ref, shift_ref, weight_ref, *refs
-):
-    half = (len(refs) - 4) // 2
-    sources, targets, done = refs[:half], refs[half + 3 : -1], refs[-1]
-    probes_ref, density_ref, tables_ref = refs[half : half + 3]
+def prepare_kernel(count_ref, *refs):
+    held = (len(refs) - 13) // 2
+    sources = refs[: held + 4]
+    probes_ref, density_ref, slots_ref, rays_ref = refs[held + 4 : held + 8]
+    targets, done = refs[held + 8 : -1], refs[-1]
+    rows_ref, columns_ref, shift_ref, weight_ref = targets[held:]
     copies = [
         pltpu.make_async_copy(source, target, done.at[number])
         for number, (source, target) in enumerate(zip(sources, targets))
@@ -126,8 +126,13 @@
     slots = probes_ref.shape[0]
     width = density_ref.shape[1] - side
     density_ref[...] = jnp.zeros_like(density_ref)
-    copies[0].wait()
+    for copy in copies[:1] + copies[held:]:
+        copy.wait()
+    places = lax.broadcasted_iota(jnp.int32, slots_ref.shape[1:], 0)
     for slot in range(slots):
+        live = jnp.where(slot < count_ref[0, 0], 1, 0)
+        numbers = jnp.where(places == 0, rows_ref[0, slot], columns_ref[0, slot])
+        slots_ref[slot] = jnp.where(places == 2, live, numbers)
         turn = lax.rem(rows_ref[0, slot], side)
         probe = [
             pltpu.roll(pltpu.roll(probe_ref[part], columns_ref[0, slot], 0), turn, 1)
@@ -137,23 +142,25 @@
             probes_ref[slot, part] = probe[part]
         masks = slot_masks(rows_ref, columns_ref, count_ref, slot, side)
         place(density_ref, 0, probe[0] * probe[0] + probe[1] * probe[1], masks, width)
-    places = lax.broadcasted_iota(jnp.int32, tables_ref.shape[1:], 0)
-    for angle in range(tables_ref.shape[0]):
-        table = jnp.zeros(tables_ref.shape[1:], jnp.float32)
-        for row in range(shift_ref.shape[0]):
-            table = jnp.where(places == 2 * row, shift_ref[row, angle].astype(jnp.float32), table)
-            table = jnp.where(places == 2 * row + 1, weight_ref[row, angle], table)
-        tables_ref[angle] = table
-    for copy in copies[1:]:
+    places = lax.broadcasted_iota(jnp.int32, rays_ref.shape, 0)
+    lanes = lax.broadcasted_iota(jnp.int32, rays_ref.shape, 1)
+    rays = jnp.zeros(rays_ref.shape, jnp.float32)
+    for row in range(shift_ref.shape[0]):
+        for angle in range(shift_ref.shape[1]):
+            shift = shift_ref[row, angle].astype(jnp.float32)
+            here = lanes == angle
+            rays = jnp.where(here & (places == 2 * row), shift, rays)
+            rays = jnp.where(here & (places == 2 * row + 1), weight_ref[row, angle], rays)
+    rays_ref[...] = rays
+    for copy in copies[1:held]:
         copy.wait()
 
 
 def patch_kernel(
-    rows_ref,
-    columns_ref,
-    count_ref,
     probes_ref,
     density_ref,
+    slots_ref,
+    rays_ref,
     plane_ref,
     intensity_ref,
     volume_ref,
@@ -184,10 +191,16 @@
     forward = (forward_high_ref[...], forward_low_ref[...])
     inverse = (inverse_high_ref[...], inverse_low_ref[...])
     waves, masks = [], []
+    lanes = lax.broadcasted_iota(jnp.int32, (side, side), 1)
+    sublanes = lax.broadcasted_iota(jnp.int32, (side, side), 0)
     for slot in range(slots):
         probe = probes_ref[slot]
-        masks.append(slot_masks(rows_ref, columns_ref, count_ref, slot, side))
-        near_lanes, near_columns, _ = masks[slot]
+        row, column, live = (
+            jnp.broadcast_to(slots_ref[slot, number : number + 1], (side, side))
+            for number in range(3)
+        )
+        near_lanes, near_columns = lanes >= row, sublanes >= column
+        masks.append((near_lanes, near_columns, live > 0))
         window = []
         for part in range(2):
             near = jnp.where(near_lanes, wide[part, :side, :side], wide[part, :side, side:])
@@ -253,9 +266,12 @@
         for low, row_ref in ((jnp.logical_not(first_tile), row_a_ref), (first_tile, row_b_ref)):
             row_ref[channel, :width] = jnp.where(low, rows[0][0], rows[1][0])
             row_ref[channel, width : width + 2] = jnp.where(low, rows[0][1], rows[1][1])
-
-
-def fold_kernel(own_ref, rim_a_ref, rim_b_ref, projected_ref, dual_ref, object_ref, residual_ref):
+            row_ref[channel, width + SUBLANES :] = rays_ref[...]
+
+
+def fold_kernel(
+    own_ref, rim_a_ref, rim_b_ref, projected_ref, dual_ref, rays_ref, row_ref, object_ref, residual_ref
+):
     width = own_ref.shape[1]
     sums = [
         own_ref[part]
@@ -269,6 +285,8 @@
         updated = (sums[part] + penalty * (target - dual)) / (sums[2] + penalty)
         object_ref[0, part] = updated
         residual_ref[part * width : (part + 1) * width] = target - updated - dual
+    residual_ref[2 * width : 2 * width + SUBLANES] = rays_ref[...]
+    residual_ref[2 * width + SUBLANES :] = row_ref[0, width + SUBLANES :]
 
 
 def variation_kernel(
@@ -365,9 +383,9 @@
 
 
 def operator_kernel(*refs):
-    rays, (high_ref, low_ref) = refs[:-2], refs[-2:]
+    packed_refs, (high_ref, low_ref) = refs[:-2], refs[-2:]
     tiles = lax.axis_size("tile")
-    columns = len(rays) // tiles
+    columns = len(packed_refs)
     rows_out, reach = high_ref.shape[1:]
     width = reach // 3
     count = rows_out // (2 * width) - 1
@@ -377,14 +395,20 @@
         lanes = lax.broadcasted_iota(jnp.int32, shape, 1)
         sublanes = lax.broadcasted_iota(jnp.int32, shape, 0)
         offset = (lanes - sublanes).astype(jnp.float32) - first
-        shift = step * table[2 * row : 2 * row + 1, : shape[1]]
-        fraction = table[2 * row + 1 : 2 * row + 2, : shape[1]]
+        shift = step * table[2 * row : 2 * row + 1]
+        fraction = table[2 * row + 1 : 2 * row + 2]
         return jnp.where(offset == shift, 1.0 - fraction, 0.0) + jnp.where(
             offset == shift + step, fraction, 0.0
         )
 
     def angle_of(turn, flip):
         return lax.rem(me + turn, columns) * tiles + (tile if flip == 0 else 1 - tile)
+
+    def table_of(turn, flip, angle):
+        at = 2 * width + SUBLANES * flip
+        tile_of = packed_refs[turn][at : at + SUBLANES]
+        lanes = lax.broadcasted_iota(jnp.int32, tile_of.shape, 1)
+        return jnp.sum(jnp.where(lanes == angle, tile_of, 0.0), axis=1, keepdims=True)
 
     cells = lax.broadcasted_iota(jnp.int32, (width, 2 * width), 1)
     forward = []
@@ -399,12 +423,12 @@
             for row in range(count):
                 parts = []
                 for own in range(tiles):
-                    table = rays[turn * tiles + flip][angle_of(0, own)]
+                    table = table_of(turn, flip, angle_of(0, own))
                     part = taps((width, 2 * width), base_at.astype(jnp.float32), table, row, 1.0)
                     parts.append(jnp.where(inside, part, 0.0))
                 forward.append(jnp.concatenate(parts, axis=0))
                 for source in range(columns):
-                    table = rays[turn * tiles + flip][angle_of(source, 0)]
+                    table = table_of(turn, flip, angle_of(source, 0))
                     first = (width - base_at).astype(jnp.float32)
                     backward[source].append(taps((2 * width, reach), first, table, row, -1.0))
     left = split(jnp.concatenate(forward, axis=1))
@@ -413,7 +437,7 @@
         blocks = [both]
         for flip in range(tiles):
             for row in range(count):
-                table = rays[flip][angle_of(source, 0)]
+                table = table_of(0, flip, angle_of(source, 0))
                 blocks.append(taps((width, reach), float(width), table, row, -1.0))
         high_ref[source], low_ref[source] = split(jnp.concatenate(blocks, axis=0))
 
@@ -444,31 +468,43 @@
             send_ref[target : target + width] = total[at + count * width : at + (count + 1) * width]
 
 
-def finish_kernel(
-    keep_ref, own_ref, received_ref, base_ref, spread_ref, object_ref, dual_ref, dual_out_ref, volume_ref, projected_ref
-):
-    width = keep_ref.shape[1]
-    count = own_ref.shape[1]
+def volume_kernel(own_ref, received_ref, base_ref, volume_ref):
+    count, width = own_ref.shape[1:3]
     for channel in range(2):
-        received = received_ref[channel * width : (channel + 1) * width]
-        projection = spread_ref[channel] - step_size * (keep_ref[channel] + received)
-        projected_ref[0, channel] = projection
-        dual_out_ref[0, channel] = dual_ref[0, channel] + object_ref[0, channel] - projection
         for row in range(count):
             at = (2 + channel * count + row) * width
             descent = own_ref[channel, row] + received_ref[at : at + width]
             volume_ref[channel, row] = base_ref[channel, row] - step_size * descent
 
 
-def call(kernel, shapes, operands, scratch, flops, scalars=0, staged=(), copies=0, kind=jnp.float32):
+def finish_kernel(*refs):
+    keep_ref, received_ref, object_ref, dual_ref = refs[:4]
+    spreads, (dual_out_ref, projected_ref) = refs[4:-2], refs[-2:]
+    width = keep_ref.shape[1]
+    for channel in range(2):
+        received = received_ref[channel * width : (channel + 1) * width]
+        projection = -step_size * (keep_ref[channel] + received)
+        for spread_ref in spreads:
+            projection = projection + spread_ref[channel]
+        projected_ref[0, channel] = projection
+        dual_out_ref[0, channel] = dual_ref[0, channel] + object_ref[0, channel] - projection
+
+
+def call(
+    kernel, shapes, operands, scratch, flops, scalars=0, staged=(), numbers=(), copies=0, kind=jnp.float32, kinds={}
+):
     held = sum(operand.nbytes for operand in operands[scalars:] + staged)
     held += 4 * sum(math.prod(shape) for shape in shapes)
     own = 4 * sum(math.prod(shape) for shape in scratch)
-    outputs = [jax.ShapeDtypeStruct(shape, kind) for shape in shapes]
+    outputs = [
+        jax.ShapeDtypeStruct(shape, kinds.get(number, kind)) for number, shape in enumerate(shapes)
+    ]
     scratch_shapes = [pltpu.VMEM(shape, jnp.float32) for shape in scratch]
     if staged and not copies:
         outputs += [jax.ShapeDtypeStruct(array.shape, array.dtype) for array in staged]
-        copies = len(staged)
+        copies = len(staged) + len(numbers)
+        scratch_shapes += [pltpu.SMEM(array.shape, array.dtype) for array in numbers]
+    staged += numbers
     if copies:
         scratch_shapes.append(pltpu.SemaphoreType.DMA((copies,)))
     in_specs = [SMEM] * scalars + [VMEM] * (len(operands) - scalars) + [HBM] * len(staged)
@@ -522,33 +558,34 @@
     plane_a = exchange(plane, 0)
     plane_b = exchange(plane, 1)
     tables = [jnp.asarray(table) for table in dft_tables(probe_wave.shape[1])]
-    scalars = (slot_first_rows, slot_first_columns, patch_counts)
     slots = slot_first_rows.shape[1]
     side = probe_wave.shape[1]
-    probes, density, rays, _, *held = call(
+    probes, density, slot_numbers, rays, _, *held = call(
         prepare_kernel,
-        [(slots, 2, side, side), (1, 3 * width, length), (columns * tiles, SUBLANES, length)],
-        (*scalars, shift_table.T, tap_weight.T),
+        [
+            (slots, 2, side, side),
+            (1, 3 * width, length),
+            (slots, SUBLANES, side),
+            (SUBLANES, length),
+        ],
+        (patch_counts,),
         [],
         10**7,
-        5,
+        1,
         (probe_wave, intensities, volume, *tables),
+        (slot_first_rows, slot_first_columns, shift_table.T, tap_weight.T),
+        kinds={2: jnp.int32},
     )
     volume_here = held[1]
     turns = [[(i, (i - turn) % columns) for i in range(columns)] for turn in range(columns)]
-    by_row = [rays]
-    for turn in range(1, columns):
-        by_row.append(lax.ppermute(rays, "angle", turns[turn]))
-    by_row = [block for table in by_row for block in (table, across(table))]
     own, rim_a, rim_b, row_a, row_b = call(
         patch_kernel,
         [(3, width, length)]
         + [(3 * width, length)] * 2
-        + [(2, width + SUBLANES, length)] * 2,
-        (*scalars, probes, density, plane, *held, plane_a, plane_b),
+        + [(2, width + 2 * SUBLANES, length)] * 2,
+        (probes, density, slot_numbers, rays, plane, *held, plane_a, plane_b),
         [(2, 3 * width, length), (3, 3 * width, length)],
         10**9,
-        3,
     )
     rim_a = exchange(rim_a, 0)
     rim_b = exchange(rim_b, 1)
@@ -556,18 +593,10 @@
     bridge += [(target, source) for source, target in bridge]
     row_b = lax.ppermute(row_b, ("angle", "tile"), bridge)
     row_a = across(row_a)
-    high, low = call(
-        operator_kernel,
-        [(columns, (2 + 2 * count) * width, 3 * width)] * 2,
-        tuple(by_row),
-        [],
-        10**8,
-        kind=jnp.bfloat16,
-    )
     new_transmission, residual = call(
         fold_kernel,
-        [transmission.shape, (2 * width, length)],
-        (own, rim_a, rim_b, projected, scaled_dual),
+        [transmission.shape, (2 * width + 2 * SUBLANES, length)],
+        (own, rim_a, rim_b, projected, scaled_dual, rays, row_a),
         [],
         10**6,
     )
@@ -592,6 +621,14 @@
     here = jnp.stack(by_column)
     side_a = exchange(here, 0)
     side_b = exchange(here, 1)
+    high, low = call(
+        operator_kernel,
+        [(columns, (2 + 2 * count) * width, 3 * width)] * 2,
+        tuple(by_column),
+        [],
+        10**8,
+        kind=jnp.bfloat16,
+    )
     block = (columns, 2, width, length)
     keep, send = call(
         spread_kernel,
@@ -602,10 +639,10 @@
         2,
     )
     received = across(send)
-    spread = keep[0] + received[0]
+    spreads = [keep[0], received[0]]
     for turn in range(1, columns):
         route = [(i, (i + turn) % columns) for i in range(columns)]
-        spread = spread + lax.ppermute(keep[turn] + received[turn], "angle", route)
+        spreads.append(lax.ppermute(keep[turn] + received[turn], "angle", route))
     keep, own, send = call(
         apply_kernel,
         [(2, width, length), volume.shape, ((2 + 2 * count) * width, length)],
@@ -614,10 +651,11 @@
         10**9,
     )
     received = across(send)
-    new_dual, new_volume, new_projected = call(
+    (new_volume,) = call(volume_kernel, [volume.shape], (own, received, base), [], 10**6)
+    new_dual, new_projected = call(
         finish_kernel,
-        [transmission.shape, volume.shape, transmission.shape],
-        (keep, own, received, base, spread, new_transmission, scaled_dual),
+        [transmission.shape] * 2,
+        (keep, received, new_transmission, scaled_dual, *spreads),
         [],
         10**6,
     )

time: 51.2 us -> 48 us (0.938)
  waiting for transfers between devices: 16.9 us -> 14.5 us
  local copies, waits for them, and re-layouts: 0.68 us -> 0.02 us
    ppermute x2 -> x1, waiting for transfers between devices: 9.14 us -> 3.42 us  [body(): spreads.append(lax.ppermute(keep[turn] + received[turn], 'angle', route))]
    ppermute x6, waiting for transfers between devices: 3.47 us -> 5.48 us  [exchange(): return lax.ppermute(block, 'scan', both[number])]
    ppermute x5 -> x3, starting transfers between devices: 0.8 us -> 1.64 us  [across(): return lax.ppermute(block, 'tile', swap)]
    ppermute x5 -> x3, waiting for transfers between devices: 1.21 us -> 1.93 us  [across(): return lax.ppermute(block, 'tile', swap)]
    unnamed x14 -> x10, local copies, waits for them, and re-layouts: 0.68 us -> 0.02 us
    ppermute x1, waiting for transfers between devices: 3.05 us -> 3.63 us  [body(): beside = lax.ppermute(base, ('scan', 'angle'), route)]
    pallas_call x9 -> x10, Pallas kernels: 10.9 us -> 10.5 us  [call(): pl.pallas_call(kernel, out_shape=outputs, in_specs=in_specs, out_specs=[V...]
  transfers between devices with their start and end apart: 16 -> 13, of which waited for: 5 -> 7; matrix products, arithmetic and copies ran while one was open for 0% -> 0% of each run, Pallas kernels for 13% -> 14%
where the time goes in v5:
time: 48 us; the launch traced here: 47.7 us
  starting transfers between devices  21.2 us (44%)
  waiting for transfers between devices  14.5 us (30%)
  Pallas kernels  10.5 us (22%)
  between operations  1.43 us (3%)
    ppermute x6, starting transfers between devices, exchange(): return lax.ppermute(block, 'scan', both[number])  11.8 us
    pallas_call x10, Pallas kernels, call(): pl.pallas_call(kernel, out_shape=outputs, in_specs=in_specs, out_specs=[V...  10.5 us
    ppermute x1, starting transfers between devices, body(): beside = lax.ppermute(base, ('scan', 'angle'), route)  5.56 us
    ppermute x6, waiting for transfers between devices, exchange(): return lax.ppermute(block, 'scan', both[number])  5.48 us
    ppermute x1, waiting for transfers between devices, body(): beside = lax.ppermute(base, ('scan', 'angle'), route)  3.63 us
    ppermute x1, waiting for transfers between devices, body(): spreads.append(lax.ppermute(keep[turn] + received[turn], 'angle', route))  3.42 us
    ppermute x3, waiting for transfers between devices, across(): return lax.ppermute(block, 'tile', swap)  1.93 us
    ppermute x3, starting transfers between devices, across(): return lax.ppermute(block, 'tile', swap)  1.64 us
  transfers between devices with their start and end apart: 13, of which 7 were waited for; matrix products, arithmetic and copies ran while one was open for 0% of the time, Pallas kernels for 14%

profile of v5, /device:TPU:0, one launch (start us, length us, event | category | flops | bytes accessed | tf_op | source)
XLA Modules:
  0.0 47.7 jit_solution(3709680797936001894)
XLA Ops:
  0.6 1.0 %shard_map.175.plane_ref = f32[136,256]{1,0:T(8,128)S(1)} custom-call(f32[1,2,64,256]{3,2,1,0:T(8,128)} %plane_ref.1, f32[2,2,64,256]{3,2,1,0:T(8,128)} %volume_ref.1), custom_call_target="tpu_custom_call" | custom-call | flops 100000 | bytes 532480 | tf_op jit(solution)/shard_map/pallas_call | solution.py:511
  1.6 3.1 %collective-permute-start = (f32[136,256]{1,0:T(8,128)S(1)}, f32[136,256]{1,0:T(8,128)S(1)}, u32[]{:S(2)}, u32[]{:S(2)}) collective-permute-start(f32[136,256]{1,0:T(8,128)S(1)} %shard_map.175.plane_ref), channel_id=1, source_target_pairs={{0,4},{8,12},{4,0},{12,8},{1,5},{9,13},{5,1},{13,9},{2,6},{10,14},... | collective-permute-start | bytes 417800 | tf_op jit(solution)/shard_map/ppermute | solution.py:543
  4.7 0.7 %collective-permute-start.1 = (f32[136,256]{1,0:T(8,128)S(1)}, f32[136,256]{1,0:T(8,128)S(1)}, u32[]{:S(2)}, u32[]{:S(2)}) collective-permute-start(f32[136,256]{1,0:T(8,128)S(1)} %shard_map.175.plane_ref), channel_id=1, source_target_pairs={{4,8},{8,4},{5,9},{9,5},{6,10},{10,6},{7,11},{11,7},{20,24},{24,20... | collective-permute-start | bytes 417800 | tf_op jit(solution)/shard_map/ppermute | solution.py:543
  6.0 2.0 %shard_map.174 = (f32[4,2,128,128]{3,2,1,0:T(8,128)S(1)}, f32[1,192,256]{2,1,0:T(8,128)S(1)}, s32[4,8,128]{2,1,0:T(8,128)S(1)}, f32[8,256]{1,0:T(8,128)S(1)}, f3...) custom-call(s32[1,1]{1,0:T(1,128)S(6)} %copy.19.count_ref, ...), custom_call_target="tpu_custom_call" | custom-call | flops 10000000 | bytes 1794048 | tf_op jit(solution)/shard_map/pallas_call | solution.py:511
  8.0 0.4 collective-permute-done.plane_a_ref
  8.4 1.9 %shard_map.176 = (f32[3,64,256]{2,1,0:T(8,128)S(1)}, f32[192,256]{1,0:T(8,128)S(1)}, f32[192,256]{1,0:T(8,128)S(1)}, f32[2,80,256]{2,1,0:T(8,128)S(1)}, f32[2,80,256]{2,1,0:T(8,128)S(1)}) custom-call(f32[4,2,128,128]{3,2,1,0:T(8,128)S(1)} %get-tuple-element.30.probes_ref, f32[1,192,256]{2,1,0:T(8,128)S(1)} %get-tuple-element.31.density_ref, ...), custom_call_target="tpu_custom_call" | custom-call | flops 1000000000 | bytes 2998272 | tf_op jit(solution)/shard_map/pallas_call | solution.py:511
  10.3 4.8 %collective-permute-start.2 = (f32[192,256]{1,0:T(8,128)S(1)}, f32[192,256]{1,0:T(8,128)S(1)}, u32[]{:S(2)}, u32[]{:S(2)}) collective-permute-start(f32[192,256]{1,0:T(8,128)S(1)} %get-tuple-element.41), channel_id=1, source_target_pairs={{0,4},{8,12},{4,0},{12,8},{1,5},{9,13},{5,1},{13,9},{2,6},{10,14},... | collective-permute-start | bytes 589832 | tf_op jit(solution)/shard_map/ppermute | solution.py:543
  15.1 0.7 %collective-permute-start.3 = (f32[192,256]{1,0:T(8,128)S(1)}, f32[192,256]{1,0:T(8,128)S(1)}, u32[]{:S(2)}, u32[]{:S(2)}) collective-permute-start(f32[192,256]{1,0:T(8,128)S(1)} %get-tuple-element.42), channel_id=1, source_target_pairs={{4,8},{8,4},{5,9},{9,5},{6,10},{10,6},{7,11},{11,7},{20,24},{24,20... | collective-permute-start | bytes 589832 | tf_op jit(solution)/shard_map/ppermute | solution.py:543
  15.8 0.1 collective-permute-start.4
  15.9 0.7 %collective-permute-start.9 = (f32[2,80,256]{2,1,0:T(8,128)S(1)}, f32[2,80,256]{2,1,0:T(8,128)S(1)}, u32[]{:S(2)}, u32[]{:S(2)}) collective-permute-start(f32[2,80,256]{2,1,0:T(8,128)S(1)} %get-tuple-element.50), channel_id=1, source_target_pairs={{1,2},{2,1},{5,6},{6,5},{9,10},{10,9},{13,14},{14,13},{17,18},{18,... | collective-permute-start | bytes 491528 | tf_op jit(solution)/shard_map/ppermute | solution.py:594
  16.6 0.7 %collective-permute-done.4.row_ref.row_a_ref = f32[2,80,256]{2,1,0:T(8,128)S(1)} collective-permute-done((f32[2,80,256]{2,1,0:T(8,128)S(1)}, f32[2,80,256]{2,1,0:T(8,128)S(1)}, u32[]{:S(2)}, u32[]{:S(2)}) %collective-permute-start.4) | collective-permute-done | bytes 163872 | tf_op jit(solution)/shard_map/ppermute | solution.py:546
  17.3 1.9 %collective-permute-done.2.rim_a_ref = f32[192,256]{1,0:T(8,128)S(1)} collective-permute-done((f32[192,256]{1,0:T(8,128)S(1)}, f32[192,256]{1,0:T(8,128)S(1)}, u32[]{:S(2)}, u32[]{:S(2)}) %collective-permute-start.2) | collective-permute-done | bytes 196640 | tf_op jit(solution)/shard_map/ppermute | solution.py:543
  19.2 0.7 %shard_map.177 = (f32[1,2,64,256]{3,2,1,0:T(8,128)}, f32[144,256]{1,0:T(8,128)S(1)}) custom-call(f32[3,64,256]{2,1,0:T(8,128)S(1)} %get-tuple-element.40.own_ref, f32[192,256]{1,0:T(8,128)S(1)} %collective-permute-done.2.rim_a_ref, f32[192,256]{1,0:T(8,128)S(1)} %collective-permute-done.3.rim_b_ref, f32[1,2,64,256]{3,2,1,0:T(8,128)S(1)} %copy-done.2, ...), custom_call_target="tpu_custom_call" | custom-call | flops 1000000 | bytes 1302528 | tf_op jit(solution)/shard_map/pallas_call | solution.py:511
  19.9 1.5 %collective-permute-start.5 = (f32[144,256]{1,0:T(8,128)S(1)}, f32[144,256]{1,0:T(8,128)S(1)}, u32[]{:S(2)}, u32[]{:S(2)}) collective-permute-start(f32[144,256]{1,0:T(8,128)S(1)} %get-tuple-element.45.refs_0_), channel_id=1, source_target_pairs={{0,2},{2,0},{1,3},{3,1},{4,6},{6,4},{5,7},{7,5},{8,10},{10,8},{9,1... | collective-permute-start | bytes 442376 | tf_op jit(solution)/shard_map/ppermute | solution.py:605
  21.4 0.5 %shard_map.180.base_ref = f32[2,2,64,256]{3,2,1,0:T(8,128)S(1)} custom-call(f32[2,2,64,256]{3,2,1,0:T(8,128)S(1)} %get-tuple-element.35.volume_ref, f32[136,256]{1,0:T(8,128)S(1)} %collective-permute-done.plane_a_ref, f32[136,256]{1,0:T(8,128)S(1)} %collective-permute-done.1.plane_b_ref, f32[2,80,256]{2,1,0:T(8,128)S(1)} %collective-permute-done.4.row_ref.row_a_ref, ...), custom_call_target="tpu_custom_call" | custom-call | flops 10000000 | bytes 1130496 | tf_op jit(solution)/shard_map/pallas_call | solution.py:511
  21.9 5.6 %collective-permute-start.10 = (f32[2,2,64,256]{3,2,1,0:T(8,128)S(1)}, f32[2,2,64,256]{3,2,1,0:T(8,128)S(1)}, u32[]{:S(2)}, u32[]{:S(2)}) collective-permute-start(f32[2,2,64,256]{3,2,1,0:T(8,128)S(1)} %shard_map.180.base_ref), channel_id=1, source_target_pairs={{0,4},{4,8},{6,2},{8,12},{10,6},{14,10},{1,5},{5,9},{7,3},{9,13},{... | collective-permute-start | bytes 786440 | tf_op jit(solution)/shard_map/ppermute | solution.py:620
  27.5 0.0 copy-start.3
  27.5 0.0 copy-start.4
  27.5 1.9 %collective-permute-start.6 = (f32[2,144,256]{2,1,0:T(8,128)S(1)}, f32[2,144,256]{2,1,0:T(8,128)S(1)}, u32[]{:S(2)}, u32[]{:S(2)}) collective-permute-start(f32[2,144,256]{2,1,0:T(8,128)S(1)} %pad_maximum_fusion.here_ref), channel_id=1, source_target_pairs={{0,4},{8,12},{4,0},{12,8},{1,5},{9,13},{5,1},{13,9},{2,6},{10,14},... | collective-permute-start | bytes 884744 | tf_op jit(solution)/shard_map/ppermute | solution.py:543
  29.4 0.7 %collective-permute-start.7 = (f32[2,144,256]{2,1,0:T(8,128)S(1)}, f32[2,144,256]{2,1,0:T(8,128)S(1)}, u32[]{:S(2)}, u32[]{:S(2)}) collective-permute-start(f32[2,144,256]{2,1,0:T(8,128)S(1)} %pad_maximum_fusion.here_ref), channel_id=1, source_target_pairs={{4,8},{8,4},{5,9},{9,5},{6,10},{10,6},{7,11},{11,7},{20,24},{24,20... | collective-permute-start | bytes 884744 | tf_op jit(solution)/shard_map/ppermute | solution.py:543
  30.1 3.6 %collective-permute-done.10.beside_ref = f32[2,2,64,256]{3,2,1,0:T(8,128)S(1)} collective-permute-done((f32[2,2,64,256]{3,2,1,0:T(8,128)S(1)}, f32[2,2,64,256]{3,2,1,0:T(8,128)S(1)}, u32[]{:S(2)}, u32[]{:S(2)}) %collective-permute-start.10) | collective-permute-done | bytes 262176 | tf_op jit(solution)/shard_map/ppermute | solution.py:620
  33.7 0.8 %shard_map.181 = (f32[2,2,64,256]{3,2,1,0:T(8,128)S(1)}, f32[2,2,64,256]{3,2,1,0:T(8,128)S(1)}) custom-call(s32[2,4]{1,0:T(2,128)S(1)} %bitcast.13, f32[2,4]{1,0:T(2,128)S(1)} %bitcast.15, f32[2,2,64,256]{3,2,1,0:T(8,128)S(1)} %shard_map.180.base_ref, f32[2,2,64,256]{3,2,1,0:T(8,128)S(1)} %collective-permute-done.10.beside_ref), custom_call_target="tpu_custom_call" | custom-call | flops 10000000 | bytes 1048576 | tf_op jit(solution)/shard_map/pallas_call | solution.py:511
  34.5 1.0 %collective-permute-start.11 = (f32[2,2,64,256]{3,2,1,0:T(8,128)S(1)}, f32[2,2,64,256]{3,2,1,0:T(8,128)S(1)}, u32[]{:S(2)}, u32[]{:S(2)}) collective-permute-start(f32[2,2,64,256]{3,2,1,0:T(8,128)S(1)} %get-tuple-element.52), channel_id=1, source_target_pairs={{0,1},{1,0},{2,3},{3,2},{4,5},{5,4},{6,7},{7,6},{8,9},{9,8},{10,11... | collective-permute-start | bytes 786440 | tf_op jit(solution)/shard_map/ppermute | solution.py:546
  35.5 1.4 %shard_map.178 = (bf16[2,384,192]{2,1,0:T(8,128)(2,1)S(1)}, bf16[2,384,192]{2,1,0:T(8,128)(2,1)S(1)}) custom-call(f32[144,256]{1,0:T(8,128)S(1)} %get-tuple-element.45.refs_0_, f32[144,256]{1,0:T(8,128)S(1)} %collective-permute-done.5.refs_1_), custom_call_target="tpu_custom_call" | custom-call | flops 100000000 | bytes 1474560 | tf_op jit(solution)/shard_map/pallas_call | solution.py:511
  36.8 3.2 %collective-permute-done.6.side_a_ref = f32[2,144,256]{2,1,0:T(8,128)S(1)} collective-permute-done((f32[2,144,256]{2,1,0:T(8,128)S(1)}, f32[2,144,256]{2,1,0:T(8,128)S(1)}, u32[]{:S(2)}, u32[]{:S(2)}) %collective-permute-start.6) | collective-permute-done | bytes 294944 | tf_op jit(solution)/shard_map/ppermute | solution.py:543
  40.1 0.8 %shard_map.179 = (f32[2,64,256]{2,1,0:T(8,128)S(1)}, f32[2,2,64,256]{3,2,1,0:T(8,128)S(1)}, f32[384,256]{1,0:T(8,128)S(1)}) custom-call(f32[2,144,256]{2,1,0:T(8,128)S(1)} %pad_maximum_fusion.here_ref, f32[2,144,256]{2,1,0:T(8,128)S(1)} %collective-permute-done.6.side_a_ref, f32[2,144,256]{2,1,0:T(8,128)S(1)} %collective-permute-done.7.side_b_ref, ...), custom_call_target="tpu_custom_call" | custom-call | flops 1000000000 | bytes 2260992 | tf_op jit(solution)/shard_map/pallas_call | solution.py:511
  40.9 0.6 %collective-permute-start.8 = (f32[384,256]{1,0:T(8,128)S(1)}, f32[384,256]{1,0:T(8,128)S(1)}, u32[]{:S(2)}, u32[]{:S(2)}) collective-permute-start(f32[384,256]{1,0:T(8,128)S(1)} %get-tuple-element.49), channel_id=1, source_target_pairs={{0,1},{1,0},{2,3},{3,2},{4,5},{5,4},{6,7},{7,6},{8,9},{9,8},{10,11... | collective-permute-start | bytes 1179656 | tf_op jit(solution)/shard_map/ppermute | solution.py:546
  41.5 0.1 collective-permute-start.12
  41.6 1.2 %collective-permute-done.8.refs_1_.received_ref = f32[384,256]{1,0:T(8,128)S(1)} collective-permute-done((f32[384,256]{1,0:T(8,128)S(1)}, f32[384,256]{1,0:T(8,128)S(1)}, u32[]{:S(2)}, u32[]{:S(2)}) %collective-permute-start.8) | collective-permute-done | bytes 393248 | tf_op jit(solution)/shard_map/ppermute | solution.py:546
  42.8 0.8 %shard_map.183 = f32[2,2,64,256]{3,2,1,0:T(8,128)} custom-call(f32[2,2,64,256]{3,2,1,0:T(8,128)S(1)} %get-tuple-element.54.own_ref, f32[384,256]{1,0:T(8,128)S(1)} %collective-permute-done.8.refs_1_.received_ref, f32[2,2,64,256]{3,2,1,0:T(8,128)S(1)} %shard_map.180.base_ref), custom_call_target="tpu_custom_call" | custom-call | flops 1000000 | bytes 1179648 | tf_op jit(solution)/shard_map/pallas_call | solution.py:511
  43.6 3.4 %collective-permute-done.12.refs_6_ = f32[2,64,256]{2,1,0:T(8,128)S(1)} collective-permute-done((f32[2,64,256]{2,1,0:T(8,128)S(1)}, f32[2,64,256]{2,1,0:T(8,128)S(1)}, u32[]{:S(2)}, u32[]{:S(2)}) %collective-permute-start.12) | collective-permute-done | bytes 131104 | tf_op jit(solution)/shard_map/ppermute | solution.py:645
  47.0 0.7 %shard_map.182 = (f32[1,2,64,256]{3,2,1,0:T(8,128)}, f32[1,2,64,256]{3,2,1,0:T(8,128)}) custom-call(f32[2,64,256]{2,1,0:T(8,128)S(1)} %get-tuple-element.48.refs_0_, f32[384,256]{1,0:T(8,128)S(1)} %collective-permute-done.8.refs_1_.received_ref, f32[1,2,64,256]{3,2,1,0:T(8,128)S(1)} %copy-done.1, f32[1,2,64,256]{3,2,1,0:T(8,128)S(1)} %copy-done, ...), custom_call_target="tpu_custom_call" | custom-call | flops 1000000 | bytes 1441792 | tf_op jit(solution)/shard_map/pallas_call | solution.py:511
  (16 shorter events, 0.1 us)
Async XLA Ops:
  1.6 6.8 %collective-permute-start = (f32[136,256]{1,0:T(8,128)S(1)}, f32[136,256]{1,0:T(8,128)S(1)}, u32[]{:S(2)}, u32[]{:S(2)}) collective-permute-start(f32[136,256]{1,0:T(8,128)S(1)} %shard_map.175.plane_ref), channel_id=1, source_target_pairs={{0,4},{8,12},{4,0},{12,8},{1,5},{9,13},{5,1},{13,9},{2,6},{10,14},... | collective-permute-start | bytes 417800 | tf_op jit(solution)/shard_map/ppermute | solution.py:543
  4.7 3.7 %collective-permute-start.1 = (f32[136,256]{1,0:T(8,128)S(1)}, f32[136,256]{1,0:T(8,128)S(1)}, u32[]{:S(2)}, u32[]{:S(2)}) collective-permute-start(f32[136,256]{1,0:T(8,128)S(1)} %shard_map.175.plane_ref), channel_id=1, source_target_pairs={{4,8},{8,4},{5,9},{9,5},{6,10},{10,6},{7,11},{11,7},{20,24},{24,20... | collective-permute-start | bytes 417800 | tf_op jit(solution)/shard_map/ppermute | solution.py:543
  8.4 10.8 %copy-start = (f32[1,2,64,256]{3,2,1,0:T(8,128)S(1)}, f32[1,2,64,256]{3,2,1,0:T(8,128)}, u32[]{:S(2)}) copy-start(f32[1,2,64,256]{3,2,1,0:T(8,128)} %refs_3_.2) | copy-start | bytes 393220
  8.4 10.8 %copy-start.2 = (f32[1,2,64,256]{3,2,1,0:T(8,128)S(1)}, f32[1,2,64,256]{3,2,1,0:T(8,128)}, u32[]{:S(2)}) copy-start(f32[1,2,64,256]{3,2,1,0:T(8,128)} %projected_ref.1) | copy-start | bytes 393220
  10.3 8.9 %collective-permute-start.2 = (f32[192,256]{1,0:T(8,128)S(1)}, f32[192,256]{1,0:T(8,128)S(1)}, u32[]{:S(2)}, u32[]{:S(2)}) collective-permute-start(f32[192,256]{1,0:T(8,128)S(1)} %get-tuple-element.41), channel_id=1, source_target_pairs={{0,4},{8,12},{4,0},{12,8},{1,5},{9,13},{5,1},{13,9},{2,6},{10,14},... | collective-permute-start | bytes 589832 | tf_op jit(solution)/shard_map/ppermute | solution.py:543
  15.1 4.0 %collective-permute-start.3 = (f32[192,256]{1,0:T(8,128)S(1)}, f32[192,256]{1,0:T(8,128)S(1)}, u32[]{:S(2)}, u32[]{:S(2)}) collective-permute-start(f32[192,256]{1,0:T(8,128)S(1)} %get-tuple-element.42), channel_id=1, source_target_pairs={{4,8},{8,4},{5,9},{9,5},{6,10},{10,6},{7,11},{11,7},{20,24},{24,20... | collective-permute-start | bytes 589832 | tf_op jit(solution)/shard_map/ppermute | solution.py:543
  15.8 1.5 %collective-permute-start.4 = (f32[2,80,256]{2,1,0:T(8,128)S(1)}, f32[2,80,256]{2,1,0:T(8,128)S(1)}, u32[]{:S(2)}, u32[]{:S(2)}) collective-permute-start(f32[2,80,256]{2,1,0:T(8,128)S(1)} %get-tuple-element.43), channel_id=1, source_target_pairs={{0,1},{1,0},{2,3},{3,2},{4,5},{5,4},{6,7},{7,6},{8,9},{9,8},{10,11... | collective-permute-start | bytes 491528 | tf_op jit(solution)/shard_map/ppermute | solution.py:546
  15.9 5.5 %collective-permute-start.9 = (f32[2,80,256]{2,1,0:T(8,128)S(1)}, f32[2,80,256]{2,1,0:T(8,128)S(1)}, u32[]{:S(2)}, u32[]{:S(2)}) collective-permute-start(f32[2,80,256]{2,1,0:T(8,128)S(1)} %get-tuple-element.50), channel_id=1, source_target_pairs={{1,2},{2,1},{5,6},{6,5},{9,10},{10,9},{13,14},{14,13},{17,18},{18,... | collective-permute-start | bytes 491528 | tf_op jit(solution)/shard_map/ppermute | solution.py:594
  19.9 7.6 %collective-permute-start.5 = (f32[144,256]{1,0:T(8,128)S(1)}, f32[144,256]{1,0:T(8,128)S(1)}, u32[]{:S(2)}, u32[]{:S(2)}) collective-permute-start(f32[144,256]{1,0:T(8,128)S(1)} %get-tuple-element.45.refs_0_), channel_id=1, source_target_pairs={{0,2},{2,0},{1,3},{3,1},{4,6},{6,4},{5,7},{7,5},{8,10},{10,8},{9,1... | collective-permute-start | bytes 442376 | tf_op jit(solution)/shard_map/ppermute | solution.py:605
  21.9 11.8 %collective-permute-start.10 = (f32[2,2,64,256]{3,2,1,0:T(8,128)S(1)}, f32[2,2,64,256]{3,2,1,0:T(8,128)S(1)}, u32[]{:S(2)}, u32[]{:S(2)}) collective-permute-start(f32[2,2,64,256]{3,2,1,0:T(8,128)S(1)} %shard_map.180.base_ref), channel_id=1, source_target_pairs={{0,4},{4,8},{6,2},{8,12},{10,6},{14,10},{1,5},{5,9},{7,3},{9,13},{... | collective-permute-start | bytes 786440 | tf_op jit(solution)/shard_map/ppermute | solution.py:620
  27.5 6.3 %copy-start.3 = (s32[4,2]{0,1:T(2,128)S(1)}, s32[4,2]{0,1:T(2,128)}, u32[]{:S(2)}) copy-start(s32[4,2]{0,1:T(2,128)} %param.24) | copy-start | bytes 100
  27.5 6.2 %copy-start.4 = (f32[4,2]{0,1:T(2,128)S(1)}, f32[4,2]{0,1:T(2,128)}, u32[]{:S(2)}) copy-start(f32[4,2]{0,1:T(2,128)} %param.25) | copy-start | bytes 100
  27.5 12.5 %collective-permute-start.6 = (f32[2,144,256]{2,1,0:T(8,128)S(1)}, f32[2,144,256]{2,1,0:T(8,128)S(1)}, u32[]{:S(2)}, u32[]{:S(2)}) collective-permute-start(f32[2,144,256]{2,1,0:T(8,128)S(1)} %pad_maximum_fusion.here_ref), channel_id=1, source_target_pairs={{0,4},{8,12},{4,0},{12,8},{1,5},{9,13},{5,1},{13,9},{2,6},{10,14},... | collective-permute-start | bytes 884744 | tf_op jit(solution)/shard_map/ppermute | solution.py:543
  29.4 10.6 %collective-permute-start.7 = (f32[2,144,256]{2,1,0:T(8,128)S(1)}, f32[2,144,256]{2,1,0:T(8,128)S(1)}, u32[]{:S(2)}, u32[]{:S(2)}) collective-permute-start(f32[2,144,256]{2,1,0:T(8,128)S(1)} %pad_maximum_fusion.here_ref), channel_id=1, source_target_pairs={{4,8},{8,4},{5,9},{9,5},{6,10},{10,6},{7,11},{11,7},{20,24},{24,20... | collective-permute-start | bytes 884744 | tf_op jit(solution)/shard_map/ppermute | solution.py:543
  34.5 7.0 %collective-permute-start.11 = (f32[2,2,64,256]{3,2,1,0:T(8,128)S(1)}, f32[2,2,64,256]{3,2,1,0:T(8,128)S(1)}, u32[]{:S(2)}, u32[]{:S(2)}) collective-permute-start(f32[2,2,64,256]{3,2,1,0:T(8,128)S(1)} %get-tuple-element.52), channel_id=1, source_target_pairs={{0,1},{1,0},{2,3},{3,2},{4,5},{5,4},{6,7},{7,6},{8,9},{9,8},{10,11... | collective-permute-start | bytes 786440 | tf_op jit(solution)/shard_map/ppermute | solution.py:546
  40.9 1.9 %collective-permute-start.8 = (f32[384,256]{1,0:T(8,128)S(1)}, f32[384,256]{1,0:T(8,128)S(1)}, u32[]{:S(2)}, u32[]{:S(2)}) collective-permute-start(f32[384,256]{1,0:T(8,128)S(1)} %get-tuple-element.49), channel_id=1, source_target_pairs={{0,1},{1,0},{2,3},{3,2},{4,5},{5,4},{6,7},{7,6},{8,9},{9,8},{10,11... | collective-permute-start | bytes 1179656 | tf_op jit(solution)/shard_map/ppermute | solution.py:546
  41.5 5.5 %collective-permute-start.12 = (f32[2,64,256]{2,1,0:T(8,128)S(1)}, f32[2,64,256]{2,1,0:T(8,128)S(1)}, u32[]{:S(2)}, u32[]{:S(2)}) collective-permute-start(f32[2,64,256]{2,1,0:T(8,128)S(1)} %get-tuple-element.56), channel_id=1, source_target_pairs={{0,2},{2,0},{1,3},{3,1},{4,6},{6,4},{5,7},{7,5},{8,10},{10,8},{9,1... | collective-permute-start | bytes 393224 | tf_op jit(solution)/shard_map/ppermute | solution.py:645
  42.8 4.2 %copy-start.1 = (f32[1,2,64,256]{3,2,1,0:T(8,128)S(1)}, f32[1,2,64,256]{3,2,1,0:T(8,128)}, u32[]{:S(2)}) copy-start(f32[1,2,64,256]{3,2,1,0:T(8,128)} %get-tuple-element.26.refs_2_) | copy-start | bytes 393220

commit v6 on v5

--- a/solution.py
+++ b/solution.py
@@ -351,7 +351,10 @@
             previous_y = norm_y
 
 
-def spread_kernel(shift_ref, weight_ref, base_ref, beside_ref, keep_ref, send_ref, padded):
+def spread_kernel(
+    shift_ref, weight_ref, base_ref, beside_ref, object_ref, keep_ref, send_ref, object_out_ref, padded
+):
+    object_out_ref[...] = object_ref[...]
     width = base_ref.shape[2]
     count = base_ref.shape[1]
     columns, tiles = keep_ref.shape[0], lax.axis_size("tile")
@@ -468,19 +471,10 @@
             send_ref[target : target + width] = total[at + count * width : at + (count + 1) * width]
 
 
-def volume_kernel(own_ref, received_ref, base_ref, volume_ref):
+def finish_kernel(*refs):
+    keep_ref, own_ref, received_ref, base_ref, object_ref, dual_ref = refs[:6]
+    spreads, (dual_out_ref, volume_ref, projected_ref) = refs[6:-3], refs[-3:]
     count, width = own_ref.shape[1:3]
-    for channel in range(2):
-        for row in range(count):
-            at = (2 + channel * count + row) * width
-            descent = own_ref[channel, row] + received_ref[at : at + width]
-            volume_ref[channel, row] = base_ref[channel, row] - step_size * descent
-
-
-def finish_kernel(*refs):
-    keep_ref, received_ref, object_ref, dual_ref = refs[:4]
-    spreads, (dual_out_ref, projected_ref) = refs[4:-2], refs[-2:]
-    width = keep_ref.shape[1]
     for channel in range(2):
         received = received_ref[channel * width : (channel + 1) * width]
         projection = -step_size * (keep_ref[channel] + received)
@@ -488,6 +482,10 @@
             projection = projection + spread_ref[channel]
         projected_ref[0, channel] = projection
         dual_out_ref[0, channel] = dual_ref[0, channel] + object_ref[0, channel] - projection
+        for row in range(count):
+            at = (2 + channel * count + row) * width
+            descent = own_ref[channel, row] + received_ref[at : at + width]
+            volume_ref[channel, row] = base_ref[channel, row] - step_size * descent
 
 
 def call(
@@ -593,7 +591,7 @@
     bridge += [(target, source) for source, target in bridge]
     row_b = lax.ppermute(row_b, ("angle", "tile"), bridge)
     row_a = across(row_a)
-    new_transmission, residual = call(
+    updated, residual = call(
         fold_kernel,
         [transmission.shape, (2 * width + 2 * SUBLANES, length)],
         (own, rim_a, rim_b, projected, scaled_dual, rays, row_a),
@@ -630,10 +628,10 @@
         kind=jnp.bfloat16,
     )
     block = (columns, 2, width, length)
-    keep, send = call(
+    keep, send, new_transmission = call(
         spread_kernel,
-        [block, block],
-        (shift_table.T, tap_weight.T, base, beside),
+        [block, block, transmission.shape],
+        (shift_table.T, tap_weight.T, base, beside, updated),
         [(count, 2, length // LANES, 2 * width, LANES)],
         10**7,
         2,
@@ -651,11 +649,10 @@
         10**9,
     )
     received = across(send)
-    (new_volume,) = call(volume_kernel, [volume.shape], (own, received, base), [], 10**6)
-    new_dual, new_projected = call(
+    new_dual, new_volume, new_projected = call(
         finish_kernel,
-        [transmission.shape] * 2,
-        (keep, received, new_transmission, scaled_dual, *spreads),
+        [transmission.shape, volume.shape, transmission.shape],
+        (keep, own, received, base, updated, scaled_dual, *spreads),
         [],
         10**6,
     )

time: 48 us -> 47.9 us (level)
  starting transfers between devices: 21.2 us -> 23.5 us
  waiting for transfers between devices: 14.5 us -> 12.8 us
  Pallas kernels: 10.5 us -> 9.83 us
    ppermute x1, waiting for transfers between devices: 3.63 us -> 1.37 us  [body(): beside = lax.ppermute(base, ('scan', 'angle'), route)]
    ppermute x6, starting transfers between devices: 11.8 us -> 13.9 us  [exchange(): return lax.ppermute(block, 'scan', both[number])]
    ppermute x1, waiting for transfers between devices: 3.42 us -> 5.41 us  [body(): spreads.append(lax.ppermute(keep[turn] + received[turn], 'angle', route))]
    ppermute x3, waiting for transfers between devices: 1.93 us -> 0.71 us  [across(): return lax.ppermute(block, 'tile', swap)]
    pallas_call x10 -> x9, Pallas kernels: 10.5 us -> 9.83 us  [call(): pl.pallas_call(kernel, out_shape=outputs, in_specs=in_specs, out_specs=[V...]
  transfers between devices with their start and end apart: 13 -> 13, of which waited for: 7 -> 6; matrix products, arithmetic and copies ran while one was open for 0% -> 0% of each run, Pallas kernels for 14% -> 13%
where the time goes in v6:
time: 47.9 us; the launch traced here: 47.6 us
  starting transfers between devices  23.5 us (49%)
  waiting for transfers between devices  12.8 us (27%)
  Pallas kernels  9.83 us (21%)
  between operations  1.45 us (3%)
    ppermute x6, starting transfers between devices, exchange(): return lax.ppermute(block, 'scan', both[number])  13.9 us
    pallas_call x9, Pallas kernels, call(): pl.pallas_call(kernel, out_shape=outputs, in_specs=in_specs, out_specs=[V...  9.83 us
    ppermute x1, starting transfers between devices, body(): beside = lax.ppermute(base, ('scan', 'angle'), route)  5.7 us
    ppermute x1, waiting for transfers between devices, body(): spreads.append(lax.ppermute(keep[turn] + received[turn], 'angle', route))  5.41 us
    ppermute x6, waiting for transfers between devices, exchange(): return lax.ppermute(block, 'scan', both[number])  5.26 us
    ppermute x3, starting transfers between devices, across(): return lax.ppermute(block, 'tile', swap)  1.63 us
    ppermute x1, starting transfers between devices, body(): by_column.append(lax.ppermute(residual, 'angle', turns[turn]))  1.56 us
    ppermute x1, waiting for transfers between devices, body(): beside = lax.ppermute(base, ('scan', 'angle'), route)  1.37 us
  transfers between devices with their start and end apart: 13, of which 6 were waited for; matrix products, arithmetic and copies ran while one was open for 0% of the time, Pallas kernels for 13%

profile of v6, /device:TPU:0, one launch (start us, length us, event | category | flops | bytes accessed | tf_op | source)
XLA Modules:
  0.0 47.6 jit_solution(18232978696608411304)
XLA Ops:
  0.6 1.0 %shard_map.175.plane_ref = f32[136,256]{1,0:T(8,128)S(1)} custom-call(f32[1,2,64,256]{3,2,1,0:T(8,128)} %plane_ref.1, f32[2,2,64,256]{3,2,1,0:T(8,128)} %volume_ref.1), custom_call_target="tpu_custom_call" | custom-call | flops 100000 | bytes 532480 | tf_op jit(solution)/shard_map/pallas_call | solution.py:509
  1.6 0.7 %collective-permute-start.1 = (f32[136,256]{1,0:T(8,128)S(1)}, f32[136,256]{1,0:T(8,128)S(1)}, u32[]{:S(2)}, u32[]{:S(2)}) collective-permute-start(f32[136,256]{1,0:T(8,128)S(1)} %shard_map.175.plane_ref), channel_id=1, source_target_pairs={{4,8},{8,4},{5,9},{9,5},{6,10},{10,6},{7,11},{11,7},{20,24},{24,20... | collective-permute-start | bytes 417800 | tf_op jit(solution)/shard_map/ppermute | solution.py:541
  2.3 5.9 %collective-permute-start = (f32[136,256]{1,0:T(8,128)S(1)}, f32[136,256]{1,0:T(8,128)S(1)}, u32[]{:S(2)}, u32[]{:S(2)}) collective-permute-start(f32[136,256]{1,0:T(8,128)S(1)} %shard_map.175.plane_ref), channel_id=1, source_target_pairs={{0,4},{8,12},{4,0},{12,8},{1,5},{9,13},{5,1},{13,9},{2,6},{10,14},... | collective-permute-start | bytes 417800 | tf_op jit(solution)/shard_map/ppermute | solution.py:541
  8.9 2.0 %shard_map.174 = (f32[4,2,128,128]{3,2,1,0:T(8,128)S(1)}, f32[1,192,256]{2,1,0:T(8,128)S(1)}, s32[4,8,128]{2,1,0:T(8,128)S(1)}, f32[8,256]{1,0:T(8,128)S(1)}, f3...) custom-call(s32[1,1]{1,0:T(1,128)S(6)} %copy.19.count_ref, ...), custom_call_target="tpu_custom_call" | custom-call | flops 10000000 | bytes 1794048 | tf_op jit(solution)/shard_map/pallas_call | solution.py:509
  10.9 0.7 %collective-permute-done.plane_a_ref = f32[136,256]{1,0:T(8,128)S(1)} collective-permute-done((f32[136,256]{1,0:T(8,128)S(1)}, f32[136,256]{1,0:T(8,128)S(1)}, u32[]{:S(2)}, u32[]{:S(2)}) %collective-permute-start) | collective-permute-done | bytes 139296 | tf_op jit(solution)/shard_map/ppermute | solution.py:541
  11.6 1.9 %shard_map.176 = (f32[3,64,256]{2,1,0:T(8,128)S(1)}, f32[192,256]{1,0:T(8,128)S(1)}, f32[192,256]{1,0:T(8,128)S(1)}, f32[2,80,256]{2,1,0:T(8,128)S(1)}, f32[2,80,256]{2,1,0:T(8,128)S(1)}) custom-call(f32[4,2,128,128]{3,2,1,0:T(8,128)S(1)} %get-tuple-element.33.probes_ref, f32[1,192,256]{2,1,0:T(8,128)S(1)} %get-tuple-element.34.density_ref, ...), custom_call_target="tpu_custom_call" | custom-call | flops 1000000000 | bytes 2998272 | tf_op jit(solution)/shard_map/pallas_call | solution.py:509
  13.5 1.8 %collective-permute-start.5 = (f32[192,256]{1,0:T(8,128)S(1)}, f32[192,256]{1,0:T(8,128)S(1)}, u32[]{:S(2)}, u32[]{:S(2)}) collective-permute-start(f32[192,256]{1,0:T(8,128)S(1)} %get-tuple-element.45), channel_id=1, source_target_pairs={{0,4},{8,12},{4,0},{12,8},{1,5},{9,13},{5,1},{13,9},{2,6},{10,14},... | collective-permute-start | bytes 589832 | tf_op jit(solution)/shard_map/ppermute | solution.py:541
  15.3 0.7 %collective-permute-start.6 = (f32[192,256]{1,0:T(8,128)S(1)}, f32[192,256]{1,0:T(8,128)S(1)}, u32[]{:S(2)}, u32[]{:S(2)}) collective-permute-start(f32[192,256]{1,0:T(8,128)S(1)} %get-tuple-element.46), channel_id=1, source_target_pairs={{4,8},{8,4},{5,9},{9,5},{6,10},{10,6},{7,11},{11,7},{20,24},{24,20... | collective-permute-start | bytes 589832 | tf_op jit(solution)/shard_map/ppermute | solution.py:541
  16.0 0.1 collective-permute-start.2
  16.1 0.7 %collective-permute-start.3 = (f32[2,80,256]{2,1,0:T(8,128)S(1)}, f32[2,80,256]{2,1,0:T(8,128)S(1)}, u32[]{:S(2)}, u32[]{:S(2)}) collective-permute-start(f32[2,80,256]{2,1,0:T(8,128)S(1)} %get-tuple-element.43), channel_id=1, source_target_pairs={{1,2},{2,1},{5,6},{6,5},{9,10},{10,9},{13,14},{14,13},{17,18},{18,... | collective-permute-start | bytes 491528 | tf_op jit(solution)/shard_map/ppermute | solution.py:592
  16.7 0.7 %collective-permute-done.2.row_a_ref.row_ref = f32[2,80,256]{2,1,0:T(8,128)S(1)} collective-permute-done((f32[2,80,256]{2,1,0:T(8,128)S(1)}, f32[2,80,256]{2,1,0:T(8,128)S(1)}, u32[]{:S(2)}, u32[]{:S(2)}) %collective-permute-start.2) | collective-permute-done | bytes 163872 | tf_op jit(solution)/shard_map/ppermute | solution.py:544
  17.4 1.9 %collective-permute-done.5.rim_a_ref = f32[192,256]{1,0:T(8,128)S(1)} collective-permute-done((f32[192,256]{1,0:T(8,128)S(1)}, f32[192,256]{1,0:T(8,128)S(1)}, u32[]{:S(2)}, u32[]{:S(2)}) %collective-permute-start.5) | collective-permute-done | bytes 196640 | tf_op jit(solution)/shard_map/ppermute | solution.py:541
  19.4 0.0 collective-permute-done.6.rim_b_ref
  19.4 0.1 shard_map.178
  19.4 1.6 %collective-permute-start.7 = (f32[144,256]{1,0:T(8,128)S(1)}, f32[144,256]{1,0:T(8,128)S(1)}, u32[]{:S(2)}, u32[]{:S(2)}) collective-permute-start(f32[144,256]{1,0:T(8,128)S(1)} %get-tuple-element.49.refs_0_), channel_id=1, source_target_pairs={{0,2},{2,0},{1,3},{3,1},{4,6},{6,4},{5,7},{7,5},{8,10},{10,8},{9,1... | collective-permute-start | bytes 442376 | tf_op jit(solution)/shard_map/ppermute | solution.py:603
  21.0 0.5 %shard_map.177.base_ref.refs_3_ = f32[2,2,64,256]{3,2,1,0:T(8,128)S(1)} custom-call(f32[2,2,64,256]{3,2,1,0:T(8,128)S(1)} %get-tuple-element.32.volume_ref, f32[136,256]{1,0:T(8,128)S(1)} %collective-permute-done.plane_a_ref, f32[136,256]{1,0:T(8,128)S(1)} %collective-permute-done.1.plane_b_ref, f32[2,80,256]{2,1,0:T(8,128)S(1)} %collective-permute-done.2.row_a_ref.row_ref, ...), custom_call_target="tpu_custom_call" | custom-call | flops 10000000 | bytes 1130496 | tf_op jit(solution)/shard_map/pallas_call | solution.py:509
  21.5 5.7 %collective-permute-start.4 = (f32[2,2,64,256]{3,2,1,0:T(8,128)S(1)}, f32[2,2,64,256]{3,2,1,0:T(8,128)S(1)}, u32[]{:S(2)}, u32[]{:S(2)}) collective-permute-start(f32[2,2,64,256]{3,2,1,0:T(8,128)S(1)} %shard_map.177.base_ref.refs_3_), channel_id=1, source_target_pairs={{0,4},{4,8},{6,2},{8,12},{10,6},{14,10},{1,5},{5,9},{7,3},{9,13},{... | collective-permute-start | bytes 786440 | tf_op jit(solution)/shard_map/ppermute | solution.py:618
  27.2 0.0 copy-start.3
  27.3 0.7 %collective-permute-start.9 = (f32[2,144,256]{2,1,0:T(8,128)S(1)}, f32[2,144,256]{2,1,0:T(8,128)S(1)}, u32[]{:S(2)}, u32[]{:S(2)}) collective-permute-start(f32[2,144,256]{2,1,0:T(8,128)S(1)} %pad_maximum_fusion.here_ref), channel_id=1, source_target_pairs={{4,8},{8,4},{5,9},{9,5},{6,10},{10,6},{7,11},{11,7},{20,24},{24,20... | collective-permute-start | bytes 884744 | tf_op jit(solution)/shard_map/ppermute | solution.py:541
  28.0 4.1 %collective-permute-start.8 = (f32[2,144,256]{2,1,0:T(8,128)S(1)}, f32[2,144,256]{2,1,0:T(8,128)S(1)}, u32[]{:S(2)}, u32[]{:S(2)}) collective-permute-start(f32[2,144,256]{2,1,0:T(8,128)S(1)} %pad_maximum_fusion.here_ref), channel_id=1, source_target_pairs={{0,4},{8,12},{4,0},{12,8},{1,5},{9,13},{5,1},{13,9},{2,6},{10,14},... | collective-permute-start | bytes 884744 | tf_op jit(solution)/shard_map/ppermute | solution.py:541
  32.1 1.4 %collective-permute-done.4.beside_ref = f32[2,2,64,256]{3,2,1,0:T(8,128)S(1)} collective-permute-done((f32[2,2,64,256]{3,2,1,0:T(8,128)S(1)}, f32[2,2,64,256]{3,2,1,0:T(8,128)S(1)}, u32[]{:S(2)}, u32[]{:S(2)}) %collective-permute-start.4) | collective-permute-done | bytes 262176 | tf_op jit(solution)/shard_map/ppermute | solution.py:618
  33.5 1.4 %shard_map.179 = (f32[2,2,64,256]{3,2,1,0:T(8,128)S(1)}, f32[2,2,64,256]{3,2,1,0:T(8,128)S(1)}, f32[1,2,64,256]{3,2,1,0:T(8,128)}) custom-call(s32[2,4]{1,0:T(2,128)S(1)} %bitcast.13, f32[2,4]{1,0:T(2,128)S(1)} %bitcast.15, f32[2,2,64,256]{3,2,1,0:T(8,128)S(1)} %shard_map.177.base_ref.refs_3_, f32[2,2,64,256]{3,2,1,0:T(8,128)S(1)} %collective-permute-done.4.beside_ref, ...), custom_call_target="tpu_custom_call" | custom-call | flops 10000000 | bytes 1310720 | tf_op jit(solution)/shard_map/pallas_call | solution.py:509
  34.8 1.0 %collective-permute-start.11 = (f32[2,2,64,256]{3,2,1,0:T(8,128)S(1)}, f32[2,2,64,256]{3,2,1,0:T(8,128)S(1)}, u32[]{:S(2)}, u32[]{:S(2)}) collective-permute-start(f32[2,2,64,256]{3,2,1,0:T(8,128)S(1)} %get-tuple-element.56), channel_id=1, source_target_pairs={{0,1},{1,0},{2,3},{3,2},{4,5},{5,4},{6,7},{7,6},{8,9},{9,8},{10,11... | collective-permute-start | bytes 786440 | tf_op jit(solution)/shard_map/ppermute | solution.py:544
  35.8 1.4 %shard_map.180 = (bf16[2,384,192]{2,1,0:T(8,128)(2,1)S(1)}, bf16[2,384,192]{2,1,0:T(8,128)(2,1)S(1)}) custom-call(f32[144,256]{1,0:T(8,128)S(1)} %get-tuple-element.49.refs_0_, f32[144,256]{1,0:T(8,128)S(1)} %collective-permute-done.7.refs_1_), custom_call_target="tpu_custom_call" | custom-call | flops 100000000 | bytes 1474560 | tf_op jit(solution)/shard_map/pallas_call | solution.py:509
  37.2 0.0 collective-permute-done.9.side_b_ref
  37.2 2.6 %collective-permute-done.8.side_a_ref = f32[2,144,256]{2,1,0:T(8,128)S(1)} collective-permute-done((f32[2,144,256]{2,1,0:T(8,128)S(1)}, f32[2,144,256]{2,1,0:T(8,128)S(1)}, u32[]{:S(2)}, u32[]{:S(2)}) %collective-permute-start.8) | collective-permute-done | bytes 294944 | tf_op jit(solution)/shard_map/ppermute | solution.py:541
  39.8 0.8 %shard_map.181 = (f32[2,64,256]{2,1,0:T(8,128)S(1)}, f32[2,2,64,256]{3,2,1,0:T(8,128)S(1)}, f32[384,256]{1,0:T(8,128)S(1)}) custom-call(f32[2,144,256]{2,1,0:T(8,128)S(1)} %pad_maximum_fusion.here_ref, f32[2,144,256]{2,1,0:T(8,128)S(1)} %collective-permute-done.8.side_a_ref, f32[2,144,256]{2,1,0:T(8,128)S(1)} %collective-permute-done.9.side_b_ref, ...), custom_call_target="tpu_custom_call" | custom-call | flops 1000000000 | bytes 2260992 | tf_op jit(solution)/shard_map/pallas_call | solution.py:509
  40.6 0.6 %collective-permute-start.10 = (f32[384,256]{1,0:T(8,128)S(1)}, f32[384,256]{1,0:T(8,128)S(1)}, u32[]{:S(2)}, u32[]{:S(2)}) collective-permute-start(f32[384,256]{1,0:T(8,128)S(1)} %get-tuple-element.54), channel_id=1, source_target_pairs={{0,1},{1,0},{2,3},{3,2},{4,5},{5,4},{6,7},{7,6},{8,9},{9,8},{10,11... | collective-permute-start | bytes 1179656 | tf_op jit(solution)/shard_map/ppermute | solution.py:544
  41.2 0.0 collective-permute-done.11
  41.2 0.1 collective-permute-start.12
  41.3 5.4 %collective-permute-done.12.refs_8_ = f32[2,64,256]{2,1,0:T(8,128)S(1)} collective-permute-done((f32[2,64,256]{2,1,0:T(8,128)S(1)}, f32[2,64,256]{2,1,0:T(8,128)S(1)}, u32[]{:S(2)}, u32[]{:S(2)}) %collective-permute-start.12) | collective-permute-done | bytes 131104 | tf_op jit(solution)/shard_map/ppermute | solution.py:643
  46.7 0.9 %shard_map.182 = (f32[1,2,64,256]{3,2,1,0:T(8,128)}, f32[2,2,64,256]{3,2,1,0:T(8,128)}, f32[1,2,64,256]{3,2,1,0:T(8,128)}) custom-call(f32[2,64,256]{2,1,0:T(8,128)S(1)} %get-tuple-element.52.refs_0_, f32[2,2,64,256]{3,2,1,0:T(8,128)S(1)} %get-tuple-element.53.refs_1_, f32[384,256]{1,0:T(8,128)S(1)} %collective-permute-done.10.refs_2_, ...), custom_call_target="tpu_custom_call" | custom-call | flops 1000000 | bytes 2228224 | tf_op jit(solution)/shard_map/pallas_call | solution.py:509
  (13 shorter events, 0.1 us)
Async XLA Ops:
  1.6 9.3 %collective-permute-start.1 = (f32[136,256]{1,0:T(8,128)S(1)}, f32[136,256]{1,0:T(8,128)S(1)}, u32[]{:S(2)}, u32[]{:S(2)}) collective-permute-start(f32[136,256]{1,0:T(8,128)S(1)} %shard_map.175.plane_ref), channel_id=1, source_target_pairs={{4,8},{8,4},{5,9},{9,5},{6,10},{10,6},{7,11},{11,7},{20,24},{24,20... | collective-permute-start | bytes 417800 | tf_op jit(solution)/shard_map/ppermute | solution.py:541
  2.3 9.3 %collective-permute-start = (f32[136,256]{1,0:T(8,128)S(1)}, f32[136,256]{1,0:T(8,128)S(1)}, u32[]{:S(2)}, u32[]{:S(2)}) collective-permute-start(f32[136,256]{1,0:T(8,128)S(1)} %shard_map.175.plane_ref), channel_id=1, source_target_pairs={{0,4},{8,12},{4,0},{12,8},{1,5},{9,13},{5,1},{13,9},{2,6},{10,14},... | collective-permute-start | bytes 417800 | tf_op jit(solution)/shard_map/ppermute | solution.py:541
  11.6 7.8 %copy-start = (f32[1,2,64,256]{3,2,1,0:T(8,128)S(1)}, f32[1,2,64,256]{3,2,1,0:T(8,128)}, u32[]{:S(2)}) copy-start(f32[1,2,64,256]{3,2,1,0:T(8,128)} %refs_5_.2) | copy-start | bytes 393220
  11.6 7.8 %copy-start.1 = (f32[1,2,64,256]{3,2,1,0:T(8,128)S(1)}, f32[1,2,64,256]{3,2,1,0:T(8,128)}, u32[]{:S(2)}) copy-start(f32[1,2,64,256]{3,2,1,0:T(8,128)} %projected_ref.1) | copy-start | bytes 393220
  13.5 5.9 %collective-permute-start.5 = (f32[192,256]{1,0:T(8,128)S(1)}, f32[192,256]{1,0:T(8,128)S(1)}, u32[]{:S(2)}, u32[]{:S(2)}) collective-permute-start(f32[192,256]{1,0:T(8,128)S(1)} %get-tuple-element.45), channel_id=1, source_target_pairs={{0,4},{8,12},{4,0},{12,8},{1,5},{9,13},{5,1},{13,9},{2,6},{10,14},... | collective-permute-start | bytes 589832 | tf_op jit(solution)/shard_map/ppermute | solution.py:541
  15.3 4.0 %collective-permute-start.6 = (f32[192,256]{1,0:T(8,128)S(1)}, f32[192,256]{1,0:T(8,128)S(1)}, u32[]{:S(2)}, u32[]{:S(2)}) collective-permute-start(f32[192,256]{1,0:T(8,128)S(1)} %get-tuple-element.46), channel_id=1, source_target_pairs={{4,8},{8,4},{5,9},{9,5},{6,10},{10,6},{7,11},{11,7},{20,24},{24,20... | collective-permute-start | bytes 589832 | tf_op jit(solution)/shard_map/ppermute | solution.py:541
  16.0 1.5 %collective-permute-start.2 = (f32[2,80,256]{2,1,0:T(8,128)S(1)}, f32[2,80,256]{2,1,0:T(8,128)S(1)}, u32[]{:S(2)}, u32[]{:S(2)}) collective-permute-start(f32[2,80,256]{2,1,0:T(8,128)S(1)} %get-tuple-element.42), channel_id=1, source_target_pairs={{0,1},{1,0},{2,3},{3,2},{4,5},{5,4},{6,7},{7,6},{8,9},{9,8},{10,11... | collective-permute-start | bytes 491528 | tf_op jit(solution)/shard_map/ppermute | solution.py:544
  16.1 4.9 %collective-permute-start.3 = (f32[2,80,256]{2,1,0:T(8,128)S(1)}, f32[2,80,256]{2,1,0:T(8,128)S(1)}, u32[]{:S(2)}, u32[]{:S(2)}) collective-permute-start(f32[2,80,256]{2,1,0:T(8,128)S(1)} %get-tuple-element.43), channel_id=1, source_target_pairs={{1,2},{2,1},{5,6},{6,5},{9,10},{10,9},{13,14},{14,13},{17,18},{18,... | collective-permute-start | bytes 491528 | tf_op jit(solution)/shard_map/ppermute | solution.py:592
  19.4 7.8 %collective-permute-start.7 = (f32[144,256]{1,0:T(8,128)S(1)}, f32[144,256]{1,0:T(8,128)S(1)}, u32[]{:S(2)}, u32[]{:S(2)}) collective-permute-start(f32[144,256]{1,0:T(8,128)S(1)} %get-tuple-element.49.refs_0_), channel_id=1, source_target_pairs={{0,2},{2,0},{1,3},{3,1},{4,6},{6,4},{5,7},{7,5},{8,10},{10,8},{9,1... | collective-permute-start | bytes 442376 | tf_op jit(solution)/shard_map/ppermute | solution.py:603
  21.5 12.0 %collective-permute-start.4 = (f32[2,2,64,256]{3,2,1,0:T(8,128)S(1)}, f32[2,2,64,256]{3,2,1,0:T(8,128)S(1)}, u32[]{:S(2)}, u32[]{:S(2)}) collective-permute-start(f32[2,2,64,256]{3,2,1,0:T(8,128)S(1)} %shard_map.177.base_ref.refs_3_), channel_id=1, source_target_pairs={{0,4},{4,8},{6,2},{8,12},{10,6},{14,10},{1,5},{5,9},{7,3},{9,13},{... | collective-permute-start | bytes 786440 | tf_op jit(solution)/shard_map/ppermute | solution.py:618
  27.2 6.2 %copy-start.3 = (f32[4,2]{0,1:T(2,128)S(1)}, f32[4,2]{0,1:T(2,128)}, u32[]{:S(2)}) copy-start(f32[4,2]{0,1:T(2,128)} %param.25) | copy-start | bytes 100
  27.3 6.2 %copy-start.2 = (s32[4,2]{0,1:T(2,128)S(1)}, s32[4,2]{0,1:T(2,128)}, u32[]{:S(2)}) copy-start(s32[4,2]{0,1:T(2,128)} %param.24) | copy-start | bytes 100
  27.3 9.9 %collective-permute-start.9 = (f32[2,144,256]{2,1,0:T(8,128)S(1)}, f32[2,144,256]{2,1,0:T(8,128)S(1)}, u32[]{:S(2)}, u32[]{:S(2)}) collective-permute-start(f32[2,144,256]{2,1,0:T(8,128)S(1)} %pad_maximum_fusion.here_ref), channel_id=1, source_target_pairs={{4,8},{8,4},{5,9},{9,5},{6,10},{10,6},{7,11},{11,7},{20,24},{24,20... | collective-permute-start | bytes 884744 | tf_op jit(solution)/shard_map/ppermute | solution.py:541
  28.0 11.8 %collective-permute-start.8 = (f32[2,144,256]{2,1,0:T(8,128)S(1)}, f32[2,144,256]{2,1,0:T(8,128)S(1)}, u32[]{:S(2)}, u32[]{:S(2)}) collective-permute-start(f32[2,144,256]{2,1,0:T(8,128)S(1)} %pad_maximum_fusion.here_ref), channel_id=1, source_target_pairs={{0,4},{8,12},{4,0},{12,8},{1,5},{9,13},{5,1},{13,9},{2,6},{10,14},... | collective-permute-start | bytes 884744 | tf_op jit(solution)/shard_map/ppermute | solution.py:541
  34.8 6.4 %collective-permute-start.11 = (f32[2,2,64,256]{3,2,1,0:T(8,128)S(1)}, f32[2,2,64,256]{3,2,1,0:T(8,128)S(1)}, u32[]{:S(2)}, u32[]{:S(2)}) collective-permute-start(f32[2,2,64,256]{3,2,1,0:T(8,128)S(1)} %get-tuple-element.56), channel_id=1, source_target_pairs={{0,1},{1,0},{2,3},{3,2},{4,5},{5,4},{6,7},{7,6},{8,9},{9,8},{10,11... | collective-permute-start | bytes 786440 | tf_op jit(solution)/shard_map/ppermute | solution.py:544
  40.6 6.1 %collective-permute-start.10 = (f32[384,256]{1,0:T(8,128)S(1)}, f32[384,256]{1,0:T(8,128)S(1)}, u32[]{:S(2)}, u32[]{:S(2)}) collective-permute-start(f32[384,256]{1,0:T(8,128)S(1)} %get-tuple-element.54), channel_id=1, source_target_pairs={{0,1},{1,0},{2,3},{3,2},{4,5},{5,4},{6,7},{7,6},{8,9},{9,8},{10,11... | collective-permute-start | bytes 1179656 | tf_op jit(solution)/shard_map/ppermute | solution.py:544
  41.2 5.5 %collective-permute-start.12 = (f32[2,64,256]{2,1,0:T(8,128)S(1)}, f32[2,64,256]{2,1,0:T(8,128)S(1)}, u32[]{:S(2)}, u32[]{:S(2)}) collective-permute-start(f32[2,64,256]{2,1,0:T(8,128)S(1)} %get-tuple-element.60), channel_id=1, source_target_pairs={{0,2},{2,0},{1,3},{3,1},{4,6},{6,4},{5,7},{7,5},{8,10},{10,8},{9,1... | collective-permute-start | bytes 393224 | tf_op jit(solution)/shard_map/ppermute | solution.py:643

commit v7 on v6

--- a/solution.py
+++ b/solution.py
@@ -160,7 +160,6 @@
     probes_ref,
     density_ref,
     slots_ref,
-    rays_ref,
     plane_ref,
     intensity_ref,
     volume_ref,
@@ -266,11 +265,10 @@
         for low, row_ref in ((jnp.logical_not(first_tile), row_a_ref), (first_tile, row_b_ref)):
             row_ref[channel, :width] = jnp.where(low, rows[0][0], rows[1][0])
             row_ref[channel, width : width + 2] = jnp.where(low, rows[0][1], rows[1][1])
-            row_ref[channel, width + SUBLANES :] = rays_ref[...]
 
 
 def fold_kernel(
-    own_ref, rim_a_ref, rim_b_ref, projected_ref, dual_ref, rays_ref, row_ref, object_ref, residual_ref
+    own_ref, rim_a_ref, rim_b_ref, projected_ref, dual_ref, rays_ref, too_ref, object_ref, residual_ref
 ):
     width = own_ref.shape[1]
     sums = [
@@ -286,7 +284,7 @@
         object_ref[0, part] = updated
         residual_ref[part * width : (part + 1) * width] = target - updated - dual
     residual_ref[2 * width : 2 * width + SUBLANES] = rays_ref[...]
-    residual_ref[2 * width + SUBLANES :] = row_ref[0, width + SUBLANES :]
+    residual_ref[2 * width + SUBLANES :] = too_ref[...]
 
 
 def variation_kernel(
@@ -352,9 +350,8 @@
 
 
 def spread_kernel(
-    shift_ref, weight_ref, base_ref, beside_ref, object_ref, keep_ref, send_ref, object_out_ref, padded
+    shift_ref, weight_ref, base_ref, beside_ref, keep_ref, send_ref, padded
 ):
-    object_out_ref[...] = object_ref[...]
     width = base_ref.shape[2]
     count = base_ref.shape[1]
     columns, tiles = keep_ref.shape[0], lax.axis_size("tile")
@@ -386,7 +383,8 @@
 
 
 def operator_kernel(*refs):
-    packed_refs, (high_ref, low_ref) = refs[:-2], refs[-2:]
+    packed_refs, (object_ref, high_ref, low_ref, object_out_ref) = refs[:-4], refs[-4:]
+    object_out_ref[...] = object_ref[...]
     tiles = lax.axis_size("tile")
     columns = len(packed_refs)
     rows_out, reach = high_ref.shape[1:]
@@ -576,12 +574,13 @@
     )
     volume_here = held[1]
     turns = [[(i, (i - turn) % columns) for i in range(columns)] for turn in range(columns)]
+    rays_too = across(rays)
     own, rim_a, rim_b, row_a, row_b = call(
         patch_kernel,
         [(3, width, length)]
         + [(3 * width, length)] * 2
-        + [(2, width + 2 * SUBLANES, length)] * 2,
-        (probes, density, slot_numbers, rays, plane, *held, plane_a, plane_b),
+        + [(2, width + SUBLANES, length)] * 2,
+        (probes, density, slot_numbers, plane, *held, plane_a, plane_b),
         [(2, 3 * width, length), (3, 3 * width, length)],
         10**9,
     )
@@ -594,7 +593,7 @@
     updated, residual = call(
         fold_kernel,
         [transmission.shape, (2 * width + 2 * SUBLANES, length)],
-        (own, rim_a, rim_b, projected, scaled_dual, rays, row_a),
+        (own, rim_a, rim_b, projected, scaled_dual, rays, rays_too),
         [],
         10**6,
     )
@@ -619,19 +618,20 @@
     here = jnp.stack(by_column)
     side_a = exchange(here, 0)
     side_b = exchange(here, 1)
-    high, low = call(
+    high, low, new_transmission = call(
         operator_kernel,
-        [(columns, (2 + 2 * count) * width, 3 * width)] * 2,
-        tuple(by_column),
+        [(columns, (2 + 2 * count) * width, 3 * width)] * 2 + [transmission.shape],
+        (*by_column, updated),
         [],
         10**8,
         kind=jnp.bfloat16,
+        kinds={2: jnp.float32},
     )
     block = (columns, 2, width, length)
-    keep, send, new_transmission = call(
+    keep, send = call(
         spread_kernel,
-        [block, block, transmission.shape],
-        (shift_table.T, tap_weight.T, base, beside, updated),
+        [block, block],
+        (shift_table.T, tap_weight.T, base, beside),
         [(count, 2, length // LANES, 2 * width, LANES)],
         10**7,
         2,

time: 47.9 us -> 48 us (level)
  starting transfers between devices: 23.5 us -> 22.4 us
  waiting for transfers between devices: 12.8 us -> 13.9 us
    ppermute x3 -> x4, starting transfers between devices: 1.63 us -> 0.71 us  [across(): return lax.ppermute(block, 'tile', swap)]
    ppermute x6, waiting for transfers between devices: 5.26 us -> 6.11 us  [exchange(): return lax.ppermute(block, 'scan', both[number])]
    ppermute x3 -> x4, waiting for transfers between devices: 0.71 us -> 0.01 us  [across(): return lax.ppermute(block, 'tile', swap)]
    ppermute x1, waiting for transfers between devices: 1.37 us -> 1.92 us  [body(): beside = lax.ppermute(base, ('scan', 'angle'), route)]
  transfers between devices with their start and end apart: 13 -> 14, of which waited for: 6 -> 5; matrix products, arithmetic and copies ran while one was open for 0% -> 0% of each run, Pallas kernels for 13% -> 13%
where the time goes in v7:
time: 48 us; the launch traced here: 47.7 us
  starting transfers between devices  22.4 us (47%)
  waiting for transfers between devices  13.9 us (29%)
  Pallas kernels  9.84 us (20%)
  between operations  1.47 us (3%)
    ppermute x6, starting transfers between devices, exchange(): return lax.ppermute(block, 'scan', both[number])  13.7 us
    pallas_call x9, Pallas kernels, call(): pl.pallas_call(kernel, out_shape=outputs, in_specs=in_specs, out_specs=[V...  9.84 us
    ppermute x6, waiting for transfers between devices, exchange(): return lax.ppermute(block, 'scan', both[number])  6.11 us
    ppermute x1, waiting for transfers between devices, body(): spreads.append(lax.ppermute(keep[turn] + received[turn], 'angle', route))  5.87 us
    ppermute x1, starting transfers between devices, body(): beside = lax.ppermute(base, ('scan', 'angle'), route)  5.7 us
    ppermute x1, waiting for transfers between devices, body(): beside = lax.ppermute(base, ('scan', 'angle'), route)  1.92 us
    ppermute x1, starting transfers between devices, body(): by_column.append(lax.ppermute(residual, 'angle', turns[turn]))  1.56 us
  transfers between devices with their start and end apart: 14, of which 5 were waited for; matrix products, arithmetic and copies ran while one was open for 0% of the time, Pallas kernels for 13%

profile of v7, /device:TPU:0, one launch (start us, length us, event | category | flops | bytes accessed | tf_op | source)
XLA Modules:
  0.0 47.7 jit_solution(9247551033313649070)
XLA Ops:
  0.6 1.0 %shard_map.175.plane_ref = f32[136,256]{1,0:T(8,128)S(1)} custom-call(f32[1,2,64,256]{3,2,1,0:T(8,128)} %plane_ref.1, f32[2,2,64,256]{3,2,1,0:T(8,128)} %volume_ref.1), custom_call_target="tpu_custom_call" | custom-call | flops 100000 | bytes 532480 | tf_op jit(solution)/shard_map/pallas_call | solution.py:507
  1.6 0.7 %collective-permute-start.1 = (f32[136,256]{1,0:T(8,128)S(1)}, f32[136,256]{1,0:T(8,128)S(1)}, u32[]{:S(2)}, u32[]{:S(2)}) collective-permute-start(f32[136,256]{1,0:T(8,128)S(1)} %shard_map.175.plane_ref), channel_id=1, source_target_pairs={{4,8},{8,4},{5,9},{9,5},{6,10},{10,6},{7,11},{11,7},{20,24},{24,20... | collective-permute-start | bytes 417800 | tf_op jit(solution)/shard_map/ppermute | solution.py:539
  2.3 5.9 %collective-permute-start = (f32[136,256]{1,0:T(8,128)S(1)}, f32[136,256]{1,0:T(8,128)S(1)}, u32[]{:S(2)}, u32[]{:S(2)}) collective-permute-start(f32[136,256]{1,0:T(8,128)S(1)} %shard_map.175.plane_ref), channel_id=1, source_target_pairs={{0,4},{8,12},{4,0},{12,8},{1,5},{9,13},{5,1},{13,9},{2,6},{10,14},... | collective-permute-start | bytes 417800 | tf_op jit(solution)/shard_map/ppermute | solution.py:539
  8.9 2.0 %shard_map.174 = (f32[4,2,128,128]{3,2,1,0:T(8,128)S(1)}, f32[1,192,256]{2,1,0:T(8,128)S(1)}, s32[4,8,128]{2,1,0:T(8,128)S(1)}, f32[8,256]{1,0:T(8,128)S(1)}, f3...) custom-call(s32[1,1]{1,0:T(1,128)S(6)} %copy.19.count_ref, ...), custom_call_target="tpu_custom_call" | custom-call | flops 10000000 | bytes 1794048 | tf_op jit(solution)/shard_map/pallas_call | solution.py:507
  10.9 0.7 %collective-permute-done.plane_a_ref = f32[136,256]{1,0:T(8,128)S(1)} collective-permute-done((f32[136,256]{1,0:T(8,128)S(1)}, f32[136,256]{1,0:T(8,128)S(1)}, u32[]{:S(2)}, u32[]{:S(2)}) %collective-permute-start) | collective-permute-done | bytes 139296 | tf_op jit(solution)/shard_map/ppermute | solution.py:539
  11.6 1.9 %shard_map.176 = (f32[3,64,256]{2,1,0:T(8,128)S(1)}, f32[192,256]{1,0:T(8,128)S(1)}, f32[192,256]{1,0:T(8,128)S(1)}, f32[2,72,256]{2,1,0:T(8,128)S(1)}, f32[2,72,256]{2,1,0:T(8,128)S(1)}) custom-call(f32[4,2,128,128]{3,2,1,0:T(8,128)S(1)} %get-tuple-element.32.probes_ref, f32[1,192,256]{2,1,0:T(8,128)S(1)} %get-tuple-element.33.density_ref, ...), custom_call_target="tpu_custom_call" | custom-call | flops 1000000000 | bytes 2957312 | tf_op jit(solution)/shard_map/pallas_call | solution.py:507
  13.5 1.8 %collective-permute-start.2 = (f32[192,256]{1,0:T(8,128)S(1)}, f32[192,256]{1,0:T(8,128)S(1)}, u32[]{:S(2)}, u32[]{:S(2)}) collective-permute-start(f32[192,256]{1,0:T(8,128)S(1)} %get-tuple-element.42), channel_id=1, source_target_pairs={{0,4},{8,12},{4,0},{12,8},{1,5},{9,13},{5,1},{13,9},{2,6},{10,14},... | collective-permute-start | bytes 589832 | tf_op jit(solution)/shard_map/ppermute | solution.py:539
  15.3 0.7 %collective-permute-start.3 = (f32[192,256]{1,0:T(8,128)S(1)}, f32[192,256]{1,0:T(8,128)S(1)}, u32[]{:S(2)}, u32[]{:S(2)}) collective-permute-start(f32[192,256]{1,0:T(8,128)S(1)} %get-tuple-element.43), channel_id=1, source_target_pairs={{4,8},{8,4},{5,9},{9,5},{6,10},{10,6},{7,11},{11,7},{20,24},{24,20... | collective-permute-start | bytes 589832 | tf_op jit(solution)/shard_map/ppermute | solution.py:539
  16.0 0.1 collective-permute-start.4
  16.1 0.5 %collective-permute-start.9 = (f32[2,72,256]{2,1,0:T(8,128)S(1)}, f32[2,72,256]{2,1,0:T(8,128)S(1)}, u32[]{:S(2)}, u32[]{:S(2)}) collective-permute-start(f32[2,72,256]{2,1,0:T(8,128)S(1)} %get-tuple-element.53), channel_id=1, source_target_pairs={{0,1},{1,0},{2,3},{3,2},{4,5},{5,4},{6,7},{7,6},{8,9},{9,8},{10,11... | collective-permute-start | bytes 442376 | tf_op jit(solution)/shard_map/ppermute | solution.py:542
  16.6 0.7 %collective-permute-start.10 = (f32[2,72,256]{2,1,0:T(8,128)S(1)}, f32[2,72,256]{2,1,0:T(8,128)S(1)}, u32[]{:S(2)}, u32[]{:S(2)}) collective-permute-start(f32[2,72,256]{2,1,0:T(8,128)S(1)} %get-tuple-element.54), channel_id=1, source_target_pairs={{1,2},{2,1},{5,6},{6,5},{9,10},{10,9},{13,14},{14,13},{17,18},{18,... | collective-permute-start | bytes 442376 | tf_op jit(solution)/shard_map/ppermute | solution.py:591
  17.3 2.1 %collective-permute-done.2.rim_a_ref = f32[192,256]{1,0:T(8,128)S(1)} collective-permute-done((f32[192,256]{1,0:T(8,128)S(1)}, f32[192,256]{1,0:T(8,128)S(1)}, u32[]{:S(2)}, u32[]{:S(2)}) %collective-permute-start.2) | collective-permute-done | bytes 196640 | tf_op jit(solution)/shard_map/ppermute | solution.py:539
  19.4 0.0 collective-permute-done.3.rim_b_ref
  19.4 0.1 shard_map.177
  19.5 1.6 %collective-permute-start.5 = (f32[144,256]{1,0:T(8,128)S(1)}, f32[144,256]{1,0:T(8,128)S(1)}, u32[]{:S(2)}, u32[]{:S(2)}) collective-permute-start(f32[144,256]{1,0:T(8,128)S(1)} %get-tuple-element.45.refs_0_), channel_id=1, source_target_pairs={{0,2},{2,0},{1,3},{3,1},{4,6},{6,4},{5,7},{7,5},{8,10},{10,8},{9,1... | collective-permute-start | bytes 442376 | tf_op jit(solution)/shard_map/ppermute | solution.py:602
  21.0 0.0 collective-permute-done.9.row_a_ref
  21.0 0.5 %shard_map.180.base_ref.refs_3_ = f32[2,2,64,256]{3,2,1,0:T(8,128)S(1)} custom-call(f32[2,2,64,256]{3,2,1,0:T(8,128)S(1)} %get-tuple-element.36.volume_ref, f32[136,256]{1,0:T(8,128)S(1)} %collective-permute-done.plane_a_ref, f32[136,256]{1,0:T(8,128)S(1)} %collective-permute-done.1.plane_b_ref, f32[2,72,256]{2,1,0:T(8,128)S(1)} %collective-permute-done.9.row_a_ref, ...), custom_call_target="tpu_custom_call" | custom-call | flops 10000000 | bytes 1097728 | tf_op jit(solution)/shard_map/pallas_call | solution.py:507
  21.6 5.7 %collective-permute-start.11 = (f32[2,2,64,256]{3,2,1,0:T(8,128)S(1)}, f32[2,2,64,256]{3,2,1,0:T(8,128)S(1)}, u32[]{:S(2)}, u32[]{:S(2)}) collective-permute-start(f32[2,2,64,256]{3,2,1,0:T(8,128)S(1)} %shard_map.180.base_ref.refs_3_), channel_id=1, source_target_pairs={{0,4},{4,8},{6,2},{8,12},{10,6},{14,10},{1,5},{5,9},{7,3},{9,13},{... | collective-permute-start | bytes 786440 | tf_op jit(solution)/shard_map/ppermute | solution.py:617
  27.3 0.0 copy-start.2
  27.3 0.0 copy-start.3
  27.3 0.7 %collective-permute-start.7 = (f32[2,144,256]{2,1,0:T(8,128)S(1)}, f32[2,144,256]{2,1,0:T(8,128)S(1)}, u32[]{:S(2)}, u32[]{:S(2)}) collective-permute-start(f32[2,144,256]{2,1,0:T(8,128)S(1)} %pad_maximum_fusion.here_ref), channel_id=1, source_target_pairs={{4,8},{8,4},{5,9},{9,5},{6,10},{10,6},{7,11},{11,7},{20,24},{24,20... | collective-permute-start | bytes 884744 | tf_op jit(solution)/shard_map/ppermute | solution.py:539
  28.0 4.0 %collective-permute-start.6 = (f32[2,144,256]{2,1,0:T(8,128)S(1)}, f32[2,144,256]{2,1,0:T(8,128)S(1)}, u32[]{:S(2)}, u32[]{:S(2)}) collective-permute-start(f32[2,144,256]{2,1,0:T(8,128)S(1)} %pad_maximum_fusion.here_ref), channel_id=1, source_target_pairs={{0,4},{8,12},{4,0},{12,8},{1,5},{9,13},{5,1},{13,9},{2,6},{10,14},... | collective-permute-start | bytes 884744 | tf_op jit(solution)/shard_map/ppermute | solution.py:539
  32.0 1.9 %collective-permute-done.11.beside_ref = f32[2,2,64,256]{3,2,1,0:T(8,128)S(1)} collective-permute-done((f32[2,2,64,256]{3,2,1,0:T(8,128)S(1)}, f32[2,2,64,256]{3,2,1,0:T(8,128)S(1)}, u32[]{:S(2)}, u32[]{:S(2)}) %collective-permute-start.11) | collective-permute-done | bytes 262176 | tf_op jit(solution)/shard_map/ppermute | solution.py:617
  33.9 0.8 %shard_map.181 = (f32[2,2,64,256]{3,2,1,0:T(8,128)S(1)}, f32[2,2,64,256]{3,2,1,0:T(8,128)S(1)}) custom-call(s32[2,4]{1,0:T(2,128)S(1)} %bitcast.13, f32[2,4]{1,0:T(2,128)S(1)} %bitcast.15, f32[2,2,64,256]{3,2,1,0:T(8,128)S(1)} %shard_map.180.base_ref.refs_3_, f32[2,2,64,256]{3,2,1,0:T(8,128)S(1)} %collective-permute-done.11.beside_ref), custom_call_target="tpu_custom_call" | custom-call | flops 10000000 | bytes 1048576 | tf_op jit(solution)/shard_map/pallas_call | solution.py:507
  34.7 0.1 collective-permute-start.12
  34.8 1.9 %shard_map.178 = (bf16[2,384,192]{2,1,0:T(8,128)(2,1)S(1)}, bf16[2,384,192]{2,1,0:T(8,128)(2,1)S(1)}, f32[1,2,64,256]{3,2,1,0:T(8,128)}) custom-call(f32[144,256]{1,0:T(8,128)S(1)} %get-tuple-element.45.refs_0_, f32[144,256]{1,0:T(8,128)S(1)} %collective-permute-done.5.refs_1_, f32[1,2,64,256]{3,2,1,0:T(8,128)S(1)} %get-tuple-element.46.refs_2_.refs_4_), custom_call_target="tpu_custom_call" | custom-call | flops 100000000 | bytes 1736704 | tf_op jit(solution)/shard_map/pallas_call | solution.py:507
  36.7 3.3 %collective-permute-done.6.side_a_ref = f32[2,144,256]{2,1,0:T(8,128)S(1)} collective-permute-done((f32[2,144,256]{2,1,0:T(8,128)S(1)}, f32[2,144,256]{2,1,0:T(8,128)S(1)}, u32[]{:S(2)}, u32[]{:S(2)}) %collective-permute-start.6) | collective-permute-done | bytes 294944 | tf_op jit(solution)/shard_map/ppermute | solution.py:539
  40.0 0.8 %shard_map.179 = (f32[2,64,256]{2,1,0:T(8,128)S(1)}, f32[2,2,64,256]{3,2,1,0:T(8,128)S(1)}, f32[384,256]{1,0:T(8,128)S(1)}) custom-call(f32[2,144,256]{2,1,0:T(8,128)S(1)} %pad_maximum_fusion.here_ref, f32[2,144,256]{2,1,0:T(8,128)S(1)} %collective-permute-done.6.side_a_ref, f32[2,144,256]{2,1,0:T(8,128)S(1)} %collective-permute-done.7.side_b_ref, ...), custom_call_target="tpu_custom_call" | custom-call | flops 1000000000 | bytes 2260992 | tf_op jit(solution)/shard_map/pallas_call | solution.py:507
  40.8 0.1 collective-permute-start.8
  40.9 0.1 collective-permute-start.13
  41.0 5.9 %collective-permute-done.13.refs_8_ = f32[2,64,256]{2,1,0:T(8,128)S(1)} collective-permute-done((f32[2,64,256]{2,1,0:T(8,128)S(1)}, f32[2,64,256]{2,1,0:T(8,128)S(1)}, u32[]{:S(2)}, u32[]{:S(2)}) %collective-permute-start.13) | collective-permute-done | bytes 131104 | tf_op jit(solution)/shard_map/ppermute | solution.py:643
  46.9 0.9 %shard_map.182 = (f32[1,2,64,256]{3,2,1,0:T(8,128)}, f32[2,2,64,256]{3,2,1,0:T(8,128)}, f32[1,2,64,256]{3,2,1,0:T(8,128)}) custom-call(f32[2,64,256]{2,1,0:T(8,128)S(1)} %get-tuple-element.50.refs_0_, f32[2,2,64,256]{3,2,1,0:T(8,128)S(1)} %get-tuple-element.51.refs_1_, f32[384,256]{1,0:T(8,128)S(1)} %collective-permute-done.8.refs_2_, ...), custom_call_target="tpu_custom_call" | custom-call | flops 1000000 | bytes 2228224 | tf_op jit(solution)/shard_map/pallas_call | solution.py:507
  (15 shorter events, 0.1 us)
Async XLA Ops:
  1.6 9.3 %collective-permute-start.1 = (f32[136,256]{1,0:T(8,128)S(1)}, f32[136,256]{1,0:T(8,128)S(1)}, u32[]{:S(2)}, u32[]{:S(2)}) collective-permute-start(f32[136,256]{1,0:T(8,128)S(1)} %shard_map.175.plane_ref), channel_id=1, source_target_pairs={{4,8},{8,4},{5,9},{9,5},{6,10},{10,6},{7,11},{11,7},{20,24},{24,20... | collective-permute-start | bytes 417800 | tf_op jit(solution)/shard_map/ppermute | solution.py:539
  2.3 9.3 %collective-permute-start = (f32[136,256]{1,0:T(8,128)S(1)}, f32[136,256]{1,0:T(8,128)S(1)}, u32[]{:S(2)}, u32[]{:S(2)}) collective-permute-start(f32[136,256]{1,0:T(8,128)S(1)} %shard_map.175.plane_ref), channel_id=1, source_target_pairs={{0,4},{8,12},{4,0},{12,8},{1,5},{9,13},{5,1},{13,9},{2,6},{10,14},... | collective-permute-start | bytes 417800 | tf_op jit(solution)/shard_map/ppermute | solution.py:539
  11.6 7.8 %copy-start = (f32[1,2,64,256]{3,2,1,0:T(8,128)S(1)}, f32[1,2,64,256]{3,2,1,0:T(8,128)}, u32[]{:S(2)}) copy-start(f32[1,2,64,256]{3,2,1,0:T(8,128)} %refs_5_.2) | copy-start | bytes 393220
  11.6 7.8 %copy-start.1 = (f32[1,2,64,256]{3,2,1,0:T(8,128)S(1)}, f32[1,2,64,256]{3,2,1,0:T(8,128)}, u32[]{:S(2)}) copy-start(f32[1,2,64,256]{3,2,1,0:T(8,128)} %projected_ref.1) | copy-start | bytes 393220
  13.5 5.9 %collective-permute-start.2 = (f32[192,256]{1,0:T(8,128)S(1)}, f32[192,256]{1,0:T(8,128)S(1)}, u32[]{:S(2)}, u32[]{:S(2)}) collective-permute-start(f32[192,256]{1,0:T(8,128)S(1)} %get-tuple-element.42), channel_id=1, source_target_pairs={{0,4},{8,12},{4,0},{12,8},{1,5},{9,13},{5,1},{13,9},{2,6},{10,14},... | collective-permute-start | bytes 589832 | tf_op jit(solution)/shard_map/ppermute | solution.py:539
  15.3 4.0 %collective-permute-start.3 = (f32[192,256]{1,0:T(8,128)S(1)}, f32[192,256]{1,0:T(8,128)S(1)}, u32[]{:S(2)}, u32[]{:S(2)}) collective-permute-start(f32[192,256]{1,0:T(8,128)S(1)} %get-tuple-element.43), channel_id=1, source_target_pairs={{4,8},{8,4},{5,9},{9,5},{6,10},{10,6},{7,11},{11,7},{20,24},{24,20... | collective-permute-start | bytes 589832 | tf_op jit(solution)/shard_map/ppermute | solution.py:539
  16.0 1.2 %collective-permute-start.4 = (f32[8,256]{1,0:T(8,128)S(1)}, f32[8,256]{1,0:T(8,128)S(1)}, u32[]{:S(2)}, u32[]{:S(2)}) collective-permute-start(f32[8,256]{1,0:T(8,128)S(1)} %get-tuple-element.44.rays_ref), channel_id=1, source_target_pairs={{0,1},{1,0},{2,3},{3,2},{4,5},{5,4},{6,7},{7,6},{8,9},{9,8},{10,11... | collective-permute-start | bytes 24584 | tf_op jit(solution)/shard_map/ppermute | solution.py:542
  16.1 4.9 %collective-permute-start.9 = (f32[2,72,256]{2,1,0:T(8,128)S(1)}, f32[2,72,256]{2,1,0:T(8,128)S(1)}, u32[]{:S(2)}, u32[]{:S(2)}) collective-permute-start(f32[2,72,256]{2,1,0:T(8,128)S(1)} %get-tuple-element.53), channel_id=1, source_target_pairs={{0,1},{1,0},{2,3},{3,2},{4,5},{5,4},{6,7},{7,6},{8,9},{9,8},{10,11... | collective-permute-start | bytes 442376 | tf_op jit(solution)/shard_map/ppermute | solution.py:542
  16.6 4.4 %collective-permute-start.10 = (f32[2,72,256]{2,1,0:T(8,128)S(1)}, f32[2,72,256]{2,1,0:T(8,128)S(1)}, u32[]{:S(2)}, u32[]{:S(2)}) collective-permute-start(f32[2,72,256]{2,1,0:T(8,128)S(1)} %get-tuple-element.54), channel_id=1, source_target_pairs={{1,2},{2,1},{5,6},{6,5},{9,10},{10,9},{13,14},{14,13},{17,18},{18,... | collective-permute-start | bytes 442376 | tf_op jit(solution)/shard_map/ppermute | solution.py:591
  19.5 7.8 %collective-permute-start.5 = (f32[144,256]{1,0:T(8,128)S(1)}, f32[144,256]{1,0:T(8,128)S(1)}, u32[]{:S(2)}, u32[]{:S(2)}) collective-permute-start(f32[144,256]{1,0:T(8,128)S(1)} %get-tuple-element.45.refs_0_), channel_id=1, source_target_pairs={{0,2},{2,0},{1,3},{3,1},{4,6},{6,4},{5,7},{7,5},{8,10},{10,8},{9,1... | collective-permute-start | bytes 442376 | tf_op jit(solution)/shard_map/ppermute | solution.py:602
  21.6 12.4 %collective-permute-start.11 = (f32[2,2,64,256]{3,2,1,0:T(8,128)S(1)}, f32[2,2,64,256]{3,2,1,0:T(8,128)S(1)}, u32[]{:S(2)}, u32[]{:S(2)}) collective-permute-start(f32[2,2,64,256]{3,2,1,0:T(8,128)S(1)} %shard_map.180.base_ref.refs_3_), channel_id=1, source_target_pairs={{0,4},{4,8},{6,2},{8,12},{10,6},{14,10},{1,5},{5,9},{7,3},{9,13},{... | collective-permute-start | bytes 786440 | tf_op jit(solution)/shard_map/ppermute | solution.py:617
  27.3 6.7 %copy-start.2 = (s32[4,2]{0,1:T(2,128)S(1)}, s32[4,2]{0,1:T(2,128)}, u32[]{:S(2)}) copy-start(s32[4,2]{0,1:T(2,128)} %param.24) | copy-start | bytes 100
  27.3 6.6 %copy-start.3 = (f32[4,2]{0,1:T(2,128)S(1)}, f32[4,2]{0,1:T(2,128)}, u32[]{:S(2)}) copy-start(f32[4,2]{0,1:T(2,128)} %param.25) | copy-start | bytes 100
  27.3 9.4 %collective-permute-start.7 = (f32[2,144,256]{2,1,0:T(8,128)S(1)}, f32[2,144,256]{2,1,0:T(8,128)S(1)}, u32[]{:S(2)}, u32[]{:S(2)}) collective-permute-start(f32[2,144,256]{2,1,0:T(8,128)S(1)} %pad_maximum_fusion.here_ref), channel_id=1, source_target_pairs={{4,8},{8,4},{5,9},{9,5},{6,10},{10,6},{7,11},{11,7},{20,24},{24,20... | collective-permute-start | bytes 884744 | tf_op jit(solution)/shard_map/ppermute | solution.py:539
  28.0 11.9 %collective-permute-start.6 = (f32[2,144,256]{2,1,0:T(8,128)S(1)}, f32[2,144,256]{2,1,0:T(8,128)S(1)}, u32[]{:S(2)}, u32[]{:S(2)}) collective-permute-start(f32[2,144,256]{2,1,0:T(8,128)S(1)} %pad_maximum_fusion.here_ref), channel_id=1, source_target_pairs={{0,4},{8,12},{4,0},{12,8},{1,5},{9,13},{5,1},{13,9},{2,6},{10,14},... | collective-permute-start | bytes 884744 | tf_op jit(solution)/shard_map/ppermute | solution.py:539
  34.7 6.2 %collective-permute-start.12 = (f32[2,2,64,256]{3,2,1,0:T(8,128)S(1)}, f32[2,2,64,256]{3,2,1,0:T(8,128)S(1)}, u32[]{:S(2)}, u32[]{:S(2)}) collective-permute-start(f32[2,2,64,256]{3,2,1,0:T(8,128)S(1)} %get-tuple-element.56), channel_id=1, source_target_pairs={{0,1},{1,0},{2,3},{3,2},{4,5},{5,4},{6,7},{7,6},{8,9},{9,8},{10,11... | collective-permute-start | bytes 786440 | tf_op jit(solution)/shard_map/ppermute | solution.py:542
  40.8 6.1 %collective-permute-start.8 = (f32[384,256]{1,0:T(8,128)S(1)}, f32[384,256]{1,0:T(8,128)S(1)}, u32[]{:S(2)}, u32[]{:S(2)}) collective-permute-start(f32[384,256]{1,0:T(8,128)S(1)} %get-tuple-element.52), channel_id=1, source_target_pairs={{0,1},{1,0},{2,3},{3,2},{4,5},{5,4},{6,7},{7,6},{8,9},{9,8},{10,11... | collective-permute-start | bytes 1179656 | tf_op jit(solution)/shard_map/ppermute | solution.py:542
  40.9 6.0 %collective-permute-start.13 = (f32[2,64,256]{2,1,0:T(8,128)S(1)}, f32[2,64,256]{2,1,0:T(8,128)S(1)}, u32[]{:S(2)}, u32[]{:S(2)}) collective-permute-start(f32[2,64,256]{2,1,0:T(8,128)S(1)} %get-tuple-element.60), channel_id=1, source_target_pairs={{0,2},{2,0},{1,3},{3,1},{4,6},{6,4},{5,7},{7,5},{8,10},{10,8},{9,1... | collective-permute-start | bytes 393224 | tf_op jit(solution)/shard_map/ppermute | solution.py:643

commit v8 on v7

--- a/solution.py
+++ b/solution.py
@@ -82,11 +82,18 @@
         copy.wait()
 
 
+def has_second():
+    scan = lax.axis_index("scan")
+    return (scan > 0) & (scan < lax.axis_size("scan") - 1)
+
+
 def edges_of(plane_a_ref, plane_b_ref, number, width):
     even = scan_is_even()
     at = 2 * width + 2 * number
     first_a, last_a = plane_a_ref[at : at + 1], plane_a_ref[at + 1 : at + 2]
-    first_b, last_b = plane_b_ref[at : at + 1], plane_b_ref[at + 1 : at + 2]
+    first_b, last_b = (
+        jnp.where(has_second(), plane_b_ref[edge : edge + 1], 0.0) for edge in (at, at + 1)
+    )
     return (jnp.where(even, last_b, last_a), jnp.where(even, first_a, first_b))
 
 
@@ -186,7 +193,7 @@
         at = slice(part * width, (part + 1) * width)
         wide[part, width : 2 * width] = plane_ref[at]
         wide[part, pl.ds(at_a, width)] = plane_a_ref[at]
-        wide[part, pl.ds(at_b, width)] = plane_b_ref[at]
+        wide[part, pl.ds(at_b, width)] = jnp.where(has_second(), plane_b_ref[at], 0.0)
     forward = (forward_high_ref[...], forward_low_ref[...])
     inverse = (inverse_high_ref[...], inverse_low_ref[...])
     waves, masks = [], []
@@ -271,10 +278,11 @@
     own_ref, rim_a_ref, rim_b_ref, projected_ref, dual_ref, rays_ref, too_ref, object_ref, residual_ref
 ):
     width = own_ref.shape[1]
+    second = has_second()
     sums = [
         own_ref[part]
         + rim_a_ref[part * width : (part + 1) * width]
-        + rim_b_ref[part * width : (part + 1) * width]
+        + jnp.where(second, rim_b_ref[part * width : (part + 1) * width], 0.0)
         for part in range(3)
     ]
     for part in range(2):
@@ -295,6 +303,8 @@
     count = volume_ref.shape[1]
     margin = 8
     first_tile = tile_is_first()
+    place = lax.axis_index("angle") * 2 + lax.axis_index("tile")
+    bridged = (place > 0) & (place < 2 * lax.axis_size("angle") - 1)
     lanes = lax.broadcasted_iota(jnp.int32, (width, length), 1)
     first_lane = lanes == 0
     last_lane = lanes == length - 1
@@ -304,7 +314,7 @@
             padded[row + 1, margin : margin + width] = volume_ref[channel, row]
             padded[row + 1, margin - 1 : margin] = before
             padded[row + 1, margin + width : margin + width + 1] = after
-        row_a, row_b = row_a_ref[channel], row_b_ref[channel]
+        row_a, row_b = row_a_ref[channel], jnp.where(bridged, row_b_ref[channel], 0.0)
         for row, beside in (
             (0, jnp.where(first_tile, row_b, row_a)),
             (count + 1, jnp.where(first_tile, row_a, row_b)),
@@ -455,7 +465,9 @@
             at = slice(channel * width, (channel + 1) * width)
             wide[source, channel, width : 2 * width] = here_ref[source, at]
             wide[source, channel, pl.ds(at_a, width)] = side_a_ref[source, at]
-            wide[source, channel, pl.ds(at_b, width)] = side_b_ref[source, at]
+            wide[source, channel, pl.ds(at_b, width)] = jnp.where(
+                has_second(), side_b_ref[source, at], 0.0
+            )
     for channel in range(2):
         total = 0.0
         for source in range(columns):
@@ -531,12 +543,20 @@
     width, length = transmission.shape[2:]
     count = volume.shape[1]
     scans, columns, tiles = (lax.axis_size(axis) for axis in ("scan", "angle", "tile"))
-    rounds = [[(i, i + 1) for i in range(first, scans - 1, 2)] for first in (0, 1)]
-    both = [pairs + [(target, source) for source, target in pairs] for pairs in rounds]
+    assert scans % 2 == 0 and columns % 2 == 0 and tiles == 2
+    rounds = []
+    for first in (0, 1):
+        pairs = [(i, i + 1) for i in range(first, scans - 1, 2)]
+        route = [(s * columns + x, d * columns + x) for s, d in pairs for x in range(columns)]
+        route += [(target, source) for source, target in route]
+        ends = {i for i in range(scans)} - {i for pair in pairs for i in pair}
+        for scan in sorted(ends):
+            route += [(scan * columns + x, scan * columns + (x ^ 1)) for x in range(columns)]
+        rounds.append(route)
     swap = [(0, 1), (1, 0)]
 
     def exchange(block, number):
-        return lax.ppermute(block, "scan", both[number])
+        return lax.ppermute(block, ("scan", "angle"), rounds[number])
 
     def across(block):
         return lax.ppermute(block, "tile", swap)
@@ -587,6 +607,7 @@
     rim_a = exchange(rim_a, 0)
     rim_b = exchange(rim_b, 1)
     bridge = [(i * tiles + 1, (i + 1) * tiles) for i in range(columns - 1)]
+    bridge.append((0, columns * tiles - 1))
     bridge += [(target, source) for source, target in bridge]
     row_b = lax.ppermute(row_b, ("angle", "tile"), bridge)
     row_a = across(row_a)
@@ -607,13 +628,15 @@
         [(count + 2, width + 16, length), (width + 16, length)],
         10**7,
     )
-    lower = range(columns // 2)
     route = []
     for scan in range(scans):
         for column in range(columns):
-            target = scan + 1 if column in lower else scan - 1
-            if 0 <= target < scans:
-                route.append((scan * columns + column, target * columns + column))
+            lower = column < columns // 2
+            target = scan + 1 if lower else scan - 1
+            turned = column
+            if not 0 <= target < scans:
+                target, turned = scan, (column + columns // 2) % columns
+            route.append((scan * columns + column, target * columns + turned))
     beside = lax.ppermute(base, ("scan", "angle"), route)
     here = jnp.stack(by_column)
     side_a = exchange(here, 0)

time: 48 us -> 46.6 us (0.971)
  starting transfers between devices: 22.4 us -> 13.5 us
  waiting for transfers between devices: 13.9 us -> 21.5 us
    ppermute x1, starting transfers between devices: 5.7 us -> 0.14 us  [body(): beside = lax.ppermute(base, ('scan', 'angle'), route)]
    ppermute x6, starting transfers between devices: 13.7 us -> 10 us  [exchange(): return lax.ppermute(block, ('scan', 'angle'), rounds[number])]
    ppermute x1, waiting for transfers between devices: 1.92 us -> 5.01 us  [body(): beside = lax.ppermute(base, ('scan', 'angle'), route)]
    ppermute x1, waiting for transfers between devices: 0.01 us -> 1.96 us  [body(): by_column.append(lax.ppermute(residual, 'angle', turns[turn]))]
    ppermute x6, waiting for transfers between devices: 6.11 us -> 7.59 us  [exchange(): return lax.ppermute(block, ('scan', 'angle'), rounds[number])]
    ppermute x1, starting transfers between devices: 1.56 us -> 2.5 us  [body(): by_column.append(lax.ppermute(residual, 'angle', turns[turn]))]
    ppermute x4, waiting for transfers between devices: 0.01 us -> 0.52 us  [across(): return lax.ppermute(block, 'tile', swap)]
    ppermute x1, starting transfers between devices: 0.66 us -> 0.14 us  [body(): row_b = lax.ppermute(row_b, ('angle', 'tile'), bridge)]
  transfers between devices with their start and end apart: 14 -> 14, of which waited for: 5 -> 9; matrix products, arithmetic and copies ran while one was open for 0% -> 0% of each run, Pallas kernels for 13% -> 13%
where the time goes in v8:
time: 46.6 us; the launch traced here: 46.3 us
  waiting for transfers between devices  21.5 us (46%)
  starting transfers between devices  13.5 us (29%)
  Pallas kernels  9.9 us (21%)
  between operations  1.39 us (3%)
    ppermute x6, starting transfers between devices, exchange(): return lax.ppermute(block, ('scan', 'angle'), rounds[number])  10 us
    pallas_call x9, Pallas kernels, call(): pl.pallas_call(kernel, out_shape=outputs, in_specs=in_specs, out_specs=[V...  9.9 us
    ppermute x6, waiting for transfers between devices, exchange(): return lax.ppermute(block, ('scan', 'angle'), rounds[number])  7.59 us
    ppermute x1, waiting for transfers between devices, body(): spreads.append(lax.ppermute(keep[turn] + received[turn], 'angle', route))  5.87 us
    ppermute x1, waiting for transfers between devices, body(): beside = lax.ppermute(base, ('scan', 'angle'), route)  5.01 us
    ppermute x1, starting transfers between devices, body(): by_column.append(lax.ppermute(residual, 'angle', turns[turn]))  2.5 us
    ppermute x1, waiting for transfers between devices, body(): by_column.append(lax.ppermute(residual, 'angle', turns[turn]))  1.96 us
  transfers between devices with their start and end apart: 14, of which 9 were waited for; matrix products, arithmetic and copies ran while one was open for 0% of the time, Pallas kernels for 13%

profile of v8, /device:TPU:0, one launch (start us, length us, event | category | flops | bytes accessed | tf_op | source)
XLA Modules:
  0.0 46.3 jit_solution(2438522444725217457)
XLA Ops:
  0.6 1.0 %shard_map.175.plane_ref = f32[136,256]{1,0:T(8,128)S(1)} custom-call(f32[1,2,64,256]{3,2,1,0:T(8,128)} %plane_ref.1, f32[2,2,64,256]{3,2,1,0:T(8,128)} %volume_ref.1), custom_call_target="tpu_custom_call" | custom-call | flops 100000 | bytes 532480 | tf_op jit(solution)/shard_map/pallas_call | solution.py:519
  1.6 3.0 %collective-permute-start.1 = (f32[136,256]{1,0:T(8,128)S(1)}, f32[136,256]{1,0:T(8,128)S(1)}, u32[]{:S(2)}, u32[]{:S(2)}) collective-permute-start(f32[136,256]{1,0:T(8,128)S(1)} %shard_map.175.plane_ref), channel_id=1, source_target_pairs={{4,8},{6,10},{8,4},{10,6},{0,2},{2,0},{12,14},{14,12},{5,9},{7,11}... | collective-permute-start | bytes 417800 | tf_op jit(solution)/shard_map/ppermute | solution.py:559
  4.6 1.7 %collective-permute-start = (f32[136,256]{1,0:T(8,128)S(1)}, f32[136,256]{1,0:T(8,128)S(1)}, u32[]{:S(2)}, u32[]{:S(2)}) collective-permute-start(f32[136,256]{1,0:T(8,128)S(1)} %shard_map.175.plane_ref), channel_id=1, source_target_pairs={{0,4},{2,6},{8,12},{10,14},{4,0},{6,2},{12,8},{14,10},{1,5},{3,7},... | collective-permute-start | bytes 417800 | tf_op jit(solution)/shard_map/ppermute | solution.py:559
  6.9 2.0 %shard_map.174 = (f32[4,2,128,128]{3,2,1,0:T(8,128)S(1)}, f32[1,192,256]{2,1,0:T(8,128)S(1)}, s32[4,8,128]{2,1,0:T(8,128)S(1)}, f32[8,256]{1,0:T(8,128)S(1)}, f3...) custom-call(s32[1,1]{1,0:T(1,128)S(6)} %copy.19.count_ref, ...), custom_call_target="tpu_custom_call" | custom-call | flops 10000000 | bytes 1794048 | tf_op jit(solution)/shard_map/pallas_call | solution.py:519
  9.0 0.0 collective-permute-done.1.plane_b_ref
  9.0 0.8 %collective-permute-done.plane_a_ref = f32[136,256]{1,0:T(8,128)S(1)} collective-permute-done((f32[136,256]{1,0:T(8,128)S(1)}, f32[136,256]{1,0:T(8,128)S(1)}, u32[]{:S(2)}, u32[]{:S(2)}) %collective-permute-start) | collective-permute-done | bytes 139296 | tf_op jit(solution)/shard_map/ppermute | solution.py:559
  9.8 1.9 %shard_map.176 = (f32[3,64,256]{2,1,0:T(8,128)S(1)}, f32[192,256]{1,0:T(8,128)S(1)}, f32[192,256]{1,0:T(8,128)S(1)}, f32[2,72,256]{2,1,0:T(8,128)S(1)}, f32[2,72,256]{2,1,0:T(8,128)S(1)}) custom-call(f32[4,2,128,128]{3,2,1,0:T(8,128)S(1)} %get-tuple-element.32.probes_ref, f32[1,192,256]{2,1,0:T(8,128)S(1)} %get-tuple-element.33.density_ref, ...), custom_call_target="tpu_custom_call" | custom-call | flops 1000000000 | bytes 2957312 | tf_op jit(solution)/shard_map/pallas_call | solution.py:519
  11.7 1.7 %collective-permute-start.2 = (f32[192,256]{1,0:T(8,128)S(1)}, f32[192,256]{1,0:T(8,128)S(1)}, u32[]{:S(2)}, u32[]{:S(2)}) collective-permute-start(f32[192,256]{1,0:T(8,128)S(1)} %get-tuple-element.42), channel_id=1, source_target_pairs={{0,4},{2,6},{8,12},{10,14},{4,0},{6,2},{12,8},{14,10},{1,5},{3,7},... | collective-permute-start | bytes 589832 | tf_op jit(solution)/shard_map/ppermute | solution.py:559
  13.4 1.5 %collective-permute-start.3 = (f32[192,256]{1,0:T(8,128)S(1)}, f32[192,256]{1,0:T(8,128)S(1)}, u32[]{:S(2)}, u32[]{:S(2)}) collective-permute-start(f32[192,256]{1,0:T(8,128)S(1)} %get-tuple-element.43), channel_id=1, source_target_pairs={{4,8},{6,10},{8,4},{10,6},{0,2},{2,0},{12,14},{14,12},{5,9},{7,11}... | collective-permute-start | bytes 589832 | tf_op jit(solution)/shard_map/ppermute | solution.py:559
  14.9 0.5 %collective-permute-start.9 = (f32[2,72,256]{2,1,0:T(8,128)S(1)}, f32[2,72,256]{2,1,0:T(8,128)S(1)}, u32[]{:S(2)}, u32[]{:S(2)}) collective-permute-start(f32[2,72,256]{2,1,0:T(8,128)S(1)} %get-tuple-element.53), channel_id=1, source_target_pairs={{0,1},{1,0},{2,3},{3,2},{4,5},{5,4},{6,7},{7,6},{8,9},{9,8},{10,11... | collective-permute-start | bytes 442376 | tf_op jit(solution)/shard_map/ppermute | solution.py:562
  15.4 0.1 collective-permute-start.10
  15.6 0.5 %collective-permute-done.4.too_ref = f32[8,256]{1,0:T(8,128)S(1)} collective-permute-done((f32[8,256]{1,0:T(8,128)S(1)}, f32[8,256]{1,0:T(8,128)S(1)}, u32[]{:S(2)}, u32[]{:S(2)}) %collective-permute-start.4) | collective-permute-done | bytes 8224 | tf_op jit(solution)/shard_map/ppermute | solution.py:562
  16.1 1.3 %collective-permute-done.2.rim_a_ref = f32[192,256]{1,0:T(8,128)S(1)} collective-permute-done((f32[192,256]{1,0:T(8,128)S(1)}, f32[192,256]{1,0:T(8,128)S(1)}, u32[]{:S(2)}, u32[]{:S(2)}) %collective-permute-start.2) | collective-permute-done | bytes 196640 | tf_op jit(solution)/shard_map/ppermute | solution.py:559
  17.4 2.3 %collective-permute-done.3.rim_b_ref = f32[192,256]{1,0:T(8,128)S(1)} collective-permute-done((f32[192,256]{1,0:T(8,128)S(1)}, f32[192,256]{1,0:T(8,128)S(1)}, u32[]{:S(2)}, u32[]{:S(2)}) %collective-permute-start.3) | collective-permute-done | bytes 196640 | tf_op jit(solution)/shard_map/ppermute | solution.py:559
  19.8 0.1 shard_map.177
  19.9 2.5 %collective-permute-start.5 = (f32[144,256]{1,0:T(8,128)S(1)}, f32[144,256]{1,0:T(8,128)S(1)}, u32[]{:S(2)}, u32[]{:S(2)}) collective-permute-start(f32[144,256]{1,0:T(8,128)S(1)} %get-tuple-element.45.refs_0_), channel_id=1, source_target_pairs={{0,2},{2,0},{1,3},{3,1},{4,6},{6,4},{5,7},{7,5},{8,10},{10,8},{9,1... | collective-permute-start | bytes 442376 | tf_op jit(solution)/shard_map/ppermute | solution.py:623
  22.4 0.5 %collective-permute-done.10.row_b_ref = f32[2,72,256]{2,1,0:T(8,128)S(1)} collective-permute-done((f32[2,72,256]{2,1,0:T(8,128)S(1)}, f32[2,72,256]{2,1,0:T(8,128)S(1)}, u32[]{:S(2)}, u32[]{:S(2)}) %collective-permute-start.10) | collective-permute-done | bytes 147488 | tf_op jit(solution)/shard_map/ppermute | solution.py:612
  22.9 0.5 %shard_map.180.base_ref.refs_3_ = f32[2,2,64,256]{3,2,1,0:T(8,128)S(1)} custom-call(f32[2,2,64,256]{3,2,1,0:T(8,128)S(1)} %get-tuple-element.36.volume_ref, f32[136,256]{1,0:T(8,128)S(1)} %collective-permute-done.plane_a_ref, f32[136,256]{1,0:T(8,128)S(1)} %collective-permute-done.1.plane_b_ref, f32[2,72,256]{2,1,0:T(8,128)S(1)} %collective-permute-done.9.row_a_ref, ...), custom_call_target="tpu_custom_call" | custom-call | flops 10000000 | bytes 1097728 | tf_op jit(solution)/shard_map/pallas_call | solution.py:519
  23.4 0.1 collective-permute-start.11
  23.5 2.0 %collective-permute-done.5.refs_1_ = f32[144,256]{1,0:T(8,128)S(1)} collective-permute-done((f32[144,256]{1,0:T(8,128)S(1)}, f32[144,256]{1,0:T(8,128)S(1)}, u32[]{:S(2)}, u32[]{:S(2)}) %collective-permute-start.5) | collective-permute-done | bytes 147488 | tf_op jit(solution)/shard_map/ppermute | solution.py:623
  25.5 2.1 %collective-permute-start.7 = (f32[2,144,256]{2,1,0:T(8,128)S(1)}, f32[2,144,256]{2,1,0:T(8,128)S(1)}, u32[]{:S(2)}, u32[]{:S(2)}) collective-permute-start(f32[2,144,256]{2,1,0:T(8,128)S(1)} %pad_maximum_fusion.here_ref), channel_id=1, source_target_pairs={{4,8},{6,10},{8,4},{10,6},{0,2},{2,0},{12,14},{14,12},{5,9},{7,11}... | collective-permute-start | bytes 884744 | tf_op jit(solution)/shard_map/ppermute | solution.py:559
  27.6 5.0 %collective-permute-done.11.beside_ref = f32[2,2,64,256]{3,2,1,0:T(8,128)S(1)} collective-permute-done((f32[2,2,64,256]{3,2,1,0:T(8,128)S(1)}, f32[2,2,64,256]{3,2,1,0:T(8,128)S(1)}, u32[]{:S(2)}, u32[]{:S(2)}) %collective-permute-start.11) | collective-permute-done | bytes 262176 | tf_op jit(solution)/shard_map/ppermute | solution.py:640
  32.6 0.8 %shard_map.181 = (f32[2,2,64,256]{3,2,1,0:T(8,128)S(1)}, f32[2,2,64,256]{3,2,1,0:T(8,128)S(1)}) custom-call(s32[2,4]{1,0:T(2,128)S(1)} %bitcast.13, f32[2,4]{1,0:T(2,128)S(1)} %bitcast.15, f32[2,2,64,256]{3,2,1,0:T(8,128)S(1)} %shard_map.180.base_ref.refs_3_, f32[2,2,64,256]{3,2,1,0:T(8,128)S(1)} %collective-permute-done.11.beside_ref), custom_call_target="tpu_custom_call" | custom-call | flops 10000000 | bytes 1048576 | tf_op jit(solution)/shard_map/pallas_call | solution.py:519
  33.4 0.1 collective-permute-start.12
  33.5 1.9 %shard_map.178 = (bf16[2,384,192]{2,1,0:T(8,128)(2,1)S(1)}, bf16[2,384,192]{2,1,0:T(8,128)(2,1)S(1)}, f32[1,2,64,256]{3,2,1,0:T(8,128)}) custom-call(f32[144,256]{1,0:T(8,128)S(1)} %get-tuple-element.45.refs_0_, f32[144,256]{1,0:T(8,128)S(1)} %collective-permute-done.5.refs_1_, f32[1,2,64,256]{3,2,1,0:T(8,128)S(1)} %get-tuple-element.46.refs_2_.refs_4_), custom_call_target="tpu_custom_call" | custom-call | flops 100000000 | bytes 1736704 | tf_op jit(solution)/shard_map/pallas_call | solution.py:519
  35.4 3.1 %collective-permute-done.7.side_b_ref = f32[2,144,256]{2,1,0:T(8,128)S(1)} collective-permute-done((f32[2,144,256]{2,1,0:T(8,128)S(1)}, f32[2,144,256]{2,1,0:T(8,128)S(1)}, u32[]{:S(2)}, u32[]{:S(2)}) %collective-permute-start.7) | collective-permute-done | bytes 294944 | tf_op jit(solution)/shard_map/ppermute | solution.py:559
  38.5 0.9 %shard_map.179 = (f32[2,64,256]{2,1,0:T(8,128)S(1)}, f32[2,2,64,256]{3,2,1,0:T(8,128)S(1)}, f32[384,256]{1,0:T(8,128)S(1)}) custom-call(f32[2,144,256]{2,1,0:T(8,128)S(1)} %pad_maximum_fusion.here_ref, f32[2,144,256]{2,1,0:T(8,128)S(1)} %collective-permute-done.6.side_a_ref, f32[2,144,256]{2,1,0:T(8,128)S(1)} %collective-permute-done.7.side_b_ref, ...), custom_call_target="tpu_custom_call" | custom-call | flops 1000000000 | bytes 2260992 | tf_op jit(solution)/shard_map/pallas_call | solution.py:519
  39.4 0.1 collective-permute-start.8
  39.5 0.0 collective-permute-done.12
  39.5 0.1 collective-permute-start.13
  39.6 5.9 %collective-permute-done.13.refs_8_ = f32[2,64,256]{2,1,0:T(8,128)S(1)} collective-permute-done((f32[2,64,256]{2,1,0:T(8,128)S(1)}, f32[2,64,256]{2,1,0:T(8,128)S(1)}, u32[]{:S(2)}, u32[]{:S(2)}) %collective-permute-start.13) | collective-permute-done | bytes 131104 | tf_op jit(solution)/shard_map/ppermute | solution.py:666
  45.5 0.9 %shard_map.182 = (f32[1,2,64,256]{3,2,1,0:T(8,128)}, f32[2,2,64,256]{3,2,1,0:T(8,128)}, f32[1,2,64,256]{3,2,1,0:T(8,128)}) custom-call(f32[2,64,256]{2,1,0:T(8,128)S(1)} %get-tuple-element.50.refs_0_, f32[2,2,64,256]{3,2,1,0:T(8,128)S(1)} %get-tuple-element.51.refs_1_, f32[384,256]{1,0:T(8,128)S(1)} %collective-permute-done.8.refs_2_, ...), custom_call_target="tpu_custom_call" | custom-call | flops 1000000 | bytes 2228224 | tf_op jit(solution)/shard_map/pallas_call | solution.py:519
  (15 shorter events, 0.1 us)
Async XLA Ops:
  1.6 7.4 %collective-permute-start.1 = (f32[136,256]{1,0:T(8,128)S(1)}, f32[136,256]{1,0:T(8,128)S(1)}, u32[]{:S(2)}, u32[]{:S(2)}) collective-permute-start(f32[136,256]{1,0:T(8,128)S(1)} %shard_map.175.plane_ref), channel_id=1, source_target_pairs={{4,8},{6,10},{8,4},{10,6},{0,2},{2,0},{12,14},{14,12},{5,9},{7,11}... | collective-permute-start | bytes 417800 | tf_op jit(solution)/shard_map/ppermute | solution.py:559
  4.6 5.1 %collective-permute-start = (f32[136,256]{1,0:T(8,128)S(1)}, f32[136,256]{1,0:T(8,128)S(1)}, u32[]{:S(2)}, u32[]{:S(2)}) collective-permute-start(f32[136,256]{1,0:T(8,128)S(1)} %shard_map.175.plane_ref), channel_id=1, source_target_pairs={{0,4},{2,6},{8,12},{10,14},{4,0},{6,2},{12,8},{14,10},{1,5},{3,7},... | collective-permute-start | bytes 417800 | tf_op jit(solution)/shard_map/ppermute | solution.py:559
  9.8 10.0 %copy-start = (f32[1,2,64,256]{3,2,1,0:T(8,128)S(1)}, f32[1,2,64,256]{3,2,1,0:T(8,128)}, u32[]{:S(2)}) copy-start(f32[1,2,64,256]{3,2,1,0:T(8,128)} %refs_5_.2) | copy-start | bytes 393220
  9.8 10.0 %copy-start.1 = (f32[1,2,64,256]{3,2,1,0:T(8,128)S(1)}, f32[1,2,64,256]{3,2,1,0:T(8,128)}, u32[]{:S(2)}) copy-start(f32[1,2,64,256]{3,2,1,0:T(8,128)} %projected_ref.1) | copy-start | bytes 393220
  11.7 5.7 %collective-permute-start.2 = (f32[192,256]{1,0:T(8,128)S(1)}, f32[192,256]{1,0:T(8,128)S(1)}, u32[]{:S(2)}, u32[]{:S(2)}) collective-permute-start(f32[192,256]{1,0:T(8,128)S(1)} %get-tuple-element.42), channel_id=1, source_target_pairs={{0,4},{2,6},{8,12},{10,14},{4,0},{6,2},{12,8},{14,10},{1,5},{3,7},... | collective-permute-start | bytes 589832 | tf_op jit(solution)/shard_map/ppermute | solution.py:559
  13.4 6.4 %collective-permute-start.3 = (f32[192,256]{1,0:T(8,128)S(1)}, f32[192,256]{1,0:T(8,128)S(1)}, u32[]{:S(2)}, u32[]{:S(2)}) collective-permute-start(f32[192,256]{1,0:T(8,128)S(1)} %get-tuple-element.43), channel_id=1, source_target_pairs={{4,8},{6,10},{8,4},{10,6},{0,2},{2,0},{12,14},{14,12},{5,9},{7,11}... | collective-permute-start | bytes 589832 | tf_op jit(solution)/shard_map/ppermute | solution.py:559
  14.9 1.2 %collective-permute-start.4 = (f32[8,256]{1,0:T(8,128)S(1)}, f32[8,256]{1,0:T(8,128)S(1)}, u32[]{:S(2)}, u32[]{:S(2)}) collective-permute-start(f32[8,256]{1,0:T(8,128)S(1)} %get-tuple-element.44.rays_ref), channel_id=1, source_target_pairs={{0,1},{1,0},{2,3},{3,2},{4,5},{5,4},{6,7},{7,6},{8,9},{9,8},{10,11... | collective-permute-start | bytes 24584 | tf_op jit(solution)/shard_map/ppermute | solution.py:562
  14.9 7.4 %collective-permute-start.9 = (f32[2,72,256]{2,1,0:T(8,128)S(1)}, f32[2,72,256]{2,1,0:T(8,128)S(1)}, u32[]{:S(2)}, u32[]{:S(2)}) collective-permute-start(f32[2,72,256]{2,1,0:T(8,128)S(1)} %get-tuple-element.53), channel_id=1, source_target_pairs={{0,1},{1,0},{2,3},{3,2},{4,5},{5,4},{6,7},{7,6},{8,9},{9,8},{10,11... | collective-permute-start | bytes 442376 | tf_op jit(solution)/shard_map/ppermute | solution.py:562
  15.4 7.5 %collective-permute-start.10 = (f32[2,72,256]{2,1,0:T(8,128)S(1)}, f32[2,72,256]{2,1,0:T(8,128)S(1)}, u32[]{:S(2)}, u32[]{:S(2)}) collective-permute-start(f32[2,72,256]{2,1,0:T(8,128)S(1)} %get-tuple-element.54), channel_id=1, source_target_pairs={{1,2},{0,3},{2,1},{3,0},{5,6},{4,7},{6,5},{7,4},{9,10},{8,11},{10,... | collective-permute-start | bytes 442376 | tf_op jit(solution)/shard_map/ppermute | solution.py:612
  19.9 5.6 %collective-permute-start.5 = (f32[144,256]{1,0:T(8,128)S(1)}, f32[144,256]{1,0:T(8,128)S(1)}, u32[]{:S(2)}, u32[]{:S(2)}) collective-permute-start(f32[144,256]{1,0:T(8,128)S(1)} %get-tuple-element.45.refs_0_), channel_id=1, source_target_pairs={{0,2},{2,0},{1,3},{3,1},{4,6},{6,4},{5,7},{7,5},{8,10},{10,8},{9,1... | collective-permute-start | bytes 442376 | tf_op jit(solution)/shard_map/ppermute | solution.py:623
  23.4 9.2 %collective-permute-start.11 = (f32[2,2,64,256]{3,2,1,0:T(8,128)S(1)}, f32[2,2,64,256]{3,2,1,0:T(8,128)S(1)}, u32[]{:S(2)}, u32[]{:S(2)}) collective-permute-start(f32[2,2,64,256]{3,2,1,0:T(8,128)S(1)} %shard_map.180.base_ref.refs_3_), channel_id=1, source_target_pairs={{0,4},{2,0},{4,8},{6,2},{8,12},{10,6},{12,14},{14,10},{1,5},{3,1},... | collective-permute-start | bytes 786440 | tf_op jit(solution)/shard_map/ppermute | solution.py:640
  25.5 7.1 %copy-start.2 = (s32[4,2]{0,1:T(2,128)S(1)}, s32[4,2]{0,1:T(2,128)}, u32[]{:S(2)}) copy-start(s32[4,2]{0,1:T(2,128)} %param.24) | copy-start | bytes 100
  25.5 7.1 %copy-start.3 = (f32[4,2]{0,1:T(2,128)S(1)}, f32[4,2]{0,1:T(2,128)}, u32[]{:S(2)}) copy-start(f32[4,2]{0,1:T(2,128)} %param.25) | copy-start | bytes 100
  25.5 13.0 %collective-permute-start.7 = (f32[2,144,256]{2,1,0:T(8,128)S(1)}, f32[2,144,256]{2,1,0:T(8,128)S(1)}, u32[]{:S(2)}, u32[]{:S(2)}) collective-permute-start(f32[2,144,256]{2,1,0:T(8,128)S(1)} %pad_maximum_fusion.here_ref), channel_id=1, source_target_pairs={{4,8},{6,10},{8,4},{10,6},{0,2},{2,0},{12,14},{14,12},{5,9},{7,11}... | collective-permute-start | bytes 884744 | tf_op jit(solution)/shard_map/ppermute | solution.py:559
  27.6 10.9 %collective-permute-start.6 = (f32[2,144,256]{2,1,0:T(8,128)S(1)}, f32[2,144,256]{2,1,0:T(8,128)S(1)}, u32[]{:S(2)}, u32[]{:S(2)}) collective-permute-start(f32[2,144,256]{2,1,0:T(8,128)S(1)} %pad_maximum_fusion.here_ref), channel_id=1, source_target_pairs={{0,4},{2,6},{8,12},{10,14},{4,0},{6,2},{12,8},{14,10},{1,5},{3,7},... | collective-permute-start | bytes 884744 | tf_op jit(solution)/shard_map/ppermute | solution.py:559
  33.4 6.1 %collective-permute-start.12 = (f32[2,2,64,256]{3,2,1,0:T(8,128)S(1)}, f32[2,2,64,256]{3,2,1,0:T(8,128)S(1)}, u32[]{:S(2)}, u32[]{:S(2)}) collective-permute-start(f32[2,2,64,256]{3,2,1,0:T(8,128)S(1)} %get-tuple-element.56), channel_id=1, source_target_pairs={{0,1},{1,0},{2,3},{3,2},{4,5},{5,4},{6,7},{7,6},{8,9},{9,8},{10,11... | collective-permute-start | bytes 786440 | tf_op jit(solution)/shard_map/ppermute | solution.py:562
  39.4 6.1 %collective-permute-start.8 = (f32[384,256]{1,0:T(8,128)S(1)}, f32[384,256]{1,0:T(8,128)S(1)}, u32[]{:S(2)}, u32[]{:S(2)}) collective-permute-start(f32[384,256]{1,0:T(8,128)S(1)} %get-tuple-element.52), channel_id=1, source_target_pairs={{0,1},{1,0},{2,3},{3,2},{4,5},{5,4},{6,7},{7,6},{8,9},{9,8},{10,11... | collective-permute-start | bytes 1179656 | tf_op jit(solution)/shard_map/ppermute | solution.py:562
  39.5 6.0 %collective-permute-start.13 = (f32[2,64,256]{2,1,0:T(8,128)S(1)}, f32[2,64,256]{2,1,0:T(8,128)S(1)}, u32[]{:S(2)}, u32[]{:S(2)}) collective-permute-start(f32[2,64,256]{2,1,0:T(8,128)S(1)} %get-tuple-element.60), channel_id=1, source_target_pairs={{0,2},{2,0},{1,3},{3,1},{4,6},{6,4},{5,7},{7,5},{8,10},{10,8},{9,1... | collective-permute-start | bytes 393224 | tf_op jit(solution)/shard_map/ppermute | solution.py:666

commit v9 on v8

--- a/solution.py
+++ b/solution.py
@@ -543,20 +543,20 @@
     width, length = transmission.shape[2:]
     count = volume.shape[1]
     scans, columns, tiles = (lax.axis_size(axis) for axis in ("scan", "angle", "tile"))
-    assert scans % 2 == 0 and columns % 2 == 0 and tiles == 2
+    assert scans % 2 == 0 and columns % 2 == 0 and tiles == 2 and lax.axis_size("groups") % 2 == 0
     rounds = []
     for first in (0, 1):
         pairs = [(i, i + 1) for i in range(first, scans - 1, 2)]
-        route = [(s * columns + x, d * columns + x) for s, d in pairs for x in range(columns)]
+        route = [(s * tiles + t, d * tiles + t) for s, d in pairs for t in range(tiles)]
         route += [(target, source) for source, target in route]
         ends = {i for i in range(scans)} - {i for pair in pairs for i in pair}
         for scan in sorted(ends):
-            route += [(scan * columns + x, scan * columns + (x ^ 1)) for x in range(columns)]
+            route += [(scan * tiles + t, scan * tiles + 1 - t) for t in range(tiles)]
         rounds.append(route)
     swap = [(0, 1), (1, 0)]
 
     def exchange(block, number):
-        return lax.ppermute(block, ("scan", "angle"), rounds[number])
+        return lax.ppermute(block, ("scan", "tile"), rounds[number])
 
     def across(block):
         return lax.ppermute(block, "tile", swap)
@@ -606,10 +606,16 @@
     )
     rim_a = exchange(rim_a, 0)
     rim_b = exchange(rim_b, 1)
-    bridge = [(i * tiles + 1, (i + 1) * tiles) for i in range(columns - 1)]
-    bridge.append((0, columns * tiles - 1))
-    bridge += [(target, source) for source, target in bridge]
-    row_b = lax.ppermute(row_b, ("angle", "tile"), bridge)
+    per_group, groups = columns * tiles, lax.axis_size("groups")
+    bridge = []
+    for group in range(groups):
+        at = group * per_group
+        pairs = [(at + i * tiles + 1, at + (i + 1) * tiles) for i in range(columns - 1)]
+        bridge += pairs + [(target, source) for source, target in pairs]
+        beyond = (groups - 1 - group) * per_group
+        for outer in (0, per_group - 1):
+            bridge.append((at + outer, beyond + outer))
+    row_b = lax.ppermute(row_b, ("groups", "angle", "tile"), bridge)
     row_a = across(row_a)
     updated, residual = call(
         fold_kernel,

time: 46.6 us -> 42 us (0.901)
  waiting for transfers between devices: 21.5 us -> 10.9 us
  starting transfers between devices: 13.5 us -> 19.5 us
    ppermute x7, waiting for transfers between devices: 8.1 us -> 4.67 us  [the longest x6 4.66 us: exchange(): return lax.ppermute(block, ('scan', 'tile'), rounds[number])]
    ppermute x1, waiting for transfers between devices: 5.01 us -> 1.77 us  [body(): beside = lax.ppermute(base, ('scan', 'angle'), route)]
    ppermute x1, starting transfers between devices: 0.14 us -> 2.89 us  [body(): beside = lax.ppermute(base, ('scan', 'angle'), route)]
    ppermute x7, starting transfers between devices: 10.1 us -> 12.7 us  [the longest x6 11.2 us: exchange(): return lax.ppermute(block, ('scan', 'tile'), rounds[number])]
    ppermute x1, waiting for transfers between devices: 1.96 us -> 0.24 us  [body(): by_column.append(lax.ppermute(residual, 'angle', turns[turn]))]
    ppermute x1, starting transfers between devices: 0.07 us -> 1.72 us  [body(): spreads.append(lax.ppermute(keep[turn] + received[turn], 'angle', route))]
    ppermute x1, waiting for transfers between devices: 5.87 us -> 4.23 us  [body(): spreads.append(lax.ppermute(keep[turn] + received[turn], 'angle', route))]
    ppermute x1, starting transfers between devices: 2.5 us -> 1.56 us  [body(): by_column.append(lax.ppermute(residual, 'angle', turns[turn]))]
  transfers between devices with their start and end apart: 14 -> 14, of which waited for: 9 -> 6; matrix products, arithmetic and copies ran while one was open for 0% -> 0% of each run, Pallas kernels for 13% -> 15%
where the time goes in v9:
time: 42 us; the launch traced here: 41.8 us
  starting transfers between devices  19.5 us (46%)
  waiting for transfers between devices  10.9 us (26%)
  Pallas kernels  9.91 us (24%)
  between operations  1.39 us (3%)
    ppermute x6, starting transfers between devices, exchange(): return lax.ppermute(block, ('scan', 'tile'), rounds[number])  11.2 us
    pallas_call x9, Pallas kernels, call(): pl.pallas_call(kernel, out_shape=outputs, in_specs=in_specs, out_specs=[V...  9.91 us
    ppermute x6, waiting for transfers between devices, exchange(): return lax.ppermute(block, ('scan', 'tile'), rounds[number])  4.66 us
    ppermute x1, waiting for transfers between devices, body(): spreads.append(lax.ppermute(keep[turn] + received[turn], 'angle', route))  4.23 us
    ppermute x1, starting transfers between devices, body(): beside = lax.ppermute(base, ('scan', 'angle'), route)  2.89 us
    ppermute x1, waiting for transfers between devices, body(): beside = lax.ppermute(base, ('scan', 'angle'), route)  1.77 us
    ppermute x1, starting transfers between devices, body(): spreads.append(lax.ppermute(keep[turn] + received[turn], 'angle', route))  1.72 us
    ppermute x1, starting transfers between devices, body(): by_column.append(lax.ppermute(residual, 'angle', turns[turn]))  1.56 us
  transfers between devices with their start and end apart: 14, of which 6 were waited for; matrix products, arithmetic and copies ran while one was open for 0% of the time, Pallas kernels for 15%

profile of v9, /device:TPU:0, one launch (start us, length us, event | category | flops | bytes accessed | tf_op | source)
XLA Modules:
  0.0 41.8 jit_solution(3868168036839029890)
XLA Ops:
  0.6 1.0 %shard_map.175.plane_ref = f32[136,256]{1,0:T(8,128)S(1)} custom-call(f32[1,2,64,256]{3,2,1,0:T(8,128)} %plane_ref.1, f32[2,2,64,256]{3,2,1,0:T(8,128)} %volume_ref.1), custom_call_target="tpu_custom_call" | custom-call | flops 100000 | bytes 532480 | tf_op jit(solution)/shard_map/pallas_call | solution.py:519
  1.6 0.6 %collective-permute-start.1 = (f32[136,256]{1,0:T(8,128)S(1)}, f32[136,256]{1,0:T(8,128)S(1)}, u32[]{:S(2)}, u32[]{:S(2)}) collective-permute-start(f32[136,256]{1,0:T(8,128)S(1)} %shard_map.175.plane_ref), channel_id=1, source_target_pairs={{4,8},{5,9},{8,4},{9,5},{0,1},{1,0},{12,13},{13,12},{6,10},{7,11},... | collective-permute-start | bytes 417800 | tf_op jit(solution)/shard_map/ppermute | solution.py:559
  2.2 4.1 %collective-permute-start = (f32[136,256]{1,0:T(8,128)S(1)}, f32[136,256]{1,0:T(8,128)S(1)}, u32[]{:S(2)}, u32[]{:S(2)}) collective-permute-start(f32[136,256]{1,0:T(8,128)S(1)} %shard_map.175.plane_ref), channel_id=1, source_target_pairs={{0,4},{1,5},{8,12},{9,13},{4,0},{5,1},{12,8},{13,9},{2,6},{3,7},{1... | collective-permute-start | bytes 417800 | tf_op jit(solution)/shard_map/ppermute | solution.py:559
  6.9 2.0 %shard_map.174 = (f32[4,2,128,128]{3,2,1,0:T(8,128)S(1)}, f32[1,192,256]{2,1,0:T(8,128)S(1)}, s32[4,8,128]{2,1,0:T(8,128)S(1)}, f32[8,256]{1,0:T(8,128)S(1)}, f3...) custom-call(s32[1,1]{1,0:T(1,128)S(6)} %copy.19.count_ref, ...), custom_call_target="tpu_custom_call" | custom-call | flops 10000000 | bytes 1794048 | tf_op jit(solution)/shard_map/pallas_call | solution.py:519
  9.0 0.0 collective-permute-done.1.plane_b_ref
  9.0 0.7 %collective-permute-done.plane_a_ref = f32[136,256]{1,0:T(8,128)S(1)} collective-permute-done((f32[136,256]{1,0:T(8,128)S(1)}, f32[136,256]{1,0:T(8,128)S(1)}, u32[]{:S(2)}, u32[]{:S(2)}) %collective-permute-start) | collective-permute-done | bytes 139296 | tf_op jit(solution)/shard_map/ppermute | solution.py:559
  9.7 1.9 %shard_map.176 = (f32[3,64,256]{2,1,0:T(8,128)S(1)}, f32[192,256]{1,0:T(8,128)S(1)}, f32[192,256]{1,0:T(8,128)S(1)}, f32[2,72,256]{2,1,0:T(8,128)S(1)}, f32[2,72,256]{2,1,0:T(8,128)S(1)}) custom-call(f32[4,2,128,128]{3,2,1,0:T(8,128)S(1)} %get-tuple-element.32.probes_ref, f32[1,192,256]{2,1,0:T(8,128)S(1)} %get-tuple-element.33.density_ref, ...), custom_call_target="tpu_custom_call" | custom-call | flops 1000000000 | bytes 2957312 | tf_op jit(solution)/shard_map/pallas_call | solution.py:519
  11.6 1.8 %collective-permute-start.2 = (f32[192,256]{1,0:T(8,128)S(1)}, f32[192,256]{1,0:T(8,128)S(1)}, u32[]{:S(2)}, u32[]{:S(2)}) collective-permute-start(f32[192,256]{1,0:T(8,128)S(1)} %get-tuple-element.42), channel_id=1, source_target_pairs={{0,4},{1,5},{8,12},{9,13},{4,0},{5,1},{12,8},{13,9},{2,6},{3,7},{1... | collective-permute-start | bytes 589832 | tf_op jit(solution)/shard_map/ppermute | solution.py:559
  13.4 0.5 %collective-permute-start.4 = (f32[8,256]{1,0:T(8,128)S(1)}, f32[8,256]{1,0:T(8,128)S(1)}, u32[]{:S(2)}, u32[]{:S(2)}) collective-permute-start(f32[8,256]{1,0:T(8,128)S(1)} %get-tuple-element.44.rays_ref), channel_id=1, source_target_pairs={{0,1},{1,0},{2,3},{3,2},{4,5},{5,4},{6,7},{7,6},{8,9},{9,8},{10,11... | collective-permute-start | bytes 24584 | tf_op jit(solution)/shard_map/ppermute | solution.py:562
  13.9 1.5 %collective-permute-start.10 = (f32[2,72,256]{2,1,0:T(8,128)S(1)}, f32[2,72,256]{2,1,0:T(8,128)S(1)}, u32[]{:S(2)}, u32[]{:S(2)}) collective-permute-start(f32[2,72,256]{2,1,0:T(8,128)S(1)} %get-tuple-element.54), channel_id=1, source_target_pairs={{1,2},{2,1},{0,16},{3,19},{17,18},{18,17},{16,0},{19,3},{5,6},{6,5... | collective-permute-start | bytes 442376 | tf_op jit(solution)/shard_map/ppermute | solution.py:618
  15.5 2.0 %collective-permute-done.2.rim_a_ref = f32[192,256]{1,0:T(8,128)S(1)} collective-permute-done((f32[192,256]{1,0:T(8,128)S(1)}, f32[192,256]{1,0:T(8,128)S(1)}, u32[]{:S(2)}, u32[]{:S(2)}) %collective-permute-start.2) | collective-permute-done | bytes 196640 | tf_op jit(solution)/shard_map/ppermute | solution.py:559
  17.5 0.0 collective-permute-done.3.rim_b_ref
  17.5 0.1 shard_map.177
  17.6 1.6 %collective-permute-start.5 = (f32[144,256]{1,0:T(8,128)S(1)}, f32[144,256]{1,0:T(8,128)S(1)}, u32[]{:S(2)}, u32[]{:S(2)}) collective-permute-start(f32[144,256]{1,0:T(8,128)S(1)} %get-tuple-element.45.refs_0_), channel_id=1, source_target_pairs={{0,2},{2,0},{1,3},{3,1},{4,6},{6,4},{5,7},{7,5},{8,10},{10,8},{9,1... | collective-permute-start | bytes 442376 | tf_op jit(solution)/shard_map/ppermute | solution.py:629
  19.1 0.0 collective-permute-done.9.row_a_ref
  19.1 0.5 %shard_map.180.base_ref.refs_3_ = f32[2,2,64,256]{3,2,1,0:T(8,128)S(1)} custom-call(f32[2,2,64,256]{3,2,1,0:T(8,128)S(1)} %get-tuple-element.36.volume_ref, f32[136,256]{1,0:T(8,128)S(1)} %collective-permute-done.plane_a_ref, f32[136,256]{1,0:T(8,128)S(1)} %collective-permute-done.1.plane_b_ref, f32[2,72,256]{2,1,0:T(8,128)S(1)} %collective-permute-done.9.row_a_ref, ...), custom_call_target="tpu_custom_call" | custom-call | flops 10000000 | bytes 1097728 | tf_op jit(solution)/shard_map/pallas_call | solution.py:519
  19.6 2.9 %collective-permute-start.11 = (f32[2,2,64,256]{3,2,1,0:T(8,128)S(1)}, f32[2,2,64,256]{3,2,1,0:T(8,128)S(1)}, u32[]{:S(2)}, u32[]{:S(2)}) collective-permute-start(f32[2,2,64,256]{3,2,1,0:T(8,128)S(1)} %shard_map.180.base_ref.refs_3_), channel_id=1, source_target_pairs={{0,4},{2,0},{4,8},{6,2},{8,12},{10,6},{12,14},{14,10},{1,5},{3,1},... | collective-permute-start | bytes 786440 | tf_op jit(solution)/shard_map/ppermute | solution.py:646
  22.5 0.2 collective-permute-done.5.refs_1_
  22.8 0.1 collective-permute-start.7
  22.9 4.6 %collective-permute-start.6 = (f32[2,144,256]{2,1,0:T(8,128)S(1)}, f32[2,144,256]{2,1,0:T(8,128)S(1)}, u32[]{:S(2)}, u32[]{:S(2)}) collective-permute-start(f32[2,144,256]{2,1,0:T(8,128)S(1)} %pad_maximum_fusion.here_ref), channel_id=1, source_target_pairs={{0,4},{1,5},{8,12},{9,13},{4,0},{5,1},{12,8},{13,9},{2,6},{3,7},{1... | collective-permute-start | bytes 884744 | tf_op jit(solution)/shard_map/ppermute | solution.py:559
  27.4 1.8 %collective-permute-done.11.beside_ref = f32[2,2,64,256]{3,2,1,0:T(8,128)S(1)} collective-permute-done((f32[2,2,64,256]{3,2,1,0:T(8,128)S(1)}, f32[2,2,64,256]{3,2,1,0:T(8,128)S(1)}, u32[]{:S(2)}, u32[]{:S(2)}) %collective-permute-start.11) | collective-permute-done | bytes 262176 | tf_op jit(solution)/shard_map/ppermute | solution.py:646
  29.2 0.8 %shard_map.181 = (f32[2,2,64,256]{3,2,1,0:T(8,128)S(1)}, f32[2,2,64,256]{3,2,1,0:T(8,128)S(1)}) custom-call(s32[2,4]{1,0:T(2,128)S(1)} %bitcast.13, f32[2,4]{1,0:T(2,128)S(1)} %bitcast.15, f32[2,2,64,256]{3,2,1,0:T(8,128)S(1)} %shard_map.180.base_ref.refs_3_, f32[2,2,64,256]{3,2,1,0:T(8,128)S(1)} %collective-permute-done.11.beside_ref), custom_call_target="tpu_custom_call" | custom-call | flops 10000000 | bytes 1048576 | tf_op jit(solution)/shard_map/pallas_call | solution.py:519
  30.0 0.1 collective-permute-start.12
  30.1 1.9 %shard_map.178 = (bf16[2,384,192]{2,1,0:T(8,128)(2,1)S(1)}, bf16[2,384,192]{2,1,0:T(8,128)(2,1)S(1)}, f32[1,2,64,256]{3,2,1,0:T(8,128)}) custom-call(f32[144,256]{1,0:T(8,128)S(1)} %get-tuple-element.45.refs_0_, f32[144,256]{1,0:T(8,128)S(1)} %collective-permute-done.5.refs_1_, f32[1,2,64,256]{3,2,1,0:T(8,128)S(1)} %get-tuple-element.46.refs_2_.refs_4_), custom_call_target="tpu_custom_call" | custom-call | flops 100000000 | bytes 1736704 | tf_op jit(solution)/shard_map/pallas_call | solution.py:519
  32.0 0.0 collective-permute-done.7.side_b_ref
  32.0 1.9 %collective-permute-done.6.side_a_ref = f32[2,144,256]{2,1,0:T(8,128)S(1)} collective-permute-done((f32[2,144,256]{2,1,0:T(8,128)S(1)}, f32[2,144,256]{2,1,0:T(8,128)S(1)}, u32[]{:S(2)}, u32[]{:S(2)}) %collective-permute-start.6) | collective-permute-done | bytes 294944 | tf_op jit(solution)/shard_map/ppermute | solution.py:559
  33.9 0.9 %shard_map.179 = (f32[2,64,256]{2,1,0:T(8,128)S(1)}, f32[2,2,64,256]{3,2,1,0:T(8,128)S(1)}, f32[384,256]{1,0:T(8,128)S(1)}) custom-call(f32[2,144,256]{2,1,0:T(8,128)S(1)} %pad_maximum_fusion.here_ref, f32[2,144,256]{2,1,0:T(8,128)S(1)} %collective-permute-done.6.side_a_ref, f32[2,144,256]{2,1,0:T(8,128)S(1)} %collective-permute-done.7.side_b_ref, ...), custom_call_target="tpu_custom_call" | custom-call | flops 1000000000 | bytes 2260992 | tf_op jit(solution)/shard_map/pallas_call | solution.py:519
  34.8 0.1 collective-permute-start.8
  34.9 0.0 collective-permute-done.12
  34.9 1.7 %collective-permute-start.13 = (f32[2,64,256]{2,1,0:T(8,128)S(1)}, f32[2,64,256]{2,1,0:T(8,128)S(1)}, u32[]{:S(2)}, u32[]{:S(2)}) collective-permute-start(f32[2,64,256]{2,1,0:T(8,128)S(1)} %get-tuple-element.60), channel_id=1, source_target_pairs={{0,2},{2,0},{1,3},{3,1},{4,6},{6,4},{5,7},{7,5},{8,10},{10,8},{9,1... | collective-permute-start | bytes 393224 | tf_op jit(solution)/shard_map/ppermute | solution.py:672
  36.7 4.2 %collective-permute-done.13.refs_8_ = f32[2,64,256]{2,1,0:T(8,128)S(1)} collective-permute-done((f32[2,64,256]{2,1,0:T(8,128)S(1)}, f32[2,64,256]{2,1,0:T(8,128)S(1)}, u32[]{:S(2)}, u32[]{:S(2)}) %collective-permute-start.13) | collective-permute-done | bytes 131104 | tf_op jit(solution)/shard_map/ppermute | solution.py:672
  40.9 0.9 %shard_map.182 = (f32[1,2,64,256]{3,2,1,0:T(8,128)}, f32[2,2,64,256]{3,2,1,0:T(8,128)}, f32[1,2,64,256]{3,2,1,0:T(8,128)}) custom-call(f32[2,64,256]{2,1,0:T(8,128)S(1)} %get-tuple-element.50.refs_0_, f32[2,2,64,256]{3,2,1,0:T(8,128)S(1)} %get-tuple-element.51.refs_1_, f32[384,256]{1,0:T(8,128)S(1)} %collective-permute-done.8.refs_2_, ...), custom_call_target="tpu_custom_call" | custom-call | flops 1000000 | bytes 2228224 | tf_op jit(solution)/shard_map/pallas_call | solution.py:519
  (15 shorter events, 0.1 us)
Async XLA Ops:
  1.6 7.4 %collective-permute-start.1 = (f32[136,256]{1,0:T(8,128)S(1)}, f32[136,256]{1,0:T(8,128)S(1)}, u32[]{:S(2)}, u32[]{:S(2)}) collective-permute-start(f32[136,256]{1,0:T(8,128)S(1)} %shard_map.175.plane_ref), channel_id=1, source_target_pairs={{4,8},{5,9},{8,4},{9,5},{0,1},{1,0},{12,13},{13,12},{6,10},{7,11},... | collective-permute-start | bytes 417800 | tf_op jit(solution)/shard_map/ppermute | solution.py:559
  2.2 7.5 %collective-permute-start = (f32[136,256]{1,0:T(8,128)S(1)}, f32[136,256]{1,0:T(8,128)S(1)}, u32[]{:S(2)}, u32[]{:S(2)}) collective-permute-start(f32[136,256]{1,0:T(8,128)S(1)} %shard_map.175.plane_ref), channel_id=1, source_target_pairs={{0,4},{1,5},{8,12},{9,13},{4,0},{5,1},{12,8},{13,9},{2,6},{3,7},{1... | collective-permute-start | bytes 417800 | tf_op jit(solution)/shard_map/ppermute | solution.py:559
  9.7 7.8 %copy-start = (f32[1,2,64,256]{3,2,1,0:T(8,128)S(1)}, f32[1,2,64,256]{3,2,1,0:T(8,128)}, u32[]{:S(2)}) copy-start(f32[1,2,64,256]{3,2,1,0:T(8,128)} %refs_5_.2) | copy-start | bytes 393220
  9.7 7.8 %copy-start.1 = (f32[1,2,64,256]{3,2,1,0:T(8,128)S(1)}, f32[1,2,64,256]{3,2,1,0:T(8,128)}, u32[]{:S(2)}) copy-start(f32[1,2,64,256]{3,2,1,0:T(8,128)} %projected_ref.1) | copy-start | bytes 393220
  11.6 5.8 %collective-permute-start.2 = (f32[192,256]{1,0:T(8,128)S(1)}, f32[192,256]{1,0:T(8,128)S(1)}, u32[]{:S(2)}, u32[]{:S(2)}) collective-permute-start(f32[192,256]{1,0:T(8,128)S(1)} %get-tuple-element.42), channel_id=1, source_target_pairs={{0,4},{1,5},{8,12},{9,13},{4,0},{5,1},{12,8},{13,9},{2,6},{3,7},{1... | collective-permute-start | bytes 589832 | tf_op jit(solution)/shard_map/ppermute | solution.py:559
  13.4 4.0 %collective-permute-start.3 = (f32[192,256]{1,0:T(8,128)S(1)}, f32[192,256]{1,0:T(8,128)S(1)}, u32[]{:S(2)}, u32[]{:S(2)}) collective-permute-start(f32[192,256]{1,0:T(8,128)S(1)} %get-tuple-element.43), channel_id=1, source_target_pairs={{4,8},{5,9},{8,4},{9,5},{0,1},{1,0},{12,13},{13,12},{6,10},{7,11},... | collective-permute-start | bytes 589832 | tf_op jit(solution)/shard_map/ppermute | solution.py:559
  13.4 2.0 %collective-permute-start.4 = (f32[8,256]{1,0:T(8,128)S(1)}, f32[8,256]{1,0:T(8,128)S(1)}, u32[]{:S(2)}, u32[]{:S(2)}) collective-permute-start(f32[8,256]{1,0:T(8,128)S(1)} %get-tuple-element.44.rays_ref), channel_id=1, source_target_pairs={{0,1},{1,0},{2,3},{3,2},{4,5},{5,4},{6,7},{7,6},{8,9},{9,8},{10,11... | collective-permute-start | bytes 24584 | tf_op jit(solution)/shard_map/ppermute | solution.py:562
  13.9 5.2 %collective-permute-start.9 = (f32[2,72,256]{2,1,0:T(8,128)S(1)}, f32[2,72,256]{2,1,0:T(8,128)S(1)}, u32[]{:S(2)}, u32[]{:S(2)}) collective-permute-start(f32[2,72,256]{2,1,0:T(8,128)S(1)} %get-tuple-element.53), channel_id=1, source_target_pairs={{0,1},{1,0},{2,3},{3,2},{4,5},{5,4},{6,7},{7,6},{8,9},{9,8},{10,11... | collective-permute-start | bytes 442376 | tf_op jit(solution)/shard_map/ppermute | solution.py:562
  13.9 5.2 %collective-permute-start.10 = (f32[2,72,256]{2,1,0:T(8,128)S(1)}, f32[2,72,256]{2,1,0:T(8,128)S(1)}, u32[]{:S(2)}, u32[]{:S(2)}) collective-permute-start(f32[2,72,256]{2,1,0:T(8,128)S(1)} %get-tuple-element.54), channel_id=1, source_target_pairs={{1,2},{2,1},{0,16},{3,19},{17,18},{18,17},{16,0},{19,3},{5,6},{6,5... | collective-permute-start | bytes 442376 | tf_op jit(solution)/shard_map/ppermute | solution.py:618
  17.6 5.2 %collective-permute-start.5 = (f32[144,256]{1,0:T(8,128)S(1)}, f32[144,256]{1,0:T(8,128)S(1)}, u32[]{:S(2)}, u32[]{:S(2)}) collective-permute-start(f32[144,256]{1,0:T(8,128)S(1)} %get-tuple-element.45.refs_0_), channel_id=1, source_target_pairs={{0,2},{2,0},{1,3},{3,1},{4,6},{6,4},{5,7},{7,5},{8,10},{10,8},{9,1... | collective-permute-start | bytes 442376 | tf_op jit(solution)/shard_map/ppermute | solution.py:629
  19.6 9.6 %collective-permute-start.11 = (f32[2,2,64,256]{3,2,1,0:T(8,128)S(1)}, f32[2,2,64,256]{3,2,1,0:T(8,128)S(1)}, u32[]{:S(2)}, u32[]{:S(2)}) collective-permute-start(f32[2,2,64,256]{3,2,1,0:T(8,128)S(1)} %shard_map.180.base_ref.refs_3_), channel_id=1, source_target_pairs={{0,4},{2,0},{4,8},{6,2},{8,12},{10,6},{12,14},{14,10},{1,5},{3,1},... | collective-permute-start | bytes 786440 | tf_op jit(solution)/shard_map/ppermute | solution.py:646
  22.8 6.5 %copy-start.2 = (s32[4,2]{0,1:T(2,128)S(1)}, s32[4,2]{0,1:T(2,128)}, u32[]{:S(2)}) copy-start(s32[4,2]{0,1:T(2,128)} %param.24) | copy-start | bytes 100
  22.8 6.5 %copy-start.3 = (f32[4,2]{0,1:T(2,128)S(1)}, f32[4,2]{0,1:T(2,128)}, u32[]{:S(2)}) copy-start(f32[4,2]{0,1:T(2,128)} %param.25) | copy-start | bytes 100
  22.8 9.2 %collective-permute-start.7 = (f32[2,144,256]{2,1,0:T(8,128)S(1)}, f32[2,144,256]{2,1,0:T(8,128)S(1)}, u32[]{:S(2)}, u32[]{:S(2)}) collective-permute-start(f32[2,144,256]{2,1,0:T(8,128)S(1)} %pad_maximum_fusion.here_ref), channel_id=1, source_target_pairs={{4,8},{5,9},{8,4},{9,5},{0,1},{1,0},{12,13},{13,12},{6,10},{7,11},... | collective-permute-start | bytes 884744 | tf_op jit(solution)/shard_map/ppermute | solution.py:559
  22.9 11.1 %collective-permute-start.6 = (f32[2,144,256]{2,1,0:T(8,128)S(1)}, f32[2,144,256]{2,1,0:T(8,128)S(1)}, u32[]{:S(2)}, u32[]{:S(2)}) collective-permute-start(f32[2,144,256]{2,1,0:T(8,128)S(1)} %pad_maximum_fusion.here_ref), channel_id=1, source_target_pairs={{0,4},{1,5},{8,12},{9,13},{4,0},{5,1},{12,8},{13,9},{2,6},{3,7},{1... | collective-permute-start | bytes 884744 | tf_op jit(solution)/shard_map/ppermute | solution.py:559
  30.0 4.9 %collective-permute-start.12 = (f32[2,2,64,256]{3,2,1,0:T(8,128)S(1)}, f32[2,2,64,256]{3,2,1,0:T(8,128)S(1)}, u32[]{:S(2)}, u32[]{:S(2)}) collective-permute-start(f32[2,2,64,256]{3,2,1,0:T(8,128)S(1)} %get-tuple-element.56), channel_id=1, source_target_pairs={{0,1},{1,0},{2,3},{3,2},{4,5},{5,4},{6,7},{7,6},{8,9},{9,8},{10,11... | collective-permute-start | bytes 786440 | tf_op jit(solution)/shard_map/ppermute | solution.py:562
  34.8 6.1 %collective-permute-start.8 = (f32[384,256]{1,0:T(8,128)S(1)}, f32[384,256]{1,0:T(8,128)S(1)}, u32[]{:S(2)}, u32[]{:S(2)}) collective-permute-start(f32[384,256]{1,0:T(8,128)S(1)} %get-tuple-element.52), channel_id=1, source_target_pairs={{0,1},{1,0},{2,3},{3,2},{4,5},{5,4},{6,7},{7,6},{8,9},{9,8},{10,11... | collective-permute-start | bytes 1179656 | tf_op jit(solution)/shard_map/ppermute | solution.py:562
  34.9 6.0 %collective-permute-start.13 = (f32[2,64,256]{2,1,0:T(8,128)S(1)}, f32[2,64,256]{2,1,0:T(8,128)S(1)}, u32[]{:S(2)}, u32[]{:S(2)}) collective-permute-start(f32[2,64,256]{2,1,0:T(8,128)S(1)} %get-tuple-element.60), channel_id=1, source_target_pairs={{0,2},{2,0},{1,3},{3,1},{4,6},{6,4},{5,7},{7,5},{8,10},{10,8},{9,1... | collective-permute-start | bytes 393224 | tf_op jit(solution)/shard_map/ppermute | solution.py:672

commit v10 on v9

--- a/solution.py
+++ b/solution.py
@@ -360,7 +360,7 @@
 
 
 def spread_kernel(
-    shift_ref, weight_ref, base_ref, beside_ref, keep_ref, send_ref, padded
+    shift_ref, weight_ref, base_ref, beside_ref, _, keep_ref, send_ref, padded
 ):
     width = base_ref.shape[2]
     count = base_ref.shape[1]
@@ -644,6 +644,7 @@
                 target, turned = scan, (column + columns // 2) % columns
             route.append((scan * columns + column, target * columns + turned))
     beside = lax.ppermute(base, ("scan", "angle"), route)
+    level = across(base[0, 0, :SUBLANES])
     here = jnp.stack(by_column)
     side_a = exchange(here, 0)
     side_b = exchange(here, 1)
@@ -660,7 +661,7 @@
     keep, send = call(
         spread_kernel,
         [block, block],
-        (shift_table.T, tap_weight.T, base, beside),
+        (shift_table.T, tap_weight.T, base, beside, level),
         [(count, 2, length // LANES, 2 * width, LANES)],
         10**7,
         2,

time: 42 us -> 42 us (level)
    ppermute x1, waiting for transfers between devices: 1.77 us -> 0.58 us  [body(): beside = lax.ppermute(base, ('scan', 'angle'), route)]
    ppermute x4 -> x5, waiting for transfers between devices: 0.01 us -> 1.18 us  [across(): return lax.ppermute(block, 'tile', swap)]
  transfers between devices with their start and end apart: 14 -> 15, of which waited for: 6 -> 7; matrix products, arithmetic and copies ran while one was open for 0% -> 0% of each run, Pallas kernels for 15% -> 15%
where the time goes in v10:
time: 42 us; the launch traced here: 41.8 us
  starting transfers between devices  19.5 us (46%)
  waiting for transfers between devices  10.9 us (26%)
  Pallas kernels  9.91 us (24%)
  between operations  1.41 us (3%)
    ppermute x6, starting transfers between devices, exchange(): return lax.ppermute(block, ('scan', 'tile'), rounds[number])  11.2 us
    pallas_call x9, Pallas kernels, call(): pl.pallas_call(kernel, out_shape=outputs, in_specs=in_specs, out_specs=[V...  9.91 us
    ppermute x6, waiting for transfers between devices, exchange(): return lax.ppermute(block, ('scan', 'tile'), rounds[number])  4.66 us
    ppermute x1, waiting for transfers between devices, body(): spreads.append(lax.ppermute(keep[turn] + received[turn], 'angle', route))  4.23 us
    ppermute x1, starting transfers between devices, body(): beside = lax.ppermute(base, ('scan', 'angle'), route)  2.89 us
    ppermute x1, starting transfers between devices, body(): spreads.append(lax.ppermute(keep[turn] + received[turn], 'angle', route))  1.72 us
    ppermute x1, starting transfers between devices, body(): by_column.append(lax.ppermute(residual, 'angle', turns[turn]))  1.56 us
    ppermute x1, starting transfers between devices, body(): row_b = lax.ppermute(row_b, ('groups', 'angle', 'tile'), bridge)  1.52 us
  transfers between devices with their start and end apart: 15, of which 7 were waited for; matrix products, arithmetic and copies ran while one was open for 0% of the time, Pallas kernels for 15%

profile of v10, /device:TPU:0, one launch (start us, length us, event | category | flops | bytes accessed | tf_op | source)
XLA Modules:
  0.0 41.8 jit_solution(3651944965373359416)
XLA Ops:
  0.6 1.0 %shard_map.175.plane_ref = f32[136,256]{1,0:T(8,128)S(1)} custom-call(f32[1,2,64,256]{3,2,1,0:T(8,128)} %plane_ref.1, f32[2,2,64,256]{3,2,1,0:T(8,128)} %volume_ref.1), custom_call_target="tpu_custom_call" | custom-call | flops 100000 | bytes 532480 | tf_op jit(solution)/shard_map/pallas_call | solution.py:519
  1.6 0.6 %collective-permute-start.1 = (f32[136,256]{1,0:T(8,128)S(1)}, f32[136,256]{1,0:T(8,128)S(1)}, u32[]{:S(2)}, u32[]{:S(2)}) collective-permute-start(f32[136,256]{1,0:T(8,128)S(1)} %shard_map.175.plane_ref), channel_id=1, source_target_pairs={{4,8},{5,9},{8,4},{9,5},{0,1},{1,0},{12,13},{13,12},{6,10},{7,11},... | collective-permute-start | bytes 417800 | tf_op jit(solution)/shard_map/ppermute | solution.py:559
  2.2 4.1 %collective-permute-start = (f32[136,256]{1,0:T(8,128)S(1)}, f32[136,256]{1,0:T(8,128)S(1)}, u32[]{:S(2)}, u32[]{:S(2)}) collective-permute-start(f32[136,256]{1,0:T(8,128)S(1)} %shard_map.175.plane_ref), channel_id=1, source_target_pairs={{0,4},{1,5},{8,12},{9,13},{4,0},{5,1},{12,8},{13,9},{2,6},{3,7},{1... | collective-permute-start | bytes 417800 | tf_op jit(solution)/shard_map/ppermute | solution.py:559
  6.9 2.0 %shard_map.174 = (f32[4,2,128,128]{3,2,1,0:T(8,128)S(1)}, f32[1,192,256]{2,1,0:T(8,128)S(1)}, s32[4,8,128]{2,1,0:T(8,128)S(1)}, f32[8,256]{1,0:T(8,128)S(1)}, f3...) custom-call(s32[1,1]{1,0:T(1,128)S(6)} %copy.19.count_ref, ...), custom_call_target="tpu_custom_call" | custom-call | flops 10000000 | bytes 1794048 | tf_op jit(solution)/shard_map/pallas_call | solution.py:519
  9.0 0.0 collective-permute-done.1.plane_b_ref
  9.0 0.7 %collective-permute-done.plane_a_ref = f32[136,256]{1,0:T(8,128)S(1)} collective-permute-done((f32[136,256]{1,0:T(8,128)S(1)}, f32[136,256]{1,0:T(8,128)S(1)}, u32[]{:S(2)}, u32[]{:S(2)}) %collective-permute-start) | collective-permute-done | bytes 139296 | tf_op jit(solution)/shard_map/ppermute | solution.py:559
  9.7 1.9 %shard_map.176 = (f32[3,64,256]{2,1,0:T(8,128)S(1)}, f32[192,256]{1,0:T(8,128)S(1)}, f32[192,256]{1,0:T(8,128)S(1)}, f32[2,72,256]{2,1,0:T(8,128)S(1)}, f32[2,72,256]{2,1,0:T(8,128)S(1)}) custom-call(f32[4,2,128,128]{3,2,1,0:T(8,128)S(1)} %get-tuple-element.32.probes_ref, f32[1,192,256]{2,1,0:T(8,128)S(1)} %get-tuple-element.33.density_ref, ...), custom_call_target="tpu_custom_call" | custom-call | flops 1000000000 | bytes 2957312 | tf_op jit(solution)/shard_map/pallas_call | solution.py:519
  11.6 1.8 %collective-permute-start.2 = (f32[192,256]{1,0:T(8,128)S(1)}, f32[192,256]{1,0:T(8,128)S(1)}, u32[]{:S(2)}, u32[]{:S(2)}) collective-permute-start(f32[192,256]{1,0:T(8,128)S(1)} %get-tuple-element.42), channel_id=1, source_target_pairs={{0,4},{1,5},{8,12},{9,13},{4,0},{5,1},{12,8},{13,9},{2,6},{3,7},{1... | collective-permute-start | bytes 589832 | tf_op jit(solution)/shard_map/ppermute | solution.py:559
  13.4 0.5 %collective-permute-start.4 = (f32[8,256]{1,0:T(8,128)S(1)}, f32[8,256]{1,0:T(8,128)S(1)}, u32[]{:S(2)}, u32[]{:S(2)}) collective-permute-start(f32[8,256]{1,0:T(8,128)S(1)} %get-tuple-element.44.rays_ref), channel_id=1, source_target_pairs={{0,1},{1,0},{2,3},{3,2},{4,5},{5,4},{6,7},{7,6},{8,9},{9,8},{10,11... | collective-permute-start | bytes 24584 | tf_op jit(solution)/shard_map/ppermute | solution.py:562
  13.9 1.5 %collective-permute-start.10 = (f32[2,72,256]{2,1,0:T(8,128)S(1)}, f32[2,72,256]{2,1,0:T(8,128)S(1)}, u32[]{:S(2)}, u32[]{:S(2)}) collective-permute-start(f32[2,72,256]{2,1,0:T(8,128)S(1)} %get-tuple-element.54), channel_id=1, source_target_pairs={{1,2},{2,1},{0,16},{3,19},{17,18},{18,17},{16,0},{19,3},{5,6},{6,5... | collective-permute-start | bytes 442376 | tf_op jit(solution)/shard_map/ppermute | solution.py:618
  15.5 2.0 %collective-permute-done.2.rim_a_ref = f32[192,256]{1,0:T(8,128)S(1)} collective-permute-done((f32[192,256]{1,0:T(8,128)S(1)}, f32[192,256]{1,0:T(8,128)S(1)}, u32[]{:S(2)}, u32[]{:S(2)}) %collective-permute-start.2) | collective-permute-done | bytes 196640 | tf_op jit(solution)/shard_map/ppermute | solution.py:559
  17.5 0.0 collective-permute-done.3.rim_b_ref
  17.5 0.1 shard_map.177
  17.6 1.6 %collective-permute-start.5 = (f32[144,256]{1,0:T(8,128)S(1)}, f32[144,256]{1,0:T(8,128)S(1)}, u32[]{:S(2)}, u32[]{:S(2)}) collective-permute-start(f32[144,256]{1,0:T(8,128)S(1)} %get-tuple-element.45.refs_0_), channel_id=1, source_target_pairs={{0,2},{2,0},{1,3},{3,1},{4,6},{6,4},{5,7},{7,5},{8,10},{10,8},{9,1... | collective-permute-start | bytes 442376 | tf_op jit(solution)/shard_map/ppermute | solution.py:629
  19.1 0.5 %shard_map.180.base_ref.refs_3_ = f32[2,2,64,256]{3,2,1,0:T(8,128)S(1)} custom-call(f32[2,2,64,256]{3,2,1,0:T(8,128)S(1)} %get-tuple-element.36.volume_ref, f32[136,256]{1,0:T(8,128)S(1)} %collective-permute-done.plane_a_ref, f32[136,256]{1,0:T(8,128)S(1)} %collective-permute-done.1.plane_b_ref, f32[2,72,256]{2,1,0:T(8,128)S(1)} %collective-permute-done.9.row_a_ref, ...), custom_call_target="tpu_custom_call" | custom-call | flops 10000000 | bytes 1097728 | tf_op jit(solution)/shard_map/pallas_call | solution.py:519
  19.6 2.9 %collective-permute-start.11 = (f32[2,2,64,256]{3,2,1,0:T(8,128)S(1)}, f32[2,2,64,256]{3,2,1,0:T(8,128)S(1)}, u32[]{:S(2)}, u32[]{:S(2)}) collective-permute-start(f32[2,2,64,256]{3,2,1,0:T(8,128)S(1)} %shard_map.180.base_ref.refs_3_), channel_id=1, source_target_pairs={{0,4},{2,0},{4,8},{6,2},{8,12},{10,6},{12,14},{14,10},{1,5},{3,1},... | collective-permute-start | bytes 786440 | tf_op jit(solution)/shard_map/ppermute | solution.py:646
  22.5 0.2 collective-permute-done.5.refs_1_
  22.8 0.0 copy-start.2
  22.8 0.0 copy-start.3
  22.8 0.1 collective-permute-start.7
  22.9 4.6 %collective-permute-start.6 = (f32[2,144,256]{2,1,0:T(8,128)S(1)}, f32[2,144,256]{2,1,0:T(8,128)S(1)}, u32[]{:S(2)}, u32[]{:S(2)}) collective-permute-start(f32[2,144,256]{2,1,0:T(8,128)S(1)} %pad_maximum_fusion.here_ref), channel_id=1, source_target_pairs={{0,4},{1,5},{8,12},{9,13},{4,0},{5,1},{12,8},{13,9},{2,6},{3,7},{1... | collective-permute-start | bytes 884744 | tf_op jit(solution)/shard_map/ppermute | solution.py:559
  27.5 1.2 %collective-permute-done.12._ = f32[8,256]{1,0:T(8,128)S(1)} collective-permute-done((f32[8,256]{1,0:T(8,128)S(1)}, f32[8,256]{1,0:T(8,128)S(1)}, u32[]{:S(2)}, u32[]{:S(2)}) %collective-permute-start.12) | collective-permute-done | bytes 8224 | tf_op jit(solution)/shard_map/ppermute | solution.py:562
  28.6 0.6 %collective-permute-done.11.beside_ref = f32[2,2,64,256]{3,2,1,0:T(8,128)S(1)} collective-permute-done((f32[2,2,64,256]{3,2,1,0:T(8,128)S(1)}, f32[2,2,64,256]{3,2,1,0:T(8,128)S(1)}, u32[]{:S(2)}, u32[]{:S(2)}) %collective-permute-start.11) | collective-permute-done | bytes 262176 | tf_op jit(solution)/shard_map/ppermute | solution.py:646
  29.2 0.8 %shard_map.181 = (f32[2,2,64,256]{3,2,1,0:T(8,128)S(1)}, f32[2,2,64,256]{3,2,1,0:T(8,128)S(1)}) custom-call(s32[2,4]{1,0:T(2,128)S(1)} %bitcast.15, f32[2,4]{1,0:T(2,128)S(1)} %bitcast.17, f32[2,2,64,256]{3,2,1,0:T(8,128)S(1)} %shard_map.180.base_ref.refs_3_, f32[2,2,64,256]{3,2,1,0:T(8,128)S(1)} %collective-permute-done.11.beside_ref, ...), custom_call_target="tpu_custom_call" | custom-call | flops 10000000 | bytes 1056768 | tf_op jit(solution)/shard_map/pallas_call | solution.py:519
  30.0 0.1 collective-permute-start.13
  30.1 1.9 %shard_map.178 = (bf16[2,384,192]{2,1,0:T(8,128)(2,1)S(1)}, bf16[2,384,192]{2,1,0:T(8,128)(2,1)S(1)}, f32[1,2,64,256]{3,2,1,0:T(8,128)}) custom-call(f32[144,256]{1,0:T(8,128)S(1)} %get-tuple-element.45.refs_0_, f32[144,256]{1,0:T(8,128)S(1)} %collective-permute-done.5.refs_1_, f32[1,2,64,256]{3,2,1,0:T(8,128)S(1)} %get-tuple-element.46.refs_2_.refs_4_), custom_call_target="tpu_custom_call" | custom-call | flops 100000000 | bytes 1736704 | tf_op jit(solution)/shard_map/pallas_call | solution.py:519
  32.0 1.9 %collective-permute-done.6.side_a_ref = f32[2,144,256]{2,1,0:T(8,128)S(1)} collective-permute-done((f32[2,144,256]{2,1,0:T(8,128)S(1)}, f32[2,144,256]{2,1,0:T(8,128)S(1)}, u32[]{:S(2)}, u32[]{:S(2)}) %collective-permute-start.6) | collective-permute-done | bytes 294944 | tf_op jit(solution)/shard_map/ppermute | solution.py:559
  33.9 0.9 %shard_map.179 = (f32[2,64,256]{2,1,0:T(8,128)S(1)}, f32[2,2,64,256]{3,2,1,0:T(8,128)S(1)}, f32[384,256]{1,0:T(8,128)S(1)}) custom-call(f32[2,144,256]{2,1,0:T(8,128)S(1)} %pad_maximum_fusion.here_ref, f32[2,144,256]{2,1,0:T(8,128)S(1)} %collective-permute-done.6.side_a_ref, f32[2,144,256]{2,1,0:T(8,128)S(1)} %collective-permute-done.7.side_b_ref, ...), custom_call_target="tpu_custom_call" | custom-call | flops 1000000000 | bytes 2260992 | tf_op jit(solution)/shard_map/pallas_call | solution.py:519
  34.8 0.1 collective-permute-start.8
  34.9 1.7 %collective-permute-start.14 = (f32[2,64,256]{2,1,0:T(8,128)S(1)}, f32[2,64,256]{2,1,0:T(8,128)S(1)}, u32[]{:S(2)}, u32[]{:S(2)}) collective-permute-start(f32[2,64,256]{2,1,0:T(8,128)S(1)} %get-tuple-element.60), channel_id=1, source_target_pairs={{0,2},{2,0},{1,3},{3,1},{4,6},{6,4},{5,7},{7,5},{8,10},{10,8},{9,1... | collective-permute-start | bytes 393224 | tf_op jit(solution)/shard_map/ppermute | solution.py:673
  36.7 4.2 %collective-permute-done.14.refs_8_ = f32[2,64,256]{2,1,0:T(8,128)S(1)} collective-permute-done((f32[2,64,256]{2,1,0:T(8,128)S(1)}, f32[2,64,256]{2,1,0:T(8,128)S(1)}, u32[]{:S(2)}, u32[]{:S(2)}) %collective-permute-start.14) | collective-permute-done | bytes 131104 | tf_op jit(solution)/shard_map/ppermute | solution.py:673
  40.9 0.9 %shard_map.182 = (f32[1,2,64,256]{3,2,1,0:T(8,128)}, f32[2,2,64,256]{3,2,1,0:T(8,128)}, f32[1,2,64,256]{3,2,1,0:T(8,128)}) custom-call(f32[2,64,256]{2,1,0:T(8,128)S(1)} %get-tuple-element.50.refs_0_, f32[2,2,64,256]{3,2,1,0:T(8,128)S(1)} %get-tuple-element.51.refs_1_, f32[384,256]{1,0:T(8,128)S(1)} %collective-permute-done.8.refs_2_, ...), custom_call_target="tpu_custom_call" | custom-call | flops 1000000 | bytes 2228224 | tf_op jit(solution)/shard_map/pallas_call | solution.py:519
  (18 shorter events, 0.1 us)
Async XLA Ops:
  1.6 7.4 %collective-permute-start.1 = (f32[136,256]{1,0:T(8,128)S(1)}, f32[136,256]{1,0:T(8,128)S(1)}, u32[]{:S(2)}, u32[]{:S(2)}) collective-permute-start(f32[136,256]{1,0:T(8,128)S(1)} %shard_map.175.plane_ref), channel_id=1, source_target_pairs={{4,8},{5,9},{8,4},{9,5},{0,1},{1,0},{12,13},{13,12},{6,10},{7,11},... | collective-permute-start | bytes 417800 | tf_op jit(solution)/shard_map/ppermute | solution.py:559
  2.2 7.5 %collective-permute-start = (f32[136,256]{1,0:T(8,128)S(1)}, f32[136,256]{1,0:T(8,128)S(1)}, u32[]{:S(2)}, u32[]{:S(2)}) collective-permute-start(f32[136,256]{1,0:T(8,128)S(1)} %shard_map.175.plane_ref), channel_id=1, source_target_pairs={{0,4},{1,5},{8,12},{9,13},{4,0},{5,1},{12,8},{13,9},{2,6},{3,7},{1... | collective-permute-start | bytes 417800 | tf_op jit(solution)/shard_map/ppermute | solution.py:559
  9.7 7.8 %copy-start = (f32[1,2,64,256]{3,2,1,0:T(8,128)S(1)}, f32[1,2,64,256]{3,2,1,0:T(8,128)}, u32[]{:S(2)}) copy-start(f32[1,2,64,256]{3,2,1,0:T(8,128)} %refs_5_.2) | copy-start | bytes 393220
  9.7 7.8 %copy-start.1 = (f32[1,2,64,256]{3,2,1,0:T(8,128)S(1)}, f32[1,2,64,256]{3,2,1,0:T(8,128)}, u32[]{:S(2)}) copy-start(f32[1,2,64,256]{3,2,1,0:T(8,128)} %projected_ref.1) | copy-start | bytes 393220
  11.6 5.8 %collective-permute-start.2 = (f32[192,256]{1,0:T(8,128)S(1)}, f32[192,256]{1,0:T(8,128)S(1)}, u32[]{:S(2)}, u32[]{:S(2)}) collective-permute-start(f32[192,256]{1,0:T(8,128)S(1)} %get-tuple-element.42), channel_id=1, source_target_pairs={{0,4},{1,5},{8,12},{9,13},{4,0},{5,1},{12,8},{13,9},{2,6},{3,7},{1... | collective-permute-start | bytes 589832 | tf_op jit(solution)/shard_map/ppermute | solution.py:559
  13.4 4.0 %collective-permute-start.3 = (f32[192,256]{1,0:T(8,128)S(1)}, f32[192,256]{1,0:T(8,128)S(1)}, u32[]{:S(2)}, u32[]{:S(2)}) collective-permute-start(f32[192,256]{1,0:T(8,128)S(1)} %get-tuple-element.43), channel_id=1, source_target_pairs={{4,8},{5,9},{8,4},{9,5},{0,1},{1,0},{12,13},{13,12},{6,10},{7,11},... | collective-permute-start | bytes 589832 | tf_op jit(solution)/shard_map/ppermute | solution.py:559
  13.4 2.0 %collective-permute-start.4 = (f32[8,256]{1,0:T(8,128)S(1)}, f32[8,256]{1,0:T(8,128)S(1)}, u32[]{:S(2)}, u32[]{:S(2)}) collective-permute-start(f32[8,256]{1,0:T(8,128)S(1)} %get-tuple-element.44.rays_ref), channel_id=1, source_target_pairs={{0,1},{1,0},{2,3},{3,2},{4,5},{5,4},{6,7},{7,6},{8,9},{9,8},{10,11... | collective-permute-start | bytes 24584 | tf_op jit(solution)/shard_map/ppermute | solution.py:562
  13.9 5.2 %collective-permute-start.9 = (f32[2,72,256]{2,1,0:T(8,128)S(1)}, f32[2,72,256]{2,1,0:T(8,128)S(1)}, u32[]{:S(2)}, u32[]{:S(2)}) collective-permute-start(f32[2,72,256]{2,1,0:T(8,128)S(1)} %get-tuple-element.53), channel_id=1, source_target_pairs={{0,1},{1,0},{2,3},{3,2},{4,5},{5,4},{6,7},{7,6},{8,9},{9,8},{10,11... | collective-permute-start | bytes 442376 | tf_op jit(solution)/shard_map/ppermute | solution.py:562
  13.9 5.2 %collective-permute-start.10 = (f32[2,72,256]{2,1,0:T(8,128)S(1)}, f32[2,72,256]{2,1,0:T(8,128)S(1)}, u32[]{:S(2)}, u32[]{:S(2)}) collective-permute-start(f32[2,72,256]{2,1,0:T(8,128)S(1)} %get-tuple-element.54), channel_id=1, source_target_pairs={{1,2},{2,1},{0,16},{3,19},{17,18},{18,17},{16,0},{19,3},{5,6},{6,5... | collective-permute-start | bytes 442376 | tf_op jit(solution)/shard_map/ppermute | solution.py:618
  17.6 5.2 %collective-permute-start.5 = (f32[144,256]{1,0:T(8,128)S(1)}, f32[144,256]{1,0:T(8,128)S(1)}, u32[]{:S(2)}, u32[]{:S(2)}) collective-permute-start(f32[144,256]{1,0:T(8,128)S(1)} %get-tuple-element.45.refs_0_), channel_id=1, source_target_pairs={{0,2},{2,0},{1,3},{3,1},{4,6},{6,4},{5,7},{7,5},{8,10},{10,8},{9,1... | collective-permute-start | bytes 442376 | tf_op jit(solution)/shard_map/ppermute | solution.py:629
  19.6 9.6 %collective-permute-start.11 = (f32[2,2,64,256]{3,2,1,0:T(8,128)S(1)}, f32[2,2,64,256]{3,2,1,0:T(8,128)S(1)}, u32[]{:S(2)}, u32[]{:S(2)}) collective-permute-start(f32[2,2,64,256]{3,2,1,0:T(8,128)S(1)} %shard_map.180.base_ref.refs_3_), channel_id=1, source_target_pairs={{0,4},{2,0},{4,8},{6,2},{8,12},{10,6},{12,14},{14,10},{1,5},{3,1},... | collective-permute-start | bytes 786440 | tf_op jit(solution)/shard_map/ppermute | solution.py:646
  22.8 6.4 %copy-start.2 = (s32[4,2]{0,1:T(2,128)S(1)}, s32[4,2]{0,1:T(2,128)}, u32[]{:S(2)}) copy-start(s32[4,2]{0,1:T(2,128)} %param.24) | copy-start | bytes 100
  22.8 6.4 %copy-start.3 = (f32[4,2]{0,1:T(2,128)S(1)}, f32[4,2]{0,1:T(2,128)}, u32[]{:S(2)}) copy-start(f32[4,2]{0,1:T(2,128)} %param.25) | copy-start | bytes 100
  22.8 9.2 %collective-permute-start.7 = (f32[2,144,256]{2,1,0:T(8,128)S(1)}, f32[2,144,256]{2,1,0:T(8,128)S(1)}, u32[]{:S(2)}, u32[]{:S(2)}) collective-permute-start(f32[2,144,256]{2,1,0:T(8,128)S(1)} %pad_maximum_fusion.here_ref), channel_id=1, source_target_pairs={{4,8},{5,9},{8,4},{9,5},{0,1},{1,0},{12,13},{13,12},{6,10},{7,11},... | collective-permute-start | bytes 884744 | tf_op jit(solution)/shard_map/ppermute | solution.py:559
  22.9 11.1 %collective-permute-start.6 = (f32[2,144,256]{2,1,0:T(8,128)S(1)}, f32[2,144,256]{2,1,0:T(8,128)S(1)}, u32[]{:S(2)}, u32[]{:S(2)}) collective-permute-start(f32[2,144,256]{2,1,0:T(8,128)S(1)} %pad_maximum_fusion.here_ref), channel_id=1, source_target_pairs={{0,4},{1,5},{8,12},{9,13},{4,0},{5,1},{12,8},{13,9},{2,6},{3,7},{1... | collective-permute-start | bytes 884744 | tf_op jit(solution)/shard_map/ppermute | solution.py:559
  27.5 1.2 %collective-permute-start.12 = (f32[8,256]{1,0:T(8,128)S(1)}, f32[8,256]{1,0:T(8,128)S(1)}, u32[]{:S(2)}, u32[]{:S(2)}) collective-permute-start(f32[8,256]{1,0:T(8,128)S(1)} %slice_bitcast_fusion.2), channel_id=1, source_target_pairs={{0,1},{1,0},{2,3},{3,2},{4,5},{5,4},{6,7},{7,6},{8,9},{9,8},{10,11... | collective-permute-start | bytes 24584 | tf_op jit(solution)/shard_map/ppermute | solution.py:562
  30.0 4.9 %collective-permute-start.13 = (f32[2,2,64,256]{3,2,1,0:T(8,128)S(1)}, f32[2,2,64,256]{3,2,1,0:T(8,128)S(1)}, u32[]{:S(2)}, u32[]{:S(2)}) collective-permute-start(f32[2,2,64,256]{3,2,1,0:T(8,128)S(1)} %get-tuple-element.56), channel_id=1, source_target_pairs={{0,1},{1,0},{2,3},{3,2},{4,5},{5,4},{6,7},{7,6},{8,9},{9,8},{10,11... | collective-permute-start | bytes 786440 | tf_op jit(solution)/shard_map/ppermute | solution.py:562
  34.8 6.1 %collective-permute-start.8 = (f32[384,256]{1,0:T(8,128)S(1)}, f32[384,256]{1,0:T(8,128)S(1)}, u32[]{:S(2)}, u32[]{:S(2)}) collective-permute-start(f32[384,256]{1,0:T(8,128)S(1)} %get-tuple-element.52), channel_id=1, source_target_pairs={{0,1},{1,0},{2,3},{3,2},{4,5},{5,4},{6,7},{7,6},{8,9},{9,8},{10,11... | collective-permute-start | bytes 1179656 | tf_op jit(solution)/shard_map/ppermute | solution.py:562
  34.9 6.0 %collective-permute-start.14 = (f32[2,64,256]{2,1,0:T(8,128)S(1)}, f32[2,64,256]{2,1,0:T(8,128)S(1)}, u32[]{:S(2)}, u32[]{:S(2)}) collective-permute-start(f32[2,64,256]{2,1,0:T(8,128)S(1)} %get-tuple-element.60), channel_id=1, source_target_pairs={{0,2},{2,0},{1,3},{3,1},{4,6},{6,4},{5,7},{7,5},{8,10},{10,8},{9,1... | collective-permute-start | bytes 393224 | tf_op jit(solution)/shard_map/ppermute | solution.py:673

commit v11 on v9

--- a/solution.py
+++ b/solution.py
@@ -275,7 +275,7 @@
 
 
 def fold_kernel(
-    own_ref, rim_a_ref, rim_b_ref, projected_ref, dual_ref, rays_ref, too_ref, object_ref, residual_ref
+    own_ref, rim_a_ref, rim_b_ref, projected_ref, dual_ref, rays_ref, too_ref, object_ref, residual_ref, packed_ref
 ):
     width = own_ref.shape[1]
     second = has_second()
@@ -290,9 +290,11 @@
         dual = dual_ref[0, part]
         updated = (sums[part] + penalty * (target - dual)) / (sums[2] + penalty)
         object_ref[0, part] = updated
-        residual_ref[part * width : (part + 1) * width] = target - updated - dual
-    residual_ref[2 * width : 2 * width + SUBLANES] = rays_ref[...]
-    residual_ref[2 * width + SUBLANES :] = too_ref[...]
+        residual = target - updated - dual
+        residual_ref[part * width : (part + 1) * width] = residual
+        packed_ref[part * width : (part + 1) * width] = residual
+    packed_ref[2 * width : 2 * width + SUBLANES] = rays_ref[...]
+    packed_ref[2 * width + SUBLANES :] = too_ref[...]
 
 
 def variation_kernel(
@@ -617,16 +619,20 @@
             bridge.append((at + outer, beyond + outer))
     row_b = lax.ppermute(row_b, ("groups", "angle", "tile"), bridge)
     row_a = across(row_a)
-    updated, residual = call(
+    updated, residual, packed = call(
         fold_kernel,
-        [transmission.shape, (2 * width + 2 * SUBLANES, length)],
+        [
+            transmission.shape,
+            (2 * width, length),
+            (2 * width + 2 * SUBLANES, length),
+        ],
         (own, rim_a, rim_b, projected, scaled_dual, rays, rays_too),
         [],
         10**6,
     )
-    by_column = [residual]
+    by_column = [packed]
     for turn in range(1, columns):
-        by_column.append(lax.ppermute(residual, "angle", turns[turn]))
+        by_column.append(lax.ppermute(packed, "angle", turns[turn]))
     (base,) = call(
         variation_kernel,
         [volume.shape],
@@ -644,7 +650,7 @@
                 target, turned = scan, (column + columns // 2) % columns
             route.append((scan * columns + column, target * columns + turned))
     beside = lax.ppermute(base, ("scan", "angle"), route)
-    here = jnp.stack(by_column)
+    here = jnp.stack([residual] + [block[: 2 * width] for block in by_column[1:]])
     side_a = exchange(here, 0)
     side_b = exchange(here, 1)
     high, low, new_transmission = call(

time: 42 us -> 41.3 us (0.983)
  waiting for transfers between devices: 10.9 us -> 10.2 us
    ppermute x6, waiting for transfers between devices: 4.66 us -> 3.96 us  [exchange(): return lax.ppermute(block, ('scan', 'tile'), rounds[number])]
where the time goes in v11:
time: 41.3 us; the launch traced here: 41.1 us
  starting transfers between devices  19.5 us (47%)
  waiting for transfers between devices  10.2 us (25%)
  Pallas kernels  9.93 us (24%)
  between operations  1.42 us (3%)
    ppermute x6, starting transfers between devices, exchange(): return lax.ppermute(block, ('scan', 'tile'), rounds[number])  11.2 us
    pallas_call x9, Pallas kernels, call(): pl.pallas_call(kernel, out_shape=outputs, in_specs=in_specs, out_specs=[V...  9.93 us
    ppermute x1, waiting for transfers between devices, body(): spreads.append(lax.ppermute(keep[turn] + received[turn], 'angle', route))  4.24 us
    ppermute x6, waiting for transfers between devices, exchange(): return lax.ppermute(block, ('scan', 'tile'), rounds[number])  3.96 us
    ppermute x1, starting transfers between devices, body(): beside = lax.ppermute(base, ('scan', 'angle'), route)  2.9 us
    ppermute x1, waiting for transfers between devices, body(): beside = lax.ppermute(base, ('scan', 'angle'), route)  1.74 us
    ppermute x1, starting transfers between devices, body(): spreads.append(lax.ppermute(keep[turn] + received[turn], 'angle', route))  1.71 us
    ppermute x1, starting transfers between devices, body(): by_column.append(lax.ppermute(packed, 'angle', turns[turn]))  1.56 us
  transfers between devices with their start and end apart: 14, of which 6 were waited for; matrix products, arithmetic and copies ran while one was open for 0% of the time, Pallas kernels for 15%

profile of v11, /device:TPU:0, one launch (start us, length us, event | category | flops | bytes accessed | tf_op | source)
XLA Modules:
  0.0 41.1 jit_solution(5890443971999323567)
XLA Ops:
  0.6 1.0 %shard_map.175.plane_ref = f32[136,256]{1,0:T(8,128)S(1)} custom-call(f32[1,2,64,256]{3,2,1,0:T(8,128)} %plane_ref.1, f32[2,2,64,256]{3,2,1,0:T(8,128)} %volume_ref.1), custom_call_target="tpu_custom_call" | custom-call | flops 100000 | bytes 532480 | tf_op jit(solution)/shard_map/pallas_call | solution.py:521
  1.6 0.6 %collective-permute-start.1 = (f32[136,256]{1,0:T(8,128)S(1)}, f32[136,256]{1,0:T(8,128)S(1)}, u32[]{:S(2)}, u32[]{:S(2)}) collective-permute-start(f32[136,256]{1,0:T(8,128)S(1)} %shard_map.175.plane_ref), channel_id=1, source_target_pairs={{4,8},{5,9},{8,4},{9,5},{0,1},{1,0},{12,13},{13,12},{6,10},{7,11},... | collective-permute-start | bytes 417800 | tf_op jit(solution)/shard_map/ppermute | solution.py:561
  2.2 4.1 %collective-permute-start = (f32[136,256]{1,0:T(8,128)S(1)}, f32[136,256]{1,0:T(8,128)S(1)}, u32[]{:S(2)}, u32[]{:S(2)}) collective-permute-start(f32[136,256]{1,0:T(8,128)S(1)} %shard_map.175.plane_ref), channel_id=1, source_target_pairs={{0,4},{1,5},{8,12},{9,13},{4,0},{5,1},{12,8},{13,9},{2,6},{3,7},{1... | collective-permute-start | bytes 417800 | tf_op jit(solution)/shard_map/ppermute | solution.py:561
  6.9 2.0 %shard_map.174 = (f32[4,2,128,128]{3,2,1,0:T(8,128)S(1)}, f32[1,192,256]{2,1,0:T(8,128)S(1)}, s32[4,8,128]{2,1,0:T(8,128)S(1)}, f32[8,256]{1,0:T(8,128)S(1)}, f3...) custom-call(s32[1,1]{1,0:T(1,128)S(6)} %copy.19.count_ref, ...), custom_call_target="tpu_custom_call" | custom-call | flops 10000000 | bytes 1794048 | tf_op jit(solution)/shard_map/pallas_call | solution.py:521
  9.0 0.0 collective-permute-done.1.plane_b_ref
  9.0 0.7 %collective-permute-done.plane_a_ref = f32[136,256]{1,0:T(8,128)S(1)} collective-permute-done((f32[136,256]{1,0:T(8,128)S(1)}, f32[136,256]{1,0:T(8,128)S(1)}, u32[]{:S(2)}, u32[]{:S(2)}) %collective-permute-start) | collective-permute-done | bytes 139296 | tf_op jit(solution)/shard_map/ppermute | solution.py:561
  9.7 1.9 %shard_map.176 = (f32[3,64,256]{2,1,0:T(8,128)S(1)}, f32[192,256]{1,0:T(8,128)S(1)}, f32[192,256]{1,0:T(8,128)S(1)}, f32[2,72,256]{2,1,0:T(8,128)S(1)}, f32[2,72,256]{2,1,0:T(8,128)S(1)}) custom-call(f32[4,2,128,128]{3,2,1,0:T(8,128)S(1)} %get-tuple-element.33.probes_ref, f32[1,192,256]{2,1,0:T(8,128)S(1)} %get-tuple-element.34.density_ref, ...), custom_call_target="tpu_custom_call" | custom-call | flops 1000000000 | bytes 2957312 | tf_op jit(solution)/shard_map/pallas_call | solution.py:521
  11.6 1.8 %collective-permute-start.2 = (f32[192,256]{1,0:T(8,128)S(1)}, f32[192,256]{1,0:T(8,128)S(1)}, u32[]{:S(2)}, u32[]{:S(2)}) collective-permute-start(f32[192,256]{1,0:T(8,128)S(1)} %get-tuple-element.43), channel_id=1, source_target_pairs={{0,4},{1,5},{8,12},{9,13},{4,0},{5,1},{12,8},{13,9},{2,6},{3,7},{1... | collective-permute-start | bytes 589832 | tf_op jit(solution)/shard_map/ppermute | solution.py:561
  13.4 0.0 collective-permute-start.3
  13.4 0.5 %collective-permute-start.4 = (f32[8,256]{1,0:T(8,128)S(1)}, f32[8,256]{1,0:T(8,128)S(1)}, u32[]{:S(2)}, u32[]{:S(2)}) collective-permute-start(f32[8,256]{1,0:T(8,128)S(1)} %get-tuple-element.45.rays_ref), channel_id=1, source_target_pairs={{0,1},{1,0},{2,3},{3,2},{4,5},{5,4},{6,7},{7,6},{8,9},{9,8},{10,11... | collective-permute-start | bytes 24584 | tf_op jit(solution)/shard_map/ppermute | solution.py:564
  13.9 0.0 collective-permute-start.9
  13.9 1.5 %collective-permute-start.10 = (f32[2,72,256]{2,1,0:T(8,128)S(1)}, f32[2,72,256]{2,1,0:T(8,128)S(1)}, u32[]{:S(2)}, u32[]{:S(2)}) collective-permute-start(f32[2,72,256]{2,1,0:T(8,128)S(1)} %get-tuple-element.56), channel_id=1, source_target_pairs={{1,2},{2,1},{0,16},{3,19},{17,18},{18,17},{16,0},{19,3},{5,6},{6,5... | collective-permute-start | bytes 442376 | tf_op jit(solution)/shard_map/ppermute | solution.py:620
  15.5 2.0 %collective-permute-done.2.rim_a_ref = f32[192,256]{1,0:T(8,128)S(1)} collective-permute-done((f32[192,256]{1,0:T(8,128)S(1)}, f32[192,256]{1,0:T(8,128)S(1)}, u32[]{:S(2)}, u32[]{:S(2)}) %collective-permute-start.2) | collective-permute-done | bytes 196640 | tf_op jit(solution)/shard_map/ppermute | solution.py:561
  17.5 0.1 shard_map.177
  17.6 1.6 %collective-permute-start.5 = (f32[144,256]{1,0:T(8,128)S(1)}, f32[144,256]{1,0:T(8,128)S(1)}, u32[]{:S(2)}, u32[]{:S(2)}) collective-permute-start(f32[144,256]{1,0:T(8,128)S(1)} %get-tuple-element.46.refs_0_), channel_id=1, source_target_pairs={{0,2},{2,0},{1,3},{3,1},{4,6},{6,4},{5,7},{7,5},{8,10},{10,8},{9,1... | collective-permute-start | bytes 442376 | tf_op jit(solution)/shard_map/ppermute | solution.py:635
  19.1 0.5 %shard_map.180.base_ref.refs_3_ = f32[2,2,64,256]{3,2,1,0:T(8,128)S(1)} custom-call(f32[2,2,64,256]{3,2,1,0:T(8,128)S(1)} %get-tuple-element.37.volume_ref, f32[136,256]{1,0:T(8,128)S(1)} %collective-permute-done.plane_a_ref, f32[136,256]{1,0:T(8,128)S(1)} %collective-permute-done.1.plane_b_ref, f32[2,72,256]{2,1,0:T(8,128)S(1)} %collective-permute-done.9.row_a_ref, ...), custom_call_target="tpu_custom_call" | custom-call | flops 10000000 | bytes 1097728 | tf_op jit(solution)/shard_map/pallas_call | solution.py:521
  19.6 2.9 %collective-permute-start.11 = (f32[2,2,64,256]{3,2,1,0:T(8,128)S(1)}, f32[2,2,64,256]{3,2,1,0:T(8,128)S(1)}, u32[]{:S(2)}, u32[]{:S(2)}) collective-permute-start(f32[2,2,64,256]{3,2,1,0:T(8,128)S(1)} %shard_map.180.base_ref.refs_3_), channel_id=1, source_target_pairs={{0,4},{2,0},{4,8},{6,2},{8,12},{10,6},{12,14},{14,10},{1,5},{3,1},... | collective-permute-start | bytes 786440 | tf_op jit(solution)/shard_map/ppermute | solution.py:652
  22.5 0.2 collective-permute-done.5.refs_1_
  22.8 0.0 copy-start.2
  22.8 0.0 copy-start.3
  22.8 0.1 collective-permute-start.7
  22.9 4.6 %collective-permute-start.6 = (f32[2,128,256]{2,1,0:T(8,128)S(1)}, f32[2,128,256]{2,1,0:T(8,128)S(1)}, u32[]{:S(2)}, u32[]{:S(2)}) collective-permute-start(f32[2,128,256]{2,1,0:T(8,128)S(1)} %pad_maximum_fusion.here_ref), channel_id=1, source_target_pairs={{0,4},{1,5},{8,12},{9,13},{4,0},{5,1},{12,8},{13,9},{2,6},{3,7},{1... | collective-permute-start | bytes 786440 | tf_op jit(solution)/shard_map/ppermute | solution.py:561
  27.5 1.7 %collective-permute-done.11.beside_ref = f32[2,2,64,256]{3,2,1,0:T(8,128)S(1)} collective-permute-done((f32[2,2,64,256]{3,2,1,0:T(8,128)S(1)}, f32[2,2,64,256]{3,2,1,0:T(8,128)S(1)}, u32[]{:S(2)}, u32[]{:S(2)}) %collective-permute-start.11) | collective-permute-done | bytes 262176 | tf_op jit(solution)/shard_map/ppermute | solution.py:652
  29.2 0.8 %shard_map.181 = (f32[2,2,64,256]{3,2,1,0:T(8,128)S(1)}, f32[2,2,64,256]{3,2,1,0:T(8,128)S(1)}) custom-call(s32[2,4]{1,0:T(2,128)S(1)} %bitcast.13, f32[2,4]{1,0:T(2,128)S(1)} %bitcast.15, f32[2,2,64,256]{3,2,1,0:T(8,128)S(1)} %shard_map.180.base_ref.refs_3_, f32[2,2,64,256]{3,2,1,0:T(8,128)S(1)} %collective-permute-done.11.beside_ref), custom_call_target="tpu_custom_call" | custom-call | flops 10000000 | bytes 1048576 | tf_op jit(solution)/shard_map/pallas_call | solution.py:521
  30.0 0.1 collective-permute-start.12
  30.1 1.9 %shard_map.178 = (bf16[2,384,192]{2,1,0:T(8,128)(2,1)S(1)}, bf16[2,384,192]{2,1,0:T(8,128)(2,1)S(1)}, f32[1,2,64,256]{3,2,1,0:T(8,128)}) custom-call(f32[144,256]{1,0:T(8,128)S(1)} %get-tuple-element.46.refs_0_, f32[144,256]{1,0:T(8,128)S(1)} %collective-permute-done.5.refs_1_, f32[1,2,64,256]{3,2,1,0:T(8,128)S(1)} %get-tuple-element.47.refs_2_.refs_4_), custom_call_target="tpu_custom_call" | custom-call | flops 100000000 | bytes 1736704 | tf_op jit(solution)/shard_map/pallas_call | solution.py:521
  32.0 1.2 %collective-permute-done.6.side_a_ref = f32[2,128,256]{2,1,0:T(8,128)S(1)} collective-permute-done((f32[2,128,256]{2,1,0:T(8,128)S(1)}, f32[2,128,256]{2,1,0:T(8,128)S(1)}, u32[]{:S(2)}, u32[]{:S(2)}) %collective-permute-start.6) | collective-permute-done | bytes 262176 | tf_op jit(solution)/shard_map/ppermute | solution.py:561
  33.3 0.9 %shard_map.179 = (f32[2,64,256]{2,1,0:T(8,128)S(1)}, f32[2,2,64,256]{3,2,1,0:T(8,128)S(1)}, f32[384,256]{1,0:T(8,128)S(1)}) custom-call(f32[2,128,256]{2,1,0:T(8,128)S(1)} %pad_maximum_fusion.here_ref, f32[2,128,256]{2,1,0:T(8,128)S(1)} %collective-permute-done.6.side_a_ref, f32[2,128,256]{2,1,0:T(8,128)S(1)} %collective-permute-done.7.side_b_ref, ...), custom_call_target="tpu_custom_call" | custom-call | flops 1000000000 | bytes 2162688 | tf_op jit(solution)/shard_map/pallas_call | solution.py:521
  34.1 0.1 collective-permute-start.8
  34.3 1.7 %collective-permute-start.13 = (f32[2,64,256]{2,1,0:T(8,128)S(1)}, f32[2,64,256]{2,1,0:T(8,128)S(1)}, u32[]{:S(2)}, u32[]{:S(2)}) collective-permute-start(f32[2,64,256]{2,1,0:T(8,128)S(1)} %get-tuple-element.62), channel_id=1, source_target_pairs={{0,2},{2,0},{1,3},{3,1},{4,6},{6,4},{5,7},{7,5},{8,10},{10,8},{9,1... | collective-permute-start | bytes 393224 | tf_op jit(solution)/shard_map/ppermute | solution.py:678
  36.0 4.2 %collective-permute-done.13.refs_8_ = f32[2,64,256]{2,1,0:T(8,128)S(1)} collective-permute-done((f32[2,64,256]{2,1,0:T(8,128)S(1)}, f32[2,64,256]{2,1,0:T(8,128)S(1)}, u32[]{:S(2)}, u32[]{:S(2)}) %collective-permute-start.13) | collective-permute-done | bytes 131104 | tf_op jit(solution)/shard_map/ppermute | solution.py:678
  40.2 0.9 %shard_map.182 = (f32[1,2,64,256]{3,2,1,0:T(8,128)}, f32[2,2,64,256]{3,2,1,0:T(8,128)}, f32[1,2,64,256]{3,2,1,0:T(8,128)}) custom-call(f32[2,64,256]{2,1,0:T(8,128)S(1)} %get-tuple-element.52.refs_0_, f32[2,2,64,256]{3,2,1,0:T(8,128)S(1)} %get-tuple-element.53.refs_1_, f32[384,256]{1,0:T(8,128)S(1)} %collective-permute-done.8.refs_2_, ...), custom_call_target="tpu_custom_call" | custom-call | flops 1000000 | bytes 2228224 | tf_op jit(solution)/shard_map/pallas_call | solution.py:521
  (16 shorter events, 0.1 us)
Async XLA Ops:
  1.6 7.4 %collective-permute-start.1 = (f32[136,256]{1,0:T(8,128)S(1)}, f32[136,256]{1,0:T(8,128)S(1)}, u32[]{:S(2)}, u32[]{:S(2)}) collective-permute-start(f32[136,256]{1,0:T(8,128)S(1)} %shard_map.175.plane_ref), channel_id=1, source_target_pairs={{4,8},{5,9},{8,4},{9,5},{0,1},{1,0},{12,13},{13,12},{6,10},{7,11},... | collective-permute-start | bytes 417800 | tf_op jit(solution)/shard_map/ppermute | solution.py:561
  2.2 7.5 %collective-permute-start = (f32[136,256]{1,0:T(8,128)S(1)}, f32[136,256]{1,0:T(8,128)S(1)}, u32[]{:S(2)}, u32[]{:S(2)}) collective-permute-start(f32[136,256]{1,0:T(8,128)S(1)} %shard_map.175.plane_ref), channel_id=1, source_target_pairs={{0,4},{1,5},{8,12},{9,13},{4,0},{5,1},{12,8},{13,9},{2,6},{3,7},{1... | collective-permute-start | bytes 417800 | tf_op jit(solution)/shard_map/ppermute | solution.py:561
  9.7 7.8 %copy-start = (f32[1,2,64,256]{3,2,1,0:T(8,128)S(1)}, f32[1,2,64,256]{3,2,1,0:T(8,128)}, u32[]{:S(2)}) copy-start(f32[1,2,64,256]{3,2,1,0:T(8,128)} %refs_5_.2) | copy-start | bytes 393220
  9.7 7.8 %copy-start.1 = (f32[1,2,64,256]{3,2,1,0:T(8,128)S(1)}, f32[1,2,64,256]{3,2,1,0:T(8,128)}, u32[]{:S(2)}) copy-start(f32[1,2,64,256]{3,2,1,0:T(8,128)} %projected_ref.1) | copy-start | bytes 393220
  11.6 5.8 %collective-permute-start.2 = (f32[192,256]{1,0:T(8,128)S(1)}, f32[192,256]{1,0:T(8,128)S(1)}, u32[]{:S(2)}, u32[]{:S(2)}) collective-permute-start(f32[192,256]{1,0:T(8,128)S(1)} %get-tuple-element.43), channel_id=1, source_target_pairs={{0,4},{1,5},{8,12},{9,13},{4,0},{5,1},{12,8},{13,9},{2,6},{3,7},{1... | collective-permute-start | bytes 589832 | tf_op jit(solution)/shard_map/ppermute | solution.py:561
  13.4 4.0 %collective-permute-start.3 = (f32[192,256]{1,0:T(8,128)S(1)}, f32[192,256]{1,0:T(8,128)S(1)}, u32[]{:S(2)}, u32[]{:S(2)}) collective-permute-start(f32[192,256]{1,0:T(8,128)S(1)} %get-tuple-element.44), channel_id=1, source_target_pairs={{4,8},{5,9},{8,4},{9,5},{0,1},{1,0},{12,13},{13,12},{6,10},{7,11},... | collective-permute-start | bytes 589832 | tf_op jit(solution)/shard_map/ppermute | solution.py:561
  13.4 2.0 %collective-permute-start.4 = (f32[8,256]{1,0:T(8,128)S(1)}, f32[8,256]{1,0:T(8,128)S(1)}, u32[]{:S(2)}, u32[]{:S(2)}) collective-permute-start(f32[8,256]{1,0:T(8,128)S(1)} %get-tuple-element.45.rays_ref), channel_id=1, source_target_pairs={{0,1},{1,0},{2,3},{3,2},{4,5},{5,4},{6,7},{7,6},{8,9},{9,8},{10,11... | collective-permute-start | bytes 24584 | tf_op jit(solution)/shard_map/ppermute | solution.py:564
  13.9 5.2 %collective-permute-start.9 = (f32[2,72,256]{2,1,0:T(8,128)S(1)}, f32[2,72,256]{2,1,0:T(8,128)S(1)}, u32[]{:S(2)}, u32[]{:S(2)}) collective-permute-start(f32[2,72,256]{2,1,0:T(8,128)S(1)} %get-tuple-element.55), channel_id=1, source_target_pairs={{0,1},{1,0},{2,3},{3,2},{4,5},{5,4},{6,7},{7,6},{8,9},{9,8},{10,11... | collective-permute-start | bytes 442376 | tf_op jit(solution)/shard_map/ppermute | solution.py:564
  13.9 5.2 %collective-permute-start.10 = (f32[2,72,256]{2,1,0:T(8,128)S(1)}, f32[2,72,256]{2,1,0:T(8,128)S(1)}, u32[]{:S(2)}, u32[]{:S(2)}) collective-permute-start(f32[2,72,256]{2,1,0:T(8,128)S(1)} %get-tuple-element.56), channel_id=1, source_target_pairs={{1,2},{2,1},{0,16},{3,19},{17,18},{18,17},{16,0},{19,3},{5,6},{6,5... | collective-permute-start | bytes 442376 | tf_op jit(solution)/shard_map/ppermute | solution.py:620
  17.6 5.2 %collective-permute-start.5 = (f32[144,256]{1,0:T(8,128)S(1)}, f32[144,256]{1,0:T(8,128)S(1)}, u32[]{:S(2)}, u32[]{:S(2)}) collective-permute-start(f32[144,256]{1,0:T(8,128)S(1)} %get-tuple-element.46.refs_0_), channel_id=1, source_target_pairs={{0,2},{2,0},{1,3},{3,1},{4,6},{6,4},{5,7},{7,5},{8,10},{10,8},{9,1... | collective-permute-start | bytes 442376 | tf_op jit(solution)/shard_map/ppermute | solution.py:635
  19.6 9.6 %collective-permute-start.11 = (f32[2,2,64,256]{3,2,1,0:T(8,128)S(1)}, f32[2,2,64,256]{3,2,1,0:T(8,128)S(1)}, u32[]{:S(2)}, u32[]{:S(2)}) collective-permute-start(f32[2,2,64,256]{3,2,1,0:T(8,128)S(1)} %shard_map.180.base_ref.refs_3_), channel_id=1, source_target_pairs={{0,4},{2,0},{4,8},{6,2},{8,12},{10,6},{12,14},{14,10},{1,5},{3,1},... | collective-permute-start | bytes 786440 | tf_op jit(solution)/shard_map/ppermute | solution.py:652
  22.8 6.4 %copy-start.2 = (s32[4,2]{0,1:T(2,128)S(1)}, s32[4,2]{0,1:T(2,128)}, u32[]{:S(2)}) copy-start(s32[4,2]{0,1:T(2,128)} %param.24) | copy-start | bytes 100
  22.8 6.4 %copy-start.3 = (f32[4,2]{0,1:T(2,128)S(1)}, f32[4,2]{0,1:T(2,128)}, u32[]{:S(2)}) copy-start(f32[4,2]{0,1:T(2,128)} %param.25) | copy-start | bytes 100
  22.8 9.2 %collective-permute-start.7 = (f32[2,128,256]{2,1,0:T(8,128)S(1)}, f32[2,128,256]{2,1,0:T(8,128)S(1)}, u32[]{:S(2)}, u32[]{:S(2)}) collective-permute-start(f32[2,128,256]{2,1,0:T(8,128)S(1)} %pad_maximum_fusion.here_ref), channel_id=1, source_target_pairs={{4,8},{5,9},{8,4},{9,5},{0,1},{1,0},{12,13},{13,12},{6,10},{7,11},... | collective-permute-start | bytes 786440 | tf_op jit(solution)/shard_map/ppermute | solution.py:561
  22.9 10.3 %collective-permute-start.6 = (f32[2,128,256]{2,1,0:T(8,128)S(1)}, f32[2,128,256]{2,1,0:T(8,128)S(1)}, u32[]{:S(2)}, u32[]{:S(2)}) collective-permute-start(f32[2,128,256]{2,1,0:T(8,128)S(1)} %pad_maximum_fusion.here_ref), channel_id=1, source_target_pairs={{0,4},{1,5},{8,12},{9,13},{4,0},{5,1},{12,8},{13,9},{2,6},{3,7},{1... | collective-permute-start | bytes 786440 | tf_op jit(solution)/shard_map/ppermute | solution.py:561
  30.0 4.2 %collective-permute-start.12 = (f32[2,2,64,256]{3,2,1,0:T(8,128)S(1)}, f32[2,2,64,256]{3,2,1,0:T(8,128)S(1)}, u32[]{:S(2)}, u32[]{:S(2)}) collective-permute-start(f32[2,2,64,256]{3,2,1,0:T(8,128)S(1)} %get-tuple-element.58), channel_id=1, source_target_pairs={{0,1},{1,0},{2,3},{3,2},{4,5},{5,4},{6,7},{7,6},{8,9},{9,8},{10,11... | collective-permute-start | bytes 786440 | tf_op jit(solution)/shard_map/ppermute | solution.py:564
  34.1 6.1 %collective-permute-start.8 = (f32[384,256]{1,0:T(8,128)S(1)}, f32[384,256]{1,0:T(8,128)S(1)}, u32[]{:S(2)}, u32[]{:S(2)}) collective-permute-start(f32[384,256]{1,0:T(8,128)S(1)} %get-tuple-element.54), channel_id=1, source_target_pairs={{0,1},{1,0},{2,3},{3,2},{4,5},{5,4},{6,7},{7,6},{8,9},{9,8},{10,11... | collective-permute-start | bytes 1179656 | tf_op jit(solution)/shard_map/ppermute | solution.py:564
  34.3 6.0 %collective-permute-start.13 = (f32[2,64,256]{2,1,0:T(8,128)S(1)}, f32[2,64,256]{2,1,0:T(8,128)S(1)}, u32[]{:S(2)}, u32[]{:S(2)}) collective-permute-start(f32[2,64,256]{2,1,0:T(8,128)S(1)} %get-tuple-element.62), channel_id=1, source_target_pairs={{0,2},{2,0},{1,3},{3,1},{4,6},{6,4},{5,7},{7,5},{8,10},{10,8},{9,1... | collective-permute-start | bytes 393224 | tf_op jit(solution)/shard_map/ppermute | solution.py:678

commit v12 on v11

--- a/solution.py
+++ b/solution.py
@@ -362,11 +362,12 @@
 
 
 def spread_kernel(
-    shift_ref, weight_ref, base_ref, beside_ref, keep_ref, send_ref, padded
+    shift_ref, weight_ref, base_ref, beside_ref, *refs
 ):
     width = base_ref.shape[2]
     count = base_ref.shape[1]
-    columns, tiles = keep_ref.shape[0], lax.axis_size("tile")
+    padded, tiles = refs[-1], lax.axis_size("tile")
+    columns = (len(refs) - 1) // tiles
     me, tile, scan = lax.axis_index("angle"), lax.axis_index("tile"), lax.axis_index("scan")
     upper = me >= columns // 2
     chunks = [slice(at, at + LANES) for at in range(0, base_ref.shape[3], LANES)]
@@ -381,7 +382,7 @@
                     beside_ref[channel, row, :, at] * exists
                 )
     for turn in range(columns):
-        for flip, out_ref in ((0, keep_ref), (1, send_ref)):
+        for flip, out_ref in ((0, refs[turn]), (1, refs[columns + turn])):
             angle = lax.rem(me + turn, columns) * tiles + (tile if flip == 0 else 1 - tile)
             for channel in range(2):
                 for chunk, at in enumerate(chunks):
@@ -391,7 +392,7 @@
                         fraction = weight_ref[row, angle]
                         total += (1.0 - fraction) * padded[row, channel, chunk, pl.ds(start, width)]
                         total += fraction * padded[row, channel, chunk, pl.ds(start + 1, width)]
-                    out_ref[turn, channel, :, at] = total
+                    out_ref[channel, :, at] = total
 
 
 def operator_kernel(*refs):
@@ -662,20 +663,24 @@
         kind=jnp.bfloat16,
         kinds={2: jnp.float32},
     )
-    block = (columns, 2, width, length)
-    keep, send = call(
+    parts = call(
         spread_kernel,
-        [block, block],
+        [(2, width, length)] * (columns * tiles),
         (shift_table.T, tap_weight.T, base, beside),
         [(count, 2, length // LANES, 2 * width, LANES)],
         10**7,
         2,
     )
-    received = across(send)
-    spreads = [keep[0], received[0]]
-    for turn in range(1, columns):
-        route = [(i, (i + turn) % columns) for i in range(columns)]
-        spreads.append(lax.ppermute(keep[turn] + received[turn], "angle", route))
+    spreads = [parts[0]]
+    for turn in range(columns):
+        for flip in range(tiles):
+            route = [
+                (x * tiles + t, (x + turn) % columns * tiles + (t ^ flip))
+                for x in range(columns)
+                for t in range(tiles)
+            ]
+            if turn or flip:
+                spreads.append(lax.ppermute(parts[flip * columns + turn], ("angle", "tile"), route))
     keep, own, send = call(
         apply_kernel,
         [(2, width, length), volume.shape, ((2 + 2 * count) * width, length)],

time: 41.3 us -> 51.6 us (1.25)
  waiting for transfers between devices: 10.2 us -> 23.1 us
  starting transfers between devices: 19.5 us -> 16.9 us
    ppermute x1, waiting for transfers between devices: 0.01 us -> 3.62 us  [body(): row_b = lax.ppermute(row_b, ('groups', 'angle', 'tile'), bridge)]
    ppermute x1, waiting for transfers between devices: 1.74 us -> 5.29 us  [body(): beside = lax.ppermute(base, ('scan', 'angle'), route)]
    ppermute x1, waiting for transfers between devices: 0.24 us -> 3.65 us  [body(): by_column.append(lax.ppermute(packed, 'angle', turns[turn]))]
    ppermute x1, starting transfers between devices: 2.9 us -> 0.06 us  [body(): beside = lax.ppermute(base, ('scan', 'angle'), route)]
    ppermute x1 -> x3, waiting for transfers between devices: 4.24 us -> 6.32 us  [body(): lax.ppermute(parts[flip * columns + turn], ('angle', 'tile'), route)]
    ppermute x4 -> x3, waiting for transfers between devices: 0.01 us -> 0.95 us  [across(): return lax.ppermute(block, 'tile', swap)]
    ppermute x6, waiting for transfers between devices: 3.96 us -> 3.31 us  [exchange(): return lax.ppermute(block, ('scan', 'tile'), rounds[number])]
    ppermute x1 -> x3, starting transfers between devices: 1.71 us -> 1.92 us  [body(): lax.ppermute(parts[flip * columns + turn], ('angle', 'tile'), route)]
  transfers between devices with their start and end apart: 14 -> 15, of which waited for: 6 -> 8; matrix products, arithmetic and copies ran while one was open for 0% -> 0% of each run, Pallas kernels for 15% -> 12%
where the time goes in v12:
time: 51.6 us; the launch traced here: 51.4 us
  waiting for transfers between devices  23.1 us (45%)
  starting transfers between devices  16.9 us (33%)
  Pallas kernels  9.9 us (19%)
  between operations  1.4 us (3%)
    ppermute x6, starting transfers between devices, exchange(): return lax.ppermute(block, ('scan', 'tile'), rounds[number])  11.2 us
    pallas_call x9, Pallas kernels, call(): pl.pallas_call(kernel, out_shape=outputs, in_specs=in_specs, out_specs=[V...  9.9 us
    ppermute x3, waiting for transfers between devices, body(): lax.ppermute(parts[flip * columns + turn], ('angle', 'tile'), route)  6.32 us
    ppermute x1, waiting for transfers between devices, body(): beside = lax.ppermute(base, ('scan', 'angle'), route)  5.29 us
    ppermute x1, waiting for transfers between devices, body(): by_column.append(lax.ppermute(packed, 'angle', turns[turn]))  3.65 us
    ppermute x1, waiting for transfers between devices, body(): row_b = lax.ppermute(row_b, ('groups', 'angle', 'tile'), bridge)  3.62 us
    ppermute x6, waiting for transfers between devices, exchange(): return lax.ppermute(block, ('scan', 'tile'), rounds[number])  3.31 us
    ppermute x3, starting transfers between devices, body(): lax.ppermute(parts[flip * columns + turn], ('angle', 'tile'), route)  1.92 us
  transfers between devices with their start and end apart: 15, of which 8 were waited for; matrix products, arithmetic and copies ran while one was open for 0% of the time, Pallas kernels for 12%

profile of v12, /device:TPU:0, one launch (start us, length us, event | category | flops | bytes accessed | tf_op | source)
XLA Modules:
  0.0 51.4 jit_solution(5280556685384434679)
XLA Ops:
  0.6 1.0 %shard_map.175.plane_ref = f32[136,256]{1,0:T(8,128)S(1)} custom-call(f32[1,2,64,256]{3,2,1,0:T(8,128)} %plane_ref.1, f32[2,2,64,256]{3,2,1,0:T(8,128)} %volume_ref.1), custom_call_target="tpu_custom_call" | custom-call | flops 100000 | bytes 532480 | tf_op jit(solution)/shard_map/pallas_call | solution.py:522
  1.6 0.6 %collective-permute-start.1 = (f32[136,256]{1,0:T(8,128)S(1)}, f32[136,256]{1,0:T(8,128)S(1)}, u32[]{:S(2)}, u32[]{:S(2)}) collective-permute-start(f32[136,256]{1,0:T(8,128)S(1)} %shard_map.175.plane_ref), channel_id=1, source_target_pairs={{4,8},{5,9},{8,4},{9,5},{0,1},{1,0},{12,13},{13,12},{6,10},{7,11},... | collective-permute-start | bytes 417800 | tf_op jit(solution)/shard_map/ppermute | solution.py:562
  2.2 4.1 %collective-permute-start = (f32[136,256]{1,0:T(8,128)S(1)}, f32[136,256]{1,0:T(8,128)S(1)}, u32[]{:S(2)}, u32[]{:S(2)}) collective-permute-start(f32[136,256]{1,0:T(8,128)S(1)} %shard_map.175.plane_ref), channel_id=1, source_target_pairs={{0,4},{1,5},{8,12},{9,13},{4,0},{5,1},{12,8},{13,9},{2,6},{3,7},{1... | collective-permute-start | bytes 417800 | tf_op jit(solution)/shard_map/ppermute | solution.py:562
  6.9 2.0 %shard_map.174 = (f32[4,2,128,128]{3,2,1,0:T(8,128)S(1)}, f32[1,192,256]{2,1,0:T(8,128)S(1)}, s32[4,8,128]{2,1,0:T(8,128)S(1)}, f32[8,256]{1,0:T(8,128)S(1)}, f3...) custom-call(s32[1,1]{1,0:T(1,128)S(6)} %copy.19.count_ref, ...), custom_call_target="tpu_custom_call" | custom-call | flops 10000000 | bytes 1794048 | tf_op jit(solution)/shard_map/pallas_call | solution.py:522
  9.0 0.0 collective-permute-done.1.plane_b_ref
  9.0 0.7 %collective-permute-done.plane_a_ref = f32[136,256]{1,0:T(8,128)S(1)} collective-permute-done((f32[136,256]{1,0:T(8,128)S(1)}, f32[136,256]{1,0:T(8,128)S(1)}, u32[]{:S(2)}, u32[]{:S(2)}) %collective-permute-start) | collective-permute-done | bytes 139296 | tf_op jit(solution)/shard_map/ppermute | solution.py:562
  9.7 1.9 %shard_map.176 = (f32[3,64,256]{2,1,0:T(8,128)S(1)}, f32[192,256]{1,0:T(8,128)S(1)}, f32[192,256]{1,0:T(8,128)S(1)}, f32[2,72,256]{2,1,0:T(8,128)S(1)}, f32[2,72,256]{2,1,0:T(8,128)S(1)}) custom-call(f32[4,2,128,128]{3,2,1,0:T(8,128)S(1)} %get-tuple-element.35.probes_ref, f32[1,192,256]{2,1,0:T(8,128)S(1)} %get-tuple-element.36.density_ref, ...), custom_call_target="tpu_custom_call" | custom-call | flops 1000000000 | bytes 2957312 | tf_op jit(solution)/shard_map/pallas_call | solution.py:522
  11.6 1.8 %collective-permute-start.2 = (f32[192,256]{1,0:T(8,128)S(1)}, f32[192,256]{1,0:T(8,128)S(1)}, u32[]{:S(2)}, u32[]{:S(2)}) collective-permute-start(f32[192,256]{1,0:T(8,128)S(1)} %get-tuple-element.45), channel_id=1, source_target_pairs={{0,4},{1,5},{8,12},{9,13},{4,0},{5,1},{12,8},{13,9},{2,6},{3,7},{1... | collective-permute-start | bytes 589832 | tf_op jit(solution)/shard_map/ppermute | solution.py:562
  13.4 0.5 collective-permute-start.4
  13.9 0.9 %collective-permute-done.4.too_ref = f32[8,256]{1,0:T(8,128)S(1)} collective-permute-done((f32[8,256]{1,0:T(8,128)S(1)}, f32[8,256]{1,0:T(8,128)S(1)}, u32[]{:S(2)}, u32[]{:S(2)}) %collective-permute-start.4) | collective-permute-done | bytes 8224 | tf_op jit(solution)/shard_map/ppermute | solution.py:565
  14.9 2.6 %collective-permute-done.2.rim_a_ref = f32[192,256]{1,0:T(8,128)S(1)} collective-permute-done((f32[192,256]{1,0:T(8,128)S(1)}, f32[192,256]{1,0:T(8,128)S(1)}, u32[]{:S(2)}, u32[]{:S(2)}) %collective-permute-start.2) | collective-permute-done | bytes 196640 | tf_op jit(solution)/shard_map/ppermute | solution.py:562
  17.5 0.1 shard_map.177
  17.6 1.6 %collective-permute-start.5 = (f32[144,256]{1,0:T(8,128)S(1)}, f32[144,256]{1,0:T(8,128)S(1)}, u32[]{:S(2)}, u32[]{:S(2)}) collective-permute-start(f32[144,256]{1,0:T(8,128)S(1)} %get-tuple-element.48.refs_0_), channel_id=1, source_target_pairs={{0,2},{2,0},{1,3},{3,1},{4,6},{6,4},{5,7},{7,5},{8,10},{10,8},{9,1... | collective-permute-start | bytes 442376 | tf_op jit(solution)/shard_map/ppermute | solution.py:636
  19.1 3.7 %collective-permute-done.5.refs_1_ = f32[144,256]{1,0:T(8,128)S(1)} collective-permute-done((f32[144,256]{1,0:T(8,128)S(1)}, f32[144,256]{1,0:T(8,128)S(1)}, u32[]{:S(2)}, u32[]{:S(2)}) %collective-permute-start.5) | collective-permute-done | bytes 147488 | tf_op jit(solution)/shard_map/ppermute | solution.py:636
  22.8 0.1 collective-permute-start.7
  22.9 4.6 %collective-permute-start.6 = (f32[2,128,256]{2,1,0:T(8,128)S(1)}, f32[2,128,256]{2,1,0:T(8,128)S(1)}, u32[]{:S(2)}, u32[]{:S(2)}) collective-permute-start(f32[2,128,256]{2,1,0:T(8,128)S(1)} %pad_maximum_fusion.here_ref), channel_id=1, source_target_pairs={{0,4},{1,5},{8,12},{9,13},{4,0},{5,1},{12,8},{13,9},{2,6},{3,7},{1... | collective-permute-start | bytes 786440 | tf_op jit(solution)/shard_map/ppermute | solution.py:562
  27.5 1.5 %collective-permute-start.10 = (f32[2,72,256]{2,1,0:T(8,128)S(1)}, f32[2,72,256]{2,1,0:T(8,128)S(1)}, u32[]{:S(2)}, u32[]{:S(2)}) collective-permute-start(f32[2,72,256]{2,1,0:T(8,128)S(1)} %get-tuple-element.58), channel_id=1, source_target_pairs={{1,2},{2,1},{0,16},{3,19},{17,18},{18,17},{16,0},{19,3},{5,6},{6,5... | collective-permute-start | bytes 442376 | tf_op jit(solution)/shard_map/ppermute | solution.py:621
  29.0 3.6 %collective-permute-done.10.row_b_ref = f32[2,72,256]{2,1,0:T(8,128)S(1)} collective-permute-done((f32[2,72,256]{2,1,0:T(8,128)S(1)}, f32[2,72,256]{2,1,0:T(8,128)S(1)}, u32[]{:S(2)}, u32[]{:S(2)}) %collective-permute-start.10) | collective-permute-done | bytes 147488 | tf_op jit(solution)/shard_map/ppermute | solution.py:621
  32.6 0.5 shard_map.180.base_ref.refs_3_
  33.1 0.1 collective-permute-start.11
  33.2 1.9 %shard_map.178 = (bf16[2,384,192]{2,1,0:T(8,128)(2,1)S(1)}, bf16[2,384,192]{2,1,0:T(8,128)(2,1)S(1)}, f32[1,2,64,256]{3,2,1,0:T(8,128)}) custom-call(f32[144,256]{1,0:T(8,128)S(1)} %get-tuple-element.48.refs_0_, f32[144,256]{1,0:T(8,128)S(1)} %collective-permute-done.5.refs_1_, f32[1,2,64,256]{3,2,1,0:T(8,128)S(1)} %get-tuple-element.49.refs_2_.refs_4_), custom_call_target="tpu_custom_call" | custom-call | flops 100000000 | bytes 1736704 | tf_op jit(solution)/shard_map/pallas_call | solution.py:522
  35.1 0.9 %shard_map.179 = (f32[2,64,256]{2,1,0:T(8,128)S(1)}, f32[2,2,64,256]{3,2,1,0:T(8,128)S(1)}, f32[384,256]{1,0:T(8,128)S(1)}) custom-call(f32[2,128,256]{2,1,0:T(8,128)S(1)} %pad_maximum_fusion.here_ref, f32[2,128,256]{2,1,0:T(8,128)S(1)} %collective-permute-done.6.side_a_ref, f32[2,128,256]{2,1,0:T(8,128)S(1)} %collective-permute-done.7.side_b_ref, ...), custom_call_target="tpu_custom_call" | custom-call | flops 1000000000 | bytes 2162688 | tf_op jit(solution)/shard_map/pallas_call | solution.py:522
  36.0 0.0 copy-start.2
  36.0 0.2 collective-permute-start.8
  36.2 5.3 %collective-permute-done.11.beside_ref = f32[2,2,64,256]{3,2,1,0:T(8,128)S(1)} collective-permute-done((f32[2,2,64,256]{3,2,1,0:T(8,128)S(1)}, f32[2,2,64,256]{3,2,1,0:T(8,128)S(1)}, u32[]{:S(2)}, u32[]{:S(2)}) %collective-permute-start.11) | collective-permute-done | bytes 262176 | tf_op jit(solution)/shard_map/ppermute | solution.py:653
  41.5 0.8 %shard_map.181 = (f32[2,64,256]{2,1,0:T(8,128)S(1)}, f32[2,64,256]{2,1,0:T(8,128)S(1)}, f32[2,64,256]{2,1,0:T(8,128)S(1)}, f32[2,64,256]{2,1,0:T(8,128)S(1)}) custom-call(s32[2,4]{1,0:T(2,128)S(1)} %bitcast.7, f32[2,4]{1,0:T(2,128)S(1)} %bitcast.9, f32[2,2,64,256]{3,2,1,0:T(8,128)S(1)} %shard_map.180.base_ref.refs_3_, ...), custom_call_target="tpu_custom_call" | custom-call | flops 10000000 | bytes 1048576 | tf_op jit(solution)/shard_map/pallas_call | solution.py:522
  42.3 0.1 collective-permute-start.12
  42.3 1.0 %collective-permute-start.13 = (f32[2,64,256]{2,1,0:T(8,128)S(1)}, f32[2,64,256]{2,1,0:T(8,128)S(1)}, u32[]{:S(2)}, u32[]{:S(2)}) collective-permute-start(f32[2,64,256]{2,1,0:T(8,128)S(1)} %get-tuple-element.61), channel_id=1, source_target_pairs={{0,2},{1,3},{2,0},{3,1},{4,6},{5,7},{6,4},{7,5},{8,10},{9,11},{10,... | collective-permute-start | bytes 393224 | tf_op jit(solution)/shard_map/ppermute | solution.py:683
  43.3 0.9 %collective-permute-start.14 = (f32[2,64,256]{2,1,0:T(8,128)S(1)}, f32[2,64,256]{2,1,0:T(8,128)S(1)}, u32[]{:S(2)}, u32[]{:S(2)}) collective-permute-start(f32[2,64,256]{2,1,0:T(8,128)S(1)} %get-tuple-element.62), channel_id=1, source_target_pairs={{0,3},{1,2},{2,1},{3,0},{4,7},{5,6},{6,5},{7,4},{8,11},{9,10},{10,... | collective-permute-start | bytes 393224 | tf_op jit(solution)/shard_map/ppermute | solution.py:683
  44.2 4.6 %collective-permute-done.13.refs_8_ = f32[2,64,256]{2,1,0:T(8,128)S(1)} collective-permute-done((f32[2,64,256]{2,1,0:T(8,128)S(1)}, f32[2,64,256]{2,1,0:T(8,128)S(1)}, u32[]{:S(2)}, u32[]{:S(2)}) %collective-permute-start.13) | collective-permute-done | bytes 131104 | tf_op jit(solution)/shard_map/ppermute | solution.py:683
  48.8 1.7 %collective-permute-done.14.refs_9_ = f32[2,64,256]{2,1,0:T(8,128)S(1)} collective-permute-done((f32[2,64,256]{2,1,0:T(8,128)S(1)}, f32[2,64,256]{2,1,0:T(8,128)S(1)}, u32[]{:S(2)}, u32[]{:S(2)}) %collective-permute-start.14) | collective-permute-done | bytes 131104 | tf_op jit(solution)/shard_map/ppermute | solution.py:683
  50.5 0.9 %shard_map.182 = (f32[1,2,64,256]{3,2,1,0:T(8,128)}, f32[2,2,64,256]{3,2,1,0:T(8,128)}, f32[1,2,64,256]{3,2,1,0:T(8,128)}) custom-call(f32[2,64,256]{2,1,0:T(8,128)S(1)} %get-tuple-element.54.refs_0_, f32[2,2,64,256]{3,2,1,0:T(8,128)S(1)} %get-tuple-element.55.refs_1_, f32[384,256]{1,0:T(8,128)S(1)} %collective-permute-done.8.refs_2_, ...), custom_call_target="tpu_custom_call" | custom-call | flops 1000000 | bytes 2359296 | tf_op jit(solution)/shard_map/pallas_call | solution.py:522
  (17 shorter events, 0.1 us)
Async XLA Ops:
  1.6 7.4 %collective-permute-start.1 = (f32[136,256]{1,0:T(8,128)S(1)}, f32[136,256]{1,0:T(8,128)S(1)}, u32[]{:S(2)}, u32[]{:S(2)}) collective-permute-start(f32[136,256]{1,0:T(8,128)S(1)} %shard_map.175.plane_ref), channel_id=1, source_target_pairs={{4,8},{5,9},{8,4},{9,5},{0,1},{1,0},{12,13},{13,12},{6,10},{7,11},... | collective-permute-start | bytes 417800 | tf_op jit(solution)/shard_map/ppermute | solution.py:562
  2.2 7.5 %collective-permute-start = (f32[136,256]{1,0:T(8,128)S(1)}, f32[136,256]{1,0:T(8,128)S(1)}, u32[]{:S(2)}, u32[]{:S(2)}) collective-permute-start(f32[136,256]{1,0:T(8,128)S(1)} %shard_map.175.plane_ref), channel_id=1, source_target_pairs={{0,4},{1,5},{8,12},{9,13},{4,0},{5,1},{12,8},{13,9},{2,6},{3,7},{1... | collective-permute-start | bytes 417800 | tf_op jit(solution)/shard_map/ppermute | solution.py:562
  9.7 7.8 %copy-start = (f32[1,2,64,256]{3,2,1,0:T(8,128)S(1)}, f32[1,2,64,256]{3,2,1,0:T(8,128)}, u32[]{:S(2)}) copy-start(f32[1,2,64,256]{3,2,1,0:T(8,128)} %refs_5_.2) | copy-start | bytes 393220
  9.7 7.8 %copy-start.1 = (f32[1,2,64,256]{3,2,1,0:T(8,128)S(1)}, f32[1,2,64,256]{3,2,1,0:T(8,128)}, u32[]{:S(2)}) copy-start(f32[1,2,64,256]{3,2,1,0:T(8,128)} %projected_ref.1) | copy-start | bytes 393220
  11.6 5.8 %collective-permute-start.2 = (f32[192,256]{1,0:T(8,128)S(1)}, f32[192,256]{1,0:T(8,128)S(1)}, u32[]{:S(2)}, u32[]{:S(2)}) collective-permute-start(f32[192,256]{1,0:T(8,128)S(1)} %get-tuple-element.45), channel_id=1, source_target_pairs={{0,4},{1,5},{8,12},{9,13},{4,0},{5,1},{12,8},{13,9},{2,6},{3,7},{1... | collective-permute-start | bytes 589832 | tf_op jit(solution)/shard_map/ppermute | solution.py:562
  13.4 4.0 %collective-permute-start.3 = (f32[192,256]{1,0:T(8,128)S(1)}, f32[192,256]{1,0:T(8,128)S(1)}, u32[]{:S(2)}, u32[]{:S(2)}) collective-permute-start(f32[192,256]{1,0:T(8,128)S(1)} %get-tuple-element.46), channel_id=1, source_target_pairs={{4,8},{5,9},{8,4},{9,5},{0,1},{1,0},{12,13},{13,12},{6,10},{7,11},... | collective-permute-start | bytes 589832 | tf_op jit(solution)/shard_map/ppermute | solution.py:562
  13.4 1.5 %collective-permute-start.4 = (f32[8,256]{1,0:T(8,128)S(1)}, f32[8,256]{1,0:T(8,128)S(1)}, u32[]{:S(2)}, u32[]{:S(2)}) collective-permute-start(f32[8,256]{1,0:T(8,128)S(1)} %get-tuple-element.47.rays_ref), channel_id=1, source_target_pairs={{0,1},{1,0},{2,3},{3,2},{4,5},{5,4},{6,7},{7,6},{8,9},{9,8},{10,11... | collective-permute-start | bytes 24584 | tf_op jit(solution)/shard_map/ppermute | solution.py:565
  17.6 5.2 %collective-permute-start.5 = (f32[144,256]{1,0:T(8,128)S(1)}, f32[144,256]{1,0:T(8,128)S(1)}, u32[]{:S(2)}, u32[]{:S(2)}) collective-permute-start(f32[144,256]{1,0:T(8,128)S(1)} %get-tuple-element.48.refs_0_), channel_id=1, source_target_pairs={{0,2},{2,0},{1,3},{3,1},{4,6},{6,4},{5,7},{7,5},{8,10},{10,8},{9,1... | collective-permute-start | bytes 442376 | tf_op jit(solution)/shard_map/ppermute | solution.py:636
  22.8 12.3 %collective-permute-start.7 = (f32[2,128,256]{2,1,0:T(8,128)S(1)}, f32[2,128,256]{2,1,0:T(8,128)S(1)}, u32[]{:S(2)}, u32[]{:S(2)}) collective-permute-start(f32[2,128,256]{2,1,0:T(8,128)S(1)} %pad_maximum_fusion.here_ref), channel_id=1, source_target_pairs={{4,8},{5,9},{8,4},{9,5},{0,1},{1,0},{12,13},{13,12},{6,10},{7,11},... | collective-permute-start | bytes 786440 | tf_op jit(solution)/shard_map/ppermute | solution.py:562
  22.9 12.2 %collective-permute-start.6 = (f32[2,128,256]{2,1,0:T(8,128)S(1)}, f32[2,128,256]{2,1,0:T(8,128)S(1)}, u32[]{:S(2)}, u32[]{:S(2)}) collective-permute-start(f32[2,128,256]{2,1,0:T(8,128)S(1)} %pad_maximum_fusion.here_ref), channel_id=1, source_target_pairs={{0,4},{1,5},{8,12},{9,13},{4,0},{5,1},{12,8},{13,9},{2,6},{3,7},{1... | collective-permute-start | bytes 786440 | tf_op jit(solution)/shard_map/ppermute | solution.py:562
  27.5 1.5 %collective-permute-start.9 = (f32[2,72,256]{2,1,0:T(8,128)S(1)}, f32[2,72,256]{2,1,0:T(8,128)S(1)}, u32[]{:S(2)}, u32[]{:S(2)}) collective-permute-start(f32[2,72,256]{2,1,0:T(8,128)S(1)} %get-tuple-element.57), channel_id=1, source_target_pairs={{0,1},{1,0},{2,3},{3,2},{4,5},{5,4},{6,7},{7,6},{8,9},{9,8},{10,11... | collective-permute-start | bytes 442376 | tf_op jit(solution)/shard_map/ppermute | solution.py:565
  27.5 5.1 %collective-permute-start.10 = (f32[2,72,256]{2,1,0:T(8,128)S(1)}, f32[2,72,256]{2,1,0:T(8,128)S(1)}, u32[]{:S(2)}, u32[]{:S(2)}) collective-permute-start(f32[2,72,256]{2,1,0:T(8,128)S(1)} %get-tuple-element.58), channel_id=1, source_target_pairs={{1,2},{2,1},{0,16},{3,19},{17,18},{18,17},{16,0},{19,3},{5,6},{6,5... | collective-permute-start | bytes 442376 | tf_op jit(solution)/shard_map/ppermute | solution.py:621
  33.1 8.4 %collective-permute-start.11 = (f32[2,2,64,256]{3,2,1,0:T(8,128)S(1)}, f32[2,2,64,256]{3,2,1,0:T(8,128)S(1)}, u32[]{:S(2)}, u32[]{:S(2)}) collective-permute-start(f32[2,2,64,256]{3,2,1,0:T(8,128)S(1)} %shard_map.180.base_ref.refs_3_), channel_id=1, source_target_pairs={{0,4},{2,0},{4,8},{6,2},{8,12},{10,6},{12,14},{14,10},{1,5},{3,1},... | collective-permute-start | bytes 786440 | tf_op jit(solution)/shard_map/ppermute | solution.py:653
  35.1 6.4 %copy-start.3 = (f32[4,2]{0,1:T(2,128)S(1)}, f32[4,2]{0,1:T(2,128)}, u32[]{:S(2)}) copy-start(f32[4,2]{0,1:T(2,128)} %param.25) | copy-start | bytes 100
  36.0 5.5 %copy-start.2 = (s32[4,2]{0,1:T(2,128)S(1)}, s32[4,2]{0,1:T(2,128)}, u32[]{:S(2)}) copy-start(s32[4,2]{0,1:T(2,128)} %param.24) | copy-start | bytes 100
  36.0 14.5 %collective-permute-start.8 = (f32[384,256]{1,0:T(8,128)S(1)}, f32[384,256]{1,0:T(8,128)S(1)}, u32[]{:S(2)}, u32[]{:S(2)}) collective-permute-start(f32[384,256]{1,0:T(8,128)S(1)} %get-tuple-element.56), channel_id=1, source_target_pairs={{0,1},{1,0},{2,3},{3,2},{4,5},{5,4},{6,7},{7,6},{8,9},{9,8},{10,11... | collective-permute-start | bytes 1179656 | tf_op jit(solution)/shard_map/ppermute | solution.py:565
  42.3 1.9 %collective-permute-start.12 = (f32[2,64,256]{2,1,0:T(8,128)S(1)}, f32[2,64,256]{2,1,0:T(8,128)S(1)}, u32[]{:S(2)}, u32[]{:S(2)}) collective-permute-start(f32[2,64,256]{2,1,0:T(8,128)S(1)} %get-tuple-element.60), channel_id=1, source_target_pairs={{0,1},{1,0},{2,3},{3,2},{4,5},{5,4},{6,7},{7,6},{8,9},{9,8},{10,11... | collective-permute-start | bytes 393224 | tf_op jit(solution)/shard_map/ppermute | solution.py:683
  42.3 6.4 %collective-permute-start.13 = (f32[2,64,256]{2,1,0:T(8,128)S(1)}, f32[2,64,256]{2,1,0:T(8,128)S(1)}, u32[]{:S(2)}, u32[]{:S(2)}) collective-permute-start(f32[2,64,256]{2,1,0:T(8,128)S(1)} %get-tuple-element.61), channel_id=1, source_target_pairs={{0,2},{1,3},{2,0},{3,1},{4,6},{5,7},{6,4},{7,5},{8,10},{9,11},{10,... | collective-permute-start | bytes 393224 | tf_op jit(solution)/shard_map/ppermute | solution.py:683
  43.3 7.2 %collective-permute-start.14 = (f32[2,64,256]{2,1,0:T(8,128)S(1)}, f32[2,64,256]{2,1,0:T(8,128)S(1)}, u32[]{:S(2)}, u32[]{:S(2)}) collective-permute-start(f32[2,64,256]{2,1,0:T(8,128)S(1)} %get-tuple-element.62), channel_id=1, source_target_pairs={{0,3},{1,2},{2,1},{3,0},{4,7},{5,6},{6,5},{7,4},{8,11},{9,10},{10,... | collective-permute-start | bytes 393224 | tf_op jit(solution)/shard_map/ppermute | solution.py:683

commit v13 on v11

--- a/solution.py
+++ b/solution.py
@@ -483,10 +483,19 @@
             send_ref[target : target + width] = total[at + count * width : at + (count + 1) * width]
 
 
+def volume_kernel(own_ref, received_ref, base_ref, volume_ref):
+    count, width = own_ref.shape[1:3]
+    for channel in range(2):
+        for row in range(count):
+            at = (2 + channel * count + row) * width
+            descent = own_ref[channel, row] + received_ref[at : at + width]
+            volume_ref[channel, row] = base_ref[channel, row] - step_size * descent
+
+
 def finish_kernel(*refs):
-    keep_ref, own_ref, received_ref, base_ref, object_ref, dual_ref = refs[:6]
-    spreads, (dual_out_ref, volume_ref, projected_ref) = refs[6:-3], refs[-3:]
-    count, width = own_ref.shape[1:3]
+    keep_ref, received_ref, object_ref, dual_ref = refs[:4]
+    spreads, (dual_out_ref, projected_ref) = refs[4:-2], refs[-2:]
+    width = keep_ref.shape[1]
     for channel in range(2):
         received = received_ref[channel * width : (channel + 1) * width]
         projection = -step_size * (keep_ref[channel] + received)
@@ -494,10 +503,6 @@
             projection = projection + spread_ref[channel]
         projected_ref[0, channel] = projection
         dual_out_ref[0, channel] = dual_ref[0, channel] + object_ref[0, channel] - projection
-        for row in range(count):
-            at = (2 + channel * count + row) * width
-            descent = own_ref[channel, row] + received_ref[at : at + width]
-            volume_ref[channel, row] = base_ref[channel, row] - step_size * descent
 
 
 def call(
@@ -684,10 +689,11 @@
         10**9,
     )
     received = across(send)
-    new_dual, new_volume, new_projected = call(
+    (new_volume,) = call(volume_kernel, [volume.shape], (own, received, base), [], 10**6)
+    new_dual, new_projected = call(
         finish_kernel,
-        [transmission.shape, volume.shape, transmission.shape],
-        (keep, own, received, base, updated, scaled_dual, *spreads),
+        [transmission.shape] * 2,
+        (keep, received, updated, scaled_dual, *spreads),
         [],
         10**6,
     )

time: 41.3 us -> 40.7 us (0.985)
  starting transfers between devices: 19.5 us -> 14.3 us
  waiting for transfers between devices: 10.2 us -> 14.1 us
  Pallas kernels: 9.93 us -> 10.5 us
    ppermute x6, starting transfers between devices: 11.2 us -> 7.13 us  [exchange(): return lax.ppermute(block, ('scan', 'tile'), rounds[number])]
    ppermute x1, waiting for transfers between devices: 1.74 us -> 3.67 us  [body(): beside = lax.ppermute(base, ('scan', 'angle'), route)]
    ppermute x1, waiting for transfers between devices: 0.24 us -> 2.07 us  [body(): by_column.append(lax.ppermute(packed, 'angle', turns[turn]))]
    ppermute x1, starting transfers between devices: 2.9 us -> 1.87 us  [body(): beside = lax.ppermute(base, ('scan', 'angle'), route)]
    ppermute x1, waiting for transfers between devices: 4.24 us -> 3.54 us  [body(): spreads.append(lax.ppermute(keep[turn] + received[turn], 'angle', route))]
    ppermute x6, waiting for transfers between devices: 3.96 us -> 4.66 us  [exchange(): return lax.ppermute(block, ('scan', 'tile'), rounds[number])]
    pallas_call x9 -> x10, Pallas kernels: 9.93 us -> 10.5 us  [call(): pl.pallas_call(kernel, out_shape=outputs, in_specs=in_specs, out_specs=[V...]
  transfers between devices with their start and end apart: 14 -> 14, of which waited for: 6 -> 7; matrix products, arithmetic and copies ran while one was open for 0% -> 0% of each run, Pallas kernels for 15% -> 17%
where the time goes in v13:
time: 40.7 us; the launch traced here: 40.4 us
  starting transfers between devices  14.3 us (35%)
  waiting for transfers between devices  14.1 us (35%)
  Pallas kernels  10.5 us (26%)
  between operations  1.4 us (3%)
    pallas_call x10, Pallas kernels, call(): pl.pallas_call(kernel, out_shape=outputs, in_specs=in_specs, out_specs=[V...  10.5 us
    ppermute x6, starting transfers between devices, exchange(): return lax.ppermute(block, ('scan', 'tile'), rounds[number])  7.13 us
    ppermute x6, waiting for transfers between devices, exchange(): return lax.ppermute(block, ('scan', 'tile'), rounds[number])  4.66 us
    ppermute x1, waiting for transfers between devices, body(): beside = lax.ppermute(base, ('scan', 'angle'), route)  3.67 us
    ppermute x1, waiting for transfers between devices, body(): spreads.append(lax.ppermute(keep[turn] + received[turn], 'angle', route))  3.54 us
    ppermute x1, waiting for transfers between devices, body(): by_column.append(lax.ppermute(packed, 'angle', turns[turn]))  2.07 us
    ppermute x1, starting transfers between devices, body(): beside = lax.ppermute(base, ('scan', 'angle'), route)  1.87 us
    ppermute x1, starting transfers between devices, body(): by_column.append(lax.ppermute(packed, 'angle', turns[turn]))  1.55 us
  transfers between devices with their start and end apart: 14, of which 7 were waited for; matrix products, arithmetic and copies ran while one was open for 0% of the time, Pallas kernels for 17%

profile of v13, /device:TPU:0, one launch (start us, length us, event | category | flops | bytes accessed | tf_op | source)
XLA Modules:
  0.0 40.4 jit_solution(14644858924706981340)
XLA Ops:
  0.6 1.0 %shard_map.175.plane_ref = f32[136,256]{1,0:T(8,128)S(1)} custom-call(f32[1,2,64,256]{3,2,1,0:T(8,128)} %plane_ref.1, f32[2,2,64,256]{3,2,1,0:T(8,128)} %volume_ref.1), custom_call_target="tpu_custom_call" | custom-call | flops 100000 | bytes 532480 | tf_op jit(solution)/shard_map/pallas_call | solution.py:526
  1.6 3.1 %collective-permute-start = (f32[136,256]{1,0:T(8,128)S(1)}, f32[136,256]{1,0:T(8,128)S(1)}, u32[]{:S(2)}, u32[]{:S(2)}) collective-permute-start(f32[136,256]{1,0:T(8,128)S(1)} %shard_map.175.plane_ref), channel_id=1, source_target_pairs={{0,4},{1,5},{8,12},{9,13},{4,0},{5,1},{12,8},{13,9},{2,6},{3,7},{1... | collective-permute-start | bytes 417800 | tf_op jit(solution)/shard_map/ppermute | solution.py:566
  4.7 0.0 collective-permute-start.1
  5.4 2.0 %shard_map.174 = (f32[4,2,128,128]{3,2,1,0:T(8,128)S(1)}, f32[1,192,256]{2,1,0:T(8,128)S(1)}, s32[4,8,128]{2,1,0:T(8,128)S(1)}, f32[8,256]{1,0:T(8,128)S(1)}, f3...) custom-call(s32[1,1]{1,0:T(1,128)S(6)} %copy.19.count_ref, ...), custom_call_target="tpu_custom_call" | custom-call | flops 10000000 | bytes 1794048 | tf_op jit(solution)/shard_map/pallas_call | solution.py:526
  7.4 1.0 %collective-permute-done.plane_a_ref = f32[136,256]{1,0:T(8,128)S(1)} collective-permute-done((f32[136,256]{1,0:T(8,128)S(1)}, f32[136,256]{1,0:T(8,128)S(1)}, u32[]{:S(2)}, u32[]{:S(2)}) %collective-permute-start) | collective-permute-done | bytes 139296 | tf_op jit(solution)/shard_map/ppermute | solution.py:566
  8.4 1.9 %shard_map.176 = (f32[3,64,256]{2,1,0:T(8,128)S(1)}, f32[192,256]{1,0:T(8,128)S(1)}, f32[192,256]{1,0:T(8,128)S(1)}, f32[2,72,256]{2,1,0:T(8,128)S(1)}, f32[2,72,256]{2,1,0:T(8,128)S(1)}) custom-call(f32[4,2,128,128]{3,2,1,0:T(8,128)S(1)} %get-tuple-element.32.probes_ref, f32[1,192,256]{2,1,0:T(8,128)S(1)} %get-tuple-element.33.density_ref, ...), custom_call_target="tpu_custom_call" | custom-call | flops 1000000000 | bytes 2957312 | tf_op jit(solution)/shard_map/pallas_call | solution.py:526
  10.3 2.9 %collective-permute-start.2 = (f32[192,256]{1,0:T(8,128)S(1)}, f32[192,256]{1,0:T(8,128)S(1)}, u32[]{:S(2)}, u32[]{:S(2)}) collective-permute-start(f32[192,256]{1,0:T(8,128)S(1)} %get-tuple-element.42), channel_id=1, source_target_pairs={{0,4},{1,5},{8,12},{9,13},{4,0},{5,1},{12,8},{13,9},{2,6},{3,7},{1... | collective-permute-start | bytes 589832 | tf_op jit(solution)/shard_map/ppermute | solution.py:566
  13.3 0.5 %collective-permute-start.4 = (f32[8,256]{1,0:T(8,128)S(1)}, f32[8,256]{1,0:T(8,128)S(1)}, u32[]{:S(2)}, u32[]{:S(2)}) collective-permute-start(f32[8,256]{1,0:T(8,128)S(1)} %get-tuple-element.44.rays_ref), channel_id=1, source_target_pairs={{0,1},{1,0},{2,3},{3,2},{4,5},{5,4},{6,7},{7,6},{8,9},{9,8},{10,11... | collective-permute-start | bytes 24584 | tf_op jit(solution)/shard_map/ppermute | solution.py:569
  13.8 1.5 %collective-permute-start.10 = (f32[2,72,256]{2,1,0:T(8,128)S(1)}, f32[2,72,256]{2,1,0:T(8,128)S(1)}, u32[]{:S(2)}, u32[]{:S(2)}) collective-permute-start(f32[2,72,256]{2,1,0:T(8,128)S(1)} %get-tuple-element.54), channel_id=1, source_target_pairs={{1,2},{2,1},{0,16},{3,19},{17,18},{18,17},{16,0},{19,3},{5,6},{6,5... | collective-permute-start | bytes 442376 | tf_op jit(solution)/shard_map/ppermute | solution.py:625
  15.3 0.1 collective-permute-start.9
  15.4 1.9 %collective-permute-done.2.rim_a_ref = f32[192,256]{1,0:T(8,128)S(1)} collective-permute-done((f32[192,256]{1,0:T(8,128)S(1)}, f32[192,256]{1,0:T(8,128)S(1)}, u32[]{:S(2)}, u32[]{:S(2)}) %collective-permute-start.2) | collective-permute-done | bytes 196640 | tf_op jit(solution)/shard_map/ppermute | solution.py:566
  17.3 0.0 collective-permute-done.3.rim_b_ref
  17.3 0.1 shard_map.177
  17.4 1.6 %collective-permute-start.5 = (f32[144,256]{1,0:T(8,128)S(1)}, f32[144,256]{1,0:T(8,128)S(1)}, u32[]{:S(2)}, u32[]{:S(2)}) collective-permute-start(f32[144,256]{1,0:T(8,128)S(1)} %get-tuple-element.45.refs_0_), channel_id=1, source_target_pairs={{0,2},{2,0},{1,3},{3,1},{4,6},{6,4},{5,7},{7,5},{8,10},{10,8},{9,1... | collective-permute-start | bytes 442376 | tf_op jit(solution)/shard_map/ppermute | solution.py:640
  19.0 0.5 %shard_map.180.base_ref = f32[2,2,64,256]{3,2,1,0:T(8,128)S(1)} custom-call(f32[2,2,64,256]{3,2,1,0:T(8,128)S(1)} %get-tuple-element.36.volume_ref, f32[136,256]{1,0:T(8,128)S(1)} %collective-permute-done.plane_a_ref, f32[136,256]{1,0:T(8,128)S(1)} %collective-permute-done.1.plane_b_ref, f32[2,72,256]{2,1,0:T(8,128)S(1)} %collective-permute-done.9.row_a_ref, ...), custom_call_target="tpu_custom_call" | custom-call | flops 10000000 | bytes 1097728 | tf_op jit(solution)/shard_map/pallas_call | solution.py:526
  19.5 1.9 %collective-permute-start.11 = (f32[2,2,64,256]{3,2,1,0:T(8,128)S(1)}, f32[2,2,64,256]{3,2,1,0:T(8,128)S(1)}, u32[]{:S(2)}, u32[]{:S(2)}) collective-permute-start(f32[2,2,64,256]{3,2,1,0:T(8,128)S(1)} %shard_map.180.base_ref), channel_id=1, source_target_pairs={{0,4},{2,0},{4,8},{6,2},{8,12},{10,6},{12,14},{14,10},{1,5},{3,1},... | collective-permute-start | bytes 786440 | tf_op jit(solution)/shard_map/ppermute | solution.py:657
  21.3 2.1 %collective-permute-done.5.refs_1_ = f32[144,256]{1,0:T(8,128)S(1)} collective-permute-done((f32[144,256]{1,0:T(8,128)S(1)}, f32[144,256]{1,0:T(8,128)S(1)}, u32[]{:S(2)}, u32[]{:S(2)}) %collective-permute-start.5) | collective-permute-done | bytes 147488 | tf_op jit(solution)/shard_map/ppermute | solution.py:640
  23.4 0.0 copy-start.2
  23.4 0.0 copy-start.3
  23.5 1.1 %collective-permute-start.6 = (f32[2,128,256]{2,1,0:T(8,128)S(1)}, f32[2,128,256]{2,1,0:T(8,128)S(1)}, u32[]{:S(2)}, u32[]{:S(2)}) collective-permute-start(f32[2,128,256]{2,1,0:T(8,128)S(1)} %pad_maximum_fusion.here_ref), channel_id=1, source_target_pairs={{0,4},{1,5},{8,12},{9,13},{4,0},{5,1},{12,8},{13,9},{2,6},{3,7},{1... | collective-permute-start | bytes 786440 | tf_op jit(solution)/shard_map/ppermute | solution.py:566
  24.6 3.7 %collective-permute-done.11.beside_ref = f32[2,2,64,256]{3,2,1,0:T(8,128)S(1)} collective-permute-done((f32[2,2,64,256]{3,2,1,0:T(8,128)S(1)}, f32[2,2,64,256]{3,2,1,0:T(8,128)S(1)}, u32[]{:S(2)}, u32[]{:S(2)}) %collective-permute-start.11) | collective-permute-done | bytes 262176 | tf_op jit(solution)/shard_map/ppermute | solution.py:657
  28.2 0.8 %shard_map.181 = (f32[2,2,64,256]{3,2,1,0:T(8,128)S(1)}, f32[2,2,64,256]{3,2,1,0:T(8,128)S(1)}) custom-call(s32[2,4]{1,0:T(2,128)S(1)} %bitcast.13, f32[2,4]{1,0:T(2,128)S(1)} %bitcast.15, f32[2,2,64,256]{3,2,1,0:T(8,128)S(1)} %shard_map.180.base_ref, f32[2,2,64,256]{3,2,1,0:T(8,128)S(1)} %collective-permute-done.11.beside_ref), custom_call_target="tpu_custom_call" | custom-call | flops 10000000 | bytes 1048576 | tf_op jit(solution)/shard_map/pallas_call | solution.py:526
  29.0 0.1 collective-permute-start.12
  29.1 1.9 %shard_map.178 = (bf16[2,384,192]{2,1,0:T(8,128)(2,1)S(1)}, bf16[2,384,192]{2,1,0:T(8,128)(2,1)S(1)}, f32[1,2,64,256]{3,2,1,0:T(8,128)}) custom-call(f32[144,256]{1,0:T(8,128)S(1)} %get-tuple-element.45.refs_0_, f32[144,256]{1,0:T(8,128)S(1)} %collective-permute-done.5.refs_1_, f32[1,2,64,256]{3,2,1,0:T(8,128)S(1)} %get-tuple-element.46.refs_2_), custom_call_target="tpu_custom_call" | custom-call | flops 100000000 | bytes 1736704 | tf_op jit(solution)/shard_map/pallas_call | solution.py:526
  31.0 1.7 %collective-permute-done.6.side_a_ref = f32[2,128,256]{2,1,0:T(8,128)S(1)} collective-permute-done((f32[2,128,256]{2,1,0:T(8,128)S(1)}, f32[2,128,256]{2,1,0:T(8,128)S(1)}, u32[]{:S(2)}, u32[]{:S(2)}) %collective-permute-start.6) | collective-permute-done | bytes 262176 | tf_op jit(solution)/shard_map/ppermute | solution.py:566
  32.7 0.9 %shard_map.179 = (f32[2,64,256]{2,1,0:T(8,128)S(1)}, f32[2,2,64,256]{3,2,1,0:T(8,128)S(1)}, f32[384,256]{1,0:T(8,128)S(1)}) custom-call(f32[2,128,256]{2,1,0:T(8,128)S(1)} %pad_maximum_fusion.here_ref, f32[2,128,256]{2,1,0:T(8,128)S(1)} %collective-permute-done.6.side_a_ref, f32[2,128,256]{2,1,0:T(8,128)S(1)} %collective-permute-done.7.side_b_ref, ...), custom_call_target="tpu_custom_call" | custom-call | flops 1000000000 | bytes 2162688 | tf_op jit(solution)/shard_map/pallas_call | solution.py:526
  33.6 0.1 collective-permute-start.8
  33.7 1.5 %collective-permute-start.13 = (f32[2,64,256]{2,1,0:T(8,128)S(1)}, f32[2,64,256]{2,1,0:T(8,128)S(1)}, u32[]{:S(2)}, u32[]{:S(2)}) collective-permute-start(f32[2,64,256]{2,1,0:T(8,128)S(1)} %get-tuple-element.60), channel_id=1, source_target_pairs={{0,2},{2,0},{1,3},{3,1},{4,6},{6,4},{5,7},{7,5},{8,10},{10,8},{9,1... | collective-permute-start | bytes 393224 | tf_op jit(solution)/shard_map/ppermute | solution.py:683
  35.2 0.2 collective-permute-done.8.refs_1_.received_ref
  35.4 0.8 %shard_map.183 = f32[2,2,64,256]{3,2,1,0:T(8,128)} custom-call(f32[2,2,64,256]{3,2,1,0:T(8,128)S(1)} %get-tuple-element.58.own_ref, f32[384,256]{1,0:T(8,128)S(1)} %collective-permute-done.8.refs_1_.received_ref, f32[2,2,64,256]{3,2,1,0:T(8,128)S(1)} %shard_map.180.base_ref), custom_call_target="tpu_custom_call" | custom-call | flops 1000000 | bytes 1179648 | tf_op jit(solution)/shard_map/pallas_call | solution.py:526
  36.2 3.5 %collective-permute-done.13.refs_6_ = f32[2,64,256]{2,1,0:T(8,128)S(1)} collective-permute-done((f32[2,64,256]{2,1,0:T(8,128)S(1)}, f32[2,64,256]{2,1,0:T(8,128)S(1)}, u32[]{:S(2)}, u32[]{:S(2)}) %collective-permute-start.13) | collective-permute-done | bytes 131104 | tf_op jit(solution)/shard_map/ppermute | solution.py:683
  39.7 0.8 %shard_map.182 = (f32[1,2,64,256]{3,2,1,0:T(8,128)}, f32[1,2,64,256]{3,2,1,0:T(8,128)}) custom-call(f32[2,64,256]{2,1,0:T(8,128)S(1)} %get-tuple-element.51.refs_0_, f32[384,256]{1,0:T(8,128)S(1)} %collective-permute-done.8.refs_1_.received_ref, f32[1,2,64,256]{3,2,1,0:T(8,128)S(1)} %get-tuple-element.46.refs_2_, f32[1,2,64,256]{3,2,1,0:T(8,128)S(1)} %copy-done, ...), custom_call_target="tpu_custom_call" | custom-call | flops 1000000 | bytes 1441792 | tf_op jit(solution)/shard_map/pallas_call | solution.py:526
  (17 shorter events, 0.1 us)
Async XLA Ops:
  1.6 6.8 %collective-permute-start = (f32[136,256]{1,0:T(8,128)S(1)}, f32[136,256]{1,0:T(8,128)S(1)}, u32[]{:S(2)}, u32[]{:S(2)}) collective-permute-start(f32[136,256]{1,0:T(8,128)S(1)} %shard_map.175.plane_ref), channel_id=1, source_target_pairs={{0,4},{1,5},{8,12},{9,13},{4,0},{5,1},{12,8},{13,9},{2,6},{3,7},{1... | collective-permute-start | bytes 417800 | tf_op jit(solution)/shard_map/ppermute | solution.py:566
  4.7 3.7 %collective-permute-start.1 = (f32[136,256]{1,0:T(8,128)S(1)}, f32[136,256]{1,0:T(8,128)S(1)}, u32[]{:S(2)}, u32[]{:S(2)}) collective-permute-start(f32[136,256]{1,0:T(8,128)S(1)} %shard_map.175.plane_ref), channel_id=1, source_target_pairs={{4,8},{5,9},{8,4},{9,5},{0,1},{1,0},{12,13},{13,12},{6,10},{7,11},... | collective-permute-start | bytes 417800 | tf_op jit(solution)/shard_map/ppermute | solution.py:566
  8.4 8.9 %copy-start = (f32[1,2,64,256]{3,2,1,0:T(8,128)S(1)}, f32[1,2,64,256]{3,2,1,0:T(8,128)}, u32[]{:S(2)}) copy-start(f32[1,2,64,256]{3,2,1,0:T(8,128)} %refs_3_.2) | copy-start | bytes 393220
  8.4 8.9 %copy-start.1 = (f32[1,2,64,256]{3,2,1,0:T(8,128)S(1)}, f32[1,2,64,256]{3,2,1,0:T(8,128)}, u32[]{:S(2)}) copy-start(f32[1,2,64,256]{3,2,1,0:T(8,128)} %projected_ref.1) | copy-start | bytes 393220
  10.3 7.0 %collective-permute-start.2 = (f32[192,256]{1,0:T(8,128)S(1)}, f32[192,256]{1,0:T(8,128)S(1)}, u32[]{:S(2)}, u32[]{:S(2)}) collective-permute-start(f32[192,256]{1,0:T(8,128)S(1)} %get-tuple-element.42), channel_id=1, source_target_pairs={{0,4},{1,5},{8,12},{9,13},{4,0},{5,1},{12,8},{13,9},{2,6},{3,7},{1... | collective-permute-start | bytes 589832 | tf_op jit(solution)/shard_map/ppermute | solution.py:566
  13.3 4.1 %collective-permute-start.3 = (f32[192,256]{1,0:T(8,128)S(1)}, f32[192,256]{1,0:T(8,128)S(1)}, u32[]{:S(2)}, u32[]{:S(2)}) collective-permute-start(f32[192,256]{1,0:T(8,128)S(1)} %get-tuple-element.43), channel_id=1, source_target_pairs={{4,8},{5,9},{8,4},{9,5},{0,1},{1,0},{12,13},{13,12},{6,10},{7,11},... | collective-permute-start | bytes 589832 | tf_op jit(solution)/shard_map/ppermute | solution.py:566
  13.3 2.1 %collective-permute-start.4 = (f32[8,256]{1,0:T(8,128)S(1)}, f32[8,256]{1,0:T(8,128)S(1)}, u32[]{:S(2)}, u32[]{:S(2)}) collective-permute-start(f32[8,256]{1,0:T(8,128)S(1)} %get-tuple-element.44.rays_ref), channel_id=1, source_target_pairs={{0,1},{1,0},{2,3},{3,2},{4,5},{5,4},{6,7},{7,6},{8,9},{9,8},{10,11... | collective-permute-start | bytes 24584 | tf_op jit(solution)/shard_map/ppermute | solution.py:569
  13.8 5.2 %collective-permute-start.10 = (f32[2,72,256]{2,1,0:T(8,128)S(1)}, f32[2,72,256]{2,1,0:T(8,128)S(1)}, u32[]{:S(2)}, u32[]{:S(2)}) collective-permute-start(f32[2,72,256]{2,1,0:T(8,128)S(1)} %get-tuple-element.54), channel_id=1, source_target_pairs={{1,2},{2,1},{0,16},{3,19},{17,18},{18,17},{16,0},{19,3},{5,6},{6,5... | collective-permute-start | bytes 442376 | tf_op jit(solution)/shard_map/ppermute | solution.py:625
  15.3 3.7 %collective-permute-start.9 = (f32[2,72,256]{2,1,0:T(8,128)S(1)}, f32[2,72,256]{2,1,0:T(8,128)S(1)}, u32[]{:S(2)}, u32[]{:S(2)}) collective-permute-start(f32[2,72,256]{2,1,0:T(8,128)S(1)} %get-tuple-element.53), channel_id=1, source_target_pairs={{0,1},{1,0},{2,3},{3,2},{4,5},{5,4},{6,7},{7,6},{8,9},{9,8},{10,11... | collective-permute-start | bytes 442376 | tf_op jit(solution)/shard_map/ppermute | solution.py:569
  17.4 6.0 %collective-permute-start.5 = (f32[144,256]{1,0:T(8,128)S(1)}, f32[144,256]{1,0:T(8,128)S(1)}, u32[]{:S(2)}, u32[]{:S(2)}) collective-permute-start(f32[144,256]{1,0:T(8,128)S(1)} %get-tuple-element.45.refs_0_), channel_id=1, source_target_pairs={{0,2},{2,0},{1,3},{3,1},{4,6},{6,4},{5,7},{7,5},{8,10},{10,8},{9,1... | collective-permute-start | bytes 442376 | tf_op jit(solution)/shard_map/ppermute | solution.py:640
  19.5 8.8 %collective-permute-start.11 = (f32[2,2,64,256]{3,2,1,0:T(8,128)S(1)}, f32[2,2,64,256]{3,2,1,0:T(8,128)S(1)}, u32[]{:S(2)}, u32[]{:S(2)}) collective-permute-start(f32[2,2,64,256]{3,2,1,0:T(8,128)S(1)} %shard_map.180.base_ref), channel_id=1, source_target_pairs={{0,4},{2,0},{4,8},{6,2},{8,12},{10,6},{12,14},{14,10},{1,5},{3,1},... | collective-permute-start | bytes 786440 | tf_op jit(solution)/shard_map/ppermute | solution.py:657
  23.4 4.8 %copy-start.2 = (s32[4,2]{0,1:T(2,128)S(1)}, s32[4,2]{0,1:T(2,128)}, u32[]{:S(2)}) copy-start(s32[4,2]{0,1:T(2,128)} %param.24) | copy-start | bytes 100
  23.4 4.8 %copy-start.3 = (f32[4,2]{0,1:T(2,128)S(1)}, f32[4,2]{0,1:T(2,128)}, u32[]{:S(2)}) copy-start(f32[4,2]{0,1:T(2,128)} %param.25) | copy-start | bytes 100
  23.5 9.2 %collective-permute-start.6 = (f32[2,128,256]{2,1,0:T(8,128)S(1)}, f32[2,128,256]{2,1,0:T(8,128)S(1)}, u32[]{:S(2)}, u32[]{:S(2)}) collective-permute-start(f32[2,128,256]{2,1,0:T(8,128)S(1)} %pad_maximum_fusion.here_ref), channel_id=1, source_target_pairs={{0,4},{1,5},{8,12},{9,13},{4,0},{5,1},{12,8},{13,9},{2,6},{3,7},{1... | collective-permute-start | bytes 786440 | tf_op jit(solution)/shard_map/ppermute | solution.py:566
  24.6 8.2 %collective-permute-start.7 = (f32[2,128,256]{2,1,0:T(8,128)S(1)}, f32[2,128,256]{2,1,0:T(8,128)S(1)}, u32[]{:S(2)}, u32[]{:S(2)}) collective-permute-start(f32[2,128,256]{2,1,0:T(8,128)S(1)} %pad_maximum_fusion.here_ref), channel_id=1, source_target_pairs={{4,8},{5,9},{8,4},{9,5},{0,1},{1,0},{12,13},{13,12},{6,10},{7,11},... | collective-permute-start | bytes 786440 | tf_op jit(solution)/shard_map/ppermute | solution.py:566
  29.0 4.7 %collective-permute-start.12 = (f32[2,2,64,256]{3,2,1,0:T(8,128)S(1)}, f32[2,2,64,256]{3,2,1,0:T(8,128)S(1)}, u32[]{:S(2)}, u32[]{:S(2)}) collective-permute-start(f32[2,2,64,256]{3,2,1,0:T(8,128)S(1)} %get-tuple-element.56), channel_id=1, source_target_pairs={{0,1},{1,0},{2,3},{3,2},{4,5},{5,4},{6,7},{7,6},{8,9},{9,8},{10,11... | collective-permute-start | bytes 786440 | tf_op jit(solution)/shard_map/ppermute | solution.py:569
  33.6 1.8 %collective-permute-start.8 = (f32[384,256]{1,0:T(8,128)S(1)}, f32[384,256]{1,0:T(8,128)S(1)}, u32[]{:S(2)}, u32[]{:S(2)}) collective-permute-start(f32[384,256]{1,0:T(8,128)S(1)} %get-tuple-element.52), channel_id=1, source_target_pairs={{0,1},{1,0},{2,3},{3,2},{4,5},{5,4},{6,7},{7,6},{8,9},{9,8},{10,11... | collective-permute-start | bytes 1179656 | tf_op jit(solution)/shard_map/ppermute | solution.py:569
  33.7 6.0 %collective-permute-start.13 = (f32[2,64,256]{2,1,0:T(8,128)S(1)}, f32[2,64,256]{2,1,0:T(8,128)S(1)}, u32[]{:S(2)}, u32[]{:S(2)}) collective-permute-start(f32[2,64,256]{2,1,0:T(8,128)S(1)} %get-tuple-element.60), channel_id=1, source_target_pairs={{0,2},{2,0},{1,3},{3,1},{4,6},{6,4},{5,7},{7,5},{8,10},{10,8},{9,1... | collective-permute-start | bytes 393224 | tf_op jit(solution)/shard_map/ppermute | solution.py:683
